TPU v7x, 32 devices: a whole 2x2x4 slice. The times are simulated.
32 devices in a mesh: rows: 8 (over z, y), tp: 4 (over x, core).
Axes of the slice: x: 2, y: 2, z: 4, core: 2. Of those that a mesh axis runs over, the one named last changes fastest.
Arguments:
- layer_input: bfloat16 [8, 1536, 1024], P('rows', 'tp'), may hold values from -6 to 6
- cotangent: bfloat16 [8, 1536, 1024], P('rows', 'tp'), may hold values from -6 to 6
- segments: int32 [8, 1536], P('rows'), may hold values from 0 to 23, as said below
- valid_frames: int32 [8, 1536], P('rows'), may hold values from 0 to 1, as said below
- gain_first: bfloat16 [1024], replicated, may hold values from 0.5 to 1.5
- up_first: bfloat16 [1024, 4096], P(None, 'tp'), may hold values from -0.1875 to 0.1875
- down_first: bfloat16 [4096, 1024], P('tp'), may hold values from -0.09375 to 0.09375
- gain_attend: bfloat16 [1024], replicated, may hold values from 0.5 to 1.5
- query_weight: bfloat16 [1024, 1024], P(None, 'tp'), may hold values from -0.1875 to 0.1875
- key_weight: bfloat16 [1024, 1024], P(None, 'tp'), may hold values from -0.1875 to 0.1875
- value_weight: bfloat16 [1024, 1024], P(None, 'tp'), may hold values from -0.1875 to 0.1875
- attend_out: bfloat16 [1024, 1024], P('tp'), may hold values from -0.75 to 0.75
- pos_weight: bfloat16 [1024, 1024], P(None, 'tp'), may hold values from -0.25 to 0.25
- content_bias: bfloat16 [8, 128], P('tp'), may hold values from -3 to 3
- position_bias: bfloat16 [8, 128], P('tp'), may hold values from -3 to 3
- gain_conv: bfloat16 [1024], replicated, may hold values from 0.5 to 1.5
- point_in: bfloat16 [1024, 2, 1024], P(None, None, 'tp'), may hold values from -0.1875 to 0.1875
- depth_kernel: bfloat16 [5, 1024], P(None, 'tp'), may hold values from -2.5 to 2.5
- gain_inner: bfloat16 [1024], P('tp'), may hold values from 0.5 to 1.5
- point_out: bfloat16 [1024, 1024], P('tp'), may hold values from -0.1875 to 0.1875
- gain_second: bfloat16 [1024], replicated, may hold values from 0.5 to 1.5
- up_second: bfloat16 [1024, 4096], P(None, 'tp'), may hold values from -0.1875 to 0.1875
- down_second: bfloat16 [4096, 1024], P('tp'), may hold values from -0.09375 to 0.09375
- gain_final: bfloat16 [1024], replicated, may hold values from 0.5 to 1.5
Outputs:
- layer_output: bfloat16 [8, 1536, 1024], P('rows', 'tp')
- input_grad: float32 [8, 1536, 1024], P('rows', 'tp')
- grad_gain_first: float32 [1024], replicated
- grad_up_first: float32 [1024, 4096], P(None, 'tp')
- grad_down_first: float32 [4096, 1024], P('tp')
- grad_gain_attend: float32 [1024], replicated
- grad_query_weight: float32 [1024, 1024], P(None, 'tp')
- grad_key_weight: float32 [1024, 1024], P(None, 'tp')
- grad_value_weight: float32 [1024, 1024], P(None, 'tp')
- grad_attend_out: float32 [1024, 1024], P('tp')
- grad_pos_weight: float32 [1024, 1024], P(None, 'tp')
- grad_content_bias: float32 [8, 128], P('tp')
- grad_position_bias: float32 [8, 128], P('tp')
- grad_gain_conv: float32 [1024], replicated
- grad_point_in: float32 [1024, 2, 1024], P(None, None, 'tp')
- grad_depth_kernel: float32 [5, 1024], P(None, 'tp')
- grad_gain_inner: float32 [1024], P('tp')
- grad_point_out: float32 [1024, 1024], P('tp')
- grad_gain_second: float32 [1024], replicated
- grad_up_second: float32 [1024, 4096], P(None, 'tp')
- grad_down_second: float32 [4096, 1024], P('tp')
- grad_gain_final: float32 [1024], replicated
Inputs may be any that keep to these rules, and one draw needn't show every extreme that they name: `segments`: along each row, ids start at 0 and rise by one from utterance to utterance; padding slots, all at the row's end, carry the id one past the row's last utterance. Every utterance has at least 64 and at most 512 frames. `valid_frames`: 1 exactly on the slots of utterances; the padding slots of a row follow all of them.
All inputs are finite; a program needn't handle non-finite values.
Results may differ from a plain program's by a relative error of at most 0.025.
Values may be sent and summed in bfloat16 or wider, within the bound.
No kernel may reach another device: no remote copies, remote signals or barrier semaphores. Data moves between devices by JAX's collectives and lax.ppermute only.
A program may use at most 256 MiB of HBM per device.

v0:
```python
import math

import jax
import jax.numpy as jnp
from jax import lax
from jax.sharding import PartitionSpec as P

CONV = 1024
QUERY_BLOCK = 512


EPS = 1e-05
MASKED = -1e30
F32 = jnp.float32
B16 = jnp.bfloat16


def normalize(values, gain):
    mean = jnp.mean(values, axis=-1, keepdims=True)
    centered = values - mean
    inverse = lax.rsqrt(jnp.mean(centered * centered, axis=-1, keepdims=True) + EPS)
    unit = centered * inverse
    return (unit * gain.astype(F32), unit, inverse)


def normalize_back(grad, unit, inverse, gain):
    scaled = grad * gain.astype(F32)
    first = jnp.mean(scaled, axis=-1, keepdims=True)
    second = jnp.mean(scaled * unit, axis=-1, keepdims=True)
    result = inverse * (scaled - first - unit * second)
    return (result, jnp.sum(grad * unit, axis=tuple(range(grad.ndim - 1))))


def swish_slope(values):
    gate = jax.nn.sigmoid(values)
    return gate * (1.0 + values * (1.0 - gate))


def distance_table(slots, width):
    place = (slots - 1 - jnp.arange(2 * slots)).astype(F32)
    column = jnp.arange(width)
    rate = jnp.exp(-(column - column % 2).astype(F32) * (math.log(10000.0) / width))
    angle = place[:, None] * rate[None, :]
    return jnp.where(column[None, :] % 2 == 0, jnp.sin(angle), jnp.cos(angle))


def skew(grid, slots):
    heads, block, _ = grid.shape
    width = slots + block - 1
    flat = grid.reshape(heads, block * (width + 1))
    cut = lax.slice_in_dim(flat, block - 1, block - 1 + block * width, axis=1)
    return cut.reshape(heads, block, width)[:, :, :slots]


def unskew(grad, block):
    heads, _, slots = grad.shape
    width = slots + block - 1
    padded = jnp.concatenate([grad, jnp.zeros((heads, block, width - slots), grad.dtype)], 2)
    flat = padded.reshape(heads, block * width)
    whole = jnp.concatenate(
        [jnp.zeros((heads, block - 1), grad.dtype), flat, jnp.zeros((heads, 1), grad.dtype)], 1
    )
    return whole.reshape(heads, block, slots + block)


def shift_time(values, offset, fill):
    if offset == 0:
        return values
    filler = jnp.full(values.shape[:1] + (abs(offset),) + values.shape[2:], fill, values.dtype)
    if offset > 0:
        return jnp.concatenate([values[:, offset:], filler], 1)
    return jnp.concatenate([filler, values[:, :offset]], 1)


def neighbour_mask(segments, valid, offset):
    other_segment = shift_time(segments, offset, -1)
    other_valid = shift_time(valid, offset, 0)
    return ((other_segment == segments) & (other_valid == 1)).astype(F32)


def allow_block(segment_row, valid_row, start, block):
    slots = segment_row.shape[0]
    same = segment_row[start : start + block, None] == segment_row[None, :]
    itself = (jnp.arange(block) + start)[:, None] == jnp.arange(slots)[None, :]
    return same & ((valid_row[None, :] == 1) | itself)


def widen(normed):
    return lax.all_gather(normed.astype(B16), "tp", axis=1, tiled=True)


def narrow(partial_out):
    return lax.psum_scatter(partial_out, "tp", scatter_dimension=1, tiled=True)


def widen_back(grad):
    return lax.all_gather(grad.astype(B16), "tp", axis=1, tiled=True)


def narrow_back(partial_grad):
    return lax.psum_scatter(
        partial_grad.astype(jnp.bfloat16), "tp", scatter_dimension=1, tiled=True
    ).astype(jnp.float32)


def ffn_forward(values, gain, weight_up, weight_down):
    normed, unit, inverse = normalize(values, gain)
    wide = widen(normed)
    pre = jnp.einsum("rld,df->rlf", wide, weight_up, preferred_element_type=F32)
    act = (pre * jax.nn.sigmoid(pre)).astype(B16)
    part = jnp.einsum("rlf,fd->rld", act, weight_down, preferred_element_type=F32)
    return (values + 0.5 * narrow(part), (unit, inverse, wide, pre, act))


def ffn_backward(grad, kept, gain, weight_up, weight_down):
    unit, inverse, wide, pre, act = kept
    cot = widen_back(0.5 * grad)
    d_act = jnp.einsum("rld,fd->rlf", cot, weight_down, preferred_element_type=F32)
    d_pre = (d_act * swish_slope(pre)).astype(B16)
    grad_down = jnp.einsum("rlf,rld->fd", act, cot, preferred_element_type=F32)
    grad_up = jnp.einsum("rld,rlf->df", wide, d_pre, preferred_element_type=F32)
    d_norm = narrow_back(jnp.einsum("rlf,df->rld", d_pre, weight_up, preferred_element_type=F32))
    d_in, grad_gain = normalize_back(d_norm, unit, inverse, gain)
    return (grad + d_in, grad_gain, (grad_up, grad_down))


def block_scores(q_content_b, q_position_b, key_row, rel, segment_row, valid_row, start):
    block, slots, size = (q_content_b.shape[0], key_row.shape[0], key_row.shape[2])
    window = lax.slice_in_dim(rel, slots - block - start, 2 * slots - start, axis=0)
    raw = jnp.einsum("qhd,khd->hqk", q_content_b, key_row, preferred_element_type=F32)
    grid = jnp.einsum("qhd,whd->hqw", q_position_b, window, preferred_element_type=F32)
    raw = raw + skew(grid, slots)
    allow = allow_block(segment_row, valid_row, start, block)
    return (jnp.where(allow[None], raw * size ** (-0.5), MASKED), window)


def row_forward(item, rel):
    q_content_row, q_position_row, key_row, value_row, segment_row, valid_row = item
    slots = key_row.shape[0]
    outs, totals = ([], [])
    for start in range(0, slots, QUERY_BLOCK):
        scores, window = block_scores(
            q_content_row[start : start + QUERY_BLOCK],
            q_position_row[start : start + QUERY_BLOCK],
            key_row,
            rel,
            segment_row,
            valid_row,
            start,
        )
        top = jnp.max(scores, axis=-1, keepdims=True)
        weights = jnp.exp(scores - top)
        total = jnp.sum(weights, axis=-1, keepdims=True)
        probs = (weights / total).astype(B16)
        outs.append(jnp.einsum("hqk,khd->qhd", probs, value_row, preferred_element_type=F32))
        totals.append((top + jnp.log(total))[..., 0])
    return (jnp.concatenate(outs, 0), jnp.concatenate(totals, 1))


def row_backward(d_rel, item, rel):
    (
        q_content_row,
        q_position_row,
        key_row,
        value_row,
        segment_row,
        valid_row,
        d_heads_row,
        sums_row,
    ) = item
    slots, heads, size = key_row.shape
    d_content, d_position = ([], [])
    d_key = jnp.zeros((slots, heads, size), F32)
    d_value = jnp.zeros((slots, heads, size), F32)
    for start in range(0, slots, QUERY_BLOCK):
        stop = start + QUERY_BLOCK
        q_content_b = q_content_row[start:stop]
        q_position_b = q_position_row[start:stop]
        scores, window = block_scores(
            q_content_b, q_position_b, key_row, rel, segment_row, valid_row, start
        )
        probs = jnp.exp(scores - sums_row[:, start:stop, None])
        d_heads_b = d_heads_row[start:stop]
        d_probs = jnp.einsum("qhd,khd->hqk", d_heads_b, value_row, preferred_element_type=F32)
        d_scores = probs * (d_probs - jnp.sum(probs * d_probs, axis=-1, keepdims=True))
        d_raw = (d_scores * size ** (-0.5)).astype(B16)
        d_content.append(jnp.einsum("hqk,khd->qhd", d_raw, key_row, preferred_element_type=F32))
        d_key = d_key + jnp.einsum("hqk,qhd->khd", d_raw, q_content_b, preferred_element_type=F32)
        d_grid = unskew(d_raw, QUERY_BLOCK)
        d_position.append(jnp.einsum("hqw,whd->qhd", d_grid, window, preferred_element_type=F32))
        d_window = jnp.einsum("hqw,qhd->whd", d_grid, q_position_b, preferred_element_type=F32)
        d_rel = d_rel.at[slots - QUERY_BLOCK - start : 2 * slots - start].add(d_window)
        d_value = d_value + jnp.einsum(
            "hqk,qhd->khd", probs.astype(B16), d_heads_b, preferred_element_type=F32
        )
    return (d_rel, (jnp.concatenate(d_content, 0), jnp.concatenate(d_position, 0), d_key, d_value))


def attend_forward(
    values,
    gain,
    query_weight,
    key_weight,
    value_weight,
    attend_out,
    pos_weight,
    content_bias,
    position_bias,
    segments,
    valid,
):
    normed, unit, inverse = normalize(values, gain)
    wide = widen(normed)
    count, slots, width = wide.shape
    heads, size = content_bias.shape
    shape = (count, slots, heads, size)
    query = jnp.einsum("rld,dk->rlk", wide, query_weight, preferred_element_type=F32).reshape(shape)
    key = (
        jnp.einsum("rld,dk->rlk", wide, key_weight, preferred_element_type=F32)
        .astype(B16)
        .reshape(shape)
    )
    value = (
        jnp.einsum("rld,dk->rlk", wide, value_weight, preferred_element_type=F32)
        .astype(B16)
        .reshape(shape)
    )
    q_content = (query + content_bias.astype(F32)).astype(B16)
    q_position = (query + position_bias.astype(F32)).astype(B16)
    table = distance_table(slots, width).astype(B16)
    rel = (
        jnp.dot(table, pos_weight, preferred_element_type=F32)
        .astype(B16)
        .reshape(2 * slots, heads, size)
    )
    outs, sums = lax.map(
        lambda item: row_forward(item, rel), (q_content, q_position, key, value, segments, valid)
    )
    heads_out = outs.astype(B16).reshape(count, slots, heads * size)
    part = jnp.einsum("rlk,kd->rld", heads_out, attend_out, preferred_element_type=F32)
    kept = (unit, inverse, wide, q_content, q_position, key, value, rel, table, sums, heads_out)
    return (values + narrow(part), kept)


def attend_backward(
    grad, kept, gain, query_weight, key_weight, value_weight, attend_out, segments, valid
):
    unit, inverse, wide, q_content, q_position, key, value, rel, table, sums, heads_out = kept
    count, slots, heads, size = key.shape
    cot = widen_back(grad)
    d_heads = jnp.einsum("rld,kd->rlk", cot, attend_out, preferred_element_type=F32).astype(B16)
    d_heads = d_heads.reshape(count, slots, heads, size)
    grad_attend_out = jnp.einsum("rlk,rld->kd", heads_out, cot, preferred_element_type=F32)
    d_rel, (d_content, d_position, d_key, d_value) = lax.scan(
        lambda carry, item: row_backward(carry, item, rel),
        jnp.zeros((2 * slots, heads, size), F32),
        (q_content, q_position, key, value, segments, valid, d_heads, sums),
    )
    grad_content = jnp.sum(d_content, axis=(0, 1))
    grad_position = jnp.sum(d_position, axis=(0, 1))
    flat = (count, slots, heads * size)
    d_query = (d_content + d_position).astype(B16).reshape(flat)
    d_key = d_key.astype(B16).reshape(flat)
    d_value = d_value.astype(B16).reshape(flat)
    grad_query = jnp.einsum("rld,rlk->dk", wide, d_query, preferred_element_type=F32)
    grad_key = jnp.einsum("rld,rlk->dk", wide, d_key, preferred_element_type=F32)
    grad_value = jnp.einsum("rld,rlk->dk", wide, d_value, preferred_element_type=F32)
    grad_pos = jnp.einsum(
        "td,tk->dk",
        table,
        d_rel.astype(B16).reshape(2 * slots, heads * size),
        preferred_element_type=F32,
    )
    d_norm = jnp.einsum("rlk,dk->rld", d_query, query_weight, preferred_element_type=F32)
    d_norm = d_norm + jnp.einsum("rlk,dk->rld", d_key, key_weight, preferred_element_type=F32)
    d_norm = d_norm + jnp.einsum("rlk,dk->rld", d_value, value_weight, preferred_element_type=F32)
    d_in, grad_gain = normalize_back(narrow_back(d_norm), unit, inverse, gain)
    grads = (
        grad_query,
        grad_key,
        grad_value,
        grad_attend_out,
        grad_pos,
        grad_content,
        grad_position,
    )
    return (grad + d_in, grad_gain, grads)


def conv_forward(values, gain, point_in, depth_kernel, gain_inner, point_out, segments, valid):
    normed, unit, inverse = normalize(values, gain)
    wide = widen(normed)
    mixed = jnp.einsum("rld,dgc->rlgc", wide, point_in, preferred_element_type=F32)
    gate = jax.nn.sigmoid(mixed[:, :, 1])
    glu = mixed[:, :, 0] * gate
    kernel = depth_kernel.astype(F32)
    taps = kernel.shape[0]
    depth = jnp.zeros_like(glu)
    for tap in range(taps):
        offset = tap - taps // 2
        depth = depth + kernel[tap] * neighbour_mask(segments, valid, offset)[
            ..., None
        ] * shift_time(glu, offset, 0.0)
    total = lax.psum(jnp.sum(depth, axis=-1, keepdims=True), "tp")
    mean = total / CONV
    centered = depth - mean
    spread = lax.psum(jnp.sum(centered * centered, axis=-1, keepdims=True), "tp")
    variance = spread / CONV
    inner_inverse = lax.rsqrt(variance + EPS)
    inner_unit = centered * inner_inverse
    depth_norm = inner_unit * gain_inner.astype(F32)
    inner = (depth_norm * jax.nn.sigmoid(depth_norm)).astype(B16)
    part = jnp.einsum("rlc,cd->rld", inner, point_out, preferred_element_type=F32)
    kept = (unit, inverse, wide, mixed, gate, glu, inner_unit, inner_inverse, depth_norm, inner)
    return (values + narrow(part), kept)


def conv_backward(grad, kept, gain, point_in, depth_kernel, gain_inner, point_out, segments, valid):
    unit, inverse, wide, mixed, gate, glu, inner_unit, inner_inverse, depth_norm, inner = kept
    cot = widen_back(grad)
    grad_point_out = jnp.einsum("rlc,rld->cd", inner, cot, preferred_element_type=F32)
    d_act = jnp.einsum("rld,cd->rlc", cot, point_out, preferred_element_type=F32)
    d_depth_norm = d_act * swish_slope(depth_norm)
    grad_gain_inner = jnp.sum(d_depth_norm * inner_unit, axis=(0, 1))
    scaled = d_depth_norm * gain_inner.astype(F32)
    first, second = lax.psum(
        (
            jnp.sum(scaled, axis=-1, keepdims=True),
            jnp.sum(scaled * inner_unit, axis=-1, keepdims=True),
        ),
        "tp",
    )
    d_depth = inner_inverse * (scaled - first / CONV - inner_unit * (second / CONV))
    kernel = depth_kernel.astype(F32)
    taps = kernel.shape[0]
    d_glu = jnp.zeros_like(d_depth)
    kernel_rows = []
    for tap in range(taps):
        offset = tap - taps // 2
        weighted = d_depth * neighbour_mask(segments, valid, offset)[..., None]
        d_glu = d_glu + shift_time(kernel[tap] * weighted, -offset, 0.0)
        kernel_rows.append(jnp.sum(weighted * shift_time(glu, offset, 0.0), axis=(0, 1)))
    grad_kernel = jnp.stack(kernel_rows, 0)
    d_mixed = jnp.stack([d_glu * gate, d_glu * mixed[:, :, 0] * gate * (1.0 - gate)], 2).astype(B16)
    grad_point_in = jnp.einsum("rld,rlgc->dgc", wide, d_mixed, preferred_element_type=F32)
    d_norm = narrow_back(jnp.einsum("rlgc,dgc->rld", d_mixed, point_in, preferred_element_type=F32))
    d_in, grad_gain = normalize_back(d_norm, unit, inverse, gain)
    return (grad + d_in, grad_gain, (grad_point_in, grad_kernel, grad_gain_inner, grad_point_out))


def body(
    layer_input,
    cotangent,
    segments,
    valid_frames,
    gain_first,
    up_first,
    down_first,
    gain_attend,
    query_weight,
    key_weight,
    value_weight,
    attend_out,
    pos_weight,
    content_bias,
    position_bias,
    gain_conv,
    point_in,
    depth_kernel,
    gain_inner,
    point_out,
    gain_second,
    up_second,
    down_second,
    gain_final,
):
    values = layer_input.astype(F32)
    values, kept_first = ffn_forward(values, gain_first, up_first, down_first)
    values, kept_attend = attend_forward(
        values,
        gain_attend,
        query_weight,
        key_weight,
        value_weight,
        attend_out,
        pos_weight,
        content_bias,
        position_bias,
        segments,
        valid_frames,
    )
    values, kept_conv = conv_forward(
        values, gain_conv, point_in, depth_kernel, gain_inner, point_out, segments, valid_frames
    )
    values, kept_second = ffn_forward(values, gain_second, up_second, down_second)
    final, final_unit, final_inverse = normalize(values, gain_final)
    layer_output = final.astype(B16)
    grad, sum_final = normalize_back(cotangent.astype(F32), final_unit, final_inverse, gain_final)
    grad, sum_second, second_grads = ffn_backward(
        grad, kept_second, gain_second, up_second, down_second
    )
    grad, sum_conv, conv_grads = conv_backward(
        grad,
        kept_conv,
        gain_conv,
        point_in,
        depth_kernel,
        gain_inner,
        point_out,
        segments,
        valid_frames,
    )
    grad, sum_attend, attend_grads = attend_backward(
        grad,
        kept_attend,
        gain_attend,
        query_weight,
        key_weight,
        value_weight,
        attend_out,
        segments,
        valid_frames,
    )
    grad, sum_first, first_grads = ffn_backward(grad, kept_first, gain_first, up_first, down_first)
    summed = (
        lax.psum(first_grads[0].astype(jnp.bfloat16), "rows").astype(jnp.float32),
        lax.psum(first_grads[1].astype(jnp.bfloat16), "rows").astype(jnp.float32),
        lax.psum(attend_grads[0].astype(jnp.bfloat16), "rows").astype(jnp.float32),
        lax.psum(attend_grads[1].astype(jnp.bfloat16), "rows").astype(jnp.float32),
        lax.psum(attend_grads[2].astype(jnp.bfloat16), "rows").astype(jnp.float32),
        lax.psum(attend_grads[3].astype(jnp.bfloat16), "rows").astype(jnp.float32),
        lax.psum(attend_grads[4].astype(jnp.bfloat16), "rows").astype(jnp.float32),
        lax.psum(attend_grads[5].astype(jnp.bfloat16), "rows").astype(jnp.float32),
        lax.psum(attend_grads[6].astype(jnp.bfloat16), "rows").astype(jnp.float32),
        lax.psum(conv_grads[0].astype(jnp.bfloat16), "rows").astype(jnp.float32),
        lax.psum(conv_grads[1].astype(jnp.bfloat16), "rows").astype(jnp.float32),
        lax.psum(conv_grads[2].astype(jnp.bfloat16), "rows").astype(jnp.float32),
        lax.psum(conv_grads[3].astype(jnp.bfloat16), "rows").astype(jnp.float32),
        lax.psum(second_grads[0].astype(jnp.bfloat16), "rows").astype(jnp.float32),
        lax.psum(second_grads[1].astype(jnp.bfloat16), "rows").astype(jnp.float32),
    )
    first_grads = summed[0:2]
    attend_grads = summed[2:9]
    conv_grads = summed[9:13]
    second_grads = summed[13:15]
    gains = lax.psum((sum_first, sum_attend, sum_conv, sum_second, sum_final), ("rows", "tp"))
    return (
        layer_output,
        grad,
        gains[0],
        first_grads[0],
        first_grads[1],
        gains[1],
        attend_grads[0],
        attend_grads[1],
        attend_grads[2],
        attend_grads[3],
        attend_grads[4],
        attend_grads[5],
        attend_grads[6],
        gains[2],
        conv_grads[0],
        conv_grads[1],
        conv_grads[2],
        conv_grads[3],
        gains[3],
        second_grads[0],
        second_grads[1],
        gains[4],
    )


def solution(mesh):
    in_specs = (
        P("rows", "tp", None),
        P("rows", "tp", None),
        P("rows", None),
        P("rows", None),
        P(),
        P(None, "tp"),
        P("tp", None),
        P(),
        P(None, "tp"),
        P(None, "tp"),
        P(None, "tp"),
        P("tp", None),
        P(None, "tp"),
        P("tp", None),
        P("tp", None),
        P(),
        P(None, None, "tp"),
        P(None, "tp"),
        P("tp"),
        P("tp", None),
        P(),
        P(None, "tp"),
        P("tp", None),
        P(),
    )
    out_specs = (
        P("rows", "tp", None),
        P("rows", "tp", None),
        P(),
        P(None, "tp"),
        P("tp", None),
        P(),
        P(None, "tp"),
        P(None, "tp"),
        P(None, "tp"),
        P("tp", None),
        P(None, "tp"),
        P("tp", None),
        P("tp", None),
        P(),
        P(None, None, "tp"),
        P(None, "tp"),
        P("tp"),
        P("tp", None),
        P(),
        P(None, "tp"),
        P("tp", None),
        P(),
    )
    return jax.shard_map(body, mesh=mesh, in_specs=in_specs, out_specs=out_specs, check_vma=False)
```

profile of v0, /device:TPU:0, one launch (start us, length us, event | category | flops | bytes accessed | tf_op | source)
XLA Modules:
  0.0 1816.5 jit_solution(5114369533336170171)
XLA Ops:
  12.8 31.3 %all-gather.9.cloned.1.call-done = bf16[1,1536,1024]{2,1,0:T(8,128)(2,1)} async-done(((bf16[1,384,1024]{2,1,0:T(8,128)(2,1)}), bf16[1,1536,1024]{2,1,0:T(8,128)(2,1)}) %all-gather.9.cloned.1.call-update) | async-done | bytes 3145744 | tf_op jit(solution)/shard_map/all_gather | solution.py:89
  58.9 57.9 %reduce-scatter.9.cloned.1.call-done = f32[1,384,1024]{2,1,0:T(8,128)} async-done(((f32[1,1536,1024]{2,1,0:T(8,128)}), f32[1,384,1024]{2,1,0:T(8,128)}) %reduce-scatter.9.cloned.1.call-update) | async-done | bytes 1572880 | tf_op jit(solution)/shard_map/reduce_scatter | solution.py:93
  121.5 46.3 %fusion.371 = bf16[3072,1024]{1,0:T(8,128)(2,1)S(1)} fusion(f32[1024]{0:T(1024)S(1)} %multiply_exponential_fusion, f32[3072]{0:T(1024)S(1)} %subtract_convert_fusion, pred[1024]{0:T(1024)(128)(4,1)S(1)} %fusion.268), kind=kLoop, calls=%fused_computation.6.clone.1.clone.clone.clone.1 | loop fusion | flops 9437184 | bytes 6308864 | tf_op jit(solution)/shard_map/dot_general | solution.py:232
  204.4 17.5 reshape.1455
  242.2 17.5 reshape.1453
  303.5 17.4 reshape.1451
  335.3 57.9 %reduce-scatter.11.cloned.1.call-done = f32[1,384,1024]{2,1,0:T(8,128)} async-done(((f32[1,1536,1024]{2,1,0:T(8,128)}), f32[1,384,1024]{2,1,0:T(8,128)}) %reduce-scatter.11.cloned.1.call-update) | async-done | bytes 1572880 | tf_op jit(solution)/shard_map/reduce_scatter | solution.py:93
  398.1 28.3 %all-gather.13.cloned.1.call-done = bf16[1,1536,1024]{2,1,0:T(8,128)(2,1)} async-done(((bf16[1,384,1024]{2,1,0:T(8,128)(2,1)}), bf16[1,1536,1024]{2,1,0:T(8,128)(2,1)}) %all-gather.13.cloned.1.call-update) | async-done | bytes 3145744 | tf_op jit(solution)/shard_map/all_gather | solution.py:89
  456.0 59.2 %reduce-scatter.13.cloned.1.call-done = f32[1,384,1024]{2,1,0:T(8,128)} async-done(((f32[1,1536,1024]{2,1,0:T(8,128)}), f32[1,384,1024]{2,1,0:T(8,128)}) %reduce-scatter.13.cloned.1.call-update) | async-done | bytes 1572880 | tf_op jit(solution)/shard_map/reduce_scatter | solution.py:93
  519.7 28.7 %all-gather.15.cloned.1.call-done = bf16[1,1536,1024]{2,1,0:T(8,128)(2,1)} async-done(((bf16[1,384,1024]{2,1,0:T(8,128)(2,1)}), bf16[1,1536,1024]{2,1,0:T(8,128)(2,1)}) %all-gather.15.cloned.1.call-update) | async-done | bytes 3145744 | tf_op jit(solution)/shard_map/all_gather | solution.py:89
  563.4 57.8 %reduce-scatter.15.cloned.1.call-done = f32[1,384,1024]{2,1,0:T(8,128)} async-done(((f32[1,1536,1024]{2,1,0:T(8,128)}), f32[1,384,1024]{2,1,0:T(8,128)}) %reduce-scatter.15.cloned.1.call-update) | async-done | bytes 1572880 | tf_op jit(solution)/shard_map/reduce_scatter | solution.py:93
  626.6 28.7 %all-gather.17.cloned.1.call-done = bf16[1,1536,1024]{2,1,0:T(8,128)(2,1)} async-done(((bf16[1,384,1024]{2,1,0:T(8,128)(2,1)}), bf16[1,1536,1024]{2,1,0:T(8,128)(2,1)}) %all-gather.17.cloned.1.call-update) | async-done | bytes 3145744 | tf_op jit(solution)/shard_map/all_gather | solution.py:97
  670.5 38.1 %reduce-scatter.17.cloned.1.call-done = bf16[1,384,1024]{2,1,0:T(8,128)(2,1)} async-done(((bf16[1,1536,1024]{2,1,0:T(8,128)(2,1)}), bf16[1,384,1024]{2,1,0:T(8,128)(2,1)}) %reduce-scatter.17.cloned.1.call-update) | async-done | bytes 786448 | tf_op jit(solution)/shard_map/reduce_scatter | solution.py:101
  714.7 28.6 %all-gather.19.cloned.1.call-done = bf16[1,1536,1024]{2,1,0:T(8,128)(2,1)} async-done(((bf16[1,384,1024]{2,1,0:T(8,128)(2,1)}), bf16[1,1536,1024]{2,1,0:T(8,128)(2,1)}) %all-gather.19.cloned.1.call-update) | async-done | bytes 3145744 | tf_op jit(solution)/shard_map/all_gather | solution.py:97
  777.7 39.1 %reduce-scatter.19.cloned.1.call-done = bf16[1,384,1024]{2,1,0:T(8,128)(2,1)} async-done(((bf16[1,1536,1024]{2,1,0:T(8,128)(2,1)}), bf16[1,384,1024]{2,1,0:T(8,128)(2,1)}) %reduce-scatter.19.cloned.1.call-update) | async-done | bytes 786448 | tf_op jit(solution)/shard_map/reduce_scatter | solution.py:101
  825.8 24.3 %all-gather.21.cloned.1.call-done = bf16[1,1536,1024]{2,1,0:T(8,128)(2,1)} async-done(((bf16[1,384,1024]{2,1,0:T(8,128)(2,1)}), bf16[1,1536,1024]{2,1,0:T(8,128)(2,1)}) %all-gather.21.cloned.1.call-update) | async-done | bytes 3145744 | tf_op jit(solution)/shard_map/all_gather | solution.py:97
  926.5 72.1 %dynamic-update-slice.13 = bf16[2,1048576]{1,0:T(2,128)(2,1)} dynamic-update-slice(bf16[2,1048576]{1,0:T(2,128)(2,1)} %dynamic-update-slice.12, bf16[2,1048064]{1,0:T(2,128)(2,1)} %reshape.1466, s32[]{} %constant.291, s32[]{} %constant.292) | dynamic-update-slice | bytes 8384516
  1021.2 72.1 %dynamic-update-slice.16 = bf16[2,1048576]{1,0:T(2,128)(2,1)} dynamic-update-slice(bf16[2,1048576]{1,0:T(2,128)(2,1)} %dynamic-update-slice.15, bf16[2,1048064]{1,0:T(2,128)(2,1)} %reshape.1464, s32[]{} %constant.291, s32[]{} %constant.292) | dynamic-update-slice | bytes 8384516
  1115.5 71.7 %dynamic-update-slice.19 = bf16[2,1048576]{1,0:T(2,128)(2,1)} dynamic-update-slice(bf16[2,1048576]{1,0:T(2,128)(2,1)} %dynamic-update-slice.18, bf16[2,1048064]{1,0:T(2,128)(2,1)} %reshape.1462, s32[]{} %constant.291, s32[]{} %constant.292) | dynamic-update-slice | bytes 8384516
  1203.9 38.0 %reduce-scatter.21.cloned.1.call-done = bf16[1,384,1024]{2,1,0:T(8,128)(2,1)} async-done(((bf16[1,1536,1024]{2,1,0:T(8,128)(2,1)}), bf16[1,384,1024]{2,1,0:T(8,128)(2,1)}) %reduce-scatter.21.cloned.1.call-update) | async-done | bytes 786448 | tf_op jit(solution)/shard_map/reduce_scatter | solution.py:101
  1320.1 48.8 %fusion.243 = bf16[1024,256]{1,0:T(8,128)(2,1)} fusion(bf16[3072,256]{0,1:T(8,128)(2,1)S(1)} %bitcast.396, f32[1024]{0:T(1024)S(1)} %copy-done.111, f32[3072]{0:T(1024)S(1)} %copy-done.106, pred[1024]{0:T(1024)(128)(4,1)S(1)} %copy-done.142), kind=kOutput, calls=%fused_computation.276 | convolution fusion | flops 1620312064 | bytes 2114560 | tf_op jit(solution)/shard_map/td,tk->dk/dot_general | solution.py:268
  1379.2 22.3 %all-reduce.18 = (bf16[2,128]{1,0:T(2,128)(2,1)S(1)}, bf16[2,128]{1,0:T(2,128)(2,1)S(1)}, bf16[5,256]{1,0:T(8,128)(2,1)S(1)}, bf16[256]{0:T(256)(128)(2,1)S(1)}) all-reduce(bf16[2,128]{1,0:T(2,128)(2,1)S(1)} %add_convert_fusion.4, bf16[2,128]{1,0:T(2,128)(2,1)S(1)} %add_convert_fusion.3, ...), channel_id=1, replica_groups=mesh['rows'=8,'tp'=4] {'rows'}, use_global_device_ids=true, to_apply=%region_59.60 | all-reduce | flops 2048 | bytes 8192 | tf_op jit(solution)/shard_map/psum | solution.py:433
  1405.9 41.5 %all-reduce.16 = (f32[1024]{0:T(1024)}, f32[1024]{0:T(1024)}, f32[1024]{0:T(1024)}, f32[1024]{0:T(1024)}, f32[1024]{0:T(1024)}) all-reduce(f32[1024]{0:T(1024)S(1)} %get-tuple-element.202, f32[1024]{0:T(1024)S(1)} %get-tuple-element.200, f32[1024]{0:T(1024)S(1)} %copy-done.104, ...), channel_id=1, replica_groups=mesh['rows'=8,'tp'=4] {'rows','tp'}, use_global_device_ids=true, to_apply=%region_46.47 | all-reduce | flops 5120 | bytes 40960 | tf_op jit(solution)/shard_map/psum | solution.py:446
  1450.5 338.7 %all-reduce.22.cloned.1.call-done = (bf16[1024,2,256]{2,0,1:T(8,128)(2,1)}, bf16[1024,1024]{1,0:T(8,128)(2,1)}, bf16[1024,1024]{1,0:T(8,128)(2,1)}, bf16[1024,25...) async-done(((bf16[1024,2,256]{2,0,1:T(8,128)(2,1)}, ...) | async-done | bytes 12582928 | tf_op jit(solution)/shard_map/psum | solution.py:435
  (557 shorter events, 516.8 us)
Async XLA Ops:
  7.2 549.8 %copy-start = (bf16[1024,1024]{1,0:T(8,128)(2,1)S(1)}, bf16[1024,1024]{1,0:T(8,128)(2,1)}, u32[]{:S(2)}) copy-start(bf16[1024,1024]{1,0:T(8,128)(2,1)} %param.52) | copy-start | bytes 6291460
  7.2 36.9 %all-gather.9.cloned.1.call-start = ((), (), s32[]{:S(2)}) async-start(), calls=%async_computation.8 | async-start | bytes 3932160 | tf_op jit(solution)/shard_map/all_gather | solution.py:89
  12.8 104.0 %reduce-scatter.9.cloned.1.call-start = ((), (), s32[]{:S(2)}) async-start(), calls=%async_computation.9 | async-start | bytes 7864320 | tf_op jit(solution)/shard_map/reduce_scatter | solution.py:93
  58.2 117.4 %all-gather.11.cloned.1.call-start = ((), (), s32[]{:S(2)}) async-start(), calls=%async_computation.10 | async-start | bytes 3932160 | tf_op jit(solution)/shard_map/all_gather | solution.py:89
  58.9 59.9 %copy-start.88 = (f32[1024]{0:T(1024)}, f32[1024]{0:T(1024)S(1)}, u32[]{:S(2)}) copy-start(f32[1024]{0:T(1024)S(1)} %convert_element_type.376) | copy-start | bytes 12292
  120.7 272.5 %reduce-scatter.11.cloned.1.call-start = ((), (), s32[]{:S(2)}) async-start(), calls=%async_computation.11 | async-start | bytes 7864320 | tf_op jit(solution)/shard_map/reduce_scatter | solution.py:93
  334.7 91.7 %all-gather.13.cloned.1.call-start = ((), (), s32[]{:S(2)}) async-start(), calls=%async_computation.12 | async-start | bytes 3932160 | tf_op jit(solution)/shard_map/all_gather | solution.py:89
  397.6 117.6 %reduce-scatter.13.cloned.1.call-start = ((), (), s32[]{:S(2)}) async-start(), calls=%async_computation.13 | async-start | bytes 7864320 | tf_op jit(solution)/shard_map/reduce_scatter | solution.py:93
  455.3 93.0 %all-gather.15.cloned.1.call-start = ((), (), s32[]{:S(2)}) async-start(), calls=%async_computation.14 | async-start | bytes 3932160 | tf_op jit(solution)/shard_map/all_gather | solution.py:89
  519.7 101.6 %reduce-scatter.15.cloned.1.call-start = ((), (), s32[]{:S(2)}) async-start(), calls=%async_computation.15 | async-start | bytes 7864320 | tf_op jit(solution)/shard_map/reduce_scatter | solution.py:93
  562.8 92.5 %all-gather.17.cloned.1.call-start = ((), (), s32[]{:S(2)}) async-start(), calls=%async_computation.16 | async-start | bytes 3932160 | tf_op jit(solution)/shard_map/all_gather | solution.py:97
  626.5 82.0 %reduce-scatter.17.cloned.1.call-start = ((), (), s32[]{:S(2)}) async-start(), calls=%async_computation.17 | async-start | bytes 3932160 | tf_op jit(solution)/shard_map/reduce_scatter | solution.py:101
  670.4 72.9 %all-gather.19.cloned.1.call-start = ((), (), s32[]{:S(2)}) async-start(), calls=%async_computation.18 | async-start | bytes 3932160 | tf_op jit(solution)/shard_map/all_gather | solution.py:97
  714.6 102.1 %reduce-scatter.19.cloned.1.call-start = ((), (), s32[]{:S(2)}) async-start(), calls=%async_computation.19 | async-start | bytes 3932160 | tf_op jit(solution)/shard_map/reduce_scatter | solution.py:101
  777.6 72.5 %all-gather.21.cloned.1.call-start = ((), (), s32[]{:S(2)}) async-start(), calls=%async_computation.20 | async-start | bytes 3932160 | tf_op jit(solution)/shard_map/all_gather | solution.py:97
  821.4 420.5 %reduce-scatter.21.cloned.1.call-start = ((), (), s32[]{:S(2)}) async-start(), calls=%async_computation.21 | async-start | bytes 3932160 | tf_op jit(solution)/shard_map/reduce_scatter | solution.py:101
  926.5 73.8 %copy-start.48 = (bf16[2048,256]{0,1:T(8,128)(2,1)S(1)}, bf16[2048,256]{0,1:T(8,128)(2,1)}, u32[]{:S(2)}) copy-start(bf16[2048,256]{0,1:T(8,128)(2,1)} %get-tuple-element.274) | copy-start | bytes 3145732
  1021.2 73.5 %copy-start.46 = (bf16[2048,256]{0,1:T(8,128)(2,1)S(1)}, bf16[2048,256]{0,1:T(8,128)(2,1)}, u32[]{:S(2)}) copy-start(bf16[2048,256]{0,1:T(8,128)(2,1)} %get-tuple-element.275) | copy-start | bytes 3145732
  1115.5 73.0 %copy-start.45 = (bf16[2048,256]{0,1:T(8,128)(2,1)S(1)}, bf16[2048,256]{0,1:T(8,128)(2,1)}, u32[]{:S(2)}) copy-start(bf16[2048,256]{0,1:T(8,128)(2,1)} %get-tuple-element.273) | copy-start | bytes 3145732
  1203.8 72.2 %all-gather.23.cloned.1.call-start = ((), (), s32[]{:S(2)}) async-start(), calls=%async_computation.22 | async-start | bytes 3932160 | tf_op jit(solution)/shard_map/all_gather | solution.py:97
  1247.3 156.5 %reduce-scatter.23.cloned.1.call-start = ((), (), s32[]{:S(2)}) async-start(), calls=%async_computation.23 | async-start | bytes 3932160 | tf_op jit(solution)/shard_map/reduce_scatter | solution.py:101
  1291.3 498.0 %all-reduce.22.cloned.1.call-start = ((), (), s32[]{:S(2)}) async-start(), calls=%async_computation.24 | async-start | bytes 25165824 | tf_op jit(solution)/shard_map/psum | solution.py:435
  1318.3 55.4 %slice-start.4 = ((s8[6291456]{0:T(1024)(128)(4,1)}), s8[4194304]{0:T(1024)(128)(4,1)S(1)}, s32[]{:S(2)}) async-start(s8[6291456]{0:T(1024)(128)(4,1)} %bitcast.431), calls=%async_computation.29 | async-start | bytes 8388608
  1320.1 53.5 %slice-start.5 = ((s8[6291456]{0:T(1024)(128)(4,1)}), s8[2097152]{0:T(1024)(128)(4,1)S(1)}, s32[]{:S(2)}) async-start(s8[6291456]{0:T(1024)(128)(4,1)} %bitcast.431), calls=%async_computation.30 | async-start | bytes 4194304
  (147 other events, 1217.4 us)
Sparse Core Ops, SparseCore 0:
  12.9 31.2 all-gather.8
  58.3 58.3 reduce-scatter.8
  120.8 28.5 all-gather.10
  334.8 58.3 reduce-scatter.10
  397.7 28.5 all-gather.12
  455.4 59.7 reduce-scatter.12
  519.8 28.5 all-gather.14
  562.9 58.3 reduce-scatter.14
  626.6 28.5 all-gather.16
  670.5 37.9 reduce-scatter.16
  714.7 28.5 all-gather.18
  777.7 38.9 reduce-scatter.18
  821.5 28.5 all-gather.20
  1204.0 37.9 reduce-scatter.20
  1247.4 28.5 all-gather.22
  1291.4 37.9 reduce-scatter.22
  1378.7 410.4 all-reduce.21
where the time goes:
time: 1850 us; the launch traced here: 1820 us
  waiting for transfers between devices  869 us (47%)
  local copies, waits for them, and re-layouts  430 us (23%)
  matrix products  279 us (15%)
  other arithmetic  134 us (7%)
  blocking collectives  86.1 us (5%)
    psum x1, waiting for transfers between devices, body(): lax.psum(conv_grads[0].astype(jnp.bfloat16), 'rows').astype(jnp.float32)  339 us
    unnamed x321, local copies, waits for them, and re-layouts  312 us
    reduce_scatter x4, waiting for transfers between devices, narrow(): return lax.psum_scatter(partial_out, 'tp', scatter_dimension=1, tiled=True)  233 us
    reduce_scatter x4, waiting for transfers between devices, narrow_back(): lax.psum_scatter(partial_grad.astype(jnp.bfloat16), 'tp', scatter_dimensi...  115 us
    all_gather x4, waiting for transfers between devices, widen_back(): return lax.all_gather(grad.astype(B16), 'tp', axis=1, tiled=True)  94.1 us
    all_gather x4, waiting for transfers between devices, widen(): return lax.all_gather(normed.astype(B16), 'tp', axis=1, tiled=True)  88.2 us
    reshape x3, local copies, waits for them, and re-layouts, skew(): return cut.reshape(heads, block, width)[:, :, :slots]  52.4 us
    dot_general x1, matrix products, attend_backward(): jnp.einsum('td,tk->dk', table, d_rel.astype(B16).reshape(2 * slots, heads...  48.8 us
  transfers between devices with their start and end apart: 17, of which 15 were waited for; matrix products, arithmetic and copies ran while one was open for 9% of the time, Pallas kernels for 0%

commit v1 on v0

v1 whole, which is shorter than its diff:
```python
import functools
import math

import jax
import jax.numpy as jnp
from jax import lax
from jax.experimental import pallas as pl
from jax.experimental.pallas import tpu as pltpu
from jax.sharding import PartitionSpec as P

EPS = 1e-05
NEG = -1e30
F32 = jnp.float32
B16 = jnp.bfloat16
TQ = 128
TK = 384
HD = 128
STEP = 64
SM = pl.BlockSpec(memory_space=pltpu.SMEM)
VM = pl.BlockSpec(memory_space=pltpu.VMEM)

def dotx(a, b, ca, cb):
    return lax.dot_general(a, b, (((ca,), (cb,)), ((), ())), preferred_element_type=F32)

def skew_tile(grid):
    return pltpu.roll(grid, TK + 1, 1, stride=1, stride_axis=0)[:, :TK]

def unskew_flipped(flipped):
    wide = jnp.concatenate([flipped, jnp.zeros((TQ, TQ), F32)], axis=1)
    return pltpu.roll(wide, 0, 1, stride=1, stride_axis=0)

def attend_kernel(heads, spans, q_at, k_at, qc_ref, qp_ref, k_ref, v_ref, rel_ref, code_q_ref, code_k_ref,
                  out_ref, wide_ref, lse_ref):
    slots = qc_ref.shape[0]
    scale = HD ** -0.5
    blocks, tiles = slots // TQ, slots // TK

    def q_step(qb, _):
        at = pl.multiple_of(q_at[qb], TQ)
        true_at = pl.multiple_of(qb * TQ, TQ)
        code_q = code_q_ref[pl.ds(true_at, TQ), :]
        qc = [qc_ref[pl.ds(at, TQ), h * HD:(h + 1) * HD] for h in range(heads)]
        qp = [qp_ref[pl.ds(at, TQ), h * HD:(h + 1) * HD] for h in range(heads)]

        def k_step(kt, carry):
            ko = pl.multiple_of(k_at[kt], TQ)
            to = pl.multiple_of((blocks - 1 + kt * (TK // TQ) - qb) * TQ, TQ)
            mask = code_q == code_k_ref[kt]
            new = []
            for h in range(heads):
                lanes = slice(h * HD, (h + 1) * HD)
                top, total, acc = carry[h]
                grid = dotx(qp[h], rel_ref[pl.ds(to, TK + TQ), lanes], 1, 1)
                raw = dotx(qc[h], k_ref[pl.ds(ko, TK), lanes], 1, 1) + skew_tile(grid)
                scores = jnp.where(mask, raw * scale, NEG)
                top_new = jnp.maximum(top, jnp.max(scores, axis=1, keepdims=True))
                shrink = jnp.exp(top - top_new)
                weights = jnp.exp(scores - top_new)
                total = total * shrink + jnp.sum(weights, axis=1, keepdims=True)
                acc = acc * shrink + dotx(weights.astype(B16), v_ref[pl.ds(ko, TK), lanes], 1, 0)
                new.append((top_new, total, acc))
            return tuple(new)

        first = tuple((jnp.full((TQ, 1), NEG, F32), jnp.zeros((TQ, 1), F32), jnp.zeros((TQ, HD), F32))
                      for _ in range(heads))
        final = lax.fori_loop(spans[0, qb], spans[1, qb], k_step, first)
        for h in range(heads):
            lanes = slice(h * HD, (h + 1) * HD)
            top, total, acc = final[h]
            out = acc / total
            wide_ref[pl.ds(at, TQ), lanes] = out
            out_ref[pl.ds(at, TQ), lanes] = out.astype(B16)
            lse_ref[pl.ds(at, TQ), h:h + 1] = top + jnp.log(total)
        return 0

    lax.fori_loop(0, blocks, q_step, 0)

def attend_back_kernel(heads, spans, q_at, k_at, qc_ref, qp_ref, k_ref, v_ref, rel_ref, code_q_ref, code_k_ref,
                       d_out_ref, wide_ref, lse_ref,
                       dq_ref, dk_ref, dv_ref, drel_ref, bias_ref, dk_acc, dv_acc, drel_acc):
    slots = qc_ref.shape[0]
    scale = HD ** -0.5
    blocks, tiles = slots // TQ, slots // TK
    dk_acc[...] = jnp.zeros_like(dk_acc)
    dv_acc[...] = jnp.zeros_like(dv_acc)
    drel_acc[...] = jnp.zeros_like(drel_acc)
    bias_ref[...] = jnp.zeros_like(bias_ref)
    row = lax.broadcasted_iota(jnp.int32, (TQ, TQ), 0)
    column = lax.broadcasted_iota(jnp.int32, (TQ, TQ), 1)
    flip = (row + column == TQ - 1).astype(F32)
    flip_low = flip.astype(B16)

    def q_step(qb, _):
        at = pl.multiple_of(q_at[qb], TQ)
        true_at = pl.multiple_of(qb * TQ, TQ)
        code_q = code_q_ref[pl.ds(true_at, TQ), :]
        cols = [slice(h * HD, (h + 1) * HD) for h in range(heads)]
        qc = [qc_ref[pl.ds(at, TQ), c] for c in cols]
        qp = [qp_ref[pl.ds(at, TQ), c] for c in cols]
        qp_flipped = [dotx(flip_low, item, 1, 0).astype(B16) for item in qp]
        d_out = [d_out_ref[pl.ds(at, TQ), c] for c in cols]
        lse = [lse_ref[pl.ds(at, TQ), h:h + 1] for h in range(heads)]
        delta = [jnp.sum(d_out[h].astype(F32) * wide_ref[pl.ds(at, TQ), cols[h]], axis=1, keepdims=True)
                 for h in range(heads)]

        def k_step(kt, carry):
            ko = pl.multiple_of(k_at[kt], TQ)
            to = pl.multiple_of((blocks - 1 + kt * (TK // TQ) - qb) * TQ, TQ)
            mask = code_q == code_k_ref[kt]
            new = []
            for h in range(heads):
                lanes = cols[h]
                d_content, d_position = carry[h]
                window = rel_ref[pl.ds(to, TK + TQ), lanes]
                key = k_ref[pl.ds(ko, TK), lanes]
                grid = dotx(qp[h], window, 1, 1)
                raw = dotx(qc[h], key, 1, 1) + skew_tile(grid)
                probs = jnp.exp(jnp.where(mask, raw * scale - lse[h], NEG))
                d_probs = dotx(d_out[h], v_ref[pl.ds(ko, TK), lanes], 1, 1)
                d_raw = probs * (d_probs - delta[h]) * scale
                d_low = d_raw.astype(B16)
                d_grid = unskew_flipped(dotx(flip_low, d_low, 1, 0)).astype(B16)
                dv_acc[pl.ds(ko, TK), lanes] += dotx(probs.astype(B16), d_out[h], 0, 0)
                dk_acc[pl.ds(ko, TK), lanes] += dotx(d_low, qc[h], 0, 0)
                drel_acc[pl.ds(to, TK + TQ), lanes] += dotx(d_grid, qp_flipped[h], 0, 0)
                d_content = d_content + dotx(d_low, key, 1, 0)
                d_position = d_position + dotx(d_grid, window, 1, 0)
                new.append((d_content, d_position))
            return tuple(new)

        first = tuple((jnp.zeros((TQ, HD), F32),) * 2 for _ in range(heads))
        final = lax.fori_loop(spans[0, qb], spans[1, qb], k_step, first)
        for h in range(heads):
            d_content, d_position = final[h]
            d_position = lax.dot_general(flip, d_position, (((1,), (0,)), ((), ())),
                                         precision=lax.Precision.HIGHEST, preferred_element_type=F32)
            dq_ref[pl.ds(at, TQ), cols[h]] = (d_content + d_position).astype(B16)
            bias_ref[0:1, cols[h]] += jnp.sum(d_content, axis=0, keepdims=True)
            bias_ref[1:2, cols[h]] += jnp.sum(d_position, axis=0, keepdims=True)
        return 0

    lax.fori_loop(0, blocks, q_step, 0)
    dk_ref[...] = dk_acc[...].astype(B16)
    dv_ref[...] = dv_acc[...].astype(B16)
    drel_ref[...] = drel_acc[...].astype(B16)

def sds(s, d): return jax.ShapeDtypeStruct(s, d)

def attend(spans, q_at, k_at, qc, qp, k, v, rel, code_q, code_k):
    slots, width = qc.shape
    heads = width // HD
    return pl.pallas_call(
        functools.partial(attend_kernel, heads),
        out_shape=(sds((slots, width), B16), sds((slots, width), F32), sds((slots, heads), F32)),
        in_specs=[SM] * 3 + [VM] * 7, out_specs=(VM,) * 3,
        compiler_params=pltpu.CompilerParams(vmem_limit_bytes=40 << 20),
        cost_estimate=pl.CostEstimate(flops=int(4e9), bytes_accessed=int(9e6), transcendentals=int(2e6)),
    )(spans, q_at, k_at, qc, qp, k, v, rel, code_q, code_k)

def attend_back(spans, q_at, k_at, qc, qp, k, v, rel, code_q, code_k, d_out, wide, lse):
    slots, width = qc.shape
    heads = width // HD
    return pl.pallas_call(
        functools.partial(attend_back_kernel, heads),
        out_shape=(sds((slots, width), B16),) * 3 + (sds((2 * slots, width), B16), sds((8, width), F32)),
        in_specs=[SM] * 3 + [VM] * 10, out_specs=(VM,) * 5,
        scratch_shapes=[pltpu.VMEM((slots, width), F32), pltpu.VMEM((slots, width), F32), pltpu.VMEM((2 * slots, width), F32)],
        compiler_params=pltpu.CompilerParams(vmem_limit_bytes=48 << 20),
        cost_estimate=pl.CostEstimate(flops=int(12e9), bytes_accessed=int(12e6), transcendentals=int(2e6)),
    )(spans, q_at, k_at, qc, qp, k, v, rel, code_q, code_k, d_out, wide, lse)

def codes(segments, valid):
    slots = segments.shape[0]
    place = jnp.arange(slots, dtype=jnp.int32)
    code = jnp.where(valid == 1, segments, -1 - place)
    return code

def spans_of(code):
    slots = code.shape[0]
    same = code[:, None] == code[None, :]
    touch = jnp.any(same.reshape(slots // TQ, TQ, slots // TK, TK), axis=(1, 3))
    tiles = slots // TK
    idx = jnp.arange(tiles, dtype=jnp.int32)
    lo = jnp.min(jnp.where(touch, idx, tiles), axis=1)
    hi = jnp.max(jnp.where(touch, idx + 1, 0), axis=1)
    return jnp.stack([lo, hi], 0).astype(jnp.int32)


def normalize(values, gain):
    mean = jnp.mean(values, axis=-1, keepdims=True)
    centered = values - mean
    inverse = lax.rsqrt(jnp.mean(centered * centered, axis=-1, keepdims=True) + EPS)
    unit = centered * inverse
    return (unit * gain.astype(F32), unit, inverse)


def normalize_back(grad, unit, inverse, gain):
    scaled = grad * gain.astype(F32)
    first = jnp.mean(scaled, axis=-1, keepdims=True)
    second = jnp.mean(scaled * unit, axis=-1, keepdims=True)
    return (inverse * (scaled - first - unit * second), jnp.sum(grad * unit, axis=0))


def swish_slope(values):
    gate = jax.nn.sigmoid(values)
    return gate * (1.0 + values * (1.0 - gate))


def distance_table(slots, width, first):
    column = jnp.arange(width)
    even = (column % 2 == 0)[None, :]
    rate = jnp.exp(-(column - column % 2).astype(F32) * (math.log(10000.0) / width))
    coarse = (slots - 1 - STEP * jnp.arange(2 * slots // STEP)).astype(F32)[:, None] * rate[None, :]
    fine = jnp.arange(STEP).astype(F32)[:, None] * rate[None, :]
    sin_c, cos_c = jnp.sin(coarse), jnp.cos(coarse)
    with_cos = jnp.where(even, sin_c, cos_c)
    with_sin = jnp.where(even, -cos_c, sin_c)
    with_cos, with_sin, sin_f, cos_f = after((with_cos, with_sin, jnp.sin(fine), jnp.cos(fine)), first)
    table = with_cos[:, None, :] * cos_f[None] + with_sin[:, None, :] * sin_f[None]
    return table.reshape(2 * slots, width).astype(B16)


def dot(left, right, contract=(1, 0)):
    return lax.dot_general(
        left, right, (((contract[0],), (contract[1],)), ((), ())), preferred_element_type=F32
    )


def swap(values, distance):
    size = lax.axis_size("tp")
    return lax.ppermute(values, "tp", [(i, i ^ distance) for i in range(size)])


def distances():
    size = lax.axis_size("tp")
    return [1 << bit for bit in range(size.bit_length() - 1)]


def gather(own):
    slots = {0: own}
    for distance in reversed(distances()):
        for slot in list(slots):
            slots[slot ^ distance] = swap(slots[slot], distance)
    return [slots[slot] for slot in range(len(slots))]


def scatter(parts):
    parts = dict(enumerate(parts))
    sent = got = None
    for distance in distances():
        for slot in sorted(parts, reverse=True):
            if slot & distance:
                sent = parts.pop(slot).astype(B16)
                got = swap(sent, distance)
                parts[slot ^ distance] = parts[slot ^ distance].astype(F32) + got.astype(F32)
    return parts[0], (sent, got)


def after(values, *others):
    return lax.optimization_barrier((values, others))[0]


def halves(slots):
    half = len(slots) // 2
    return jnp.concatenate(slots[:half], 0), jnp.concatenate(slots[half:], 0)


def pieces(near, far, weight, contract):
    count = lax.axis_size("tp") // 2
    rows = near.shape[0] // count
    outs = {}
    for slot in reversed(range(2 * count)):
        source, place = (near, slot) if slot < count else (far, slot - count)
        outs[slot] = dot(source[place * rows : (place + 1) * rows], weight, contract)
    return [outs[slot] for slot in range(2 * count)]


def ring():
    size, mine = lax.axis_size("rows"), lax.axis_index("rows")
    order = list(range(0, size, 2)) + list(range(size - 1, 0, -2))
    place = jnp.where(mine % 2 == 0, mine // 2, size - (mine + 1) // 2)
    right = [(order[i], order[(i + 1) % size]) for i in range(size)]
    return size, place, right, [(there, here) for here, there in right]


def sum_ring(values, gates=(), early=()):
    size, place, right, left = ring()
    rows = values.shape[0] // size
    forward, back = size // 2, size - 1 - size // 2
    gates = dict(enumerate(gates))
    gate = lambda item, stage: after(item, gates[stage]) if gates.get(stage) is not None else item
    chunk = lambda k: lax.dynamic_slice_in_dim(values, ((place + k) % size) * rows, rows, 0)
    add = lambda got, own: (got.astype(F32) + own.astype(F32)).astype(B16)
    from_left = from_right = None
    for step in range(forward):
        own = gate(chunk(forward - step), step)
        from_left = lax.ppermute(own if step == 0 else add(from_left, own), "rows", right)
        if step < back:
            own = gate(chunk(step - back), step)
            from_right = lax.ppermute(own if step == 0 else add(from_right, own), "rows", left)
    out = jnp.zeros(values.shape, F32)
    own, out = after((gate(chunk(0), forward), out), early)
    total = own.astype(F32) + from_left.astype(F32)
    if back:
        total = total + from_right.astype(F32)
    total = total.astype(B16)
    put = lambda item, k: lax.dynamic_update_slice_in_dim(
        out, item.astype(F32), ((place + k) % size) * rows, 0
    )
    out = put(total, 0)
    from_left = from_right = total
    for step in range(forward):
        from_left = lax.ppermute(gate(from_left, forward + 1 + step), "rows", right)
        out = put(from_left, -1 - step)
        if step < back:
            from_right = lax.ppermute(gate(from_right, forward + 1 + step), "rows", left)
            out = put(from_right, 1 + step)
    return out


def sum_cube(values, axis):
    size = lax.axis_size(axis)
    if size & (size - 1):
        return lax.psum(values, axis)
    distance = 1
    while distance < size:
        values = values + lax.ppermute(values, axis, [(i, i ^ distance) for i in range(size)])
        distance *= 2
    return values


def halo(own, reach):
    size = lax.axis_size("tp")
    left = lax.ppermute(own[-reach:], "tp", [(i, i + 1) for i in range(size - 1)])
    right = lax.ppermute(own[:reach], "tp", [(i + 1, i) for i in range(size - 1)])
    return jnp.concatenate([left, own, right], 0)


def to_true(values):
    size, mine = lax.axis_size("tp"), lax.axis_index("tp")
    rows = values.shape[0] // size
    return jnp.concatenate(
        [lax.dynamic_slice_in_dim(values, (mine ^ k) * rows, rows, 0) for k in range(size)], 0
    )


def ffn_forward(values, gain, weight_up, weight_down):
    normed, unit, inverse = normalize(values, gain)
    near, far = halves(gather(normed.astype(B16)))
    pre = [dot(half, weight_up) for half in (near, far)]
    act = [(item * jax.nn.sigmoid(item)).astype(B16) for item in pre]
    total, (sent, _) = scatter(pieces(act[0], act[1], weight_down, (1, 0)))
    pre = [item.astype(B16) for item in pre]
    return (values + 0.5 * total, (unit, inverse, (near, far), pre, act), sent)


def ffn_backward(grad, kept, gain, weight_up, weight_down):
    unit, inverse, wide, pre, act = kept
    own = (0.5 * grad).astype(B16)
    cot = halves(gather(own))
    d_pre = [
        (dot(cot[half], weight_down, (1, 1)) * swish_slope(pre[half].astype(F32))).astype(B16)
        for half in (0, 1)
    ]
    d_norm, (sent, _) = scatter(pieces(d_pre[0], d_pre[1], weight_up, (1, 1)))
    d_in, grad_gain = normalize_back(d_norm, unit, inverse, gain)
    cot, d_pre = after((cot, d_pre), sent)
    grad_down = dot(jnp.concatenate(act, 0), jnp.concatenate(cot, 0), (0, 0))
    grad_up = dot(jnp.concatenate(wide, 0), jnp.concatenate(d_pre, 0), (0, 0))
    return (grad + d_in, grad_gain, (grad_up.astype(B16), grad_down.astype(B16)), (own, sent))


def places(slots):
    size, mine = lax.axis_size("tp"), lax.axis_index("tp")
    rows = slots // size
    if rows % TK:
        q_at = jnp.arange(slots // TQ, dtype=jnp.int32) * TQ
        k_at = jnp.arange(slots // TK, dtype=jnp.int32) * TK
        return q_at, k_at, True
    q_true = jnp.arange(slots // TQ, dtype=jnp.int32) * TQ
    k_true = jnp.arange(slots // TK, dtype=jnp.int32) * TK
    q_at = ((q_true // rows) ^ mine) * rows + q_true % rows
    k_at = ((k_true // rows) ^ mine) * rows + k_true % rows
    return q_at.astype(jnp.int32), k_at.astype(jnp.int32), False


def attend_forward(
    values, gain, weights, attend_out, content_bias, position_bias, code, spans, rel, prefetch
):
    slots = code.shape[0]
    width = attend_out.shape[0]
    q_at, k_at, reorder = places(slots)
    where = (spans, q_at, k_at)
    normed, unit, inverse = normalize(values, gain)
    near, far = halves(gather(normed.astype(B16)))
    far = after(far, rel, spans)
    fetched, arrived = prefetch(far)
    mixed = [dot(half, weights) for half in (near, far)]
    flat = lambda bias: bias.astype(F32).reshape(1, width)
    join = lambda items: jnp.concatenate(items, 0)
    q_content = join([(item[:, :width] + flat(content_bias)).astype(B16) for item in mixed])
    q_position = join([(item[:, :width] + flat(position_bias)).astype(B16) for item in mixed])
    key = join([item[:, width : 2 * width].astype(B16) for item in mixed])
    value = join([item[:, 2 * width :].astype(B16) for item in mixed])
    if reorder:
        q_content, q_position, key, value = map(to_true, (q_content, q_position, key, value))
    operands = (
        where
        + (q_content, q_position, key, value, rel)
        + (code.reshape(slots, 1), code.reshape(slots // TK, 1, TK))
    )
    heads_out, heads_wide, sums = attend(*operands)
    sent = after(to_true(heads_out) if reorder else heads_out, arrived)
    half = slots // 2
    total, _ = scatter(pieces(sent[:half], sent[half:], attend_out, (1, 0)))
    kept = (unit, inverse, (near, far), operands, heads_wide, sums, sent)
    return (values + total, kept, fetched)


def attend_backward(grad, cot, kept, gain, weights, attend_out, table, filler):
    unit, inverse, wide, operands, heads_wide, sums, sent = kept
    slots, width = sent.shape
    _, _, reorder = places(slots)
    cot = halves(gather(cot))
    d_heads = jnp.concatenate([dot(half, attend_out, (1, 1)).astype(B16) for half in cot], 0)
    if reorder:
        d_heads = to_true(d_heads)
    d_heads = after(d_heads, filler[0])
    d_query, d_key, d_value, d_rel, d_bias = attend_back(*operands, d_heads, heads_wide, sums)
    d_query, d_key, d_value = after((d_query, d_key, d_value), filler[1])
    if reorder:
        d_query, d_key, d_value = map(to_true, (d_query, d_key, d_value))
    d_all = jnp.concatenate([d_query, d_key, d_value], 1)
    half = slots // 2
    d_norm, (last, _) = scatter(pieces(d_all[:half], d_all[half:], weights, (1, 1)))
    d_in, grad_gain = normalize_back(d_norm, unit, inverse, gain)
    cot, d_all, d_rel = after((cot, d_all, d_rel), last)
    grad_out = dot(jnp.concatenate(cot, 0), sent, (0, 0))
    grad_all = dot(jnp.concatenate(wide, 0), d_all, (0, 0))
    grad_pos = dot(table, d_rel, (0, 0))
    grads = jnp.concatenate([item.astype(B16) for item in (grad_all, grad_pos, grad_out)], 1)
    return (grad + d_in, grad_gain, grads, d_bias[:2])


def conv_weights(point_in, depth_kernel, gain_inner, point_out, first):
    taps = depth_kernel.shape[0]
    own = after((point_in[:, 0], point_in[:, 1], point_out), first)
    small = gather(jnp.concatenate([depth_kernel, gain_inner[None]], 0))
    small = jnp.concatenate(small, 1).astype(F32)
    in_a, in_b, out = map(gather, own)
    arrived = [item[2::2] for item in (in_a, in_b, out)]
    in_a, in_b = jnp.concatenate(in_a, 1), jnp.concatenate(in_b, 1)
    return (in_a, in_b, small[:taps], small[taps], jnp.concatenate(out, 0)), arrived


def conv_masks(segments, valid, rows, taps):
    edge = 8
    reach = taps // 2
    base = lax.axis_index("tp") * rows + edge - reach
    wide_segments = jnp.pad(segments, edge, constant_values=-1)
    wide_valid = jnp.pad(valid, edge)
    own = lax.dynamic_slice_in_dim(wide_segments, base, rows + 2 * reach)
    masks = []
    for tap in range(taps):
        other = lax.dynamic_slice_in_dim(wide_segments, base + tap - reach, rows + 2 * reach)
        good = lax.dynamic_slice_in_dim(wide_valid, base + tap - reach, rows + 2 * reach)
        masks.append(((other == own) & (good == 1)).astype(F32)[:, None])
    return masks


def conv_forward(values, gain, full, masks):
    in_a, in_b, kernel, gain_inner, out = full
    rows = values.shape[0]
    taps = kernel.shape[0]
    reach = taps // 2
    normed, unit, inverse = normalize(values, gain)
    low = normed.astype(B16)
    wide = halo(low, 2 * reach)
    mixed_a = dot(wide, in_a)
    gate = jax.nn.sigmoid(dot(wide, in_b))
    glu = mixed_a * gate
    depth = 0.0
    for tap in range(taps):
        depth = depth + kernel[tap] * masks[tap] * glu[tap : tap + rows + 2 * reach]
    depth_norm, inner_unit, inner_inverse = normalize(depth, gain_inner)
    inner = (depth_norm * jax.nn.sigmoid(depth_norm)).astype(B16)
    own = slice(2 * reach, 2 * reach + rows)
    kept = (unit, inverse, low, mixed_a[own], gate[own], glu, inner_unit, inner_inverse, depth_norm, inner)
    return (values + dot(inner[reach : reach + rows], out), kept)


def conv_backward(grad, kept, gain, full, masks):
    unit, inverse, low, mixed_a, gate, glu, inner_unit, inner_inverse, depth_norm, inner = kept
    in_a, in_b, kernel, gain_inner, out = full
    rows = grad.shape[0]
    taps = kernel.shape[0]
    reach = taps // 2
    mine = slice(reach, reach + rows)
    cot = grad.astype(B16)
    d_act = dot(halo(cot, reach), out, (1, 1))
    d_depth_norm = d_act * swish_slope(depth_norm)
    grad_gain_inner = jnp.sum((d_depth_norm * inner_unit)[mine], axis=0)
    d_depth, _ = normalize_back(d_depth_norm, inner_unit, inner_inverse, gain_inner)
    d_glu = 0.0
    kernel_rows = []
    for tap in range(taps):
        weighted = d_depth * masks[tap]
        back = 2 * reach - tap
        d_glu = d_glu + kernel[tap] * weighted[back : back + rows]
        kernel_rows.append(jnp.sum(weighted[mine] * glu[reach + tap : reach + tap + rows], axis=0))
    d_a = (d_glu * gate).astype(B16)
    d_b = (d_glu * mixed_a * gate * (1.0 - gate)).astype(B16)
    d_norm = dot(d_a, in_a, (1, 1)) + dot(d_b, in_b, (1, 1))
    d_in, grad_gain = normalize_back(d_norm, unit, inverse, gain)
    grad = grad + d_in
    next_cot = grad.astype(B16)
    low, cot, d_a, d_b, inner = after((low, cot, d_a, d_b, inner), next_cot)
    size = lax.axis_size("tp")
    width = in_a.shape[1] // size
    parts, small_parts = [], []
    small = jnp.stack(kernel_rows + [grad_gain_inner], 0)
    for slot in range(size):
        cols = slice(slot * width, (slot + 1) * width)
        parts.append(
            jnp.concatenate(
                [
                    dot(low, d_a[:, cols], (0, 0)),
                    dot(low, d_b[:, cols], (0, 0)),
                    dot(cot, inner[mine][:, cols], (0, 0)),
                ],
                1,
            )
        )
        small_parts.append(small[:, cols])
    total, ends = scatter(parts)
    return (grad, next_cot, grad_gain, (total.astype(B16), scatter(small_parts)[0]), ends)


def body(
    layer_input,
    cotangent,
    segments,
    valid_frames,
    gain_first,
    up_first,
    down_first,
    gain_attend,
    query_weight,
    key_weight,
    value_weight,
    attend_out,
    pos_weight,
    content_bias,
    position_bias,
    gain_conv,
    point_in,
    depth_kernel,
    gain_inner,
    point_out,
    gain_second,
    up_second,
    down_second,
    gain_final,
):
    segment_row, valid_row = segments[0], valid_frames[0]
    weights = jnp.concatenate([query_weight, key_weight, value_weight], 1)
    width = query_weight.shape[1]
    taps = depth_kernel.shape[0]
    values = layer_input[0].astype(F32)
    rows = values.shape[0]
    slots = segment_row.shape[0]
    masks = conv_masks(segment_row, valid_row, rows, taps)
    code = codes(segment_row, valid_row)
    spans = spans_of(code)
    values, kept_first, sent = ffn_forward(values, gain_first, up_first, down_first)
    table = distance_table(slots, values.shape[1], sent)
    rel = dot(table, pos_weight).astype(B16)
    prefetch = functools.partial(conv_weights, point_in, depth_kernel, gain_inner, point_out)
    values, kept_attend, full = attend_forward(
        values, gain_attend, weights, attend_out, content_bias, position_bias, code, spans, rel, prefetch
    )
    values, kept_conv = conv_forward(values, gain_conv, full, masks)
    values, kept_second, _ = ffn_forward(values, gain_second, up_second, down_second)
    final, final_unit, final_inverse = normalize(values, gain_final)
    layer_output = final.astype(B16)
    grad, sum_final = normalize_back(cotangent[0].astype(F32), final_unit, final_inverse, gain_final)
    grad, sum_second, second_grads, _ = ffn_backward(
        grad, kept_second, gain_second, up_second, down_second
    )
    second_sum = lax.psum(second_grads, "rows")
    grad, cot, sum_conv, conv_grads, ends = conv_backward(grad, kept_conv, gain_conv, full, masks)
    grad, sum_attend, attend_grads, d_bias = attend_backward(
        grad, cot, kept_attend, gain_attend, weights, attend_out, table, ends
    )
    grad, sum_first, first_grads, marks = ffn_backward(
        grad, kept_first, gain_first, up_first, down_first
    )
    middle = jnp.concatenate([attend_grads, conv_grads[0]], 1)
    gates = (None, marks[0], marks[0], marks[1], marks[1])
    middle = sum_ring(middle, gates)
    attend_sum, conv_sum = middle[:, : 5 * width], middle[:, 5 * width :]
    second_up, second_down = [item.astype(F32) for item in second_sum]
    first_down = sum_ring(first_grads[1])
    first_up = sum_ring(first_grads[0], early=(second_up, second_down))
    first_sum = (first_up, first_down)
    gains = sum_cube(jnp.stack([sum_first, sum_attend, sum_conv, sum_second, sum_final]), "tp")
    small = jnp.concatenate([conv_grads[1], d_bias], 0)
    small_shape = small.shape
    pack = jnp.concatenate([gains.reshape(-1), small.reshape(-1)]).reshape(-1, width)
    pack = sum_cube(pack, "rows").reshape(-1)
    gains, small = pack[: gains.size].reshape(gains.shape), pack[gains.size :].reshape(small_shape)
    bias_shape = content_bias.shape
    return (
        layer_output[None],
        grad[None],
        gains[0],
        first_sum[0],
        first_sum[1],
        gains[1],
        attend_sum[:, :width],
        attend_sum[:, width : 2 * width],
        attend_sum[:, 2 * width : 3 * width],
        attend_sum[:, 4 * width :].T,
        attend_sum[:, 3 * width : 4 * width],
        small[taps + 1].reshape(bias_shape),
        small[taps + 2].reshape(bias_shape),
        gains[2],
        jnp.stack([conv_sum[:, :width], conv_sum[:, width : 2 * width]], 1),
        small[:taps],
        small[taps],
        conv_sum[:, 2 * width :].T,
        gains[3],
        second_up,
        second_down,
        gains[4],
    )


def solution(mesh):
    in_specs = (
        P("rows", "tp", None),
        P("rows", "tp", None),
        P("rows", None),
        P("rows", None),
        P(),
        P(None, "tp"),
        P("tp", None),
        P(),
        P(None, "tp"),
        P(None, "tp"),
        P(None, "tp"),
        P("tp", None),
        P(None, "tp"),
        P("tp", None),
        P("tp", None),
        P(),
        P(None, None, "tp"),
        P(None, "tp"),
        P("tp"),
        P("tp", None),
        P(),
        P(None, "tp"),
        P("tp", None),
        P(),
    )
    out_specs = (
        P("rows", "tp", None),
        P("rows", "tp", None),
        P(),
        P(None, "tp"),
        P("tp", None),
        P(),
        P(None, "tp"),
        P(None, "tp"),
        P(None, "tp"),
        P("tp", None),
        P(None, "tp"),
        P("tp", None),
        P("tp", None),
        P(),
        P(None, None, "tp"),
        P(None, "tp"),
        P("tp"),
        P("tp", None),
        P(),
        P(None, "tp"),
        P("tp", None),
        P(),
    )
    return jax.shard_map(body, mesh=mesh, in_specs=in_specs, out_specs=out_specs, check_vma=False)
```

time: 1850 us -> 710 us (0.38); the launches traced: 1820 us -> 704 us
  waiting for transfers between devices: 869 us -> 278 us
  local copies, waits for them, and re-layouts: 430 us -> 65.4 us
  matrix products: 279 us -> 107 us
  starting transfers between devices: 1.81 us -> 113 us
  blocking collectives: 86.1 us -> 0 us
  other arithmetic: 134 us -> 82.4 us
  Pallas kernels: 0 us -> 40.9 us
    reduce_scatter x8 -> x0, waiting for transfers between devices: 348 us -> none  [the longest x4 233 us: narrow(): return lax.psum_scatter(partial_out, 'tp', scatter_dimension=1, tiled=True)]
    psum x1, waiting for transfers between devices: 339 us -> 21.3 us  [body(): second_sum = lax.psum(second_grads, 'rows')]
    unnamed x321 -> x291, local copies, waits for them, and re-layouts: 312 us -> 42.1 us
    ppermute x0 -> x105, waiting for transfers between devices: none -> 257 us  [the longest x54 159 us: swap(): return lax.ppermute(values, 'tp', [(i, i ^ distance) for i in range(size)])]
    all_gather x8 -> x0, waiting for transfers between devices: 182 us -> none  [the longest x4 94.1 us: widen_back(): return lax.all_gather(grad.astype(B16), 'tp', axis=1, tiled=True)]
    dot_general x56 -> x62, matrix products: 253 us -> 107 us  [dot(): lax.dot_general(left, right, (((contract[0],), (contract[1],)), ((), ()))...]
    ppermute x0 -> x105, starting transfers between devices: none -> 113 us  [the longest x12 34.8 us: sum_ring(): lax.ppermute(own if step == 0 else add(from_left, own), 'rows', right)]
    psum x5 -> x0, blocking collectives: 86.1 us -> none  [the longest x1 41.5 us: body(): lax.psum((sum_first, sum_attend, sum_conv, sum_second, sum_final), ('rows...]
  transfers between devices with their start and end apart: 17 -> 106, of which waited for: 15 -> 42; matrix products, arithmetic and copies ran while one was open for 9% -> 29% of each run, Pallas kernels for 0% -> 6%
where the time goes in v1:
time: 710 us; the launch traced here: 704 us
  waiting for transfers between devices  278 us (39%)
  starting transfers between devices  113 us (16%)
  matrix products  107 us (15%)
  other arithmetic  82.4 us (12%)
  local copies, waits for them, and re-layouts  65.4 us (9%)
  Pallas kernels  40.9 us (6%)
  between operations  17.1 us (2%)
    ppermute x54, waiting for transfers between devices, swap(): return lax.ppermute(values, 'tp', [(i, i ^ distance) for i in range(size)])  159 us
    dot_general x62, matrix products, dot(): lax.dot_general(left, right, (((contract[0],), (contract[1],)), ((), ()))...  107 us
    unnamed x291, local copies, waits for them, and re-layouts  42.1 us
    ppermute x12, waiting for transfers between devices, sum_ring(): from_left = lax.ppermute(gate(from_left, forward + 1 + step), 'rows', right)  38.4 us
    ppermute x12, starting transfers between devices, sum_ring(): lax.ppermute(own if step == 0 else add(from_left, own), 'rows', right)  34.8 us
    ppermute x12, waiting for transfers between devices, sum_ring(): lax.ppermute(own if step == 0 else add(from_left, own), 'rows', right)  33.5 us
    ppermute x54, starting transfers between devices, swap(): return lax.ppermute(values, 'tp', [(i, i ^ distance) for i in range(size)])  29.4 us
    pallas_call x1, Pallas kernels, attend_back(): pl.pallas_call(functools.partial(attend_back_kernel, heads), out_shape=(s...  28.2 us
  transfers between devices with their start and end apart: 106, of which 42 were waited for; matrix products, arithmetic and copies ran while one was open for 29% of the time, Pallas kernels for 6%

profile of v1, /device:TPU:0, one launch (start us, length us, event | category | flops | bytes accessed | tf_op | source)
XLA Modules:
  0.0 703.7 jit_solution(1089311353037132113)
XLA Ops:
  27.0 9.9 %collective-permute-done.2 = bf16[384,1024]{1,0:T(8,128)(2,1)} collective-permute-done((bf16[384,1024]{1,0:T(8,128)(2,1)}, bf16[384,1024]{1,0:T(8,128)(2,1)}, u32[]{:S(2)}, u32[]{:S(2)}) %collective-permute-start.2) | collective-permute-done | bytes 786464 | tf_op jit(solution)/shard_map/ppermute | solution.py:231
  55.5 18.5 %collective-permute-done.5 = bf16[384,1024]{1,0:T(8,128)(2,1)S(1)} collective-permute-done((bf16[384,1024]{1,0:T(8,128)(2,1)S(1)}, bf16[384,1024]{1,0:T(8,128)(2,1)S(1)}, u32[]{:S(2)}, u32[]{:S(2)}) %collective-permute-start.5) | collective-permute-done | bytes 786464 | tf_op jit(solution)/shard_map/ppermute | solution.py:231
  79.5 15.2 %collective-permute-done.7 = bf16[384,1024]{1,0:T(8,128)(2,1)S(1)} collective-permute-done((bf16[384,1024]{1,0:T(8,128)(2,1)S(1)}, bf16[384,1024]{1,0:T(8,128)(2,1)S(1)}, u32[]{:S(2)}, u32[]{:S(2)}) %collective-permute-start.7) | collective-permute-done | bytes 786464 | tf_op jit(solution)/shard_map/ppermute | solution.py:231
  104.7 12.7 %shard_map.399 = (bf16[1536,256]{1,0:T(8,128)(2,1)S(1)}, f32[1536,256]{1,0:T(8,128)S(1)}, f32[1536,2]{1,0:T(8,128)S(1)}) custom-call(s32[2,12]{1,0:T(2,128)S(1)} %pad_add_fusion.spans, s32[12]{0:T(128)S(1)} %fusion.254.q_at, s32[4]{0:T(128)S(1)} %fusion.255.k_at, bf16[1536,256]{1,0:T(8,128)(2,1)S(1)} %get-tuple-element.342.qc_ref, ...), custom_call_target="tpu_custom_call" | custom-call | flops 4000000000 | bytes 9000000 | tf_op jit(solution)/shard_map/pallas_call | solution.py:152
  117.5 7.8 %collective-permute-done.10 = bf16[1024,256]{1,0:T(8,128)(2,1)S(1)} collective-permute-done((bf16[1024,256]{1,0:T(8,128)(2,1)S(1)}, bf16[1024,256]{1,0:T(8,128)(2,1)S(1)}, u32[]{:S(2)}, u32[]{:S(2)}) %collective-permute-start.10) | collective-permute-done | bytes 524320 | tf_op jit(solution)/shard_map/ppermute | solution.py:231
  125.3 10.4 %collective-permute-done.11 = bf16[256,1024]{1,0:T(8,128)(2,1)S(1)} collective-permute-done((bf16[256,1024]{1,0:T(8,128)(2,1)S(1)}, bf16[256,1024]{1,0:T(8,128)(2,1)S(1)}, u32[]{:S(2)}, u32[]{:S(2)}) %collective-permute-start.11) | collective-permute-done | bytes 524320 | tf_op jit(solution)/shard_map/ppermute | solution.py:231
  141.1 17.3 %collective-permute-done.14 = bf16[384,1024]{1,0:T(8,128)(2,1)S(1)} collective-permute-done((bf16[384,1024]{1,0:T(8,128)(2,1)S(1)}, bf16[384,1024]{1,0:T(8,128)(2,1)S(1)}, u32[]{:S(2)}, u32[]{:S(2)}) %collective-permute-start.14) | collective-permute-done | bytes 786464 | tf_op jit(solution)/shard_map/ppermute | solution.py:231
  175.5 17.3 %collective-permute-done.28 = bf16[384,1024]{1,0:T(8,128)(2,1)S(1)} collective-permute-done((bf16[384,1024]{1,0:T(8,128)(2,1)S(1)}, bf16[384,1024]{1,0:T(8,128)(2,1)S(1)}, u32[]{:S(2)}, u32[]{:S(2)}) %collective-permute-start.28) | collective-permute-done | bytes 786464 | tf_op jit(solution)/shard_map/ppermute | solution.py:231
  209.1 16.6 %collective-permute-done.31 = bf16[384,1024]{1,0:T(8,128)(2,1)S(1)} collective-permute-done((bf16[384,1024]{1,0:T(8,128)(2,1)S(1)}, bf16[384,1024]{1,0:T(8,128)(2,1)S(1)}, u32[]{:S(2)}, u32[]{:S(2)}) %collective-permute-start.31) | collective-permute-done | bytes 786464 | tf_op jit(solution)/shard_map/ppermute | solution.py:231
  232.2 17.4 %collective-permute-done.34 = bf16[384,1024]{1,0:T(8,128)(2,1)} collective-permute-done((bf16[384,1024]{1,0:T(8,128)(2,1)S(1)}, bf16[384,1024]{1,0:T(8,128)(2,1)}, u32[]{:S(2)}, u32[]{:S(2)}) %collective-permute-start.34) | collective-permute-done | bytes 786464 | tf_op jit(solution)/shard_map/ppermute | solution.py:231
  271.8 12.7 %collective-permute-done.37 = bf16[384,1024]{1,0:T(8,128)(2,1)S(1)} collective-permute-done((bf16[384,1024]{1,0:T(8,128)(2,1)S(1)}, bf16[384,1024]{1,0:T(8,128)(2,1)S(1)}, u32[]{:S(2)}, u32[]{:S(2)}) %collective-permute-start.37) | collective-permute-done | bytes 786464 | tf_op jit(solution)/shard_map/ppermute | solution.py:231
  349.3 28.2 %shard_map.400 = (bf16[1536,256]{1,0:T(8,128)(2,1)S(1)}, bf16[1536,256]{1,0:T(8,128)(2,1)S(1)}, bf16[1536,256]{1,0:T(8,128)(2,1)S(1)}, bf16[3072,256]{1,0:T(8,128)(2,1)}, f32[8,256]{1,0:T(8,128)S(1)}) custom-call(s32[2,12]{1,0:T(2,128)S(1)} %pad_add_fusion.spans, s32[12]{0:T(128)S(1)} %fusion.254.q_at, s32[4]{0:T(128)S(1)} %fusion.255.k_at, ...), custom_call_target="tpu_custom_call" | custom-call | flops 12000000000 | bytes 12000000 | tf_op jit(solution)/shard_map/pallas_call | solution.py:163
  377.5 5.8 collective-permute-done.44
  399.7 14.3 %collective-permute-start.91 = (bf16[128,2048]{0,1:T(8,128)(2,1)S(1)}, bf16[128,2048]{0,1:T(8,128)(2,1)S(1)}, u32[]{:S(2)}, u32[]{:S(2)}) collective-permute-start(bf16[128,2048]{0,1:T(8,128)(2,1)S(1)} %get-tuple-element.254), channel_id=1, source_target_pairs={{0,8},{8,16},{16,24},{24,28},{28,20},{20,12},{12,4},{4,0},{1,9},{9... | collective-permute-start | bytes 1572872 | tf_op jit(solution)/shard_map/ppermute | solution.py:297
  418.7 18.6 %collective-permute-done.91 = bf16[128,2048]{0,1:T(8,128)(2,1)S(1)} collective-permute-done((bf16[128,2048]{0,1:T(8,128)(2,1)S(1)}, bf16[128,2048]{0,1:T(8,128)(2,1)S(1)}, u32[]{:S(2)}, u32[]{:S(2)}) %collective-permute-start.91) | collective-permute-done | bytes 524320 | tf_op jit(solution)/shard_map/ppermute | solution.py:297
  438.2 12.4 %collective-permute-start.92 = (bf16[128,2048]{0,1:T(8,128)(2,1)}, bf16[128,2048]{0,1:T(8,128)(2,1)}, u32[]{:S(2)}, u32[]{:S(2)}) collective-permute-start(bf16[128,2048]{0,1:T(8,128)(2,1)} %add_convert_fusion.12), channel_id=1, source_target_pairs={{0,8},{8,16},{16,24},{24,28},{28,20},{20,12},{12,4},{4,0},{1,9},{9... | collective-permute-start | bytes 1572872 | tf_op jit(solution)/shard_map/ppermute | solution.py:297
  454.7 21.3 %all-reduce.5.cloned.1.call-done = (bf16[1024,1024]{1,0:T(8,128)(2,1)}, bf16[1024,1024]{1,0:T(8,128)(2,1)}) async-done(((bf16[1024,1024]{1,0:T(8,128)(2,1)}, bf16[1024,1024]{1,0:T(8,128)(2,1)}), (bf16[1024,1024]{1,0:T(8,128)(2,1)}, bf16[1024,1024]{1,0:T(8,128)(2,1)})) %all-reduce.5.cloned.1.call-update) | async-done | bytes 4194320 | tf_op jit(solution)/shard_map/psum | solution.py:590
  498.9 5.4 fusion.97
  513.6 6.0 collective-permute-done.76
  529.8 6.6 collective-permute-done.63
  571.3 9.5 %collective-permute-done.60 = f32[28,256]{1,0:T(8,128)S(1)} collective-permute-done((f32[28,256]{1,0:T(8,128)S(1)}, f32[28,256]{1,0:T(8,128)S(1)}, u32[]{:S(2)}, u32[]{:S(2)}) %collective-permute-start.60) | collective-permute-done | bytes 28704 | tf_op jit(solution)/shard_map/ppermute | solution.py:327
  616.2 13.9 %collective-permute-done.71 = bf16[128,1024]{1,0:T(8,128)(2,1)S(1)} collective-permute-done((bf16[128,1024]{1,0:T(8,128)(2,1)S(1)}, bf16[128,1024]{1,0:T(8,128)(2,1)S(1)}, u32[]{:S(2)}, u32[]{:S(2)}) %collective-permute-start.71) | collective-permute-done | bytes 262176 | tf_op jit(solution)/shard_map/ppermute | solution.py:313
  644.3 11.2 %collective-permute-done.87 = bf16[128,1024]{1,0:T(8,128)(2,1)S(1)} collective-permute-done((bf16[128,1024]{1,0:T(8,128)(2,1)S(1)}, bf16[128,1024]{1,0:T(8,128)(2,1)S(1)}, u32[]{:S(2)}, u32[]{:S(2)}) %collective-permute-start.87) | collective-permute-done | bytes 262176 | tf_op jit(solution)/shard_map/ppermute | solution.py:313
  676.5 6.2 slice_bitcast_fusion
  (723 shorter events, 371.4 us)
Async XLA Ops:
  7.2 468.7 %all-reduce.5.cloned.1.call-start = ((), (), s32[]{:S(2)}) async-start(), calls=%async_computation | async-start | bytes 8388608 | tf_op jit(solution)/shard_map/psum | solution.py:590
  8.9 67.0 %collective-permute-start.16 = (bf16[6,256]{1,0:T(8,128)(2,1)S(1)}, bf16[6,256]{1,0:T(8,128)(2,1)S(1)}, u32[]{:S(2)}, u32[]{:S(2)}) collective-permute-start(bf16[6,256]{1,0:T(8,128)(2,1)S(1)} %pad_maximum_fusion.21), channel_id=1, source_target_pairs={{0,2},{1,3},{2,0},{3,1},{4,6},{5,7},{6,4},{7,5},{8,10},{9,11},{10,... | collective-permute-start | bytes 9224 | tf_op jit(solution)/shard_map/ppermute | solution.py:231
  11.9 64.2 %collective-permute-start.15 = (bf16[6,256]{1,0:T(8,128)(2,1)S(1)}, bf16[6,256]{1,0:T(8,128)(2,1)S(1)}, u32[]{:S(2)}, u32[]{:S(2)}) collective-permute-start(bf16[6,256]{1,0:T(8,128)(2,1)S(1)} %pad_maximum_fusion.21), channel_id=1, source_target_pairs={{0,1},{1,0},{2,3},{3,2},{4,5},{5,4},{6,7},{7,6},{8,9},{9,8},{10,11... | collective-permute-start | bytes 9224 | tf_op jit(solution)/shard_map/ppermute | solution.py:231
  16.7 30.6 %collective-permute-start = (bf16[384,1024]{1,0:T(8,128)(2,1)}, bf16[384,1024]{1,0:T(8,128)(2,1)}, u32[]{:S(2)}, u32[]{:S(2)}) collective-permute-start(bf16[384,1024]{1,0:T(8,128)(2,1)} %fusion.115), channel_id=1, source_target_pairs={{0,1},{1,0},{2,3},{3,2},{4,5},{5,4},{6,7},{7,6},{8,9},{9,8},{10,11... | collective-permute-start | bytes 2359304 | tf_op jit(solution)/shard_map/ppermute | solution.py:231
  98.7 38.5 %collective-permute-start.20 = (bf16[1024,256]{1,0:T(8,128)(2,1)S(1)}, bf16[1024,256]{1,0:T(8,128)(2,1)S(1)}, u32[]{:S(2)}, u32[]{:S(2)}) collective-permute-start(bf16[1024,256]{1,0:T(8,128)(2,1)S(1)} %get-tuple-element.78), channel_id=1, source_target_pairs={{0,1},{1,0},{2,3},{3,2},{4,5},{5,4},{6,7},{7,6},{8,9},{9,8},{10,11... | collective-permute-start | bytes 1572872 | tf_op jit(solution)/shard_map/ppermute | solution.py:231
  99.6 37.9 %collective-permute-start.22 = (bf16[1024,256]{1,0:T(8,128)(2,1)S(1)}, bf16[1024,256]{1,0:T(8,128)(2,1)S(1)}, u32[]{:S(2)}, u32[]{:S(2)}) collective-permute-start(bf16[1024,256]{1,0:T(8,128)(2,1)S(1)} %get-tuple-element.79), channel_id=1, source_target_pairs={{0,1},{1,0},{2,3},{3,2},{4,5},{5,4},{6,7},{7,6},{8,9},{9,8},{10,11... | collective-permute-start | bytes 1572872 | tf_op jit(solution)/shard_map/ppermute | solution.py:231
  102.7 32.9 %collective-permute-start.11 = (bf16[256,1024]{1,0:T(8,128)(2,1)S(1)}, bf16[256,1024]{1,0:T(8,128)(2,1)S(1)}, u32[]{:S(2)}, u32[]{:S(2)}) collective-permute-start(bf16[256,1024]{1,0:T(8,128)(2,1)S(1)} %copy-done.72), channel_id=1, source_target_pairs={{0,2},{1,3},{2,0},{3,1},{4,6},{5,7},{6,4},{7,5},{8,10},{9,11},{10,... | collective-permute-start | bytes 1572872 | tf_op jit(solution)/shard_map/ppermute | solution.py:231
  338.0 50.0 %collective-permute-start.90 = (bf16[1024,768]{0,1:T(8,128)(2,1)S(1)}, bf16[1024,768]{0,1:T(8,128)(2,1)S(1)}, u32[]{:S(2)}, u32[]{:S(2)}) collective-permute-start(bf16[1024,768]{0,1:T(8,128)(2,1)S(1)} %pad_maximum_fusion.7), channel_id=1, source_target_pairs={{0,1},{1,0},{2,3},{3,2},{4,5},{5,4},{6,7},{7,6},{8,9},{9,8},{10,11... | collective-permute-start | bytes 4718600 | tf_op jit(solution)/shard_map/ppermute | solution.py:231
  346.4 36.9 %collective-permute-start.44 = (bf16[1024,768]{0,1:T(8,128)(2,1)S(1)}, bf16[1024,768]{0,1:T(8,128)(2,1)S(1)}, u32[]{:S(2)}, u32[]{:S(2)}) collective-permute-start(bf16[1024,768]{0,1:T(8,128)(2,1)S(1)} %fusion.28), channel_id=1, source_target_pairs={{0,2},{1,3},{2,0},{3,1},{4,6},{5,7},{6,4},{7,5},{8,10},{9,11},{10,... | collective-permute-start | bytes 4718600 | tf_op jit(solution)/shard_map/ppermute | solution.py:231
  386.6 29.0 %collective-permute-start.45 = (bf16[384,1024]{1,0:T(8,128)(2,1)S(1)}, bf16[384,1024]{1,0:T(8,128)(2,1)S(1)}, u32[]{:S(2)}, u32[]{:S(2)}) collective-permute-start(bf16[384,1024]{1,0:T(8,128)(2,1)S(1)} %convolution_convert_fusion.2), channel_id=1, source_target_pairs={{0,1},{1,0},{2,3},{3,2},{4,5},{5,4},{6,7},{7,6},{8,9},{9,8},{10,11... | collective-permute-start | bytes 2359304 | tf_op jit(solution)/shard_map/ppermute | solution.py:231
  399.7 37.5 %collective-permute-start.91 = (bf16[128,2048]{0,1:T(8,128)(2,1)S(1)}, bf16[128,2048]{0,1:T(8,128)(2,1)S(1)}, u32[]{:S(2)}, u32[]{:S(2)}) collective-permute-start(bf16[128,2048]{0,1:T(8,128)(2,1)S(1)} %get-tuple-element.254), channel_id=1, source_target_pairs={{0,8},{8,16},{16,24},{24,28},{28,20},{20,12},{12,4},{4,0},{1,9},{9... | collective-permute-start | bytes 1572872 | tf_op jit(solution)/shard_map/ppermute | solution.py:297
  414.0 38.0 %collective-permute-start.95 = (bf16[128,2048]{0,1:T(8,128)(2,1)S(1)}, bf16[128,2048]{0,1:T(8,128)(2,1)S(1)}, u32[]{:S(2)}, u32[]{:S(2)}) collective-permute-start(bf16[128,2048]{0,1:T(8,128)(2,1)S(1)} %get-tuple-element.257), channel_id=1, source_target_pairs={{8,0},{16,8},{24,16},{28,24},{20,28},{12,20},{4,12},{0,4},{9,1},{1... | collective-permute-start | bytes 1572872 | tf_op jit(solution)/shard_map/ppermute | solution.py:300
  418.3 64.4 %collective-permute-start.50 = (bf16[384,1024]{1,0:T(8,128)(2,1)S(1)}, bf16[384,1024]{1,0:T(8,128)(2,1)S(1)}, u32[]{:S(2)}, u32[]{:S(2)}) collective-permute-start(bf16[384,1024]{1,0:T(8,128)(2,1)S(1)} %get-tuple-element.224), channel_id=1, source_target_pairs={{0,2},{1,3},{2,0},{3,1},{4,6},{5,7},{6,4},{7,5},{8,10},{9,11},{10,... | collective-permute-start | bytes 2359304 | tf_op jit(solution)/shard_map/ppermute | solution.py:231
  438.2 45.0 %collective-permute-start.92 = (bf16[128,2048]{0,1:T(8,128)(2,1)}, bf16[128,2048]{0,1:T(8,128)(2,1)}, u32[]{:S(2)}, u32[]{:S(2)}) collective-permute-start(bf16[128,2048]{0,1:T(8,128)(2,1)} %add_convert_fusion.12), channel_id=1, source_target_pairs={{0,8},{8,16},{16,24},{24,28},{28,20},{20,12},{12,4},{4,0},{1,9},{9... | collective-permute-start | bytes 1572872 | tf_op jit(solution)/shard_map/ppermute | solution.py:297
  453.0 34.3 %collective-permute-start.96 = (bf16[128,2048]{0,1:T(8,128)(2,1)}, bf16[128,2048]{0,1:T(8,128)(2,1)}, u32[]{:S(2)}, u32[]{:S(2)}) collective-permute-start(bf16[128,2048]{0,1:T(8,128)(2,1)} %add_convert_fusion.9), channel_id=1, source_target_pairs={{8,0},{16,8},{24,16},{28,24},{20,28},{12,20},{4,12},{0,4},{9,1},{1... | collective-permute-start | bytes 1572872 | tf_op jit(solution)/shard_map/ppermute | solution.py:300
  488.6 53.8 %collective-permute-start.97 = (bf16[128,2048]{0,1:T(8,128)(2,1)S(1)}, bf16[128,2048]{0,1:T(8,128)(2,1)S(1)}, u32[]{:S(2)}, u32[]{:S(2)}) collective-permute-start(bf16[128,2048]{0,1:T(8,128)(2,1)S(1)} %add_convert_fusion.8), channel_id=1, source_target_pairs={{8,0},{16,8},{24,16},{28,24},{20,28},{12,20},{4,12},{0,4},{9,1},{1... | collective-permute-start | bytes 1572872 | tf_op jit(solution)/shard_map/ppermute | solution.py:300
  512.9 30.9 %collective-permute-start.94 = (bf16[128,2048]{0,1:T(8,128)(2,1)S(1)}, bf16[128,2048]{0,1:T(8,128)(2,1)S(1)}, u32[]{:S(2)}, u32[]{:S(2)}) collective-permute-start(bf16[128,2048]{0,1:T(8,128)(2,1)S(1)} %add_convert_fusion.10), channel_id=1, source_target_pairs={{0,8},{8,16},{16,24},{24,28},{28,20},{20,12},{12,4},{4,0},{1,9},{9... | collective-permute-start | bytes 1572872 | tf_op jit(solution)/shard_map/ppermute | solution.py:297
  540.9 26.9 %collective-permute-start.64 = (bf16[128,1024]{1,0:T(8,128)(2,1)}, bf16[128,1024]{1,0:T(8,128)(2,1)}, u32[]{:S(2)}, u32[]{:S(2)}) collective-permute-start(bf16[128,1024]{1,0:T(8,128)(2,1)} %get-tuple-element.275), channel_id=1, source_target_pairs={{0,8},{8,16},{16,24},{24,28},{28,20},{20,12},{12,4},{4,0},{1,9},{9... | collective-permute-start | bytes 786440 | tf_op jit(solution)/shard_map/ppermute | solution.py:297
  543.8 37.2 %collective-permute-start.78 = (bf16[128,1024]{1,0:T(8,128)(2,1)}, bf16[128,1024]{1,0:T(8,128)(2,1)S(1)}, u32[]{:S(2)}, u32[]{:S(2)}) collective-permute-start(bf16[128,1024]{1,0:T(8,128)(2,1)} %get-tuple-element.268), channel_id=1, source_target_pairs={{0,8},{8,16},{16,24},{24,28},{28,20},{20,12},{12,4},{4,0},{1,9},{9... | collective-permute-start | bytes 786440 | tf_op jit(solution)/shard_map/ppermute | solution.py:297
  550.2 32.8 %collective-permute-start.81 = (bf16[128,1024]{1,0:T(8,128)(2,1)S(1)}, bf16[128,1024]{1,0:T(8,128)(2,1)S(1)}, u32[]{:S(2)}, u32[]{:S(2)}) collective-permute-start(bf16[128,1024]{1,0:T(8,128)(2,1)S(1)} %get-tuple-element.269), channel_id=1, source_target_pairs={{8,0},{16,8},{24,16},{28,24},{20,28},{12,20},{4,12},{0,4},{9,1},{1... | collective-permute-start | bytes 786440 | tf_op jit(solution)/shard_map/ppermute | solution.py:300
  566.2 37.8 %collective-permute-start.98 = (bf16[128,2048]{0,1:T(8,128)(2,1)S(1)}, bf16[128,2048]{0,1:T(8,128)(2,1)S(1)}, u32[]{:S(2)}, u32[]{:S(2)}) collective-permute-start(bf16[128,2048]{0,1:T(8,128)(2,1)S(1)} %get-tuple-element.218), channel_id=1, source_target_pairs={{0,8},{8,16},{16,24},{24,28},{28,20},{20,12},{12,4},{4,0},{1,9},{9... | collective-permute-start | bytes 1572872 | tf_op jit(solution)/shard_map/ppermute | solution.py:313
  567.8 39.4 %collective-permute-start.99 = (bf16[128,2048]{0,1:T(8,128)(2,1)S(1)}, bf16[128,2048]{0,1:T(8,128)(2,1)S(1)}, u32[]{:S(2)}, u32[]{:S(2)}) collective-permute-start(bf16[128,2048]{0,1:T(8,128)(2,1)S(1)} %get-tuple-element.218), channel_id=1, source_target_pairs={{8,0},{16,8},{24,16},{28,24},{20,28},{12,20},{4,12},{0,4},{9,1},{1... | collective-permute-start | bytes 1572872 | tf_op jit(solution)/shard_map/ppermute | solution.py:316
  609.2 28.5 %collective-permute-start.101 = (bf16[128,2048]{0,1:T(8,128)(2,1)S(1)}, bf16[128,2048]{0,1:T(8,128)(2,1)S(1)}, u32[]{:S(2)}, u32[]{:S(2)}) collective-permute-start(bf16[128,2048]{0,1:T(8,128)(2,1)S(1)} %collective-permute-done.99), channel_id=1, source_target_pairs={{8,0},{16,8},{24,16},{28,24},{20,28},{12,20},{4,12},{0,4},{9,1},{1... | collective-permute-start | bytes 1572872 | tf_op jit(solution)/shard_map/ppermute | solution.py:316
  641.4 28.4 %collective-permute-start.103 = (bf16[128,2048]{0,1:T(8,128)(2,1)S(1)}, bf16[128,2048]{0,1:T(8,128)(2,1)S(1)}, u32[]{:S(2)}, u32[]{:S(2)}) collective-permute-start(bf16[128,2048]{0,1:T(8,128)(2,1)S(1)} %collective-permute-done.101), channel_id=1, source_target_pairs={{8,0},{16,8},{24,16},{28,24},{20,28},{12,20},{4,12},{0,4},{9,1},{1... | collective-permute-start | bytes 1572872 | tf_op jit(solution)/shard_map/ppermute | solution.py:316
  (213 other events, 2349.9 us)
Sparse Core Ops, SparseCore 0:
  296.3 179.5 all-reduce.4

commit v2 on v1

--- a/solution.py
+++ b/solution.py
@@ -283,39 +283,106 @@
     return size, place, right, [(there, here) for here, there in right]
 
 
-def sum_ring(values, gates=(), early=()):
-    size, place, right, left = ring()
-    rows = values.shape[0] // size
-    forward, back = size // 2, size - 1 - size // 2
-    gates = dict(enumerate(gates))
-    gate = lambda item, stage: after(item, gates[stage]) if gates.get(stage) is not None else item
-    chunk = lambda k: lax.dynamic_slice_in_dim(values, ((place + k) % size) * rows, rows, 0)
-    add = lambda got, own: (got.astype(F32) + own.astype(F32)).astype(B16)
-    from_left = from_right = None
-    for step in range(forward):
-        own = gate(chunk(forward - step), step)
-        from_left = lax.ppermute(own if step == 0 else add(from_left, own), "rows", right)
-        if step < back:
-            own = gate(chunk(step - back), step)
-            from_right = lax.ppermute(own if step == 0 else add(from_right, own), "rows", left)
-    out = jnp.zeros(values.shape, F32)
-    own, out = after((gate(chunk(0), forward), out), early)
-    total = own.astype(F32) + from_left.astype(F32)
-    if back:
-        total = total + from_right.astype(F32)
-    total = total.astype(B16)
-    put = lambda item, k: lax.dynamic_update_slice_in_dim(
-        out, item.astype(F32), ((place + k) % size) * rows, 0
-    )
-    out = put(total, 0)
-    from_left = from_right = total
-    for step in range(forward):
-        from_left = lax.ppermute(gate(from_left, forward + 1 + step), "rows", right)
-        out = put(from_left, -1 - step)
-        if step < back:
-            from_right = lax.ppermute(gate(from_right, forward + 1 + step), "rows", left)
-            out = put(from_right, 1 + step)
-    return out
+def plain(piece):
+    return piece
+
+
+def turned(piece):
+    return piece.T
+
+
+def paired(piece):
+    return piece.reshape(piece.shape[0], 2, piece.shape[1] // 2)
+
+
+class RowSum:
+    def __init__(self, values, parts, fill):
+        self.size, self.place, self.right, self.left = ring()
+        self.values, self.parts, self.fill = values, parts, fill
+        self.rows = values.shape[0] // self.size
+        self.half = self.rows // 2
+        self.stages = self.size // 2
+        self.steps = 2 * self.stages
+        self.done = 0
+        self.outs = None
+
+    def chunk(self, k):
+        at = ((self.place + k) % self.size) * self.rows
+        return lax.dynamic_slice_in_dim(self.values, at, self.rows, 0)
+
+    def send(self, to_right, to_left):
+        self.from_left = lax.ppermute(to_right, "rows", self.right)
+        self.from_right = lax.ppermute(to_left, "rows", self.left)
+        return (to_right, to_left)
+
+    def put(self, item, k, first=0):
+        at = ((self.place + k) % self.size) * self.rows + first
+        new, edge = [], 0
+        for out, (width, form) in zip(self.outs, self.parts):
+            piece = form(item[:, edge : edge + width].astype(F32))
+            starts = [0] * out.ndim
+            starts[out.ndim - 1 if form is turned else 0] = at
+            new.append(lax.dynamic_update_slice(out, piece, starts))
+            edge += width
+        self.outs = new
+
+    def step(self, gate=()):
+        stage, stages, half = self.done, self.stages, self.half
+        self.done += 1
+        wide = lambda item: item.astype(F32)
+        if stage == 0:
+            first = after((self.chunk(stages)[:half], self.chunk(-stages)[half:]), gate)
+            return self.send(*first)
+        if stage <= stages:
+            to_right, to_left = self.chunk(stages - stage), self.chunk(stage - stages)
+            to_right, to_left = after((to_right, to_left), gate)
+            to_right, to_left = wide(to_right), wide(to_left)
+            from_left, from_right = wide(self.from_left), wide(self.from_right)
+            if stage == 1:
+                from_left = jnp.pad(from_left, ((0, self.rows - half), (0, 0)))
+                from_right = jnp.pad(from_right, ((half, 0), (0, 0)))
+            if stage < stages:
+                to_right, to_left = to_right + from_left, to_left + from_right
+                return self.send(to_right.astype(B16), to_left.astype(B16))
+            total = (to_right + from_left + from_right).astype(B16)
+            self.outs = []
+            for width, form in self.parts:
+                item = jax.eval_shape(form, jax.ShapeDtypeStruct((self.values.shape[0], width), F32))
+                self.outs.append(jnp.full(item.shape, self.fill, F32))
+            total, self.outs = after((total, self.outs))
+            self.put(total, 0)
+            to_right = to_left = total
+        else:
+            to_right, to_left = after((self.from_left, self.from_right), gate)
+            self.put(to_right, stages - stage)
+            self.put(to_left, stage - stages)
+        if stage == 2 * stages - 1:
+            to_right, to_left = to_right[:half], to_left[half:]
+        return self.send(to_right, to_left)
+
+    def finish(self):
+        self.put(self.from_left, -self.stages)
+        self.put(self.from_right, self.stages, self.half)
+        return self.outs
+
+
+class WholeSum(RowSum):
+    def step(self, gate=()):
+        self.done += 1
+        if self.done == 1:
+            self.total = lax.psum(after(self.values, gate), "rows").astype(F32)
+        return ()
+
+    def finish(self):
+        edges = [sum(width for width, _ in self.parts[:k]) for k in range(len(self.parts) + 1)]
+        return [
+            form(self.total[:, edges[k] : edges[k + 1]]) for k, (_, form) in enumerate(self.parts)
+        ]
+
+
+def row_sum(values, parts, fill):
+    kind = WholeSum if lax.axis_size("rows") % 2 else RowSum
+    return kind(values, parts, float(fill))
 
 
 def sum_cube(values, axis):
@@ -347,8 +414,10 @@
 def ffn_forward(values, gain, weight_up, weight_down):
     normed, unit, inverse = normalize(values, gain)
     near, far = halves(gather(normed.astype(B16)))
-    pre = [dot(half, weight_up) for half in (near, far)]
-    act = [(item * jax.nn.sigmoid(item)).astype(B16) for item in pre]
+    pre, act = [], []
+    for half in (near, far):
+        pre.append(dot(after(half, act), weight_up))
+        act.append((pre[-1] * jax.nn.sigmoid(pre[-1])).astype(B16))
     total, (sent, _) = scatter(pieces(act[0], act[1], weight_down, (1, 0)))
     pre = [item.astype(B16) for item in pre]
     return (values + 0.5 * total, (unit, inverse, (near, far), pre, act), sent)
@@ -358,10 +427,10 @@
     unit, inverse, wide, pre, act = kept
     own = (0.5 * grad).astype(B16)
     cot = halves(gather(own))
-    d_pre = [
-        (dot(cot[half], weight_down, (1, 1)) * swish_slope(pre[half].astype(F32))).astype(B16)
-        for half in (0, 1)
-    ]
+    d_pre = []
+    for half in (0, 1):
+        d_act = dot(after(cot[half], d_pre), weight_down, (1, 1))
+        d_pre.append((d_act * swish_slope(pre[half].astype(F32))).astype(B16))
     d_norm, (sent, _) = scatter(pieces(d_pre[0], d_pre[1], weight_up, (1, 1)))
     d_in, grad_gain = normalize_back(d_norm, unit, inverse, gain)
     cot, d_pre = after((cot, d_pre), sent)
@@ -393,9 +462,10 @@
     where = (spans, q_at, k_at)
     normed, unit, inverse = normalize(values, gain)
     near, far = halves(gather(normed.astype(B16)))
-    far = after(far, rel, spans)
+    mixed = [dot(near, weights)]
+    far = after(far, rel, spans, mixed)
     fetched, arrived = prefetch(far)
-    mixed = [dot(half, weights) for half in (near, far)]
+    mixed.append(dot(far, weights))
     flat = lambda bias: bias.astype(F32).reshape(1, width)
     join = lambda items: jnp.concatenate(items, 0)
     q_content = join([(item[:, :width] + flat(content_bias)).astype(B16) for item in mixed])
@@ -422,7 +492,9 @@
     slots, width = sent.shape
     _, _, reorder = places(slots)
     cot = halves(gather(cot))
-    d_heads = jnp.concatenate([dot(half, attend_out, (1, 1)).astype(B16) for half in cot], 0)
+    d_near = dot(cot[0], attend_out, (1, 1)).astype(B16)
+    cot = (cot[0], after(cot[1], d_near))
+    d_heads = jnp.concatenate([d_near, dot(cot[1], attend_out, (1, 1)).astype(B16)], 0)
     if reorder:
         d_heads = to_true(d_heads)
     d_heads = after(d_heads, filler[0])
@@ -518,19 +590,14 @@
     size = lax.axis_size("tp")
     width = in_a.shape[1] // size
     parts, small_parts = [], []
+    grads = [
+        dot(left, right, (0, 0)).astype(B16)
+        for left, right in ((low, d_a), (low, d_b), (cot, inner[mine]))
+    ]
     small = jnp.stack(kernel_rows + [grad_gain_inner], 0)
     for slot in range(size):
         cols = slice(slot * width, (slot + 1) * width)
-        parts.append(
-            jnp.concatenate(
-                [
-                    dot(low, d_a[:, cols], (0, 0)),
-                    dot(low, d_b[:, cols], (0, 0)),
-                    dot(cot, inner[mine][:, cols], (0, 0)),
-                ],
-                1,
-            )
-        )
+        parts.append(jnp.concatenate([item[:, cols] for item in grads], 1))
         small_parts.append(small[:, cols])
     total, ends = scatter(parts)
     return (grad, next_cot, grad_gain, (total.astype(B16), scatter(small_parts)[0]), ends)
@@ -596,13 +663,23 @@
         grad, kept_first, gain_first, up_first, down_first
     )
     middle = jnp.concatenate([attend_grads, conv_grads[0]], 1)
-    gates = (None, marks[0], marks[0], marks[1], marks[1])
-    middle = sum_ring(middle, gates)
-    attend_sum, conv_sum = middle[:, : 5 * width], middle[:, 5 * width :]
-    second_up, second_down = [item.astype(F32) for item in second_sum]
-    first_down = sum_ring(first_grads[1])
-    first_up = sum_ring(first_grads[0], early=(second_up, second_down))
-    first_sum = (first_up, first_down)
+    forms = [(width, plain)] * 4 + [(width, turned), (2 * width, paired), (width, turned)]
+    middle = row_sum(middle, forms, 1)
+    down = row_sum(first_grads[1], [(first_grads[1].shape[1], plain)], 2)
+    up = row_sum(first_grads[0], [(first_grads[0].shape[1], plain)], 3)
+    middle.step()
+    token = middle.step(marks[1])
+    for step in range(down.steps):
+        token = down.step(token)
+        token = up.step(token)
+        if step == 2:
+            second_sum = after(second_sum, token)
+            second_up, second_down = [item.astype(F32) for item in second_sum]
+            token = (token, second_up, second_down)
+        if middle.done < middle.steps:
+            token = middle.step(token)
+    attend_sum = middle.finish()
+    first_sum = up.finish() + down.finish()
     gains = sum_cube(jnp.stack([sum_first, sum_attend, sum_conv, sum_second, sum_final]), "tp")
     small = jnp.concatenate([conv_grads[1], d_bias], 0)
     small_shape = small.shape
@@ -617,18 +694,18 @@
         first_sum[0],
         first_sum[1],
         gains[1],
-        attend_sum[:, :width],
-        attend_sum[:, width : 2 * width],
-        attend_sum[:, 2 * width : 3 * width],
-        attend_sum[:, 4 * width :].T,
-        attend_sum[:, 3 * width : 4 * width],
+        attend_sum[0],
+        attend_sum[1],
+        attend_sum[2],
+        attend_sum[4],
+        attend_sum[3],
         small[taps + 1].reshape(bias_shape),
         small[taps + 2].reshape(bias_shape),
         gains[2],
-        jnp.stack([conv_sum[:, :width], conv_sum[:, width : 2 * width]], 1),
+        attend_sum[5],
         small[:taps],
         small[taps],
-        conv_sum[:, 2 * width :].T,
+        attend_sum[6],
         gains[3],
         second_up,
         second_down,

time: 710 us -> 730 us (1.028)
  waiting for transfers between devices: 278 us -> 201 us
  other arithmetic: 82.4 us -> 148 us
  local copies, waits for them, and re-layouts: 65.4 us -> 88.4 us
  starting transfers between devices: 113 us -> 132 us
  matrix products: 107 us -> 92.5 us
    ppermute x42 -> x48, waiting for transfers between devices: 78.9 us -> 25.7 us  [the longest x24 25.7 us: send(): self.from_right = lax.ppermute(to_left, 'rows', self.left)]
    dynamic_update_slice x24 -> x27, other arithmetic: 16.7 us -> 41.2 us  [put(): new.append(lax.dynamic_update_slice(out, piece, starts))]
    unnamed x291 -> x330, local copies, waits for them, and re-layouts: 42.1 us -> 18.4 us
    psum x1, waiting for transfers between devices: 21.3 us -> 0.01 us  [body(): second_sum = lax.psum(second_grads, 'rows')]
    dynamic_update_slice x0 -> x27, local copies, waits for them, and re-layouts: none -> 19.6 us  [put(): new.append(lax.dynamic_update_slice(out, piece, starts))]
    convert_element_type x11 -> x21, other arithmetic: 9.1 us -> 24.3 us  [the longest x18 21.1 us: step(): return self.send(to_right.astype(B16), to_left.astype(B16))]
    dot_general x62 -> x53, matrix products: 107 us -> 92.5 us  [dot(): lax.dot_general(left, right, (((contract[0],), (contract[1],)), ((), ()))...]
    slice x0 -> x12, local copies, waits for them, and re-layouts: none -> 11.1 us  [the longest x6 6.83 us: step(): to_right, to_left = (to_right[:half], to_left[half:])]
  transfers between devices with their start and end apart: 106 -> 112, of which waited for: 42 -> 28; matrix products, arithmetic and copies ran while one was open for 29% -> 39% of each run, Pallas kernels for 6% -> 6%
where the time goes in v2:
time: 730 us; the launch traced here: 721 us
  waiting for transfers between devices  201 us (28%)
  other arithmetic  148 us (20%)
  starting transfers between devices  132 us (18%)
  matrix products  92.5 us (13%)
  local copies, waits for them, and re-layouts  88.4 us (12%)
  Pallas kernels  41.3 us (6%)
  between operations  17.4 us (2%)
    ppermute x54, waiting for transfers between devices, swap(): return lax.ppermute(values, 'tp', [(i, i ^ distance) for i in range(size)])  166 us
    dot_general x53, matrix products, dot(): lax.dot_general(left, right, (((contract[0],), (contract[1],)), ((), ()))...  92.5 us
    ppermute x24, starting transfers between devices, send(): self.from_right = lax.ppermute(to_left, 'rows', self.left)  49.1 us
    dynamic_update_slice x27, other arithmetic, put(): new.append(lax.dynamic_update_slice(out, piece, starts))  41.2 us
    ppermute x54, starting transfers between devices, swap(): return lax.ppermute(values, 'tp', [(i, i ^ distance) for i in range(size)])  38.8 us
    ppermute x24, starting transfers between devices, send(): self.from_left = lax.ppermute(to_right, 'rows', self.right)  31.8 us
    pallas_call x1, Pallas kernels, attend_back(): pl.pallas_call(functools.partial(attend_back_kernel, heads), out_shape=(s...  28.5 us
    ppermute x24, waiting for transfers between devices, send(): self.from_right = lax.ppermute(to_left, 'rows', self.left)  25.7 us
  transfers between devices with their start and end apart: 112, of which 28 were waited for; matrix products, arithmetic and copies ran while one was open for 39% of the time, Pallas kernels for 6%

profile of v2, /device:TPU:0, one launch (start us, length us, event | category | flops | bytes accessed | tf_op | source)
XLA Modules:
  0.0 720.6 jit_solution(12287471038729645198)
XLA Ops:
  51.1 16.9 %collective-permute-done.5 = bf16[384,1024]{1,0:T(8,128)(2,1)S(1)} collective-permute-done((bf16[384,1024]{1,0:T(8,128)(2,1)S(1)}, bf16[384,1024]{1,0:T(8,128)(2,1)S(1)}, u32[]{:S(2)}, u32[]{:S(2)}) %collective-permute-start.5) | collective-permute-done | bytes 786464 | tf_op jit(solution)/shard_map/ppermute | solution.py:231
  74.9 13.6 %collective-permute-done.7 = bf16[384,1024]{1,0:T(8,128)(2,1)S(1)} collective-permute-done((bf16[384,1024]{1,0:T(8,128)(2,1)S(1)}, bf16[384,1024]{1,0:T(8,128)(2,1)S(1)}, u32[]{:S(2)}, u32[]{:S(2)}) %collective-permute-start.7) | collective-permute-done | bytes 786464 | tf_op jit(solution)/shard_map/ppermute | solution.py:231
  99.7 12.8 %shard_map.399 = (bf16[1536,256]{1,0:T(8,128)(2,1)S(1)}, f32[1536,256]{1,0:T(8,128)S(1)}, f32[1536,2]{1,0:T(8,128)S(1)}) custom-call(s32[2,12]{1,0:T(2,128)S(1)} %pad_add_fusion.spans, s32[12]{0:T(128)S(1)} %fusion.218.q_at, s32[4]{0:T(128)S(1)} %fusion.219.k_at, bf16[1536,256]{1,0:T(8,128)(2,1)S(1)} %get-tuple-element.437.qc_ref, ...), custom_call_target="tpu_custom_call" | custom-call | flops 4000000000 | bytes 9000000 | tf_op jit(solution)/shard_map/pallas_call | solution.py:152
  112.6 6.3 collective-permute-done.10
  118.9 10.4 %collective-permute-done.11 = bf16[256,1024]{1,0:T(8,128)(2,1)S(1)} collective-permute-done((bf16[256,1024]{1,0:T(8,128)(2,1)S(1)}, bf16[256,1024]{1,0:T(8,128)(2,1)S(1)}, u32[]{:S(2)}, u32[]{:S(2)}) %collective-permute-start.11) | collective-permute-done | bytes 524320 | tf_op jit(solution)/shard_map/ppermute | solution.py:231
  136.2 17.0 %collective-permute-done.14 = bf16[384,1024]{1,0:T(8,128)(2,1)S(1)} collective-permute-done((bf16[384,1024]{1,0:T(8,128)(2,1)S(1)}, bf16[384,1024]{1,0:T(8,128)(2,1)S(1)}, u32[]{:S(2)}, u32[]{:S(2)}) %collective-permute-start.14) | collective-permute-done | bytes 786464 | tf_op jit(solution)/shard_map/ppermute | solution.py:231
  172.0 17.2 %collective-permute-done.28 = bf16[384,1024]{1,0:T(8,128)(2,1)S(1)} collective-permute-done((bf16[384,1024]{1,0:T(8,128)(2,1)S(1)}, bf16[384,1024]{1,0:T(8,128)(2,1)S(1)}, u32[]{:S(2)}, u32[]{:S(2)}) %collective-permute-start.28) | collective-permute-done | bytes 786464 | tf_op jit(solution)/shard_map/ppermute | solution.py:231
  202.4 16.7 %collective-permute-done.31 = bf16[384,1024]{1,0:T(8,128)(2,1)S(1)} collective-permute-done((bf16[384,1024]{1,0:T(8,128)(2,1)S(1)}, bf16[384,1024]{1,0:T(8,128)(2,1)S(1)}, u32[]{:S(2)}, u32[]{:S(2)}) %collective-permute-start.31) | collective-permute-done | bytes 786464 | tf_op jit(solution)/shard_map/ppermute | solution.py:231
  225.5 17.6 %collective-permute-done.34 = bf16[384,1024]{1,0:T(8,128)(2,1)S(1)} collective-permute-done((bf16[384,1024]{1,0:T(8,128)(2,1)S(1)}, bf16[384,1024]{1,0:T(8,128)(2,1)S(1)}, u32[]{:S(2)}, u32[]{:S(2)}) %collective-permute-start.34) | collective-permute-done | bytes 786464 | tf_op jit(solution)/shard_map/ppermute | solution.py:231
  257.8 16.2 %collective-permute-done.37 = bf16[384,1024]{1,0:T(8,128)(2,1)} collective-permute-done((bf16[384,1024]{1,0:T(8,128)(2,1)}, bf16[384,1024]{1,0:T(8,128)(2,1)}, u32[]{:S(2)}, u32[]{:S(2)}) %collective-permute-start.37) | collective-permute-done | bytes 786464 | tf_op jit(solution)/shard_map/ppermute | solution.py:231
  282.2 4.9 fusion.84
  315.6 7.6 %fusion.79 = bf16[1024,1024]{1,0:T(8,128)(2,1)} fusion(bf16[768,1024]{1,0:T(8,128)(2,1)} %copy-done.98, bf16[768,1024]{1,0:T(8,128)(2,1)} %copy-done.57, bf16[768,1024]{1,0:T(8,128)(2,1)} %copy-done.147, bf16[768,1024]{1,0:T(8,128)(2,1)} %copy-done.140), kind=kOutput, calls=%fused_computation.104 | convolution fusion | flops 3234856960 | bytes 8388608 | tf_op jit(solution)/shard_map/dot_general | solution.py:224
  338.3 28.5 %shard_map.400 = (bf16[1536,256]{1,0:T(8,128)(2,1)S(1)}, bf16[1536,256]{1,0:T(8,128)(2,1)S(1)}, bf16[1536,256]{1,0:T(8,128)(2,1)S(1)}, bf16[3072,256]{1,0:T(8,128)(2,1)}, f32[8,256]{1,0:T(8,128)S(1)}) custom-call(s32[2,12]{1,0:T(2,128)S(1)} %pad_add_fusion.spans, s32[12]{0:T(128)S(1)} %fusion.218.q_at, s32[4]{0:T(128)S(1)} %fusion.219.k_at, ...), custom_call_target="tpu_custom_call" | custom-call | flops 12000000000 | bytes 12000000 | tf_op jit(solution)/shard_map/pallas_call | solution.py:163
  367.4 4.4 collective-permute-done.44
  385.5 13.5 %collective-permute-done.47 = bf16[384,1024]{1,0:T(8,128)(2,1)S(1)} collective-permute-done((bf16[384,1024]{1,0:T(8,128)(2,1)S(1)}, bf16[384,1024]{1,0:T(8,128)(2,1)S(1)}, u32[]{:S(2)}, u32[]{:S(2)}) %collective-permute-start.47) | collective-permute-done | bytes 786464 | tf_op jit(solution)/shard_map/ppermute | solution.py:231
  405.3 15.4 %collective-permute-start.64 = (bf16[64,2048]{1,0:T(8,128)(2,1)S(1)}, bf16[64,2048]{1,0:T(8,128)(2,1)S(1)}, u32[]{:S(2)}, u32[]{:S(2)}) collective-permute-start(bf16[64,2048]{1,0:T(8,128)(2,1)S(1)} %get-tuple-element.166), channel_id=1, source_target_pairs={{8,0},{16,8},{24,16},{28,24},{20,28},{12,20},{4,12},{0,4},{9,1},{1... | collective-permute-start | bytes 786440 | tf_op jit(solution)/shard_map/ppermute | solution.py:315
  433.4 15.4 %collective-permute-start.66 = (bf16[128,2048]{1,0:T(8,128)(2,1)S(1)}, bf16[128,2048]{1,0:T(8,128)(2,1)S(1)}, u32[]{:S(2)}, u32[]{:S(2)}) collective-permute-start(bf16[128,2048]{1,0:T(8,128)(2,1)S(1)} %add_convert_fusion.14), channel_id=1, source_target_pairs={{8,0},{16,8},{24,16},{28,24},{20,28},{12,20},{4,12},{0,4},{9,1},{1... | collective-permute-start | bytes 1572872 | tf_op jit(solution)/shard_map/ppermute | solution.py:315
  452.8 4.9 fusion.94
  464.0 19.6 %collective-permute-done.66 = bf16[128,2048]{1,0:T(8,128)(2,1)S(1)} collective-permute-done((bf16[128,2048]{1,0:T(8,128)(2,1)S(1)}, bf16[128,2048]{1,0:T(8,128)(2,1)S(1)}, u32[]{:S(2)}, u32[]{:S(2)}) %collective-permute-start.66) | collective-permute-done | bytes 524320 | tf_op jit(solution)/shard_map/ppermute | solution.py:315
  487.0 4.2 collective-permute-done.68
  497.6 6.7 collective-permute-done.53
  504.3 4.3 collective-permute-start.74
  522.9 3.9 collective-permute-done.60
  552.5 4.2 convert_element_type.912
  (867 shorter events, 421.2 us)
Async XLA Ops:
  7.3 545.2 %all-reduce.11.cloned.1.call-start = ((), (), s32[]{:S(2)}) async-start(), calls=%async_computation | async-start | bytes 8388608 | tf_op jit(solution)/shard_map/psum | solution.py:657
  15.2 56.1 %collective-permute-start.16 = (bf16[6,256]{1,0:T(8,128)(2,1)S(1)}, bf16[6,256]{1,0:T(8,128)(2,1)S(1)}, u32[]{:S(2)}, u32[]{:S(2)}) collective-permute-start(bf16[6,256]{1,0:T(8,128)(2,1)S(1)} %pad_maximum_fusion.25), channel_id=1, source_target_pairs={{0,2},{1,3},{2,0},{3,1},{4,6},{5,7},{6,4},{7,5},{8,10},{9,11},{10,... | collective-permute-start | bytes 9224 | tf_op jit(solution)/shard_map/ppermute | solution.py:231
  15.3 56.1 %collective-permute-start.15 = (bf16[6,256]{1,0:T(8,128)(2,1)S(1)}, bf16[6,256]{1,0:T(8,128)(2,1)S(1)}, u32[]{:S(2)}, u32[]{:S(2)}) collective-permute-start(bf16[6,256]{1,0:T(8,128)(2,1)S(1)} %pad_maximum_fusion.25), channel_id=1, source_target_pairs={{0,1},{1,0},{2,3},{3,2},{4,5},{5,4},{6,7},{7,6},{8,9},{9,8},{10,11... | collective-permute-start | bytes 9224 | tf_op jit(solution)/shard_map/ppermute | solution.py:231
  92.3 39.1 %collective-permute-start.20 = (bf16[1024,256]{1,0:T(8,128)(2,1)S(1)}, bf16[1024,256]{1,0:T(8,128)(2,1)S(1)}, u32[]{:S(2)}, u32[]{:S(2)}) collective-permute-start(bf16[1024,256]{1,0:T(8,128)(2,1)S(1)} %get-tuple-element.131), channel_id=1, source_target_pairs={{0,1},{1,0},{2,3},{3,2},{4,5},{5,4},{6,7},{7,6},{8,9},{9,8},{10,11... | collective-permute-start | bytes 1572872 | tf_op jit(solution)/shard_map/ppermute | solution.py:231
  96.4 32.8 %collective-permute-start.11 = (bf16[256,1024]{1,0:T(8,128)(2,1)S(1)}, bf16[256,1024]{1,0:T(8,128)(2,1)S(1)}, u32[]{:S(2)}, u32[]{:S(2)}) collective-permute-start(bf16[256,1024]{1,0:T(8,128)(2,1)S(1)} %copy-done.88), channel_id=1, source_target_pairs={{0,2},{1,3},{2,0},{3,1},{4,6},{5,7},{6,4},{7,5},{8,10},{9,11},{10,... | collective-permute-start | bytes 1572872 | tf_op jit(solution)/shard_map/ppermute | solution.py:231
  299.2 28.3 %collective-permute-start.40 = (bf16[384,1024]{1,0:T(8,128)(2,1)}, bf16[384,1024]{1,0:T(8,128)(2,1)}, u32[]{:S(2)}, u32[]{:S(2)}) collective-permute-start(bf16[384,1024]{1,0:T(8,128)(2,1)} %get-tuple-element.259), channel_id=1, source_target_pairs={{0,1},{1,0},{2,3},{3,2},{4,5},{5,4},{6,7},{7,6},{8,9},{9,8},{10,11... | collective-permute-start | bytes 2359304 | tf_op jit(solution)/shard_map/ppermute | solution.py:231
  326.3 50.0 %collective-permute-start.62 = (bf16[1024,768]{1,0:T(8,128)(2,1)S(1)}, bf16[1024,768]{1,0:T(8,128)(2,1)S(1)}, u32[]{:S(2)}, u32[]{:S(2)}) collective-permute-start(bf16[1024,768]{1,0:T(8,128)(2,1)S(1)} %pad_maximum_fusion.11), channel_id=1, source_target_pairs={{0,1},{1,0},{2,3},{3,2},{4,5},{5,4},{6,7},{7,6},{8,9},{9,8},{10,11... | collective-permute-start | bytes 4718600 | tf_op jit(solution)/shard_map/ppermute | solution.py:231
  336.0 35.7 %collective-permute-start.44 = (bf16[1024,768]{1,0:T(8,128)(2,1)}, bf16[1024,768]{1,0:T(8,128)(2,1)}, u32[]{:S(2)}, u32[]{:S(2)}) collective-permute-start(bf16[1024,768]{1,0:T(8,128)(2,1)} %add_convert_fusion.2), channel_id=1, source_target_pairs={{0,2},{1,3},{2,0},{3,1},{4,6},{5,7},{6,4},{7,5},{8,10},{9,11},{10,... | collective-permute-start | bytes 4718600 | tf_op jit(solution)/shard_map/ppermute | solution.py:231
  431.1 66.5 %collective-permute-start.49 = (bf16[384,1024]{1,0:T(8,128)(2,1)S(1)}, bf16[384,1024]{1,0:T(8,128)(2,1)S(1)}, u32[]{:S(2)}, u32[]{:S(2)}) collective-permute-start(bf16[384,1024]{1,0:T(8,128)(2,1)S(1)} %convolution_convert_fusion.9), channel_id=1, source_target_pairs={{0,1},{1,0},{2,3},{3,2},{4,5},{5,4},{6,7},{7,6},{8,9},{9,8},{10,11... | collective-permute-start | bytes 2359304 | tf_op jit(solution)/shard_map/ppermute | solution.py:231
  433.4 50.2 %collective-permute-start.66 = (bf16[128,2048]{1,0:T(8,128)(2,1)S(1)}, bf16[128,2048]{1,0:T(8,128)(2,1)S(1)}, u32[]{:S(2)}, u32[]{:S(2)}) collective-permute-start(bf16[128,2048]{1,0:T(8,128)(2,1)S(1)} %add_convert_fusion.14), channel_id=1, source_target_pairs={{8,0},{16,8},{24,16},{28,24},{20,28},{12,20},{4,12},{0,4},{9,1},{1... | collective-permute-start | bytes 1572872 | tf_op jit(solution)/shard_map/ppermute | solution.py:315
  448.8 35.7 %collective-permute-start.65 = (bf16[128,2048]{1,0:T(8,128)(2,1)S(1)}, bf16[128,2048]{1,0:T(8,128)(2,1)S(1)}, u32[]{:S(2)}, u32[]{:S(2)}) collective-permute-start(bf16[128,2048]{1,0:T(8,128)(2,1)S(1)} %add_convert_fusion.15), channel_id=1, source_target_pairs={{0,8},{8,16},{16,24},{24,28},{28,20},{20,12},{12,4},{4,0},{1,9},{9... | collective-permute-start | bytes 1572872 | tf_op jit(solution)/shard_map/ppermute | solution.py:314
  460.8 30.4 %collective-permute-start.68 = (bf16[64,1024]{1,0:T(8,128)(2,1)S(1)}, bf16[64,1024]{1,0:T(8,128)(2,1)S(1)}, u32[]{:S(2)}, u32[]{:S(2)}) collective-permute-start(bf16[64,1024]{1,0:T(8,128)(2,1)S(1)} %get-tuple-element.168), channel_id=1, source_target_pairs={{8,0},{16,8},{24,16},{28,24},{20,28},{12,20},{4,12},{0,4},{9,1},{1... | collective-permute-start | bytes 393224 | tf_op jit(solution)/shard_map/ppermute | solution.py:315
  464.0 29.3 %collective-permute-start.67 = (bf16[64,1024]{1,0:T(8,128)(2,1)S(1)}, bf16[64,1024]{1,0:T(8,128)(2,1)S(1)}, u32[]{:S(2)}, u32[]{:S(2)}) collective-permute-start(bf16[64,1024]{1,0:T(8,128)(2,1)S(1)} %get-tuple-element.167), channel_id=1, source_target_pairs={{0,8},{8,16},{16,24},{24,28},{28,20},{20,12},{12,4},{4,0},{1,9},{9... | collective-permute-start | bytes 393224 | tf_op jit(solution)/shard_map/ppermute | solution.py:314
  493.3 45.3 %collective-permute-start.72 = (bf16[128,2048]{1,0:T(8,128)(2,1)}, bf16[128,2048]{1,0:T(8,128)(2,1)}, u32[]{:S(2)}, u32[]{:S(2)}) collective-permute-start(bf16[128,2048]{1,0:T(8,128)(2,1)} %add_convert_fusion.12), channel_id=1, source_target_pairs={{8,0},{16,8},{24,16},{28,24},{20,28},{12,20},{4,12},{0,4},{9,1},{1... | collective-permute-start | bytes 1572872 | tf_op jit(solution)/shard_map/ppermute | solution.py:315
  497.6 42.3 %collective-permute-start.71 = (bf16[128,2048]{1,0:T(8,128)(2,1)}, bf16[128,2048]{1,0:T(8,128)(2,1)}, u32[]{:S(2)}, u32[]{:S(2)}) collective-permute-start(bf16[128,2048]{1,0:T(8,128)(2,1)} %add_convert_fusion.13), channel_id=1, source_target_pairs={{0,8},{8,16},{16,24},{24,28},{28,20},{20,12},{12,4},{4,0},{1,9},{9... | collective-permute-start | bytes 1572872 | tf_op jit(solution)/shard_map/ppermute | solution.py:314
  504.3 37.8 %collective-permute-start.74 = (bf16[128,1024]{1,0:T(8,128)(2,1)}, bf16[128,1024]{1,0:T(8,128)(2,1)}, u32[]{:S(2)}, u32[]{:S(2)}) collective-permute-start(bf16[128,1024]{1,0:T(8,128)(2,1)} %add_convert_fusion.32), channel_id=1, source_target_pairs={{8,0},{16,8},{24,16},{28,24},{20,28},{12,20},{4,12},{0,4},{9,1},{1... | collective-permute-start | bytes 786440 | tf_op jit(solution)/shard_map/ppermute | solution.py:315
  513.2 31.8 %collective-permute-start.73 = (bf16[128,1024]{1,0:T(8,128)(2,1)}, bf16[128,1024]{1,0:T(8,128)(2,1)}, u32[]{:S(2)}, u32[]{:S(2)}) collective-permute-start(bf16[128,1024]{1,0:T(8,128)(2,1)} %add_convert_fusion.33), channel_id=1, source_target_pairs={{0,8},{8,16},{16,24},{24,28},{28,20},{20,12},{12,4},{4,0},{1,9},{9... | collective-permute-start | bytes 786440 | tf_op jit(solution)/shard_map/ppermute | solution.py:314
  581.7 32.8 %collective-permute-start.93 = (bf16[128,2048]{1,0:T(8,128)(2,1)}, bf16[128,2048]{1,0:T(8,128)(2,1)}, u32[]{:S(2)}, u32[]{:S(2)}) collective-permute-start(bf16[128,2048]{1,0:T(8,128)(2,1)} %collective-permute-done.79), channel_id=1, source_target_pairs={{0,8},{8,16},{16,24},{24,28},{28,20},{20,12},{12,4},{4,0},{1,9},{9... | collective-permute-start | bytes 1572872 | tf_op jit(solution)/shard_map/ppermute | solution.py:314
  586.2 28.3 %collective-permute-start.94 = (bf16[128,2048]{1,0:T(8,128)(2,1)}, bf16[128,2048]{1,0:T(8,128)(2,1)}, u32[]{:S(2)}, u32[]{:S(2)}) collective-permute-start(bf16[128,2048]{1,0:T(8,128)(2,1)} %collective-permute-done.80), channel_id=1, source_target_pairs={{8,0},{16,8},{24,16},{28,24},{20,28},{12,20},{4,12},{0,4},{9,1},{1... | collective-permute-start | bytes 1572872 | tf_op jit(solution)/shard_map/ppermute | solution.py:315
  590.4 31.0 %collective-permute-start.91 = (bf16[128,1024]{1,0:T(8,128)(2,1)S(1)}, bf16[128,1024]{1,0:T(8,128)(2,1)}, u32[]{:S(2)}, u32[]{:S(2)}) collective-permute-start(bf16[128,1024]{1,0:T(8,128)(2,1)S(1)} %add_convert_fusion.21), channel_id=1, source_target_pairs={{0,8},{8,16},{16,24},{24,28},{28,20},{20,12},{12,4},{4,0},{1,9},{9... | collective-permute-start | bytes 786440 | tf_op jit(solution)/shard_map/ppermute | solution.py:314
  593.4 28.8 %collective-permute-start.92 = (bf16[128,1024]{1,0:T(8,128)(2,1)S(1)}, bf16[128,1024]{1,0:T(8,128)(2,1)}, u32[]{:S(2)}, u32[]{:S(2)}) collective-permute-start(bf16[128,1024]{1,0:T(8,128)(2,1)S(1)} %add_convert_fusion.21), channel_id=1, source_target_pairs={{8,0},{16,8},{24,16},{28,24},{20,28},{12,20},{4,12},{0,4},{9,1},{1... | collective-permute-start | bytes 786440 | tf_op jit(solution)/shard_map/ppermute | solution.py:315
  595.3 30.5 %collective-permute-start.89 = (bf16[128,1024]{1,0:T(8,128)(2,1)}, bf16[128,1024]{1,0:T(8,128)(2,1)}, u32[]{:S(2)}, u32[]{:S(2)}) collective-permute-start(bf16[128,1024]{1,0:T(8,128)(2,1)} %add_convert_fusion.20), channel_id=1, source_target_pairs={{0,8},{8,16},{16,24},{24,28},{28,20},{20,12},{12,4},{4,0},{1,9},{9... | collective-permute-start | bytes 786440 | tf_op jit(solution)/shard_map/ppermute | solution.py:314
  617.1 29.6 %collective-permute-start.100 = (bf16[128,2048]{1,0:T(8,128)(2,1)}, bf16[128,2048]{1,0:T(8,128)(2,1)S(1)}, u32[]{:S(2)}, u32[]{:S(2)}) collective-permute-start(bf16[128,2048]{1,0:T(8,128)(2,1)} %collective-permute-done.94), channel_id=1, source_target_pairs={{8,0},{16,8},{24,16},{28,24},{20,28},{12,20},{4,12},{0,4},{9,1},{1... | collective-permute-start | bytes 1572872 | tf_op jit(solution)/shard_map/ppermute | solution.py:315
  622.2 29.4 %collective-permute-start.97 = (bf16[128,1024]{1,0:T(8,128)(2,1)}, bf16[128,1024]{1,0:T(8,128)(2,1)}, u32[]{:S(2)}, u32[]{:S(2)}) collective-permute-start(bf16[128,1024]{1,0:T(8,128)(2,1)} %collective-permute-done.91), channel_id=1, source_target_pairs={{0,8},{8,16},{16,24},{24,28},{28,20},{20,12},{12,4},{4,0},{1,9},{9... | collective-permute-start | bytes 786440 | tf_op jit(solution)/shard_map/ppermute | solution.py:314
  (240 other events, 2770.7 us)
Sparse Core Ops, SparseCore 0:
  323.4 173.8 all-reduce.10

commit v3 on v2

--- a/solution.py
+++ b/solution.py
@@ -77,7 +77,7 @@
 
 def attend_back_kernel(heads, spans, q_at, k_at, qc_ref, qp_ref, k_ref, v_ref, rel_ref, code_q_ref, code_k_ref,
                        d_out_ref, wide_ref, lse_ref,
-                       dq_ref, dk_ref, dv_ref, drel_ref, bias_ref, dk_acc, dv_acc, drel_acc):
+                       all_ref, drel_ref, bias_ref, dk_acc, dv_acc, drel_acc):
     slots = qc_ref.shape[0]
     scale = HD ** -0.5
     blocks, tiles = slots // TQ, slots // TK
@@ -134,14 +134,15 @@
             d_content, d_position = final[h]
             d_position = lax.dot_general(flip, d_position, (((1,), (0,)), ((), ())),
                                          precision=lax.Precision.HIGHEST, preferred_element_type=F32)
-            dq_ref[pl.ds(at, TQ), cols[h]] = (d_content + d_position).astype(B16)
+            all_ref[pl.ds(at, TQ), cols[h]] = (d_content + d_position).astype(B16)
             bias_ref[0:1, cols[h]] += jnp.sum(d_content, axis=0, keepdims=True)
             bias_ref[1:2, cols[h]] += jnp.sum(d_position, axis=0, keepdims=True)
         return 0
 
     lax.fori_loop(0, blocks, q_step, 0)
-    dk_ref[...] = dk_acc[...].astype(B16)
-    dv_ref[...] = dv_acc[...].astype(B16)
+    width = dk_acc.shape[1]
+    all_ref[:, width : 2 * width] = dk_acc[...].astype(B16)
+    all_ref[:, 2 * width :] = dv_acc[...].astype(B16)
     drel_ref[...] = drel_acc[...].astype(B16)
 
 def sds(s, d): return jax.ShapeDtypeStruct(s, d)
@@ -162,8 +163,8 @@
     heads = width // HD
     return pl.pallas_call(
         functools.partial(attend_back_kernel, heads),
-        out_shape=(sds((slots, width), B16),) * 3 + (sds((2 * slots, width), B16), sds((8, width), F32)),
-        in_specs=[SM] * 3 + [VM] * 10, out_specs=(VM,) * 5,
+        out_shape=(sds((slots, 3 * width), B16), sds((2 * slots, width), B16), sds((8, width), F32)),
+        in_specs=[SM] * 3 + [VM] * 10, out_specs=(VM,) * 3,
         scratch_shapes=[pltpu.VMEM((slots, width), F32), pltpu.VMEM((slots, width), F32), pltpu.VMEM((2 * slots, width), F32)],
         compiler_params=pltpu.CompilerParams(vmem_limit_bytes=48 << 20),
         cost_estimate=pl.CostEstimate(flops=int(12e9), bytes_accessed=int(12e6), transcendentals=int(2e6)),
@@ -244,13 +245,15 @@
     return [slots[slot] for slot in range(len(slots))]
 
 
-def scatter(parts):
+def scatter(parts, late=()):
     parts = dict(enumerate(parts))
     sent = got = None
     for distance in distances():
         for slot in sorted(parts, reverse=True):
             if slot & distance:
                 sent = parts.pop(slot).astype(B16)
+                if distance == distances()[-1]:
+                    sent = after(sent, late)
                 got = swap(sent, distance)
                 parts[slot ^ distance] = parts[slot ^ distance].astype(F32) + got.astype(F32)
     return parts[0], (sent, got)
@@ -260,19 +263,41 @@
     return lax.optimization_barrier((values, others))[0]
 
 
-def halves(slots):
-    half = len(slots) // 2
-    return jnp.concatenate(slots[:half], 0), jnp.concatenate(slots[half:], 0)
-
-
-def pieces(near, far, weight, contract):
-    count = lax.axis_size("tp") // 2
-    rows = near.shape[0] // count
+def spread(own, work, late=()):
+    size = lax.axis_size("tp")
+    far = swap(own, size // 2)
+    slots = {0: own}
+    for distance in reversed(distances()[:-1]):
+        for slot in list(slots):
+            slots[slot ^ distance] = swap(slots[slot], distance)
+    outs = {slot: work(slot, slots[slot]) for slot in sorted(slots)}
+    first = size // 2
+    slots[first] = after(far, outs, late)
+    arrived = slots[first]
+    for distance in reversed(distances()[:-1]):
+        for slot in [item for item in slots if item >= first]:
+            slots[slot ^ distance] = swap(slots[slot], distance)
+    for slot in range(first, size):
+        outs[slot] = work(slot, slots[slot])
+    ordered = lambda items: [items[slot] for slot in range(size)]
+    return ordered(slots), ordered(outs), arrived
+
+
+def join(items):
+    return jnp.concatenate(items, 0)
+
+
+def pieces(blocks, weight, contract, late=()):
     outs = {}
-    for slot in reversed(range(2 * count)):
-        source, place = (near, slot) if slot < count else (far, slot - count)
-        outs[slot] = dot(source[place * rows : (place + 1) * rows], weight, contract)
-    return [outs[slot] for slot in range(2 * count)]
+    for slot in reversed(range(len(blocks))):
+        outs[slot] = dot(blocks[slot], weight, contract)
+    return [outs[slot] for slot in range(len(blocks))]
+
+
+def cut(values):
+    size = lax.axis_size("tp")
+    rows = values.shape[0] // size
+    return [values[slot * rows : (slot + 1) * rows] for slot in range(size)]
 
 
 def ring():
@@ -291,98 +316,201 @@
     return piece.T
 
 
-def paired(piece):
-    return piece.reshape(piece.shape[0], 2, piece.shape[1] // 2)
+def first_kernel(at, *refs):
+    count = (len(refs) - 2) // 2
+    refs[-2][...] = jnp.concatenate([ref[...] for ref in refs[:count]], 1)
+    refs[-1][...] = jnp.concatenate([ref[...] for ref in refs[count:-2]], 1)
+
+
+def pass_kernel(second, at, *refs):
+    count = (len(refs) - 4) // 2
+    from_left, from_right = (ref[...].astype(F32) for ref in refs[-4:-2])
+    if second:
+        top = pl.program_id(0) == 0
+        from_left = jnp.where(top, from_left, 0.0)
+        from_right = jnp.where(top, 0.0, from_right)
+    own = jnp.concatenate([ref[...] for ref in refs[:count]], 1).astype(F32)
+    refs[-2][...] = (own + from_left).astype(B16)
+    own = jnp.concatenate([ref[...] for ref in refs[count:-4]], 1).astype(F32)
+    refs[-1][...] = (own + from_right).astype(B16)
+
+
+def total_kernel(split, at, *refs):
+    count = len(refs) - 4
+    own = jnp.concatenate([ref[...] for ref in refs[:count]], 1).astype(F32)
+    from_left, from_right = (ref[...].astype(F32) for ref in refs[count : count + 2])
+    half = refs[-1].shape[0]
+    if split:
+        refs[-2][...] = (own[:half] + from_left).astype(B16)
+        refs[-1][...] = (own[half:] + from_right).astype(B16)
+    else:
+        total = (own + from_left + from_right).astype(B16)
+        refs[-2][...] = total[:half]
+        refs[-1][...] = total[half:]
+
+
+def place_kernel(forms, spots, at, *refs):
+    count = len(spots)
+    outs, scratch = refs[count : count + len(forms)], list(refs[count + len(forms) :])
+    half = refs[0].shape[0]
+    held = [out if form is plain else scratch.pop(0) for out, form in zip(outs, forms)]
+    widths = [item.shape[1] for item in held]
+    size = held[0].shape[0] // (2 * half)
+    for ref, (k, bottom) in zip(refs[:count], spots):
+        start = pl.multiple_of(((at[0] + k + size) % size) * (2 * half) + bottom * half, half)
+        edge = 0
+        for item, width in zip(held, widths):
+            item[pl.ds(start, half), :] = ref[:, edge : edge + width].astype(F32)
+            edge += width
+    for item, out, form in zip(held, outs, forms):
+        if form is turned:
+            out[...] = item[...].T
 
 
 class RowSum:
-    def __init__(self, values, parts, fill):
+    def __init__(self, arrays, parts):
         self.size, self.place, self.right, self.left = ring()
-        self.values, self.parts, self.fill = values, parts, fill
-        self.rows = values.shape[0] // self.size
+        self.arrays, self.parts = list(arrays), parts
+        self.width = sum(item.shape[1] for item in arrays)
+        self.rows = arrays[0].shape[0] // self.size
         self.half = self.rows // 2
         self.stages = self.size // 2
         self.steps = 2 * self.stages
         self.done = 0
-        self.outs = None
-
-    def chunk(self, k):
-        at = ((self.place + k) % self.size) * self.rows
-        return lax.dynamic_slice_in_dim(self.values, at, self.rows, 0)
+        self.seen = []
+
+    def call(self, kernel, at, blocks, extra, out_rows, grid, gate, out_blocks):
+        arrays, extra = after((self.arrays, extra), gate)
+        specs, operands = [], []
+        for rows, index in blocks:
+            for item in arrays:
+                specs.append(pl.BlockSpec((rows, item.shape[1]), index))
+                operands.append(item)
+        for item, (rows, index) in zip(extra, out_blocks[1]):
+            specs.append(pl.BlockSpec((rows, self.width), index))
+            operands.append(item)
+        rows, index = out_blocks[0]
+        moved = sum(2 * rows * self.width for _ in range(4))
+        return pl.pallas_call(
+            kernel,
+            grid_spec=pltpu.PrefetchScalarGridSpec(
+                num_scalar_prefetch=1,
+                grid=(grid,),
+                in_specs=specs,
+                out_specs=[pl.BlockSpec((rows, self.width), index)] * 2,
+            ),
+            out_shape=(sds((out_rows, self.width), B16),) * 2,
+            cost_estimate=pl.CostEstimate(flops=moved, bytes_accessed=moved, transcendentals=0),
+        )(at, *operands)
 
     def send(self, to_right, to_left):
-        self.from_left = lax.ppermute(to_right, "rows", self.right)
-        self.from_right = lax.ppermute(to_left, "rows", self.left)
+        over = lambda items, way: [lax.ppermute(item, "rows", way) for item in items]
+        self.from_left, self.from_right = over(to_right, self.right), over(to_left, self.left)
         return (to_right, to_left)
 
-    def put(self, item, k, first=0):
-        at = ((self.place + k) % self.size) * self.rows + first
-        new, edge = [], 0
-        for out, (width, form) in zip(self.outs, self.parts):
-            piece = form(item[:, edge : edge + width].astype(F32))
-            starts = [0] * out.ndim
-            starts[out.ndim - 1 if form is turned else 0] = at
-            new.append(lax.dynamic_update_slice(out, piece, starts))
-            edge += width
-        self.outs = new
-
     def step(self, gate=()):
-        stage, stages, half = self.done, self.stages, self.half
+        stage, stages, half, rows = self.done, self.stages, self.half, self.rows
         self.done += 1
-        wide = lambda item: item.astype(F32)
+        ids = [(self.place + k) % self.size for k in (stages - stage, stage - stages)]
+        at = jnp.stack(ids).astype(jnp.int32)
+        whole = lambda i, at: (0, 0)
         if stage == 0:
-            first = after((self.chunk(stages)[:half], self.chunk(-stages)[half:]), gate)
-            return self.send(*first)
-        if stage <= stages:
-            to_right, to_left = self.chunk(stages - stage), self.chunk(stage - stages)
-            to_right, to_left = after((to_right, to_left), gate)
-            to_right, to_left = wide(to_right), wide(to_left)
-            from_left, from_right = wide(self.from_left), wide(self.from_right)
-            if stage == 1:
-                from_left = jnp.pad(from_left, ((0, self.rows - half), (0, 0)))
-                from_right = jnp.pad(from_right, ((half, 0), (0, 0)))
-            if stage < stages:
-                to_right, to_left = to_right + from_left, to_left + from_right
-                return self.send(to_right.astype(B16), to_left.astype(B16))
-            total = (to_right + from_left + from_right).astype(B16)
-            self.outs = []
-            for width, form in self.parts:
-                item = jax.eval_shape(form, jax.ShapeDtypeStruct((self.values.shape[0], width), F32))
-                self.outs.append(jnp.full(item.shape, self.fill, F32))
-            total, self.outs = after((total, self.outs))
-            self.put(total, 0)
-            to_right = to_left = total
+            blocks = [(half, lambda i, at: (2 * at[0], 0)), (half, lambda i, at: (2 * at[1] + 1, 0))]
+            out = self.call(first_kernel, at, blocks, [], half, 1, gate, ((half, whole), []))
+            return self.send([out[0]], [out[1]])
+        if stage < stages:
+            blocks = [
+                (half, lambda i, at: (2 * at[0] + i, 0)), (half, lambda i, at: (2 * at[1] + i, 0)),
+            ]
+            here = (half, lambda i, at: (i, 0))
+            got = (half, whole) if stage == 1 else here
+            kernel = functools.partial(pass_kernel, stage == 1)
+            extra = self.from_left + self.from_right
+            out = self.call(kernel, at, blocks, extra, rows, 2, gate, (here, [got, got]))
+            return self.send([out[0]], [out[1]])
+        if stage == stages:
+            got = (half if stages == 1 else rows, whole)
+            kernel = functools.partial(total_kernel, stages == 1)
+            extra = self.from_left + self.from_right
+            blocks = [(rows, lambda i, at: (at[0], 0))]
+            out = self.call(kernel, at, blocks, extra, half, 1, gate, ((half, whole), [got, got]))
+            to_right = to_left = list(out)
+            self.see(to_right, 0)
         else:
             to_right, to_left = after((self.from_left, self.from_right), gate)
-            self.put(to_right, stages - stage)
-            self.put(to_left, stage - stages)
+            self.see(to_right, stages - stage)
+            self.see(to_left, stage - stages)
         if stage == 2 * stages - 1:
-            to_right, to_left = to_right[:half], to_left[half:]
+            to_right, to_left = to_right[:1], to_left[1:]
         return self.send(to_right, to_left)
 
-    def finish(self):
-        self.put(self.from_left, -self.stages)
-        self.put(self.from_right, self.stages, self.half)
-        return self.outs
-
-
-class WholeSum(RowSum):
+    def see(self, pair, k):
+        self.seen += [(pair[0], (k, 0)), (pair[1], (k, 1))]
+
+    def finish(self, gate=()):
+        self.seen += [(self.from_left[0], (-self.stages, 0)), (self.from_right[0], (self.stages, 1))]
+        items = after([item for item, _ in self.seen], gate)
+        spots = [((k + self.size) % self.size, bottom) for _, (k, bottom) in self.seen]
+        forms = [form for _, form in self.parts]
+        length = self.arrays[0].shape[0]
+        shapes = [(length, width) if form is plain else (width, length) for width, form in self.parts]
+        scratch = [pltpu.VMEM((length, width), F32) for width, form in self.parts if form is turned]
+        moved = 6 * length * self.width
+        return pl.pallas_call(
+            functools.partial(place_kernel, forms, spots),
+            out_shape=[sds(shape, F32) for shape in shapes],
+            in_specs=[SM] + [VM] * len(items),
+            out_specs=[VM] * len(shapes),
+            scratch_shapes=scratch,
+            compiler_params=pltpu.CompilerParams(vmem_limit_bytes=40 << 20),
+            cost_estimate=pl.CostEstimate(flops=moved, bytes_accessed=moved, transcendentals=0),
+        )(self.place.reshape(1).astype(jnp.int32), *items)
+
+
+class WholeSum:
+    def __init__(self, arrays, parts):
+        self.arrays, self.parts, self.steps, self.done = list(arrays), parts, 1, 0
+
     def step(self, gate=()):
         self.done += 1
-        if self.done == 1:
-            self.total = lax.psum(after(self.values, gate), "rows").astype(F32)
+        values = after(jnp.concatenate(self.arrays, 1), gate)
+        self.total = lax.psum(values, "rows").astype(F32)
         return ()
 
-    def finish(self):
+    def finish(self, gate=()):
         edges = [sum(width for width, _ in self.parts[:k]) for k in range(len(self.parts) + 1)]
         return [
             form(self.total[:, edges[k] : edges[k + 1]]) for k, (_, form) in enumerate(self.parts)
         ]
 
 
-def row_sum(values, parts, fill):
-    kind = WholeSum if lax.axis_size("rows") % 2 else RowSum
-    return kind(values, parts, float(fill))
+def row_sum(arrays, parts):
+    size = lax.axis_size("rows")
+    fits = size % 2 == 0 and arrays[0].shape[0] % (16 * size) == 0
+    return (RowSum if fits else WholeSum)(arrays, parts)
+
+
+class RowSums:
+    def __init__(self, arrays, parts):
+        if all(item.shape[0] == arrays[0].shape[0] for item in arrays):
+            self.items = [row_sum(arrays, parts)]
+        else:
+            self.items = [row_sum([item], [part]) for item, part in zip(arrays, parts)]
+
+    @property
+    def left(self):
+        return max(item.steps - item.done for item in self.items)
+
+    def step(self, gate=()):
+        for item in self.items:
+            if item.done < item.steps:
+                gate = item.step(gate)
+        return gate
+
+    def finish(self, gate=()):
+        while self.left:
+            gate = self.step(gate)
+        return [out for item in self.items for out in item.finish(gate)]
 
 
 def sum_cube(values, axis):
@@ -411,32 +539,40 @@
     )
 
 
-def ffn_forward(values, gain, weight_up, weight_down):
+def ffn_forward(values, gain, weight_up, weight_down, prefetch=None):
     normed, unit, inverse = normalize(values, gain)
-    near, far = halves(gather(normed.astype(B16)))
-    pre, act = [], []
-    for half in (near, far):
-        pre.append(dot(after(half, act), weight_up))
-        act.append((pre[-1] * jax.nn.sigmoid(pre[-1])).astype(B16))
-    total, (sent, _) = scatter(pieces(act[0], act[1], weight_down, (1, 0)))
-    pre = [item.astype(B16) for item in pre]
-    return (values + 0.5 * total, (unit, inverse, (near, far), pre, act), sent)
-
-
-def ffn_backward(grad, kept, gain, weight_up, weight_down):
+
+    def work(slot, block):
+        pre = dot(block, weight_up)
+        return (pre * jax.nn.sigmoid(pre)).astype(B16), pre.astype(B16)
+
+    wide, outs, arrived = spread(normed.astype(B16), work)
+    act, pre = [item[0] for item in outs], [item[1] for item in outs]
+    fetched = ()
+    parts = pieces(act, weight_down, (1, 0))
+    if prefetch is not None:
+        fetched = prefetch(arrived)
+    total, (sent, _) = scatter(parts, fetched)
+    return (values + 0.5 * total, (unit, inverse, wide, pre, act), sent, fetched)
+
+
+def ffn_backward(grad, kept, gain, weight_up, weight_down, use=None, late=lambda own: ()):
     unit, inverse, wide, pre, act = kept
     own = (0.5 * grad).astype(B16)
-    cot = halves(gather(own))
-    d_pre = []
-    for half in (0, 1):
-        d_act = dot(after(cot[half], d_pre), weight_down, (1, 1))
-        d_pre.append((d_act * swish_slope(pre[half].astype(F32))).astype(B16))
-    d_norm, (sent, _) = scatter(pieces(d_pre[0], d_pre[1], weight_up, (1, 1)))
+
+    def work(slot, block):
+        d_act = dot(block, weight_down, (1, 1))
+        return (d_act * swish_slope(pre[slot].astype(F32))).astype(B16)
+
+    cot, d_pre, _ = spread(own, work, late(own))
+    d_norm, (sent, _) = scatter(pieces(d_pre, weight_up, (1, 1)))
+    cot, d_pre = after((cot, d_pre), sent)
+    grad_down = dot(join(act), join(cot), (0, 0)).astype(B16)
+    grad_up = dot(join(wide), join(d_pre), (0, 0)).astype(B16)
+    if use is not None:
+        d_norm = after(d_norm, use((grad_up, grad_down)))
     d_in, grad_gain = normalize_back(d_norm, unit, inverse, gain)
-    cot, d_pre = after((cot, d_pre), sent)
-    grad_down = dot(jnp.concatenate(act, 0), jnp.concatenate(cot, 0), (0, 0))
-    grad_up = dot(jnp.concatenate(wide, 0), jnp.concatenate(d_pre, 0), (0, 0))
-    return (grad + d_in, grad_gain, (grad_up.astype(B16), grad_down.astype(B16)), (own, sent))
+    return (grad + d_in, grad_gain, (grad_up, grad_down), (own, sent))
 
 
 def places(slots):
@@ -461,13 +597,10 @@
     q_at, k_at, reorder = places(slots)
     where = (spans, q_at, k_at)
     normed, unit, inverse = normalize(values, gain)
-    near, far = halves(gather(normed.astype(B16)))
-    mixed = [dot(near, weights)]
-    far = after(far, rel, spans, mixed)
-    fetched, arrived = prefetch(far)
-    mixed.append(dot(far, weights))
+    work = lambda slot, block: dot(block, weights)
+    wide, mixed, first = spread(normed.astype(B16), work, (rel, spans))
+    fetched, arrived = prefetch(first)
     flat = lambda bias: bias.astype(F32).reshape(1, width)
-    join = lambda items: jnp.concatenate(items, 0)
     q_content = join([(item[:, :width] + flat(content_bias)).astype(B16) for item in mixed])
     q_position = join([(item[:, :width] + flat(position_bias)).astype(B16) for item in mixed])
     key = join([item[:, width : 2 * width].astype(B16) for item in mixed])
@@ -481,48 +614,41 @@
     )
     heads_out, heads_wide, sums = attend(*operands)
     sent = after(to_true(heads_out) if reorder else heads_out, arrived)
-    half = slots // 2
-    total, _ = scatter(pieces(sent[:half], sent[half:], attend_out, (1, 0)))
-    kept = (unit, inverse, (near, far), operands, heads_wide, sums, sent)
+    total, _ = scatter(pieces(cut(sent), attend_out, (1, 0)))
+    kept = (unit, inverse, wide, operands, heads_wide, sums, sent)
     return (values + total, kept, fetched)
 
 
-def attend_backward(grad, cot, kept, gain, weights, attend_out, table, filler):
+def attend_backward(grad, cot, kept, gain, weights, attend_out, table, filler, ring_step, use):
     unit, inverse, wide, operands, heads_wide, sums, sent = kept
     slots, width = sent.shape
     _, _, reorder = places(slots)
-    cot = halves(gather(cot))
-    d_near = dot(cot[0], attend_out, (1, 1)).astype(B16)
-    cot = (cot[0], after(cot[1], d_near))
-    d_heads = jnp.concatenate([d_near, dot(cot[1], attend_out, (1, 1)).astype(B16)], 0)
+    work = lambda slot, block: dot(block, attend_out, (1, 1)).astype(B16)
+    cot, d_heads, _ = spread(cot, work)
+    d_heads = join(d_heads)
     if reorder:
         d_heads = to_true(d_heads)
-    d_heads = after(d_heads, filler[0])
-    d_query, d_key, d_value, d_rel, d_bias = attend_back(*operands, d_heads, heads_wide, sums)
-    d_query, d_key, d_value = after((d_query, d_key, d_value), filler[1])
+    d_heads = after(d_heads, ring_step(filler[0]))
+    d_all, d_rel, d_bias = attend_back(*operands, d_heads, heads_wide, sums)
     if reorder:
-        d_query, d_key, d_value = map(to_true, (d_query, d_key, d_value))
-    d_all = jnp.concatenate([d_query, d_key, d_value], 1)
-    half = slots // 2
-    d_norm, (last, _) = scatter(pieces(d_all[:half], d_all[half:], weights, (1, 1)))
+        d_all = to_true(d_all)
+    d_all = after(d_all, filler[1])
+    d_norm, (last, _) = scatter(pieces(cut(d_all), weights, (1, 1)))
+    cot, d_all, d_rel = after((cot, d_all, d_rel), ring_step(last))
+    grads = (
+        dot(join(wide), d_all, (0, 0)),
+        dot(table, d_rel, (0, 0)),
+        dot(join(cot), sent, (0, 0)),
+    )
+    d_norm = after(d_norm, use([item.astype(B16) for item in grads]))
     d_in, grad_gain = normalize_back(d_norm, unit, inverse, gain)
-    cot, d_all, d_rel = after((cot, d_all, d_rel), last)
-    grad_out = dot(jnp.concatenate(cot, 0), sent, (0, 0))
-    grad_all = dot(jnp.concatenate(wide, 0), d_all, (0, 0))
-    grad_pos = dot(table, d_rel, (0, 0))
-    grads = jnp.concatenate([item.astype(B16) for item in (grad_all, grad_pos, grad_out)], 1)
-    return (grad + d_in, grad_gain, grads, d_bias[:2])
-
-
-def conv_weights(point_in, depth_kernel, gain_inner, point_out, first):
-    taps = depth_kernel.shape[0]
-    own = after((point_in[:, 0], point_in[:, 1], point_out), first)
-    small = gather(jnp.concatenate([depth_kernel, gain_inner[None]], 0))
-    small = jnp.concatenate(small, 1).astype(F32)
-    in_a, in_b, out = map(gather, own)
-    arrived = [item[2::2] for item in (in_a, in_b, out)]
-    in_a, in_b = jnp.concatenate(in_a, 1), jnp.concatenate(in_b, 1)
-    return (in_a, in_b, small[:taps], small[taps], jnp.concatenate(out, 0)), arrived
+    return (grad + d_in, grad_gain, d_bias[:2])
+
+
+def conv_weights(own, first):
+    slots = [gather(after(item, first)) for item in own]
+    far = lax.axis_size("tp") // 2
+    return slots, [item[far] for item in slots]
 
 
 def conv_masks(segments, valid, rows, taps):
@@ -561,7 +687,7 @@
     return (values + dot(inner[reach : reach + rows], out), kept)
 
 
-def conv_backward(grad, kept, gain, full, masks):
+def conv_backward(grad, kept, gain, full, masks, ring_step):
     unit, inverse, low, mixed_a, gate, glu, inner_unit, inner_inverse, depth_norm, inner = kept
     in_a, in_b, kernel, gain_inner, out = full
     rows = grad.shape[0]
@@ -570,9 +696,10 @@
     mine = slice(reach, reach + rows)
     cot = grad.astype(B16)
     d_act = dot(halo(cot, reach), out, (1, 1))
-    d_depth_norm = d_act * swish_slope(depth_norm)
+    d_depth_norm = after(d_act * swish_slope(depth_norm), ring_step(cot))
     grad_gain_inner = jnp.sum((d_depth_norm * inner_unit)[mine], axis=0)
     d_depth, _ = normalize_back(d_depth_norm, inner_unit, inner_inverse, gain_inner)
+    d_depth = after(d_depth, ring_step(d_depth_norm))
     d_glu = 0.0
     kernel_rows = []
     for tap in range(taps):
@@ -586,7 +713,7 @@
     d_in, grad_gain = normalize_back(d_norm, unit, inverse, gain)
     grad = grad + d_in
     next_cot = grad.astype(B16)
-    low, cot, d_a, d_b, inner = after((low, cot, d_a, d_b, inner), next_cot)
+    low, cot, d_a, d_b, inner = after((low, cot, d_a, d_b, inner), ring_step(next_cot))
     size = lax.axis_size("tp")
     width = in_a.shape[1] // size
     parts, small_parts = [], []
@@ -594,6 +721,7 @@
         dot(left, right, (0, 0)).astype(B16)
         for left, right in ((low, d_a), (low, d_b), (cot, inner[mine]))
     ]
+    grads = after(grads, ring_step(grads))
     small = jnp.stack(kernel_rows + [grad_gain_inner], 0)
     for slot in range(size):
         cols = slice(slot * width, (slot + 1) * width)
@@ -633,53 +761,76 @@
     weights = jnp.concatenate([query_weight, key_weight, value_weight], 1)
     width = query_weight.shape[1]
     taps = depth_kernel.shape[0]
+    small = gather(jnp.concatenate([depth_kernel, gain_inner[None]], 0))
+    small = jnp.concatenate(small, 1).astype(F32)
     values = layer_input[0].astype(F32)
     rows = values.shape[0]
     slots = segment_row.shape[0]
     masks = conv_masks(segment_row, valid_row, rows, taps)
     code = codes(segment_row, valid_row)
     spans = spans_of(code)
-    values, kept_first, sent = ffn_forward(values, gain_first, up_first, down_first)
+    fetched = []
+
+    def prefetch(first):
+        slots, arrived = conv_weights([point_in[:, 0]], first)
+        fetched.extend(slots)
+        return arrived
+
+    values, kept_first, sent, _ = ffn_forward(values, gain_first, up_first, down_first, prefetch)
     table = distance_table(slots, values.shape[1], sent)
     rel = dot(table, pos_weight).astype(B16)
-    prefetch = functools.partial(conv_weights, point_in, depth_kernel, gain_inner, point_out)
-    values, kept_attend, full = attend_forward(
+    prefetch = functools.partial(conv_weights, (point_in[:, 1], point_out))
+    values, kept_attend, others = attend_forward(
         values, gain_attend, weights, attend_out, content_bias, position_bias, code, spans, rel, prefetch
     )
+    full = (
+        jnp.concatenate(fetched[0], 1), jnp.concatenate(others[0], 1),
+        small[:taps], small[taps], jnp.concatenate(others[1], 0),
+    )
     values, kept_conv = conv_forward(values, gain_conv, full, masks)
-    values, kept_second, _ = ffn_forward(values, gain_second, up_second, down_second)
+    values, kept_second, _, _ = ffn_forward(values, gain_second, up_second, down_second)
     final, final_unit, final_inverse = normalize(values, gain_final)
     layer_output = final.astype(B16)
     grad, sum_final = normalize_back(cotangent[0].astype(F32), final_unit, final_inverse, gain_final)
-    grad, sum_second, second_grads, _ = ffn_backward(
-        grad, kept_second, gain_second, up_second, down_second
-    )
-    second_sum = lax.psum(second_grads, "rows")
-    grad, cot, sum_conv, conv_grads, ends = conv_backward(grad, kept_conv, gain_conv, full, masks)
-    grad, sum_attend, attend_grads, d_bias = attend_backward(
-        grad, cot, kept_attend, gain_attend, weights, attend_out, table, ends
-    )
+    rings = {}
+    lanes = lambda items: [(item.shape[1], plain) for item in items]
+
+    def start_second(grads):
+        rings["second"] = RowSums(grads, lanes(grads))
+        return rings["second"].step()
+
+    grad, sum_second, _, _ = ffn_backward(
+        grad, kept_second, gain_second, up_second, down_second, start_second
+    )
+    second = rings["second"]
+    step_second = lambda gate: second.step(gate)
+    grad, cot, sum_conv, conv_grads, ends = conv_backward(
+        grad, kept_conv, gain_conv, full, masks, step_second
+    )
+
+    def start_middle(grads):
+        forms = [(width, plain)] * 4 + [(width, turned), (2 * width, plain), (width, turned)]
+        rings["middle"] = row_sum(grads + [conv_grads[0]], forms)
+        return second.step(rings["middle"].step())
+
+    grad, sum_attend, d_bias = attend_backward(
+        grad, cot, kept_attend, gain_attend, weights, attend_out, table, ends, step_second, start_middle
+    )
+    middle = rings["middle"]
     grad, sum_first, first_grads, marks = ffn_backward(
-        grad, kept_first, gain_first, up_first, down_first
-    )
-    middle = jnp.concatenate([attend_grads, conv_grads[0]], 1)
-    forms = [(width, plain)] * 4 + [(width, turned), (2 * width, paired), (width, turned)]
-    middle = row_sum(middle, forms, 1)
-    down = row_sum(first_grads[1], [(first_grads[1].shape[1], plain)], 2)
-    up = row_sum(first_grads[0], [(first_grads[0].shape[1], plain)], 3)
-    middle.step()
+        grad, kept_first, gain_first, up_first, down_first, None, middle.step
+    )
+    first = RowSums(first_grads, lanes(first_grads))
     token = middle.step(marks[1])
-    for step in range(down.steps):
-        token = down.step(token)
-        token = up.step(token)
-        if step == 2:
-            second_sum = after(second_sum, token)
-            second_up, second_down = [item.astype(F32) for item in second_sum]
-            token = (token, second_up, second_down)
-        if middle.done < middle.steps:
-            token = middle.step(token)
-    attend_sum = middle.finish()
-    first_sum = up.finish() + down.finish()
+    token = first.step(token)
+    while middle.done < middle.steps:
+        token = middle.step(token)
+        if first.left > 1:
+            token = first.step(token)
+    second_up, second_down = second.finish(token)
+    attend_sum = middle.finish(token)
+    token = (attend_sum, second_up, second_down)
+    first_sum = first.finish(token)
     gains = sum_cube(jnp.stack([sum_first, sum_attend, sum_conv, sum_second, sum_final]), "tp")
     small = jnp.concatenate([conv_grads[1], d_bias], 0)
     small_shape = small.shape
@@ -702,7 +853,7 @@
         small[taps + 1].reshape(bias_shape),
         small[taps + 2].reshape(bias_shape),
         gains[2],
-        attend_sum[5],
+        attend_sum[5].reshape(attend_sum[5].shape[0], 2, width),
         small[:taps],
         small[taps],
         attend_sum[6],

time: 730 us -> 727 us (level)
  other arithmetic: 148 us -> 61.8 us
  Pallas kernels: 41.3 us -> 101 us
  matrix products: 92.5 us -> 151 us
  local copies, waits for them, and re-layouts: 88.4 us -> 53.1 us
  waiting for transfers between devices: 201 us -> 217 us
  between operations: 17.4 us -> 3.87 us
    ppermute x48 -> x66, waiting for transfers between devices: 25.7 us -> 88 us  [send(): lax.ppermute(item, 'rows', way)]
    pallas_call x0 -> x18, Pallas kernels: none -> 60.7 us  [the longest x15 45.3 us: call(): pl.pallas_call(kernel, grid_spec=pltpu.PrefetchScalarGridSpec(num_scalar_...]
    dot_general x53 -> x65, matrix products: 92.5 us -> 151 us  [dot(): lax.dot_general(left, right, (((contract[0],), (contract[1],)), ((), ()))...]
    ppermute x54, waiting for transfers between devices: 166 us -> 123 us  [swap(): return lax.ppermute(values, 'tp', [(i, i ^ distance) for i in range(size)])]
    dynamic_update_slice x27 -> x0, other arithmetic: 41.2 us -> none  [put(): new.append(lax.dynamic_update_slice(out, piece, starts))]
    convert_element_type x26 -> x3, other arithmetic: 32.7 us -> 1.73 us  [the longest x2 1.46 us: ffn_forward(): wide, outs, arrived = spread(normed.astype(B16), work)]
    dynamic_update_slice x27 -> x0, local copies, waits for them, and re-layouts: 19.6 us -> none  [put(): new.append(lax.dynamic_update_slice(out, piece, starts))]
    unnamed x330 -> x472, local copies, waits for them, and re-layouts: 18.4 us -> 36.4 us
  transfers between devices with their start and end apart: 112 -> 129, of which waited for: 28 -> 49; matrix products, arithmetic and copies ran while one was open for 39% -> 29% of each run, Pallas kernels for 6% -> 12%
where the time goes in v3:
time: 727 us; the launch traced here: 715 us
  waiting for transfers between devices  217 us (30%)
  matrix products  151 us (21%)
  starting transfers between devices  127 us (17%)
  Pallas kernels  101 us (14%)
  other arithmetic  61.8 us (9%)
  local copies, waits for them, and re-layouts  53.1 us (7%)
    dot_general x65, matrix products, dot(): lax.dot_general(left, right, (((contract[0],), (contract[1],)), ((), ()))...  151 us
    ppermute x54, waiting for transfers between devices, swap(): return lax.ppermute(values, 'tp', [(i, i ^ distance) for i in range(size)])  123 us
    ppermute x66, starting transfers between devices, send(): lax.ppermute(item, 'rows', way)  92.1 us
    ppermute x66, waiting for transfers between devices, send(): lax.ppermute(item, 'rows', way)  88 us
    pallas_call x15, Pallas kernels, call(): pl.pallas_call(kernel, grid_spec=pltpu.PrefetchScalarGridSpec(num_scalar_...  45.3 us
    unnamed x472, local copies, waits for them, and re-layouts  36.4 us
    pallas_call x1, Pallas kernels, attend_back(): pl.pallas_call(functools.partial(attend_back_kernel, heads), out_shape=(s...  28.1 us
    ppermute x54, starting transfers between devices, swap(): return lax.ppermute(values, 'tp', [(i, i ^ distance) for i in range(size)])  23.3 us
  transfers between devices with their start and end apart: 129, of which 49 were waited for; matrix products, arithmetic and copies ran while one was open for 29% of the time, Pallas kernels for 12%

profile of v3, /device:TPU:0, one launch (start us, length us, event | category | flops | bytes accessed | tf_op | source)
XLA Modules:
  0.0 714.8 jit_solution(12945968189520094433)
XLA Ops:
  55.6 13.4 %collective-permute-done.6 = bf16[384,1024]{1,0:T(8,128)(2,1)S(1)} collective-permute-done((bf16[384,1024]{1,0:T(8,128)(2,1)S(1)}, bf16[384,1024]{1,0:T(8,128)(2,1)S(1)}, u32[]{:S(2)}, u32[]{:S(2)}) %collective-permute-start.6) | collective-permute-done | bytes 786464 | tf_op jit(solution)/shard_map/ppermute | solution.py:232
  79.6 12.8 %collective-permute-done.8 = bf16[384,1024]{1,0:T(8,128)(2,1)S(1)} collective-permute-done((bf16[384,1024]{1,0:T(8,128)(2,1)S(1)}, bf16[384,1024]{1,0:T(8,128)(2,1)S(1)}, u32[]{:S(2)}, u32[]{:S(2)}) %collective-permute-start.8) | collective-permute-done | bytes 786464 | tf_op jit(solution)/shard_map/ppermute | solution.py:232
  100.5 12.7 %shard_map.399 = (bf16[1536,256]{1,0:T(8,128)(2,1)S(1)}, f32[1536,256]{1,0:T(8,128)S(1)}, f32[1536,2]{1,0:T(8,128)S(1)}) custom-call(s32[2,12]{1,0:T(2,128)S(1)} %pad_add_fusion.spans, s32[12]{0:T(128)S(1)} %fusion.237.q_at, s32[4]{0:T(128)S(1)} %fusion.238.k_at, bf16[1536,256]{1,0:T(8,128)(2,1)S(1)} %pad_maximum_fusion.3.qc_ref, ...), custom_call_target="tpu_custom_call" | custom-call | flops 4000000000 | bytes 9000000 | tf_op jit(solution)/shard_map/pallas_call | solution.py:153
  113.2 4.9 collective-permute-done.11
  128.3 17.1 %collective-permute-done.14 = bf16[384,1024]{1,0:T(8,128)(2,1)S(1)} collective-permute-done((bf16[384,1024]{1,0:T(8,128)(2,1)S(1)}, bf16[384,1024]{1,0:T(8,128)(2,1)S(1)}, u32[]{:S(2)}, u32[]{:S(2)}) %collective-permute-start.14) | collective-permute-done | bytes 786464 | tf_op jit(solution)/shard_map/ppermute | solution.py:232
  168.1 15.6 %collective-permute-done.28 = bf16[384,1024]{1,0:T(8,128)(2,1)S(1)} collective-permute-done((bf16[384,1024]{1,0:T(8,128)(2,1)S(1)}, bf16[384,1024]{1,0:T(8,128)(2,1)S(1)}, u32[]{:S(2)}, u32[]{:S(2)}) %collective-permute-start.28) | collective-permute-done | bytes 786464 | tf_op jit(solution)/shard_map/ppermute | solution.py:232
  195.2 18.2 %collective-permute-done.31 = bf16[384,1024]{1,0:T(8,128)(2,1)S(1)} collective-permute-done((bf16[384,1024]{1,0:T(8,128)(2,1)S(1)}, bf16[384,1024]{1,0:T(8,128)(2,1)S(1)}, u32[]{:S(2)}, u32[]{:S(2)}) %collective-permute-start.31) | collective-permute-done | bytes 786464 | tf_op jit(solution)/shard_map/ppermute | solution.py:232
  226.3 12.2 %collective-permute-done.34 = bf16[384,1024]{1,0:T(8,128)(2,1)} collective-permute-done((bf16[384,1024]{1,0:T(8,128)(2,1)}, bf16[384,1024]{1,0:T(8,128)(2,1)}, u32[]{:S(2)}, u32[]{:S(2)}) %collective-permute-start.34) | collective-permute-done | bytes 786464 | tf_op jit(solution)/shard_map/ppermute | solution.py:232
  255.3 7.4 %fusion.91.refs_1_.refs_3_ = bf16[1024,1024]{1,0:T(8,128)(2,1)} fusion(bf16[384,1024]{1,0:T(8,128)(2,1)} %collective-permute-done.35, bf16[384,1024]{1,0:T(8,128)(2,1)} %collective-permute-done.34, bf16[384,1024]{1,0:T(8,128)(2,1)} %collective-permute-done.32, bf16[384,1024]{1,0:T(8,128)(2,1)} %multiply_convert_fusion.3, ...), kind=kOutput, calls=%fused_computation.111 | convolution fusion | flops 3247439872 | bytes 8388608 | tf_op jit(solution)/shard_map/dot_general | solution.py:225
  270.2 7.7 %collective-permute-start.40 = (bf16[64,2048]{1,0:T(8,128)(2,1)}, bf16[64,2048]{1,0:T(8,128)(2,1)S(1)}, u32[]{:S(2)}, u32[]{:S(2)}) collective-permute-start(bf16[64,2048]{1,0:T(8,128)(2,1)} %get-tuple-element.292), channel_id=1, source_target_pairs={{0,8},{8,16},{16,24},{24,28},{28,20},{20,12},{12,4},{4,0},{1,9},{9... | collective-permute-start | bytes 786440 | tf_op jit(solution)/shard_map/ppermute | solution.py:407
  302.1 6.4 collective-permute-done.42.refs_4_
  358.8 16.0 %collective-permute-done.45 = bf16[384,1024]{1,0:T(8,128)(2,1)S(1)} collective-permute-done((bf16[384,1024]{1,0:T(8,128)(2,1)S(1)}, bf16[384,1024]{1,0:T(8,128)(2,1)S(1)}, u32[]{:S(2)}, u32[]{:S(2)}) %collective-permute-start.45) | collective-permute-done | bytes 786464 | tf_op jit(solution)/shard_map/ppermute | solution.py:232
  384.4 5.2 collective-permute-done.52.refs_3_
  395.5 28.1 %shard_map.405 = (bf16[1536,768]{1,0:T(8,128)(2,1)}, bf16[3072,256]{1,0:T(8,128)(2,1)}, f32[8,256]{1,0:T(8,128)S(1)}) custom-call(s32[2,12]{1,0:T(2,128)S(1)} %pad_add_fusion.spans, s32[12]{0:T(128)S(1)} %fusion.237.q_at, s32[4]{0:T(128)S(1)} %fusion.238.k_at, bf16[1536,256]{1,0:T(8,128)(2,1)S(1)} %copy-done.10, bf16[1536,256]{1,0:T(8,128)(2,1)S(1)} %copy-done.8, ...), custom_call_target="tpu_custom_call" | custom-call | flops 12000000000 | bytes 12000000 | tf_op jit(solution)/shard_map/pallas_call | solution.py:164
  432.7 14.4 %collective-permute-start.63 = (bf16[64,2048]{1,0:T(8,128)(2,1)S(1)}, bf16[64,2048]{1,0:T(8,128)(2,1)S(1)}, u32[]{:S(2)}, u32[]{:S(2)}) collective-permute-start(bf16[64,2048]{1,0:T(8,128)(2,1)S(1)} %collective-permute-done.54.refs_5_), channel_id=1, source_target_pairs={{8,0},{16,8},{24,16},{28,24},{20,28},{12,20},{4,12},{0,4},{9,1},{1... | collective-permute-start | bytes 786440 | tf_op jit(solution)/shard_map/ppermute | solution.py:407
  452.8 5.7 collective-permute-done.63.refs_9_
  515.5 7.7 %collective-permute-done.85.refs_8_ = bf16[128,2048]{1,0:T(8,128)(2,1)S(1)} collective-permute-done((bf16[128,2048]{1,0:T(8,128)(2,1)S(1)}, bf16[128,2048]{1,0:T(8,128)(2,1)S(1)}, u32[]{:S(2)}, u32[]{:S(2)}) %collective-permute-start.85) | collective-permute-done | bytes 524320 | tf_op jit(solution)/shard_map/ppermute | solution.py:407
  529.6 7.6 %fusion.81.refs_1_.refs_3_ = bf16[1024,1024]{1,0:T(8,128)(2,1)} fusion(bf16[384,1024]{1,0:T(8,128)(2,1)} %copy-done.191, bf16[384,1024]{1,0:T(8,128)(2,1)} %collective-permute-done.71, bf16[384,1024]{1,0:T(8,128)(2,1)} %collective-permute-done.69, bf16[384,1024]{1,0:T(8,128)(2,1)S(1)} %get-tuple-element.373, bf16[384,1024]{1,0:T(8,128)(2,1)} %copy-done.207, ...), kind=kOutput, calls=%fused_computation.109 | convolution fusion | flops 3247439872 | bytes 8388608 | tf_op jit(solution)/shard_map/dot_general | solution.py:225
  537.2 6.7 fusion.86.refs_0_.refs_2_
  562.0 8.3 %fusion.183 = (f32[1024]{0:T(1024)S(1)}, f32[1024]{0:T(1024)S(1)}, f32[1024]{0:T(1024)S(1)}, f32[1024]{0:T(1024)S(1)}, f32[1024]{0:T(1024)S(1)}) fusion(f32[392,1024]{1,0:T(8,128)} %copy-done.68, f32[388,1024]{1,0:T(8,128)} %copy-done.88, f32[388,1024]{1,0:T(8,128)} %copy-done.87, f32[388,1024]{1,0:T(8,128)} %copy-done.89, f32[384]{0:T(512)S(1)} %slice.398, ...), kind=kLoop, calls=%fused_computation.207 | loop fusion | flops 4320256 | bytes 15750656 | tf_op jit(solution)/shard_map/reduce_sum | solution.py:709
  593.3 8.7 %collective-permute-done.99.refs_4_ = bf16[64,2048]{1,0:T(8,128)(2,1)S(1)} collective-permute-done((bf16[64,2048]{1,0:T(8,128)(2,1)S(1)}, bf16[64,2048]{1,0:T(8,128)(2,1)S(1)}, u32[]{:S(2)}, u32[]{:S(2)}) %collective-permute-start.99) | collective-permute-done | bytes 262176 | tf_op jit(solution)/shard_map/ppermute | solution.py:407
  668.6 5.1 shard_map.417
  673.9 5.2 shard_map.416
  709.4 5.1 shard_map.418
  (932 shorter events, 458.6 us)
Async XLA Ops:
  4.9 21.7 %collective-permute-start = (bf16[384,1024]{1,0:T(8,128)(2,1)}, bf16[384,1024]{1,0:T(8,128)(2,1)}, u32[]{:S(2)}, u32[]{:S(2)}) collective-permute-start(bf16[384,1024]{1,0:T(8,128)(2,1)} %fusion.114), channel_id=1, source_target_pairs={{0,1},{1,0},{2,3},{3,2},{4,5},{5,4},{6,7},{7,6},{8,9},{9,8},{10,11... | collective-permute-start | bytes 2359304 | tf_op jit(solution)/shard_map/ppermute | solution.py:232
  5.4 24.7 %collective-permute-start.2 = (bf16[384,1024]{1,0:T(8,128)(2,1)}, bf16[384,1024]{1,0:T(8,128)(2,1)}, u32[]{:S(2)}, u32[]{:S(2)}) collective-permute-start(bf16[384,1024]{1,0:T(8,128)(2,1)} %fusion.114), channel_id=1, source_target_pairs={{0,2},{1,3},{2,0},{3,1},{4,6},{5,7},{6,4},{7,5},{8,10},{9,11},{10,... | collective-permute-start | bytes 2359304 | tf_op jit(solution)/shard_map/ppermute | solution.py:232
  7.9 27.1 %collective-permute-start.16 = (bf16[6,256]{1,0:T(8,128)(2,1)S(1)}, bf16[6,256]{1,0:T(8,128)(2,1)S(1)}, u32[]{:S(2)}, u32[]{:S(2)}) collective-permute-start(bf16[6,256]{1,0:T(8,128)(2,1)S(1)} %pad_maximum_fusion.15), channel_id=1, source_target_pairs={{0,2},{1,3},{2,0},{3,1},{4,6},{5,7},{6,4},{7,5},{8,10},{9,11},{10,... | collective-permute-start | bytes 9224 | tf_op jit(solution)/shard_map/ppermute | solution.py:232
  8.0 43.7 %collective-permute-start.15 = (bf16[6,256]{1,0:T(8,128)(2,1)S(1)}, bf16[6,256]{1,0:T(8,128)(2,1)S(1)}, u32[]{:S(2)}, u32[]{:S(2)}) collective-permute-start(bf16[6,256]{1,0:T(8,128)(2,1)S(1)} %pad_maximum_fusion.15), channel_id=1, source_target_pairs={{0,1},{1,0},{2,3},{3,2},{4,5},{5,4},{6,7},{7,6},{8,9},{9,8},{10,11... | collective-permute-start | bytes 9224 | tf_op jit(solution)/shard_map/ppermute | solution.py:232
  51.8 66.9 %collective-permute-start.20 = (bf16[1024,256]{1,0:T(8,128)(2,1)}, bf16[1024,256]{1,0:T(8,128)(2,1)}, u32[]{:S(2)}, u32[]{:S(2)}) collective-permute-start(bf16[1024,256]{1,0:T(8,128)(2,1)} %get-tuple-element.269), channel_id=1, source_target_pairs={{0,1},{1,0},{2,3},{3,2},{4,5},{5,4},{6,7},{7,6},{8,9},{9,8},{10,11... | collective-permute-start | bytes 1572872 | tf_op jit(solution)/shard_map/ppermute | solution.py:232
  53.0 67.9 %collective-permute-start.21 = (bf16[1024,256]{1,0:T(8,128)(2,1)}, bf16[1024,256]{1,0:T(8,128)(2,1)}, u32[]{:S(2)}, u32[]{:S(2)}) collective-permute-start(bf16[1024,256]{1,0:T(8,128)(2,1)} %collective-permute-done.5), channel_id=1, source_target_pairs={{0,1},{1,0},{2,3},{3,2},{4,5},{5,4},{6,7},{7,6},{8,9},{9,8},{10,11... | collective-permute-start | bytes 1572872 | tf_op jit(solution)/shard_map/ppermute | solution.py:232
  94.1 24.0 %collective-permute-start.11 = (bf16[256,1024]{1,0:T(8,128)(2,1)S(1)}, bf16[256,1024]{1,0:T(8,128)(2,1)S(1)}, u32[]{:S(2)}, u32[]{:S(2)}) collective-permute-start(bf16[256,1024]{1,0:T(8,128)(2,1)S(1)} %copy-done.135), channel_id=1, source_target_pairs={{0,2},{1,3},{2,0},{3,1},{4,6},{5,7},{6,4},{7,5},{8,10},{9,11},{10,... | collective-permute-start | bytes 1572872 | tf_op jit(solution)/shard_map/ppermute | solution.py:232
  124.5 24.7 %collective-permute-start.25 = (bf16[256,1024]{1,0:T(8,128)(2,1)S(1)}, bf16[256,1024]{1,0:T(8,128)(2,1)S(1)}, u32[]{:S(2)}, u32[]{:S(2)}) collective-permute-start(bf16[256,1024]{1,0:T(8,128)(2,1)S(1)} %collective-permute-done.11), channel_id=1, source_target_pairs={{0,1},{1,0},{2,3},{3,2},{4,5},{5,4},{6,7},{7,6},{8,9},{9,8},{10,11... | collective-permute-start | bytes 1572872 | tf_op jit(solution)/shard_map/ppermute | solution.py:232
  250.4 27.6 %collective-permute-start.33 = (bf16[384,1024]{1,0:T(8,128)(2,1)}, bf16[384,1024]{1,0:T(8,128)(2,1)}, u32[]{:S(2)}, u32[]{:S(2)}) collective-permute-start(bf16[384,1024]{1,0:T(8,128)(2,1)} %convolution_convert_fusion.11), channel_id=1, source_target_pairs={{0,1},{1,0},{2,3},{3,2},{4,5},{5,4},{6,7},{7,6},{8,9},{9,8},{10,11... | collective-permute-start | bytes 2359304 | tf_op jit(solution)/shard_map/ppermute | solution.py:232
  254.8 23.1 %collective-permute-start.37 = (bf16[384,1024]{1,0:T(8,128)(2,1)}, bf16[384,1024]{1,0:T(8,128)(2,1)}, u32[]{:S(2)}, u32[]{:S(2)}) collective-permute-start(bf16[384,1024]{1,0:T(8,128)(2,1)} %add_convert_fusion.5), channel_id=1, source_target_pairs={{0,2},{1,3},{2,0},{3,1},{4,6},{5,7},{6,4},{7,5},{8,10},{9,11},{10,... | collective-permute-start | bytes 2359304 | tf_op jit(solution)/shard_map/ppermute | solution.py:232
  353.8 25.3 %collective-permute-start.55 = (bf16[1024,768]{1,0:T(8,128)(2,1)S(1)}, bf16[1024,768]{1,0:T(8,128)(2,1)S(1)}, u32[]{:S(2)}, u32[]{:S(2)}) collective-permute-start(bf16[1024,768]{1,0:T(8,128)(2,1)S(1)} %pad_maximum_fusion), channel_id=1, source_target_pairs={{0,1},{1,0},{2,3},{3,2},{4,5},{5,4},{6,7},{7,6},{8,9},{9,8},{10,11... | collective-permute-start | bytes 4718600 | tf_op jit(solution)/shard_map/ppermute | solution.py:232
  381.2 42.4 %collective-permute-start.56 = (bf16[1024,768]{1,0:T(8,128)(2,1)}, bf16[1024,768]{1,0:T(8,128)(2,1)S(1)}, u32[]{:S(2)}, u32[]{:S(2)}) collective-permute-start(bf16[1024,768]{1,0:T(8,128)(2,1)} %add_convert_fusion.2), channel_id=1, source_target_pairs={{0,2},{1,3},{2,0},{3,1},{4,6},{5,7},{6,4},{7,5},{8,10},{9,11},{10,... | collective-permute-start | bytes 4718600 | tf_op jit(solution)/shard_map/ppermute | solution.py:232
  384.3 48.4 %collective-permute-start.68 = (bf16[1024,768]{1,0:T(8,128)(2,1)S(1)}, bf16[1024,768]{1,0:T(8,128)(2,1)S(1)}, u32[]{:S(2)}, u32[]{:S(2)}) collective-permute-start(bf16[1024,768]{1,0:T(8,128)(2,1)S(1)} %pad_maximum_fusion.1), channel_id=1, source_target_pairs={{0,1},{1,0},{2,3},{3,2},{4,5},{5,4},{6,7},{7,6},{8,9},{9,8},{10,11... | collective-permute-start | bytes 4718600 | tf_op jit(solution)/shard_map/ppermute | solution.py:232
  392.2 60.4 %collective-permute-start.60 = (bf16[64,2048]{1,0:T(8,128)(2,1)S(1)}, bf16[64,2048]{1,0:T(8,128)(2,1)S(1)}, u32[]{:S(2)}, u32[]{:S(2)}) collective-permute-start(bf16[64,2048]{1,0:T(8,128)(2,1)S(1)} %collective-permute-done.51.refs_2_), channel_id=1, source_target_pairs={{0,8},{8,16},{16,24},{24,28},{28,20},{20,12},{12,4},{4,0},{1,9},{9... | collective-permute-start | bytes 786440 | tf_op jit(solution)/shard_map/ppermute | solution.py:407
  393.4 59.4 %collective-permute-start.61 = (bf16[64,2048]{1,0:T(8,128)(2,1)S(1)}, bf16[64,2048]{1,0:T(8,128)(2,1)}, u32[]{:S(2)}, u32[]{:S(2)}) collective-permute-start(bf16[64,2048]{1,0:T(8,128)(2,1)S(1)} %collective-permute-done.52.refs_3_), channel_id=1, source_target_pairs={{0,8},{8,16},{16,24},{24,28},{28,20},{20,12},{12,4},{4,0},{1,9},{9... | collective-permute-start | bytes 786440 | tf_op jit(solution)/shard_map/ppermute | solution.py:407
  394.0 58.8 %collective-permute-start.62 = (bf16[64,2048]{1,0:T(8,128)(2,1)S(1)}, bf16[64,2048]{1,0:T(8,128)(2,1)}, u32[]{:S(2)}, u32[]{:S(2)}) collective-permute-start(bf16[64,2048]{1,0:T(8,128)(2,1)S(1)} %collective-permute-done.53.refs_4_), channel_id=1, source_target_pairs={{8,0},{16,8},{24,16},{28,24},{20,28},{12,20},{4,12},{0,4},{9,1},{1... | collective-permute-start | bytes 786440 | tf_op jit(solution)/shard_map/ppermute | solution.py:407
  426.2 22.7 %collective-permute-start.58 = (bf16[384,1024]{1,0:T(8,128)(2,1)S(1)}, bf16[384,1024]{1,0:T(8,128)(2,1)S(1)}, u32[]{:S(2)}, u32[]{:S(2)}) collective-permute-start(bf16[384,1024]{1,0:T(8,128)(2,1)S(1)} %convolution_convert_fusion.4), channel_id=1, source_target_pairs={{0,1},{1,0},{2,3},{3,2},{4,5},{5,4},{6,7},{7,6},{8,9},{9,8},{10,11... | collective-permute-start | bytes 2359304 | tf_op jit(solution)/shard_map/ppermute | solution.py:232
  432.7 25.8 %collective-permute-start.63 = (bf16[64,2048]{1,0:T(8,128)(2,1)S(1)}, bf16[64,2048]{1,0:T(8,128)(2,1)S(1)}, u32[]{:S(2)}, u32[]{:S(2)}) collective-permute-start(bf16[64,2048]{1,0:T(8,128)(2,1)S(1)} %collective-permute-done.54.refs_5_), channel_id=1, source_target_pairs={{8,0},{16,8},{24,16},{28,24},{20,28},{12,20},{4,12},{0,4},{9,1},{1... | collective-permute-start | bytes 786440 | tf_op jit(solution)/shard_map/ppermute | solution.py:407
  448.9 27.4 %collective-permute-start.57 = (bf16[384,1024]{1,0:T(8,128)(2,1)}, bf16[384,1024]{1,0:T(8,128)(2,1)}, u32[]{:S(2)}, u32[]{:S(2)}) collective-permute-start(bf16[384,1024]{1,0:T(8,128)(2,1)} %convolution_convert_fusion.5), channel_id=1, source_target_pairs={{0,1},{1,0},{2,3},{3,2},{4,5},{5,4},{6,7},{7,6},{8,9},{9,8},{10,11... | collective-permute-start | bytes 2359304 | tf_op jit(solution)/shard_map/ppermute | solution.py:232
  452.6 23.8 %collective-permute-start.59 = (bf16[384,1024]{1,0:T(8,128)(2,1)}, bf16[384,1024]{1,0:T(8,128)(2,1)}, u32[]{:S(2)}, u32[]{:S(2)}) collective-permute-start(bf16[384,1024]{1,0:T(8,128)(2,1)} %add_convert_fusion.4), channel_id=1, source_target_pairs={{0,2},{1,3},{2,0},{3,1},{4,6},{5,7},{6,4},{7,5},{8,10},{9,11},{10,... | collective-permute-start | bytes 2359304 | tf_op jit(solution)/shard_map/ppermute | solution.py:232
  527.3 23.5 %collective-permute-start.89 = (bf16[128,2048]{1,0:T(8,128)(2,1)}, bf16[128,2048]{1,0:T(8,128)(2,1)S(1)}, u32[]{:S(2)}, u32[]{:S(2)}) collective-permute-start(bf16[128,2048]{1,0:T(8,128)(2,1)} %get-tuple-element.383), channel_id=1, source_target_pairs={{0,8},{8,16},{16,24},{24,28},{28,20},{20,12},{12,4},{4,0},{1,9},{9... | collective-permute-start | bytes 1572872 | tf_op jit(solution)/shard_map/ppermute | solution.py:407
  528.9 21.9 %collective-permute-start.90 = (bf16[128,2048]{1,0:T(8,128)(2,1)}, bf16[128,2048]{1,0:T(8,128)(2,1)}, u32[]{:S(2)}, u32[]{:S(2)}) collective-permute-start(bf16[128,2048]{1,0:T(8,128)(2,1)} %get-tuple-element.384), channel_id=1, source_target_pairs={{8,0},{16,8},{24,16},{28,24},{20,28},{12,20},{4,12},{0,4},{9,1},{1... | collective-permute-start | bytes 1572872 | tf_op jit(solution)/shard_map/ppermute | solution.py:407
  589.8 21.4 %collective-permute-start.70 = (bf16[384,1024]{1,0:T(8,128)(2,1)}, bf16[384,1024]{1,0:T(8,128)(2,1)}, u32[]{:S(2)}, u32[]{:S(2)}) collective-permute-start(bf16[384,1024]{1,0:T(8,128)(2,1)} %convolution_convert_fusion.9), channel_id=1, source_target_pairs={{0,1},{1,0},{2,3},{3,2},{4,5},{5,4},{6,7},{7,6},{8,9},{9,8},{10,11... | collective-permute-start | bytes 2359304 | tf_op jit(solution)/shard_map/ppermute | solution.py:232
  656.8 22.2 %collective-permute-start.115 = (bf16[64,2048]{1,0:T(8,128)(2,1)S(1)}, bf16[64,2048]{1,0:T(8,128)(2,1)S(1)}, u32[]{:S(2)}, u32[]{:S(2)}) collective-permute-start(bf16[64,2048]{1,0:T(8,128)(2,1)S(1)} %collective-permute-done.107.refs_2_), channel_id=1, source_target_pairs={{0,8},{8,16},{16,24},{24,28},{28,20},{20,12},{12,4},{4,0},{1,9},{9... | collective-permute-start | bytes 786440 | tf_op jit(solution)/shard_map/ppermute | solution.py:407
  (332 other events, 3262.9 us)

commit v4 on v3

--- a/solution.py
+++ b/solution.py
@@ -167,7 +167,7 @@
         in_specs=[SM] * 3 + [VM] * 10, out_specs=(VM,) * 3,
         scratch_shapes=[pltpu.VMEM((slots, width), F32), pltpu.VMEM((slots, width), F32), pltpu.VMEM((2 * slots, width), F32)],
         compiler_params=pltpu.CompilerParams(vmem_limit_bytes=48 << 20),
-        cost_estimate=pl.CostEstimate(flops=int(12e9), bytes_accessed=int(12e6), transcendentals=int(2e6)),
+        cost_estimate=pl.CostEstimate(flops=int(1e6), bytes_accessed=int(1e6), transcendentals=0),
     )(spans, q_at, k_at, qc, qp, k, v, rel, code_q, code_k, d_out, wide, lse)
 
 def codes(segments, valid):
@@ -265,22 +265,22 @@
 
 def spread(own, work, late=()):
     size = lax.axis_size("tp")
-    far = swap(own, size // 2)
+    first = size // 2
+    far = swap(own, first)
     slots = {0: own}
     for distance in reversed(distances()[:-1]):
         for slot in list(slots):
             slots[slot ^ distance] = swap(slots[slot], distance)
-    outs = {slot: work(slot, slots[slot]) for slot in sorted(slots)}
-    first = size // 2
-    slots[first] = after(far, outs, late)
-    arrived = slots[first]
+    near = join([slots[slot] for slot in range(first)])
+    outs = [work(0, near)]
+    arrived = after(far, outs, late)
+    slots = {0: arrived}
     for distance in reversed(distances()[:-1]):
-        for slot in [item for item in slots if item >= first]:
+        for slot in list(slots):
             slots[slot ^ distance] = swap(slots[slot], distance)
-    for slot in range(first, size):
-        outs[slot] = work(slot, slots[slot])
-    ordered = lambda items: [items[slot] for slot in range(size)]
-    return ordered(slots), ordered(outs), arrived
+    far = join([slots[slot] for slot in range(first)])
+    outs.append(work(1, far))
+    return [near, far], outs, arrived
 
 
 def join(items):
@@ -288,16 +288,19 @@
 
 
 def pieces(blocks, weight, contract, late=()):
+    count = lax.axis_size("tp") // 2
+    rows = blocks[0].shape[0] // count
     outs = {}
-    for slot in reversed(range(len(blocks))):
-        outs[slot] = dot(blocks[slot], weight, contract)
-    return [outs[slot] for slot in range(len(blocks))]
+    for slot in reversed(range(2 * count)):
+        place = slot % count
+        block = blocks[slot // count][place * rows : (place + 1) * rows]
+        outs[slot] = dot(block, weight, contract)
+    return [outs[slot] for slot in range(2 * count)]
 
 
 def cut(values):
-    size = lax.axis_size("tp")
-    rows = values.shape[0] // size
-    return [values[slot * rows : (slot + 1) * rows] for slot in range(size)]
+    half = values.shape[0] // 2
+    return [values[:half], values[half:]]
 
 
 def ring():
@@ -336,23 +339,18 @@
 
 
 def total_kernel(split, at, *refs):
-    count = len(refs) - 4
-    own = jnp.concatenate([ref[...] for ref in refs[:count]], 1).astype(F32)
-    from_left, from_right = (ref[...].astype(F32) for ref in refs[count : count + 2])
-    half = refs[-1].shape[0]
+    own = jnp.concatenate([ref[...] for ref in refs[:-3]], 1).astype(F32)
+    from_left, from_right = (ref[...].astype(F32) for ref in refs[-3:-1])
     if split:
-        refs[-2][...] = (own[:half] + from_left).astype(B16)
-        refs[-1][...] = (own[half:] + from_right).astype(B16)
+        refs[-1][...] = (own + jnp.concatenate([from_left, from_right], 0)).astype(B16)
     else:
-        total = (own + from_left + from_right).astype(B16)
-        refs[-2][...] = total[:half]
-        refs[-1][...] = total[half:]
+        refs[-1][...] = (own + from_left + from_right).astype(B16)
 
 
 def place_kernel(forms, spots, at, *refs):
     count = len(spots)
     outs, scratch = refs[count : count + len(forms)], list(refs[count + len(forms) :])
-    half = refs[0].shape[0]
+    half = refs[count - 1].shape[0]
     held = [out if form is plain else scratch.pop(0) for out, form in zip(outs, forms)]
     widths = [item.shape[1] for item in held]
     size = held[0].shape[0] // (2 * half)
@@ -360,7 +358,7 @@
         start = pl.multiple_of(((at[0] + k + size) % size) * (2 * half) + bottom * half, half)
         edge = 0
         for item, width in zip(held, widths):
-            item[pl.ds(start, half), :] = ref[:, edge : edge + width].astype(F32)
+            item[pl.ds(start, ref.shape[0]), :] = ref[:, edge : edge + width].astype(F32)
             edge += width
     for item, out, form in zip(held, outs, forms):
         if form is turned:
@@ -379,7 +377,7 @@
         self.done = 0
         self.seen = []
 
-    def call(self, kernel, at, blocks, extra, out_rows, grid, gate, out_blocks):
+    def call(self, kernel, at, blocks, extra, out_rows, grid, gate, out_blocks, count=2):
         arrays, extra = after((self.arrays, extra), gate)
         specs, operands = [], []
         for rows, index in blocks:
@@ -397,9 +395,9 @@
                 num_scalar_prefetch=1,
                 grid=(grid,),
                 in_specs=specs,
-                out_specs=[pl.BlockSpec((rows, self.width), index)] * 2,
+                out_specs=[pl.BlockSpec((rows, self.width), index)] * count,
             ),
-            out_shape=(sds((out_rows, self.width), B16),) * 2,
+            out_shape=(sds((out_rows, self.width), B16),) * count,
             cost_estimate=pl.CostEstimate(flops=moved, bytes_accessed=moved, transcendentals=0),
         )(at, *operands)
 
@@ -433,7 +431,11 @@
             kernel = functools.partial(total_kernel, stages == 1)
             extra = self.from_left + self.from_right
             blocks = [(rows, lambda i, at: (at[0], 0))]
-            out = self.call(kernel, at, blocks, extra, half, 1, gate, ((half, whole), [got, got]))
+            blocks = [(half, lambda i, at: (2 * at[0] + i, 0))] if stages > 1 else blocks
+            here = (half, lambda i, at: (i, 0)) if stages > 1 else (rows, whole)
+            got = here if stages > 1 else got
+            grid = 2 if stages > 1 else 1
+            out = self.call(kernel, at, blocks, extra, rows, grid, gate, (here, [got, got]), 1)
             to_right = to_left = list(out)
             self.see(to_right, 0)
         else:
@@ -441,11 +443,11 @@
             self.see(to_right, stages - stage)
             self.see(to_left, stage - stages)
         if stage == 2 * stages - 1:
-            to_right, to_left = to_right[:1], to_left[1:]
+            to_right, to_left = [to_right[0][:half]], [to_left[0][half:]]
         return self.send(to_right, to_left)
 
-    def see(self, pair, k):
-        self.seen += [(pair[0], (k, 0)), (pair[1], (k, 1))]
+    def see(self, items, k):
+        self.seen.append((items[0], (k, 0)))
 
     def finish(self, gate=()):
         self.seen += [(self.from_left[0], (-self.stages, 0)), (self.from_right[0], (self.stages, 1))]
@@ -490,12 +492,29 @@
     return (RowSum if fits else WholeSum)(arrays, parts)
 
 
+def start_sum(arrays):
+    if arrays[0].shape[0] == arrays[1].shape[0]:
+        arrays = [jnp.concatenate(arrays, 1)]
+    return [lax.psum_scatter(item, "rows", scatter_dimension=0, tiled=True) for item in arrays]
+
+
+def end_sum(shares, width):
+    whole = [lax.all_gather(item, "rows", axis=0, tiled=True) for item in shares]
+    if len(whole) == 1:
+        whole = [whole[0][:, :width], whole[0][:, width:]]
+    return whole
+
+
 class RowSums:
     def __init__(self, arrays, parts):
         if all(item.shape[0] == arrays[0].shape[0] for item in arrays):
             self.items = [row_sum(arrays, parts)]
         else:
             self.items = [row_sum([item], [part]) for item, part in zip(arrays, parts)]
+
+    @property
+    def done(self):
+        return self.items[0].done
 
     @property
     def left(self):
@@ -619,7 +638,7 @@
     return (values + total, kept, fetched)
 
 
-def attend_backward(grad, cot, kept, gain, weights, attend_out, table, filler, ring_step, use):
+def attend_backward(grad, cot, kept, gain, weights, attend_out, table, filler, use):
     unit, inverse, wide, operands, heads_wide, sums, sent = kept
     slots, width = sent.shape
     _, _, reorder = places(slots)
@@ -628,13 +647,13 @@
     d_heads = join(d_heads)
     if reorder:
         d_heads = to_true(d_heads)
-    d_heads = after(d_heads, ring_step(filler[0]))
+    d_heads = after(d_heads, filler[0])
     d_all, d_rel, d_bias = attend_back(*operands, d_heads, heads_wide, sums)
     if reorder:
         d_all = to_true(d_all)
     d_all = after(d_all, filler[1])
     d_norm, (last, _) = scatter(pieces(cut(d_all), weights, (1, 1)))
-    cot, d_all, d_rel = after((cot, d_all, d_rel), ring_step(last))
+    cot, d_all, d_rel = after((cot, d_all, d_rel), last)
     grads = (
         dot(join(wide), d_all, (0, 0)),
         dot(table, d_rel, (0, 0)),
@@ -645,8 +664,8 @@
     return (grad + d_in, grad_gain, d_bias[:2])
 
 
-def conv_weights(own, first):
-    slots = [gather(after(item, first)) for item in own]
+def conv_weights(pick, own, first):
+    slots = [gather(item) for item in pick(after(own, first))]
     far = lax.axis_size("tp") // 2
     return slots, [item[far] for item in slots]
 
@@ -687,7 +706,7 @@
     return (values + dot(inner[reach : reach + rows], out), kept)
 
 
-def conv_backward(grad, kept, gain, full, masks, ring_step):
+def conv_backward(grad, kept, gain, full, masks):
     unit, inverse, low, mixed_a, gate, glu, inner_unit, inner_inverse, depth_norm, inner = kept
     in_a, in_b, kernel, gain_inner, out = full
     rows = grad.shape[0]
@@ -696,10 +715,9 @@
     mine = slice(reach, reach + rows)
     cot = grad.astype(B16)
     d_act = dot(halo(cot, reach), out, (1, 1))
-    d_depth_norm = after(d_act * swish_slope(depth_norm), ring_step(cot))
+    d_depth_norm = d_act * swish_slope(depth_norm)
     grad_gain_inner = jnp.sum((d_depth_norm * inner_unit)[mine], axis=0)
     d_depth, _ = normalize_back(d_depth_norm, inner_unit, inner_inverse, gain_inner)
-    d_depth = after(d_depth, ring_step(d_depth_norm))
     d_glu = 0.0
     kernel_rows = []
     for tap in range(taps):
@@ -713,7 +731,7 @@
     d_in, grad_gain = normalize_back(d_norm, unit, inverse, gain)
     grad = grad + d_in
     next_cot = grad.astype(B16)
-    low, cot, d_a, d_b, inner = after((low, cot, d_a, d_b, inner), ring_step(next_cot))
+    low, cot, d_a, d_b, inner = after((low, cot, d_a, d_b, inner), next_cot)
     size = lax.axis_size("tp")
     width = in_a.shape[1] // size
     parts, small_parts = [], []
@@ -721,7 +739,6 @@
         dot(left, right, (0, 0)).astype(B16)
         for left, right in ((low, d_a), (low, d_b), (cot, inner[mine]))
     ]
-    grads = after(grads, ring_step(grads))
     small = jnp.stack(kernel_rows + [grad_gain_inner], 0)
     for slot in range(size):
         cols = slice(slot * width, (slot + 1) * width)
@@ -757,32 +774,34 @@
     down_second,
     gain_final,
 ):
-    segment_row, valid_row = segments[0], valid_frames[0]
-    weights = jnp.concatenate([query_weight, key_weight, value_weight], 1)
     width = query_weight.shape[1]
     taps = depth_kernel.shape[0]
-    small = gather(jnp.concatenate([depth_kernel, gain_inner[None]], 0))
-    small = jnp.concatenate(small, 1).astype(F32)
     values = layer_input[0].astype(F32)
     rows = values.shape[0]
-    slots = segment_row.shape[0]
-    masks = conv_masks(segment_row, valid_row, rows, taps)
+    slots = segments.shape[1]
+    fetched = []
+
+    def prefetch(first):
+        slots, arrived = conv_weights(lambda own: [own[:, 0]], point_in, first)
+        fetched.extend(slots)
+        return arrived
+
+    values, kept_first, sent, _ = ffn_forward(values, gain_first, up_first, down_first, prefetch)
+    segment_row, valid_row = after((segments[0], valid_frames[0]), sent)
     code = codes(segment_row, valid_row)
     spans = spans_of(code)
-    fetched = []
-
-    def prefetch(first):
-        slots, arrived = conv_weights([point_in[:, 0]], first)
-        fetched.extend(slots)
-        return arrived
-
-    values, kept_first, sent, _ = ffn_forward(values, gain_first, up_first, down_first, prefetch)
+    weights = jnp.concatenate(after((query_weight, key_weight, value_weight), sent), 1)
     table = distance_table(slots, values.shape[1], sent)
     rel = dot(table, pos_weight).astype(B16)
-    prefetch = functools.partial(conv_weights, (point_in[:, 1], point_out))
+    pick = lambda own: [own[0][:, 1], own[1]]
+    prefetch = functools.partial(conv_weights, pick, (point_in, point_out))
     values, kept_attend, others = attend_forward(
         values, gain_attend, weights, attend_out, content_bias, position_bias, code, spans, rel, prefetch
     )
+    ready = kept_attend[2][1]
+    masks = conv_masks(*after((segment_row, valid_row), ready), rows, taps)
+    small = gather(after(jnp.concatenate([depth_kernel, gain_inner[None]], 0), ready))
+    small = jnp.concatenate(small, 1).astype(F32)
     full = (
         jnp.concatenate(fetched[0], 1), jnp.concatenate(others[0], 1),
         small[:taps], small[taps], jnp.concatenate(others[1], 0),
@@ -792,33 +811,36 @@
     final, final_unit, final_inverse = normalize(values, gain_final)
     layer_output = final.astype(B16)
     grad, sum_final = normalize_back(cotangent[0].astype(F32), final_unit, final_inverse, gain_final)
-    rings = {}
+    held = {}
     lanes = lambda items: [(item.shape[1], plain) for item in items]
 
     def start_second(grads):
-        rings["second"] = RowSums(grads, lanes(grads))
-        return rings["second"].step()
+        held["second"] = start_sum(grads)
+        return grads
 
     grad, sum_second, _, _ = ffn_backward(
         grad, kept_second, gain_second, up_second, down_second, start_second
     )
-    second = rings["second"]
-    step_second = lambda gate: second.step(gate)
-    grad, cot, sum_conv, conv_grads, ends = conv_backward(
-        grad, kept_conv, gain_conv, full, masks, step_second
-    )
+    grad, cot, sum_conv, conv_grads, ends = conv_backward(grad, kept_conv, gain_conv, full, masks)
+    ends = (ends[0], (ends[1], held["second"]))
 
     def start_middle(grads):
         forms = [(width, plain)] * 4 + [(width, turned), (2 * width, plain), (width, turned)]
-        rings["middle"] = row_sum(grads + [conv_grads[0]], forms)
-        return second.step(rings["middle"].step())
+        held["middle"] = row_sum(grads + [conv_grads[0]], forms)
+        return held["middle"].step()
 
     grad, sum_attend, d_bias = attend_backward(
-        grad, cot, kept_attend, gain_attend, weights, attend_out, table, ends, step_second, start_middle
-    )
-    middle = rings["middle"]
+        grad, cot, kept_attend, gain_attend, weights, attend_out, table, ends, start_middle
+    )
+    second_sum = end_sum(held["second"], up_second.shape[1])
+    middle = held["middle"]
+
+    def fill(own):
+        own, sums = after((own, (sum_attend, sum_conv, sum_second, sum_final)), own)
+        return jnp.stack(sums), conv_grads[1]
+
     grad, sum_first, first_grads, marks = ffn_backward(
-        grad, kept_first, gain_first, up_first, down_first, None, middle.step
+        grad, kept_first, gain_first, up_first, down_first, None, fill
     )
     first = RowSums(first_grads, lanes(first_grads))
     token = middle.step(marks[1])
@@ -827,10 +849,14 @@
         token = middle.step(token)
         if first.left > 1:
             token = first.step(token)
-    second_up, second_down = second.finish(token)
+        if first.done == 3:
+            token = (token, grad)
+        if first.done == 5:
+            second_sum = after(second_sum, token)
+            second_up, second_down = [item.astype(F32) for item in second_sum]
+            token = (token, second_up, second_down)
     attend_sum = middle.finish(token)
-    token = (attend_sum, second_up, second_down)
-    first_sum = first.finish(token)
+    first_sum = first.finish(attend_sum)
     gains = sum_cube(jnp.stack([sum_first, sum_attend, sum_conv, sum_second, sum_final]), "tp")
     small = jnp.concatenate([conv_grads[1], d_bias], 0)
     small_shape = small.shape

time: 727 us -> 745 us (1.025)
  local copies, waits for them, and re-layouts: 53.1 us -> 89.3 us
  waiting for transfers between devices: 217 us -> 253 us
  matrix products: 151 us -> 121 us
  Pallas kernels: 101 us -> 81 us
  starting transfers between devices: 127 us -> 107 us
  between operations: 3.87 us -> 16.7 us
    unnamed x472 -> x376, local copies, waits for them, and re-layouts: 36.4 us -> 69.4 us
    ppermute x54, waiting for transfers between devices: 123 us -> 155 us  [swap(): return lax.ppermute(values, 'tp', [(i, i ^ distance) for i in range(size)])]
    dot_general x65 -> x53, matrix products: 151 us -> 121 us  [dot(): lax.dot_general(left, right, (((contract[0],), (contract[1],)), ((), ()))...]
    ppermute x66 -> x32, starting transfers between devices: 92.1 us -> 66.8 us  [send(): lax.ppermute(item, 'rows', way)]
    ppermute x66 -> x32, waiting for transfers between devices: 88 us -> 65.7 us  [send(): lax.ppermute(item, 'rows', way)]
    ppermute x5, waiting for transfers between devices: 2.36 us -> 21.4 us  [sum_cube(): lax.ppermute(values, axis, [(i, i ^ distance) for i in range(size)])]
    pallas_call x15 -> x10, Pallas kernels: 45.3 us -> 30.1 us  [call(): pl.pallas_call(kernel, grid_spec=pltpu.PrefetchScalarGridSpec(num_scalar_...]
    unnamed x0 -> x3, waiting for transfers between devices: none -> 9.42 us
  transfers between devices with their start and end apart: 129 -> 97, of which waited for: 49 -> 45; matrix products, arithmetic and copies ran while one was open for 29% -> 27% of each run, Pallas kernels for 12% -> 10%
where the time goes in v4:
time: 745 us; the launch traced here: 731 us
  waiting for transfers between devices  253 us (34%)
  matrix products  121 us (16%)
  starting transfers between devices  107 us (14%)
  local copies, waits for them, and re-layouts  89.3 us (12%)
  Pallas kernels  81 us (11%)
  other arithmetic  62.8 us (8%)
  between operations  16.7 us (2%)
    ppermute x54, waiting for transfers between devices, swap(): return lax.ppermute(values, 'tp', [(i, i ^ distance) for i in range(size)])  155 us
    dot_general x53, matrix products, dot(): lax.dot_general(left, right, (((contract[0],), (contract[1],)), ((), ()))...  121 us
    unnamed x376, local copies, waits for them, and re-layouts  69.4 us
    ppermute x32, starting transfers between devices, send(): lax.ppermute(item, 'rows', way)  66.8 us
    ppermute x32, waiting for transfers between devices, send(): lax.ppermute(item, 'rows', way)  65.7 us
    ppermute x54, starting transfers between devices, swap(): return lax.ppermute(values, 'tp', [(i, i ^ distance) for i in range(size)])  31.4 us
    pallas_call x10, Pallas kernels, call(): pl.pallas_call(kernel, grid_spec=pltpu.PrefetchScalarGridSpec(num_scalar_...  30.1 us
    pallas_call x1, Pallas kernels, attend_back(): pl.pallas_call(functools.partial(attend_back_kernel, heads), out_shape=(s...  28.4 us
  transfers between devices with their start and end apart: 97, of which 45 were waited for; matrix products, arithmetic and copies ran while one was open for 27% of the time, Pallas kernels for 10%

profile of v4, /device:TPU:0, one launch (start us, length us, event | category | flops | bytes accessed | tf_op | source)
XLA Modules:
  0.0 731.5 jit_solution(3569847646275980607)
XLA Ops:
  20.1 12.9 %collective-permute-done.2 = bf16[384,1024]{1,0:T(8,128)(2,1)} collective-permute-done((bf16[384,1024]{1,0:T(8,128)(2,1)}, bf16[384,1024]{1,0:T(8,128)(2,1)}, u32[]{:S(2)}, u32[]{:S(2)}) %collective-permute-start.2) | collective-permute-done | bytes 786464 | tf_op jit(solution)/shard_map/ppermute | solution.py:232
  60.0 10.5 %constant_dynamic-update-slice_fusion.2 = bf16[1024,768]{1,0:T(8,128)(2,1)S(1)} fusion(bf16[1024,256]{1,0:T(8,128)(2,1)} %param.32), kind=kLoop, calls=%fused_computation.324 | loop fusion | bytes 1048576
  86.4 12.9 %collective-permute-done.8 = bf16[384,1024]{1,0:T(8,128)(2,1)} collective-permute-done((bf16[384,1024]{1,0:T(8,128)(2,1)S(1)}, bf16[384,1024]{1,0:T(8,128)(2,1)}, u32[]{:S(2)}, u32[]{:S(2)}) %collective-permute-start.8) | collective-permute-done | bytes 786464 | tf_op jit(solution)/shard_map/ppermute | solution.py:232
  111.6 12.7 %shard_map.399 = (bf16[1536,256]{1,0:T(8,128)(2,1)S(1)}, f32[1536,256]{1,0:T(8,128)S(1)}, f32[1536,2]{1,0:T(8,128)S(1)}) custom-call(s32[2,12]{1,0:T(2,128)S(1)} %pad_add_fusion.spans, s32[12]{0:T(128)S(1)} %fusion.233.q_at, s32[4]{0:T(128)S(1)} %fusion.234.k_at, bf16[1536,256]{1,0:T(8,128)(2,1)S(1)} %get-tuple-element.536.qc_ref, ...), custom_call_target="tpu_custom_call" | custom-call | flops 4000000000 | bytes 9000000 | tf_op jit(solution)/shard_map/pallas_call | solution.py:153
  136.4 17.0 %collective-permute-done.16 = bf16[6,256]{1,0:T(8,128)(2,1)S(1)} collective-permute-done((bf16[6,256]{1,0:T(8,128)(2,1)S(1)}, bf16[6,256]{1,0:T(8,128)(2,1)S(1)}, u32[]{:S(2)}, u32[]{:S(2)}) %collective-permute-start.16) | collective-permute-done | bytes 3104 | tf_op jit(solution)/shard_map/ppermute | solution.py:232
  177.2 15.4 %collective-permute-done.28 = bf16[384,1024]{1,0:T(8,128)(2,1)S(1)} collective-permute-done((bf16[384,1024]{1,0:T(8,128)(2,1)S(1)}, bf16[384,1024]{1,0:T(8,128)(2,1)S(1)}, u32[]{:S(2)}, u32[]{:S(2)}) %collective-permute-start.28) | collective-permute-done | bytes 786464 | tf_op jit(solution)/shard_map/ppermute | solution.py:232
  203.1 18.0 %collective-permute-done.31 = bf16[384,1024]{1,0:T(8,128)(2,1)S(1)} collective-permute-done((bf16[384,1024]{1,0:T(8,128)(2,1)S(1)}, bf16[384,1024]{1,0:T(8,128)(2,1)S(1)}, u32[]{:S(2)}, u32[]{:S(2)}) %collective-permute-start.31) | collective-permute-done | bytes 786464 | tf_op jit(solution)/shard_map/ppermute | solution.py:232
  229.3 15.2 %collective-permute-done.34 = bf16[384,1024]{1,0:T(8,128)(2,1)S(1)} collective-permute-done((bf16[384,1024]{1,0:T(8,128)(2,1)S(1)}, bf16[384,1024]{1,0:T(8,128)(2,1)S(1)}, u32[]{:S(2)}, u32[]{:S(2)}) %collective-permute-start.34) | collective-permute-done | bytes 786464 | tf_op jit(solution)/shard_map/ppermute | solution.py:232
  262.5 11.5 %collective-permute-done.37 = bf16[384,1024]{1,0:T(8,128)(2,1)S(1)} collective-permute-done((bf16[384,1024]{1,0:T(8,128)(2,1)S(1)}, bf16[384,1024]{1,0:T(8,128)(2,1)S(1)}, u32[]{:S(2)}, u32[]{:S(2)}) %collective-permute-start.37) | collective-permute-done | bytes 786464 | tf_op jit(solution)/shard_map/ppermute | solution.py:232
  283.3 6.4 copy.83
  325.3 13.6 %collective-permute-done.41 = bf16[384,1024]{1,0:T(8,128)(2,1)} collective-permute-done((bf16[384,1024]{1,0:T(8,128)(2,1)}, bf16[384,1024]{1,0:T(8,128)(2,1)}, u32[]{:S(2)}, u32[]{:S(2)}) %collective-permute-start.41) | collective-permute-done | bytes 786464 | tf_op jit(solution)/shard_map/ppermute | solution.py:232
  352.3 28.4 %shard_map.400 = (bf16[1536,768]{1,0:T(8,128)(2,1)}, bf16[3072,256]{1,0:T(8,128)(2,1)}, f32[8,256]{1,0:T(8,128)S(1)}) custom-call(s32[2,12]{1,0:T(2,128)S(1)} %pad_add_fusion.spans, s32[12]{0:T(128)S(1)} %fusion.233.q_at, s32[4]{0:T(128)S(1)} %fusion.234.k_at, bf16[1536,256]{1,0:T(8,128)(2,1)S(1)} %copy-done.7, bf16[1536,256]{1,0:T(8,128)(2,1)S(1)} %copy-done.9, ...), custom_call_target="tpu_custom_call" | custom-call | flops 1000000 | bytes 1000000 | tf_op jit(solution)/shard_map/pallas_call | solution.py:164
  380.7 9.4 %reduce-scatter.4.cloned.1.call-done = bf16[128,2048]{1,0:T(8,128)(2,1)} async-done(((bf16[1024,2048]{1,0:T(8,128)(2,1)}), bf16[128,2048]{1,0:T(8,128)(2,1)}) %reduce-scatter.4.cloned.1.call-update) | async-done | bytes 524304
  437.0 6.4 fusion.20
  443.3 10.6 %collective-permute-done.51 = bf16[384,1024]{1,0:T(8,128)(2,1)S(1)} collective-permute-done((bf16[384,1024]{1,0:T(8,128)(2,1)S(1)}, bf16[384,1024]{1,0:T(8,128)(2,1)S(1)}, u32[]{:S(2)}, u32[]{:S(2)}) %collective-permute-start.51) | collective-permute-done | bytes 786464 | tf_op jit(solution)/shard_map/ppermute | solution.py:232
  463.9 14.3 %collective-permute-start.63 = (bf16[64,2048]{1,0:T(8,128)(2,1)S(1)}, bf16[64,2048]{1,0:T(8,128)(2,1)S(1)}, u32[]{:S(2)}, u32[]{:S(2)}) collective-permute-start(bf16[64,2048]{1,0:T(8,128)(2,1)S(1)} %copy-done.166), channel_id=1, source_target_pairs={{0,8},{8,16},{16,24},{24,28},{28,20},{20,12},{12,4},{4,0},{1,9},{9... | collective-permute-start | bytes 786440 | tf_op jit(solution)/shard_map/ppermute | solution.py:405
  497.2 7.8 %fusion.86.refs_0_.refs_2_ = bf16[1024,1024]{1,0:T(8,128)(2,1)} fusion(bf16[768,1024]{1,0:T(8,128)(2,1)} %copy-done.173, bf16[768,1024]{1,0:T(8,128)(2,1)} %fusion.20, bf16[384,1024]{1,0:T(8,128)(2,1)} %copy-done.147, bf16[384,1024]{1,0:T(8,128)(2,1)} %collective-permute-done.2, bf16[384,1024]{1,0:T(8,128)(2,1)} %collective-permute-done, ...), kind=kOutput, calls=%fused_computation.109 | convolution fusion | flops 3241148416 | bytes 8388608 | tf_op jit(solution)/shard_map/dot_general | solution.py:225
  514.4 7.0 collective-permute-done.67.refs_8_
  544.2 6.2 collective-permute-start.69
  602.8 7.9 %collective-permute-done.77.refs_2_ = bf16[128,2048]{1,0:T(8,128)(2,1)S(1)} collective-permute-done((bf16[128,2048]{1,0:T(8,128)(2,1)}, bf16[128,2048]{1,0:T(8,128)(2,1)S(1)}, u32[]{:S(2)}, u32[]{:S(2)}) %collective-permute-start.77) | collective-permute-done | bytes 524320 | tf_op jit(solution)/shard_map/ppermute | solution.py:405
  626.1 7.1 collective-permute-done.81.refs_1_
  637.3 7.1 collective-permute-done.87.refs_5_
  645.9 9.0 %collective-permute-done.85.refs_3_ = bf16[128,2048]{1,0:T(8,128)(2,1)} collective-permute-done((bf16[128,2048]{1,0:T(8,128)(2,1)S(1)}, bf16[128,2048]{1,0:T(8,128)(2,1)}, u32[]{:S(2)}, u32[]{:S(2)}) %collective-permute-start.85) | collective-permute-done | bytes 524320 | tf_op jit(solution)/shard_map/ppermute | solution.py:405
  665.5 11.6 %collective-permute-done.60 = f32[28,256]{1,0:T(8,128)S(1)} collective-permute-done((f32[28,256]{1,0:T(8,128)S(1)}, f32[28,256]{1,0:T(8,128)S(1)}, u32[]{:S(2)}, u32[]{:S(2)}) %collective-permute-start.60) | collective-permute-done | bytes 28704 | tf_op jit(solution)/shard_map/ppermute | solution.py:541
  (763 shorter events, 435.7 us)
Async XLA Ops:
  7.3 382.8 %reduce-scatter.4.cloned.1.call-start = ((), (), s32[]{:S(2)}) async-start(), calls=%async_computation.2 | async-start | bytes 4718592
  47.8 25.9 %collective-permute-start.1 = (bf16[384,1024]{1,0:T(8,128)(2,1)}, bf16[384,1024]{1,0:T(8,128)(2,1)}, u32[]{:S(2)}, u32[]{:S(2)}) collective-permute-start(bf16[384,1024]{1,0:T(8,128)(2,1)} %convolution_convert_fusion.15), channel_id=1, source_target_pairs={{0,1},{1,0},{2,3},{3,2},{4,5},{5,4},{6,7},{7,6},{8,9},{9,8},{10,11... | collective-permute-start | bytes 2359304 | tf_op jit(solution)/shard_map/ppermute | solution.py:232
  101.1 25.4 %collective-permute-start.10 = (bf16[1024,256]{1,0:T(8,128)(2,1)S(1)}, bf16[1024,256]{1,0:T(8,128)(2,1)S(1)}, u32[]{:S(2)}, u32[]{:S(2)}) collective-permute-start(bf16[1024,256]{1,0:T(8,128)(2,1)S(1)} %slice_bitcast_fusion), channel_id=1, source_target_pairs={{0,2},{1,3},{2,0},{3,1},{4,6},{5,7},{6,4},{7,5},{8,10},{9,11},{10,... | collective-permute-start | bytes 1572872 | tf_op jit(solution)/shard_map/ppermute | solution.py:232
  101.8 24.9 %collective-permute-start.11 = (bf16[256,1024]{1,0:T(8,128)(2,1)S(1)}, bf16[256,1024]{1,0:T(8,128)(2,1)S(1)}, u32[]{:S(2)}, u32[]{:S(2)}) collective-permute-start(bf16[256,1024]{1,0:T(8,128)(2,1)S(1)} %copy-done.102), channel_id=1, source_target_pairs={{0,2},{1,3},{2,0},{3,1},{4,6},{5,7},{6,4},{7,5},{8,10},{9,11},{10,... | collective-permute-start | bytes 1572872 | tf_op jit(solution)/shard_map/ppermute | solution.py:232
  128.8 34.3 %collective-permute-start.20 = (bf16[1024,256]{1,0:T(8,128)(2,1)}, bf16[1024,256]{1,0:T(8,128)(2,1)S(1)}, u32[]{:S(2)}, u32[]{:S(2)}) collective-permute-start(bf16[1024,256]{1,0:T(8,128)(2,1)} %copy-done.103), channel_id=1, source_target_pairs={{0,1},{1,0},{2,3},{3,2},{4,5},{5,4},{6,7},{7,6},{8,9},{9,8},{10,11... | collective-permute-start | bytes 1572872 | tf_op jit(solution)/shard_map/ppermute | solution.py:232
  131.8 23.1 %collective-permute-start.12 = (bf16[384,1024]{1,0:T(8,128)(2,1)S(1)}, bf16[384,1024]{1,0:T(8,128)(2,1)S(1)}, u32[]{:S(2)}, u32[]{:S(2)}) collective-permute-start(bf16[384,1024]{1,0:T(8,128)(2,1)S(1)} %convolution_convert_fusion.7), channel_id=1, source_target_pairs={{0,1},{1,0},{2,3},{3,2},{4,5},{5,4},{6,7},{7,6},{8,9},{9,8},{10,11... | collective-permute-start | bytes 2359304 | tf_op jit(solution)/shard_map/ppermute | solution.py:232
  133.7 21.5 %collective-permute-start.14 = (bf16[384,1024]{1,0:T(8,128)(2,1)S(1)}, bf16[384,1024]{1,0:T(8,128)(2,1)S(1)}, u32[]{:S(2)}, u32[]{:S(2)}) collective-permute-start(bf16[384,1024]{1,0:T(8,128)(2,1)S(1)} %add_convert_fusion.7), channel_id=1, source_target_pairs={{0,2},{1,3},{2,0},{3,1},{4,6},{5,7},{6,4},{7,5},{8,10},{9,11},{10,... | collective-permute-start | bytes 2359304 | tf_op jit(solution)/shard_map/ppermute | solution.py:232
  289.8 328.0 %all-gather.2.cloned.1.call-start = ((), (), s32[]{:S(2)}) async-start(), calls=%async_computation.1 | async-start | bytes 4718592 | tf_op jit(solution)/shard_map/all_gather | solution.py:502
  316.9 22.0 %collective-permute-start.43 = (bf16[1024,768]{1,0:T(8,128)(2,1)}, bf16[1024,768]{1,0:T(8,128)(2,1)}, u32[]{:S(2)}, u32[]{:S(2)}) collective-permute-start(bf16[1024,768]{1,0:T(8,128)(2,1)} %pad_maximum_fusion.5), channel_id=1, source_target_pairs={{0,1},{1,0},{2,3},{3,2},{4,5},{5,4},{6,7},{7,6},{8,9},{9,8},{10,11... | collective-permute-start | bytes 4718600 | tf_op jit(solution)/shard_map/ppermute | solution.py:232
  322.8 71.9 %collective-permute-start.48 = (bf16[1024,768]{1,0:T(8,128)(2,1)}, bf16[1024,768]{1,0:T(8,128)(2,1)}, u32[]{:S(2)}, u32[]{:S(2)}) collective-permute-start(bf16[1024,768]{1,0:T(8,128)(2,1)} %pad_maximum_fusion.6), channel_id=1, source_target_pairs={{0,1},{1,0},{2,3},{3,2},{4,5},{5,4},{6,7},{7,6},{8,9},{9,8},{10,11... | collective-permute-start | bytes 4718600 | tf_op jit(solution)/shard_map/ppermute | solution.py:232
  342.2 49.9 %collective-permute-start.44 = (bf16[1024,768]{1,0:T(8,128)(2,1)}, bf16[1024,768]{1,0:T(8,128)(2,1)}, u32[]{:S(2)}, u32[]{:S(2)}) collective-permute-start(bf16[1024,768]{1,0:T(8,128)(2,1)} %add_convert_fusion.2), channel_id=1, source_target_pairs={{0,2},{1,3},{2,0},{3,1},{4,6},{5,7},{6,4},{7,5},{8,10},{9,11},{10,... | collective-permute-start | bytes 4718600 | tf_op jit(solution)/shard_map/ppermute | solution.py:232
  463.9 23.1 %collective-permute-start.63 = (bf16[64,2048]{1,0:T(8,128)(2,1)S(1)}, bf16[64,2048]{1,0:T(8,128)(2,1)S(1)}, u32[]{:S(2)}, u32[]{:S(2)}) collective-permute-start(bf16[64,2048]{1,0:T(8,128)(2,1)S(1)} %copy-done.166), channel_id=1, source_target_pairs={{0,8},{8,16},{16,24},{24,28},{28,20},{20,12},{12,4},{4,0},{1,9},{9... | collective-permute-start | bytes 786440 | tf_op jit(solution)/shard_map/ppermute | solution.py:405
  480.1 70.4 %collective-permute-start.50 = (bf16[384,1024]{1,0:T(8,128)(2,1)}, bf16[384,1024]{1,0:T(8,128)(2,1)}, u32[]{:S(2)}, u32[]{:S(2)}) collective-permute-start(bf16[384,1024]{1,0:T(8,128)(2,1)} %convolution_convert_fusion.9), channel_id=1, source_target_pairs={{0,1},{1,0},{2,3},{3,2},{4,5},{5,4},{6,7},{7,6},{8,9},{9,8},{10,11... | collective-permute-start | bytes 2359304 | tf_op jit(solution)/shard_map/ppermute | solution.py:232
  482.2 68.2 %collective-permute-start.57 = (bf16[384,1024]{1,0:T(8,128)(2,1)}, bf16[384,1024]{1,0:T(8,128)(2,1)}, u32[]{:S(2)}, u32[]{:S(2)}) collective-permute-start(bf16[384,1024]{1,0:T(8,128)(2,1)} %add_convert_fusion.3), channel_id=1, source_target_pairs={{0,2},{1,3},{2,0},{3,1},{4,6},{5,7},{6,4},{7,5},{8,10},{9,11},{10,... | collective-permute-start | bytes 2359304 | tf_op jit(solution)/shard_map/ppermute | solution.py:232
  495.1 26.2 %collective-permute-start.67 = (bf16[128,2048]{1,0:T(8,128)(2,1)}, bf16[128,2048]{1,0:T(8,128)(2,1)S(1)}, u32[]{:S(2)}, u32[]{:S(2)}) collective-permute-start(bf16[128,2048]{1,0:T(8,128)(2,1)} %get-tuple-element.237), channel_id=1, source_target_pairs={{0,8},{8,16},{16,24},{24,28},{28,20},{20,12},{12,4},{4,0},{1,9},{9... | collective-permute-start | bytes 1572872 | tf_op jit(solution)/shard_map/ppermute | solution.py:405
  496.9 32.1 %collective-permute-start.68 = (bf16[128,2048]{1,0:T(8,128)(2,1)}, bf16[128,2048]{1,0:T(8,128)(2,1)S(1)}, u32[]{:S(2)}, u32[]{:S(2)}) collective-permute-start(bf16[128,2048]{1,0:T(8,128)(2,1)} %get-tuple-element.238), channel_id=1, source_target_pairs={{8,0},{16,8},{24,16},{28,24},{20,28},{12,20},{4,12},{0,4},{9,1},{1... | collective-permute-start | bytes 1572872 | tf_op jit(solution)/shard_map/ppermute | solution.py:405
  533.0 21.6 %collective-permute-start.71 = (bf16[128,2048]{1,0:T(8,128)(2,1)}, bf16[128,2048]{1,0:T(8,128)(2,1)S(1)}, u32[]{:S(2)}, u32[]{:S(2)}) collective-permute-start(bf16[128,2048]{1,0:T(8,128)(2,1)} %get-tuple-element.249), channel_id=1, source_target_pairs={{0,8},{8,16},{16,24},{24,28},{28,20},{20,12},{12,4},{4,0},{1,9},{9... | collective-permute-start | bytes 1572872 | tf_op jit(solution)/shard_map/ppermute | solution.py:405
  544.2 21.6 %collective-permute-start.69 = (bf16[128,2048]{1,0:T(8,128)(2,1)}, bf16[128,2048]{1,0:T(8,128)(2,1)}, u32[]{:S(2)}, u32[]{:S(2)}) collective-permute-start(bf16[128,2048]{1,0:T(8,128)(2,1)} %get-tuple-element.255), channel_id=1, source_target_pairs={{0,8},{8,16},{16,24},{24,28},{28,20},{20,12},{12,4},{4,0},{1,9},{9... | collective-permute-start | bytes 1572872 | tf_op jit(solution)/shard_map/ppermute | solution.py:405
  599.5 23.0 %collective-permute-start.83 = (bf16[128,2048]{1,0:T(8,128)(2,1)S(1)}, bf16[128,2048]{1,0:T(8,128)(2,1)}, u32[]{:S(2)}, u32[]{:S(2)}) collective-permute-start(bf16[128,2048]{1,0:T(8,128)(2,1)S(1)} %collective-permute-done.79.refs_1_), channel_id=1, source_target_pairs={{0,8},{8,16},{16,24},{24,28},{28,20},{20,12},{12,4},{4,0},{1,9},{9... | collective-permute-start | bytes 1572872 | tf_op jit(solution)/shard_map/ppermute | solution.py:405
  633.2 21.7 %collective-permute-start.85 = (bf16[128,2048]{1,0:T(8,128)(2,1)S(1)}, bf16[128,2048]{1,0:T(8,128)(2,1)}, u32[]{:S(2)}, u32[]{:S(2)}) collective-permute-start(bf16[128,2048]{1,0:T(8,128)(2,1)S(1)} %collective-permute-done.81.refs_1_), channel_id=1, source_target_pairs={{0,8},{8,16},{16,24},{24,28},{28,20},{20,12},{12,4},{4,0},{1,9},{9... | collective-permute-start | bytes 1572872 | tf_op jit(solution)/shard_map/ppermute | solution.py:405
  655.1 40.9 %collective-permute-start.89 = (bf16[128,2048]{1,0:T(8,128)(2,1)}, bf16[128,2048]{1,0:T(8,128)(2,1)S(1)}, u32[]{:S(2)}, u32[]{:S(2)}) collective-permute-start(bf16[128,2048]{1,0:T(8,128)(2,1)} %collective-permute-done.85.refs_3_), channel_id=1, source_target_pairs={{0,8},{8,16},{16,24},{24,28},{28,20},{20,12},{12,4},{4,0},{1,9},{9... | collective-permute-start | bytes 1572872 | tf_op jit(solution)/shard_map/ppermute | solution.py:405
  659.1 37.0 %collective-permute-start.90 = (bf16[128,2048]{1,0:T(8,128)(2,1)}, bf16[128,2048]{1,0:T(8,128)(2,1)S(1)}, u32[]{:S(2)}, u32[]{:S(2)}) collective-permute-start(bf16[128,2048]{1,0:T(8,128)(2,1)} %collective-permute-done.86.refs_4_), channel_id=1, source_target_pairs={{8,0},{16,8},{24,16},{28,24},{20,28},{12,20},{4,12},{0,4},{9,1},{1... | collective-permute-start | bytes 1572872 | tf_op jit(solution)/shard_map/ppermute | solution.py:405
  661.0 24.9 %collective-permute-start.91 = (bf16[64,2048]{1,0:T(8,128)(2,1)}, bf16[64,2048]{1,0:T(8,128)(2,1)S(1)}, u32[]{:S(2)}, u32[]{:S(2)}) collective-permute-start(bf16[64,2048]{1,0:T(8,128)(2,1)} %slice.431), channel_id=1, source_target_pairs={{0,8},{8,16},{16,24},{24,28},{28,20},{20,12},{12,4},{4,0},{1,9},{9... | collective-permute-start | bytes 786440 | tf_op jit(solution)/shard_map/ppermute | solution.py:405
  663.4 22.4 %collective-permute-start.92 = (bf16[64,2048]{1,0:T(8,128)(2,1)}, bf16[64,2048]{1,0:T(8,128)(2,1)}, u32[]{:S(2)}, u32[]{:S(2)}) collective-permute-start(bf16[64,2048]{1,0:T(8,128)(2,1)} %slice.432), channel_id=1, source_target_pairs={{8,0},{16,8},{24,16},{28,24},{20,28},{12,20},{4,12},{0,4},{9,1},{1... | collective-permute-start | bytes 786440 | tf_op jit(solution)/shard_map/ppermute | solution.py:405
  (251 other events, 2340.1 us)
Sparse Core Ops, SparseCore 0:
  289.9 100.0 reduce-scatter.3
  435.5 116.9 all-gather.1

commit v5 on v4

--- a/solution.py
+++ b/solution.py
@@ -16,6 +16,7 @@
 TK = 384
 HD = 128
 STEP = 64
+LINK_BYTES = 60_000_000
 SM = pl.BlockSpec(memory_space=pltpu.SMEM)
 VM = pl.BlockSpec(memory_space=pltpu.VMEM)
 
@@ -199,7 +200,11 @@
     scaled = grad * gain.astype(F32)
     first = jnp.mean(scaled, axis=-1, keepdims=True)
     second = jnp.mean(scaled * unit, axis=-1, keepdims=True)
-    return (inverse * (scaled - first - unit * second), jnp.sum(grad * unit, axis=0))
+    return (inverse * (scaled - first - unit * second), (grad, unit))
+
+
+def gain_sums(pairs, gate):
+    return jnp.stack([jnp.sum(grad * unit, axis=0) for grad, unit in after(pairs, gate)])
 
 
 def swish_slope(values):
@@ -263,44 +268,33 @@
     return lax.optimization_barrier((values, others))[0]
 
 
-def spread(own, work, late=()):
-    size = lax.axis_size("tp")
-    first = size // 2
-    far = swap(own, first)
-    slots = {0: own}
-    for distance in reversed(distances()[:-1]):
-        for slot in list(slots):
-            slots[slot ^ distance] = swap(slots[slot], distance)
-    near = join([slots[slot] for slot in range(first)])
-    outs = [work(0, near)]
-    arrived = after(far, outs, late)
-    slots = {0: arrived}
-    for distance in reversed(distances()[:-1]):
-        for slot in list(slots):
-            slots[slot ^ distance] = swap(slots[slot], distance)
-    far = join([slots[slot] for slot in range(first)])
-    outs.append(work(1, far))
-    return [near, far], outs, arrived
-
-
-def join(items):
-    return jnp.concatenate(items, 0)
-
-
-def pieces(blocks, weight, contract, late=()):
+def join_kernel(*refs):
+    rows = refs[0].shape[0]
+    for place, ref in enumerate(refs[:-1]):
+        refs[-1][place * rows : (place + 1) * rows] = ref[...]
+
+
+def halves(slots, weight=1):
+    half = len(slots) // 2
+    rows, width = slots[0].shape
+    far = pl.pallas_call(
+        join_kernel,
+        out_shape=sds((half * rows, width), slots[0].dtype),
+        in_specs=[VM] * half,
+        out_specs=VM,
+        cost_estimate=pl.CostEstimate(flops=0, bytes_accessed=weight * LINK_BYTES, transcendentals=0),
+    )(*slots[half:])
+    return jnp.concatenate(slots[:half], 0), far
+
+
+def pieces(near, far, weight, contract):
     count = lax.axis_size("tp") // 2
-    rows = blocks[0].shape[0] // count
+    rows = near.shape[0] // count
     outs = {}
     for slot in reversed(range(2 * count)):
-        place = slot % count
-        block = blocks[slot // count][place * rows : (place + 1) * rows]
-        outs[slot] = dot(block, weight, contract)
+        source, place = (near, slot) if slot < count else (far, slot - count)
+        outs[slot] = dot(source[place * rows : (place + 1) * rows], weight, contract)
     return [outs[slot] for slot in range(2 * count)]
-
-
-def cut(values):
-    half = values.shape[0] // 2
-    return [values[:half], values[half:]]
 
 
 def ring():
@@ -347,22 +341,21 @@
         refs[-1][...] = (own + from_left + from_right).astype(B16)
 
 
-def place_kernel(forms, spots, at, *refs):
+def place_kernel(spots, spans, at, *refs):
     count = len(spots)
-    outs, scratch = refs[count : count + len(forms)], list(refs[count + len(forms) :])
+    outs, held = refs[count : count + len(spans)], refs[-1]
     half = refs[count - 1].shape[0]
-    held = [out if form is plain else scratch.pop(0) for out, form in zip(outs, forms)]
-    widths = [item.shape[1] for item in held]
-    size = held[0].shape[0] // (2 * half)
+    size = held.shape[0] // (2 * half)
     for ref, (k, bottom) in zip(refs[:count], spots):
-        start = pl.multiple_of(((at[0] + k + size) % size) * (2 * half) + bottom * half, half)
-        edge = 0
-        for item, width in zip(held, widths):
-            item[pl.ds(start, ref.shape[0]), :] = ref[:, edge : edge + width].astype(F32)
-            edge += width
-    for item, out, form in zip(held, outs, forms):
-        if form is turned:
-            out[...] = item[...].T
+        start = ((at[0] + k) % size) * (2 * half) + bottom * half
+        start = pl.multiple_of(start, half)
+        held[pl.ds(start, ref.shape[0]), :] = ref[...].astype(F32)
+    for out, (low, high, form) in zip(outs, spans):
+        here = (pl.program_id(0) >= low) & (pl.program_id(0) < high)
+
+        @pl.when(here)
+        def _(out=out, form=form):
+            out[...] = form(held[...])
 
 
 class RowSum:
@@ -453,17 +446,34 @@
         self.seen += [(self.from_left[0], (-self.stages, 0)), (self.from_right[0], (self.stages, 1))]
         items = after([item for item, _ in self.seen], gate)
         spots = [((k + self.size) % self.size, bottom) for _, (k, bottom) in self.seen]
-        forms = [form for _, form in self.parts]
         length = self.arrays[0].shape[0]
-        shapes = [(length, width) if form is plain else (width, length) for width, form in self.parts]
-        scratch = [pltpu.VMEM((length, width), F32) for width, form in self.parts if form is turned]
+        step = math.gcd(*[width for width, _ in self.parts])
+        spans, specs, shapes, low = [], [], [], 0
+        for width, form in self.parts:
+            count = width // step
+            spans.append((low, low + count, form))
+
+            def column(i, at, low=low, count=count):
+                return jnp.clip(i - low, 0, count - 1)
+
+            if form is turned:
+                shapes.append((width, length))
+                specs.append(pl.BlockSpec((step, length), lambda i, at, f=column: (f(i, at), 0)))
+            else:
+                shapes.append((length, width))
+                specs.append(pl.BlockSpec((length, step), lambda i, at, f=column: (0, f(i, at))))
+            low += count
         moved = 6 * length * self.width
         return pl.pallas_call(
-            functools.partial(place_kernel, forms, spots),
+            functools.partial(place_kernel, spots, spans),
+            grid_spec=pltpu.PrefetchScalarGridSpec(
+                num_scalar_prefetch=1,
+                grid=(low,),
+                in_specs=[pl.BlockSpec((item.shape[0], step), lambda i, at: (0, i)) for item in items],
+                out_specs=specs,
+                scratch_shapes=[pltpu.VMEM((length, step), F32)],
+            ),
             out_shape=[sds(shape, F32) for shape in shapes],
-            in_specs=[SM] + [VM] * len(items),
-            out_specs=[VM] * len(shapes),
-            scratch_shapes=scratch,
             compiler_params=pltpu.CompilerParams(vmem_limit_bytes=40 << 20),
             cost_estimate=pl.CostEstimate(flops=moved, bytes_accessed=moved, transcendentals=0),
         )(self.place.reshape(1).astype(jnp.int32), *items)
@@ -493,16 +503,19 @@
 
 
 def start_sum(arrays):
-    if arrays[0].shape[0] == arrays[1].shape[0]:
-        arrays = [jnp.concatenate(arrays, 1)]
+    if arrays[0].shape[1] == arrays[1].shape[1]:
+        arrays = [jnp.concatenate(arrays, 0)]
     return [lax.psum_scatter(item, "rows", scatter_dimension=0, tiled=True) for item in arrays]
 
 
-def end_sum(shares, width):
-    whole = [lax.all_gather(item, "rows", axis=0, tiled=True) for item in shares]
+def end_sum(shares):
+    return [lax.all_gather(item, "rows", axis=0, tiled=True) for item in shares]
+
+
+def split_sum(whole, rows):
     if len(whole) == 1:
-        whole = [whole[0][:, :width], whole[0][:, width:]]
-    return whole
+        whole = [whole[0][:rows], whole[0][rows:]]
+    return [item.astype(F32) for item in whole]
 
 
 class RowSums:
@@ -558,40 +571,35 @@
     )
 
 
-def ffn_forward(values, gain, weight_up, weight_down, prefetch=None):
+def ffn_forward(values, gain, weight_up, weight_down):
     normed, unit, inverse = normalize(values, gain)
-
-    def work(slot, block):
-        pre = dot(block, weight_up)
-        return (pre * jax.nn.sigmoid(pre)).astype(B16), pre.astype(B16)
-
-    wide, outs, arrived = spread(normed.astype(B16), work)
-    act, pre = [item[0] for item in outs], [item[1] for item in outs]
-    fetched = ()
-    parts = pieces(act, weight_down, (1, 0))
-    if prefetch is not None:
-        fetched = prefetch(arrived)
-    total, (sent, _) = scatter(parts, fetched)
-    return (values + 0.5 * total, (unit, inverse, wide, pre, act), sent, fetched)
-
-
-def ffn_backward(grad, kept, gain, weight_up, weight_down, use=None, late=lambda own: ()):
+    near, far = halves(gather(normed.astype(B16)))
+    pre, act = [], []
+    for half in (near, far):
+        pre.append(dot(half, weight_up))
+        act.append((pre[-1] * jax.nn.sigmoid(pre[-1])).astype(B16))
+    total, (sent, _) = scatter(pieces(act[0], act[1], weight_down, (1, 0)))
+    pre = [item.astype(B16) for item in pre]
+    return (values + 0.5 * total, (unit, inverse, (near, far), pre, act), sent)
+
+
+def ffn_backward(grad, kept, gain, weight_up, weight_down, use=None):
     unit, inverse, wide, pre, act = kept
     own = (0.5 * grad).astype(B16)
-
-    def work(slot, block):
-        d_act = dot(block, weight_down, (1, 1))
-        return (d_act * swish_slope(pre[slot].astype(F32))).astype(B16)
-
-    cot, d_pre, _ = spread(own, work, late(own))
-    d_norm, (sent, _) = scatter(pieces(d_pre, weight_up, (1, 1)))
+    cot = halves(gather(own))
+    d_pre = []
+    for half in (0, 1):
+        d_act = dot(cot[half], weight_down, (1, 1))
+        d_pre.append((d_act * swish_slope(pre[half].astype(F32))).astype(B16))
+    d_norm, (sent, _) = scatter(pieces(d_pre[0], d_pre[1], weight_up, (1, 1)))
     cot, d_pre = after((cot, d_pre), sent)
-    grad_down = dot(join(act), join(cot), (0, 0)).astype(B16)
-    grad_up = dot(join(wide), join(d_pre), (0, 0)).astype(B16)
+    grad_down = dot(jnp.concatenate(act, 0), jnp.concatenate(cot, 0), (0, 0))
+    grad_up = dot(jnp.concatenate(wide, 0), jnp.concatenate(d_pre, 0), (0, 0))
+    grads = (grad_up.astype(B16), grad_down.astype(B16))
     if use is not None:
-        d_norm = after(d_norm, use((grad_up, grad_down)))
+        d_norm = after(d_norm, use(grads))
     d_in, grad_gain = normalize_back(d_norm, unit, inverse, gain)
-    return (grad + d_in, grad_gain, (grad_up, grad_down), (own, sent))
+    return (grad + d_in, grad_gain, grads, (own, sent))
 
 
 def places(slots):
@@ -616,10 +624,13 @@
     q_at, k_at, reorder = places(slots)
     where = (spans, q_at, k_at)
     normed, unit, inverse = normalize(values, gain)
-    work = lambda slot, block: dot(block, weights)
-    wide, mixed, first = spread(normed.astype(B16), work, (rel, spans))
-    fetched, arrived = prefetch(first)
+    near, far = halves(gather(normed.astype(B16)))
+    mixed = [dot(near, weights)]
+    far = after(far, rel, spans)
+    fetched, arrived = prefetch(far)
+    mixed.append(dot(far, weights))
     flat = lambda bias: bias.astype(F32).reshape(1, width)
+    join = lambda items: jnp.concatenate(items, 0)
     q_content = join([(item[:, :width] + flat(content_bias)).astype(B16) for item in mixed])
     q_position = join([(item[:, :width] + flat(position_bias)).astype(B16) for item in mixed])
     key = join([item[:, width : 2 * width].astype(B16) for item in mixed])
@@ -633,18 +644,18 @@
     )
     heads_out, heads_wide, sums = attend(*operands)
     sent = after(to_true(heads_out) if reorder else heads_out, arrived)
-    total, _ = scatter(pieces(cut(sent), attend_out, (1, 0)))
-    kept = (unit, inverse, wide, operands, heads_wide, sums, sent)
+    half = slots // 2
+    total, _ = scatter(pieces(sent[:half], sent[half:], attend_out, (1, 0)))
+    kept = (unit, inverse, (near, far), operands, heads_wide, sums, sent)
     return (values + total, kept, fetched)
 
 
-def attend_backward(grad, cot, kept, gain, weights, attend_out, table, filler, use):
+def attend_backward(grad, cot, kept, gain, weights, attend_out, table, filler):
     unit, inverse, wide, operands, heads_wide, sums, sent = kept
     slots, width = sent.shape
     _, _, reorder = places(slots)
-    work = lambda slot, block: dot(block, attend_out, (1, 1)).astype(B16)
-    cot, d_heads, _ = spread(cot, work)
-    d_heads = join(d_heads)
+    d_near = dot(cot[0], attend_out, (1, 1)).astype(B16)
+    d_heads = jnp.concatenate([d_near, dot(cot[1], attend_out, (1, 1)).astype(B16)], 0)
     if reorder:
         d_heads = to_true(d_heads)
     d_heads = after(d_heads, filler[0])
@@ -652,22 +663,26 @@
     if reorder:
         d_all = to_true(d_all)
     d_all = after(d_all, filler[1])
-    d_norm, (last, _) = scatter(pieces(cut(d_all), weights, (1, 1)))
+    half = slots // 2
+    d_norm, (last, _) = scatter(pieces(d_all[:half], d_all[half:], weights, (1, 1)))
+    d_in, grad_gain = normalize_back(d_norm, unit, inverse, gain)
     cot, d_all, d_rel = after((cot, d_all, d_rel), last)
-    grads = (
-        dot(join(wide), d_all, (0, 0)),
-        dot(table, d_rel, (0, 0)),
-        dot(join(cot), sent, (0, 0)),
-    )
-    d_norm = after(d_norm, use([item.astype(B16) for item in grads]))
-    d_in, grad_gain = normalize_back(d_norm, unit, inverse, gain)
-    return (grad + d_in, grad_gain, d_bias[:2])
-
-
-def conv_weights(pick, own, first):
-    slots = [gather(item) for item in pick(after(own, first))]
-    far = lax.axis_size("tp") // 2
-    return slots, [item[far] for item in slots]
+    grad_out = dot(jnp.concatenate(cot, 0), sent, (0, 0))
+    grad_all = dot(jnp.concatenate(wide, 0), d_all, (0, 0))
+    grad_pos = dot(table, d_rel, (0, 0))
+    grads = [item.astype(B16) for item in (grad_all, grad_pos, grad_out)]
+    return (grad + d_in, grad_gain, grads, d_bias[:2])
+
+
+def conv_weights(point_in, depth_kernel, gain_inner, point_out, first):
+    taps = depth_kernel.shape[0]
+    own = after((point_in[:, 0], point_in[:, 1], point_out), first)
+    small = gather(jnp.concatenate([depth_kernel, gain_inner[None]], 0))
+    small = jnp.concatenate(small, 1).astype(F32)
+    in_a, in_b, out = map(gather, own)
+    arrived = [item[2::2] for item in (in_a, in_b, out)]
+    in_a, in_b = jnp.concatenate(in_a, 1), jnp.concatenate(in_b, 1)
+    return (in_a, in_b, small[:taps], small[taps], jnp.concatenate(out, 0)), arrived
 
 
 def conv_masks(segments, valid, rows, taps):
@@ -730,8 +745,9 @@
     d_norm = dot(d_a, in_a, (1, 1)) + dot(d_b, in_b, (1, 1))
     d_in, grad_gain = normalize_back(d_norm, unit, inverse, gain)
     grad = grad + d_in
-    next_cot = grad.astype(B16)
-    low, cot, d_a, d_b, inner = after((low, cot, d_a, d_b, inner), next_cot)
+    slots = gather(grad.astype(B16))
+    next_cot = halves(slots, 3)
+    low, cot, d_a, d_b, inner = after((low, cot, d_a, d_b, inner), slots[1])
     size = lax.axis_size("tp")
     width = in_a.shape[1] // size
     parts, small_parts = [], []
@@ -744,7 +760,7 @@
         cols = slice(slot * width, (slot + 1) * width)
         parts.append(jnp.concatenate([item[:, cols] for item in grads], 1))
         small_parts.append(small[:, cols])
-    total, ends = scatter(parts)
+    total, ends = scatter(parts, next_cot[1])
     return (grad, next_cot, grad_gain, (total.astype(B16), scatter(small_parts)[0]), ends)
 
 
@@ -774,45 +790,29 @@
     down_second,
     gain_final,
 ):
+    segment_row, valid_row = segments[0], valid_frames[0]
+    weights = jnp.concatenate([query_weight, key_weight, value_weight], 1)
     width = query_weight.shape[1]
     taps = depth_kernel.shape[0]
     values = layer_input[0].astype(F32)
     rows = values.shape[0]
-    slots = segments.shape[1]
-    fetched = []
-
-    def prefetch(first):
-        slots, arrived = conv_weights(lambda own: [own[:, 0]], point_in, first)
-        fetched.extend(slots)
-        return arrived
-
-    values, kept_first, sent, _ = ffn_forward(values, gain_first, up_first, down_first, prefetch)
-    segment_row, valid_row = after((segments[0], valid_frames[0]), sent)
+    slots = segment_row.shape[0]
+    masks = conv_masks(segment_row, valid_row, rows, taps)
     code = codes(segment_row, valid_row)
     spans = spans_of(code)
-    weights = jnp.concatenate(after((query_weight, key_weight, value_weight), sent), 1)
+    values, kept_first, sent = ffn_forward(values, gain_first, up_first, down_first)
     table = distance_table(slots, values.shape[1], sent)
     rel = dot(table, pos_weight).astype(B16)
-    pick = lambda own: [own[0][:, 1], own[1]]
-    prefetch = functools.partial(conv_weights, pick, (point_in, point_out))
-    values, kept_attend, others = attend_forward(
+    prefetch = functools.partial(conv_weights, point_in, depth_kernel, gain_inner, point_out)
+    values, kept_attend, full = attend_forward(
         values, gain_attend, weights, attend_out, content_bias, position_bias, code, spans, rel, prefetch
     )
-    ready = kept_attend[2][1]
-    masks = conv_masks(*after((segment_row, valid_row), ready), rows, taps)
-    small = gather(after(jnp.concatenate([depth_kernel, gain_inner[None]], 0), ready))
-    small = jnp.concatenate(small, 1).astype(F32)
-    full = (
-        jnp.concatenate(fetched[0], 1), jnp.concatenate(others[0], 1),
-        small[:taps], small[taps], jnp.concatenate(others[1], 0),
-    )
     values, kept_conv = conv_forward(values, gain_conv, full, masks)
-    values, kept_second, _, _ = ffn_forward(values, gain_second, up_second, down_second)
+    values, kept_second, _ = ffn_forward(values, gain_second, up_second, down_second)
     final, final_unit, final_inverse = normalize(values, gain_final)
     layer_output = final.astype(B16)
     grad, sum_final = normalize_back(cotangent[0].astype(F32), final_unit, final_inverse, gain_final)
     held = {}
-    lanes = lambda items: [(item.shape[1], plain) for item in items]
 
     def start_second(grads):
         held["second"] = start_sum(grads)
@@ -823,28 +823,27 @@
     )
     grad, cot, sum_conv, conv_grads, ends = conv_backward(grad, kept_conv, gain_conv, full, masks)
     ends = (ends[0], (ends[1], held["second"]))
-
-    def start_middle(grads):
-        forms = [(width, plain)] * 4 + [(width, turned), (2 * width, plain), (width, turned)]
-        held["middle"] = row_sum(grads + [conv_grads[0]], forms)
-        return held["middle"].step()
-
-    grad, sum_attend, d_bias = attend_backward(
-        grad, cot, kept_attend, gain_attend, weights, attend_out, table, ends, start_middle
+    grad, sum_attend, attend_grads, d_bias = attend_backward(
+        grad, cot, kept_attend, gain_attend, weights, attend_out, table, ends
     )
-    second_sum = end_sum(held["second"], up_second.shape[1])
-    middle = held["middle"]
-
-    def fill(own):
-        own, sums = after((own, (sum_attend, sum_conv, sum_second, sum_final)), own)
-        return jnp.stack(sums), conv_grads[1]
-
+    second_sum = end_sum(held["second"])
     grad, sum_first, first_grads, marks = ffn_backward(
-        grad, kept_first, gain_first, up_first, down_first, None, fill
+        grad, kept_first, gain_first, up_first, down_first
     )
-    first = RowSums(first_grads, lanes(first_grads))
+    pairs = (sum_first, sum_attend, sum_conv, sum_second, sum_final)
+    gains = sum_cube(gain_sums(pairs, marks[1]), "tp")
+    small = jnp.concatenate([conv_grads[1], d_bias], 0)
+    small_shape = small.shape
+    pack = jnp.concatenate([gains.reshape(-1), small.reshape(-1)]).reshape(-1, width)
+    pack = sum_cube(pack, "rows")
+    forms = [(width, plain)] * 4 + [(width, turned), (2 * width, plain), (width, turned)]
+    middle = row_sum(attend_grads + [conv_grads[0]], forms)
+    first = RowSums(first_grads, [(item.shape[1], plain) for item in first_grads])
+    middle.step()
     token = middle.step(marks[1])
     token = first.step(token)
+    second_sum = after(second_sum, token)
+    token = second_sum
     while middle.done < middle.steps:
         token = middle.step(token)
         if first.left > 1:
@@ -852,16 +851,11 @@
         if first.done == 3:
             token = (token, grad)
         if first.done == 5:
-            second_sum = after(second_sum, token)
-            second_up, second_down = [item.astype(F32) for item in second_sum]
-            token = (token, second_up, second_down)
+            second_up, second_down = split_sum(after(second_sum, token), up_second.shape[0])
+            token = (token, second_up, second_down, pack)
     attend_sum = middle.finish(token)
     first_sum = first.finish(attend_sum)
-    gains = sum_cube(jnp.stack([sum_first, sum_attend, sum_conv, sum_second, sum_final]), "tp")
-    small = jnp.concatenate([conv_grads[1], d_bias], 0)
-    small_shape = small.shape
-    pack = jnp.concatenate([gains.reshape(-1), small.reshape(-1)]).reshape(-1, width)
-    pack = sum_cube(pack, "rows").reshape(-1)
+    pack = pack.reshape(-1)
     gains, small = pack[: gains.size].reshape(gains.shape), pack[gains.size :].reshape(small_shape)
     bias_shape = content_bias.shape
     return (

time: 745 us -> 740 us (level)
  local copies, waits for them, and re-layouts: 89.3 us -> 65.1 us
  other arithmetic: 62.8 us -> 85.1 us
  waiting for transfers between devices: 253 us -> 232 us
  Pallas kernels: 81 us -> 98.6 us
    unnamed x376 -> x364, local copies, waits for them, and re-layouts: 69.4 us -> 45.3 us
    ppermute x32, waiting for transfers between devices: 65.7 us -> 47.9 us  [send(): lax.ppermute(item, 'rows', way)]
    pallas_call x2 -> x8, Pallas kernels: 9.88 us -> 27.4 us  [the longest x6 15.9 us: halves(): pl.pallas_call(join_kernel, out_shape=sds((half * rows, width), slots[0]....]
    convert_element_type x4 -> x5, other arithmetic: 3.68 us -> 14.3 us  [the longest x1 6.78 us: split_sum(): return [item.astype(F32) for item in whole]]
    unnamed x3 -> x2, waiting for transfers between devices: 9.42 us -> 0.03 us
  transfers between devices with their start and end apart: 97 -> 97, of which waited for: 45 -> 37; matrix products, arithmetic and copies ran while one was open for 27% -> 30% of each run, Pallas kernels for 10% -> 12%
where the time goes in v5:
time: 740 us; the launch traced here: 732 us
  waiting for transfers between devices  232 us (31%)
  matrix products  127 us (17%)
  starting transfers between devices  107 us (14%)
  Pallas kernels  98.6 us (13%)
  other arithmetic  85.1 us (12%)
  local copies, waits for them, and re-layouts  65.1 us (9%)
  between operations  16.7 us (2%)
    ppermute x54, waiting for transfers between devices, swap(): return lax.ppermute(values, 'tp', [(i, i ^ distance) for i in range(size)])  152 us
    dot_general x53, matrix products, dot(): lax.dot_general(left, right, (((contract[0],), (contract[1],)), ((), ()))...  127 us
    ppermute x32, starting transfers between devices, send(): lax.ppermute(item, 'rows', way)  61.6 us
    ppermute x32, waiting for transfers between devices, send(): lax.ppermute(item, 'rows', way)  47.9 us
    unnamed x364, local copies, waits for them, and re-layouts  45.3 us
    ppermute x54, starting transfers between devices, swap(): return lax.ppermute(values, 'tp', [(i, i ^ distance) for i in range(size)])  34 us
    pallas_call x10, Pallas kernels, call(): pl.pallas_call(kernel, grid_spec=pltpu.PrefetchScalarGridSpec(num_scalar_...  30.3 us
    pallas_call x1, Pallas kernels, attend_back(): pl.pallas_call(functools.partial(attend_back_kernel, heads), out_shape=(s...  28.2 us
  transfers between devices with their start and end apart: 97, of which 37 were waited for; matrix products, arithmetic and copies ran while one was open for 30% of the time, Pallas kernels for 12%

profile of v5, /device:TPU:0, one launch (start us, length us, event | category | flops | bytes accessed | tf_op | source)
XLA Modules:
  0.0 732.0 jit_solution(16069547684210075440)
XLA Ops:
  27.4 9.3 %collective-permute-done.2.refs_0_ = bf16[384,1024]{1,0:T(8,128)(2,1)S(1)} collective-permute-done((bf16[384,1024]{1,0:T(8,128)(2,1)}, bf16[384,1024]{1,0:T(8,128)(2,1)S(1)}, u32[]{:S(2)}, u32[]{:S(2)}) %collective-permute-start.2) | collective-permute-done | bytes 786464 | tf_op jit(solution)/shard_map/ppermute | solution.py:237
  61.3 18.0 %collective-permute-done.5 = bf16[384,1024]{1,0:T(8,128)(2,1)S(1)} collective-permute-done((bf16[384,1024]{1,0:T(8,128)(2,1)S(1)}, bf16[384,1024]{1,0:T(8,128)(2,1)S(1)}, u32[]{:S(2)}, u32[]{:S(2)}) %collective-permute-start.5) | collective-permute-done | bytes 786464 | tf_op jit(solution)/shard_map/ppermute | solution.py:237
  85.7 14.7 %collective-permute-done.7.refs_0_ = bf16[384,1024]{1,0:T(8,128)(2,1)S(1)} collective-permute-done((bf16[384,1024]{1,0:T(8,128)(2,1)S(1)}, bf16[384,1024]{1,0:T(8,128)(2,1)S(1)}, u32[]{:S(2)}, u32[]{:S(2)}) %collective-permute-start.7) | collective-permute-done | bytes 786464 | tf_op jit(solution)/shard_map/ppermute | solution.py:237
  120.6 12.8 %shard_map.401 = (bf16[1536,256]{1,0:T(8,128)(2,1)S(1)}, f32[1536,256]{1,0:T(8,128)S(1)}, f32[1536,2]{1,0:T(8,128)S(1)}) custom-call(s32[2,12]{1,0:T(2,128)S(1)} %pad_add_fusion.spans, s32[12]{0:T(128)S(1)} %fusion.201.q_at, s32[4]{0:T(128)S(1)} %fusion.202.k_at, bf16[1536,256]{1,0:T(8,128)(2,1)S(1)} %get-tuple-element.453.qc_ref, ...), custom_call_target="tpu_custom_call" | custom-call | flops 4000000000 | bytes 9000000 | tf_op jit(solution)/shard_map/pallas_call | solution.py:154
  136.6 10.3 %collective-permute-done.11 = bf16[256,1024]{1,0:T(8,128)(2,1)S(1)} collective-permute-done((bf16[256,1024]{1,0:T(8,128)(2,1)S(1)}, bf16[256,1024]{1,0:T(8,128)(2,1)S(1)}, u32[]{:S(2)}, u32[]{:S(2)}) %collective-permute-start.11) | collective-permute-done | bytes 524320 | tf_op jit(solution)/shard_map/ppermute | solution.py:237
  153.0 17.3 %collective-permute-done.14 = bf16[384,1024]{1,0:T(8,128)(2,1)S(1)} collective-permute-done((bf16[384,1024]{1,0:T(8,128)(2,1)S(1)}, bf16[384,1024]{1,0:T(8,128)(2,1)S(1)}, u32[]{:S(2)}, u32[]{:S(2)}) %collective-permute-start.14) | collective-permute-done | bytes 786464 | tf_op jit(solution)/shard_map/ppermute | solution.py:237
  190.1 17.6 %collective-permute-done.28.refs_0_ = bf16[384,1024]{1,0:T(8,128)(2,1)S(1)} collective-permute-done((bf16[384,1024]{1,0:T(8,128)(2,1)}, bf16[384,1024]{1,0:T(8,128)(2,1)S(1)}, u32[]{:S(2)}, u32[]{:S(2)}) %collective-permute-start.28) | collective-permute-done | bytes 786464 | tf_op jit(solution)/shard_map/ppermute | solution.py:237
  230.4 16.6 %collective-permute-done.31 = bf16[384,1024]{1,0:T(8,128)(2,1)S(1)} collective-permute-done((bf16[384,1024]{1,0:T(8,128)(2,1)S(1)}, bf16[384,1024]{1,0:T(8,128)(2,1)S(1)}, u32[]{:S(2)}, u32[]{:S(2)}) %collective-permute-start.31) | collective-permute-done | bytes 786464 | tf_op jit(solution)/shard_map/ppermute | solution.py:237
  252.2 17.2 %collective-permute-done.34.refs_0_ = bf16[384,1024]{1,0:T(8,128)(2,1)S(1)} collective-permute-done((bf16[384,1024]{1,0:T(8,128)(2,1)S(1)}, bf16[384,1024]{1,0:T(8,128)(2,1)S(1)}, u32[]{:S(2)}, u32[]{:S(2)}) %collective-permute-start.34) | collective-permute-done | bytes 786464 | tf_op jit(solution)/shard_map/ppermute | solution.py:237
  296.2 9.4 %collective-permute-done.37 = bf16[384,1024]{1,0:T(8,128)(2,1)S(1)} collective-permute-done((bf16[384,1024]{1,0:T(8,128)(2,1)S(1)}, bf16[384,1024]{1,0:T(8,128)(2,1)S(1)}, u32[]{:S(2)}, u32[]{:S(2)}) %collective-permute-start.37) | collective-permute-done | bytes 786464 | tf_op jit(solution)/shard_map/ppermute | solution.py:237
  378.4 28.2 %shard_map.405 = (bf16[1536,768]{1,0:T(8,128)(2,1)}, bf16[3072,256]{1,0:T(8,128)(2,1)}, f32[8,256]{1,0:T(8,128)S(1)}) custom-call(s32[2,12]{1,0:T(2,128)S(1)} %pad_add_fusion.spans, s32[12]{0:T(128)S(1)} %fusion.201.q_at, s32[4]{0:T(128)S(1)} %fusion.202.k_at, bf16[1536,256]{1,0:T(8,128)(2,1)S(1)} %copy-done.3, bf16[1536,256]{1,0:T(8,128)(2,1)S(1)} %copy-done.5, ...), custom_call_target="tpu_custom_call" | custom-call | flops 1000000 | bytes 1000000 | tf_op jit(solution)/shard_map/pallas_call | solution.py:165
  426.3 6.7 fusion.94.refs_0_.refs_4_
  433.0 9.6 %collective-permute-done.47 = bf16[384,1024]{1,0:T(8,128)(2,1)} collective-permute-done((bf16[384,1024]{1,0:T(8,128)(2,1)}, bf16[384,1024]{1,0:T(8,128)(2,1)}, u32[]{:S(2)}, u32[]{:S(2)}) %collective-permute-start.47) | collective-permute-done | bytes 786464 | tf_op jit(solution)/shard_map/ppermute | solution.py:237
  456.6 21.5 %collective-permute-start.63 = (bf16[64,2048]{1,0:T(8,128)(2,1)}, bf16[64,2048]{1,0:T(8,128)(2,1)S(1)}, u32[]{:S(2)}, u32[]{:S(2)}) collective-permute-start(bf16[64,2048]{1,0:T(8,128)(2,1)} %get-tuple-element.221), channel_id=1, source_target_pairs={{0,8},{8,16},{16,24},{24,28},{28,20},{20,12},{12,4},{4,0},{1,9},{9... | collective-permute-start | bytes 786440 | tf_op jit(solution)/shard_map/ppermute | solution.py:398
  478.6 6.5 fusion.20
  509.5 9.8 %collective-permute-start.67 = (bf16[128,2048]{1,0:T(8,128)(2,1)}, bf16[128,2048]{1,0:T(8,128)(2,1)S(1)}, u32[]{:S(2)}, u32[]{:S(2)}) collective-permute-start(bf16[128,2048]{1,0:T(8,128)(2,1)} %get-tuple-element.229), channel_id=1, source_target_pairs={{0,8},{8,16},{16,24},{24,28},{28,20},{20,12},{12,4},{4,0},{1,9},{9... | collective-permute-start | bytes 1572872 | tf_op jit(solution)/shard_map/ppermute | solution.py:398
  519.4 7.8 %fusion.72.refs_1_.refs_3_ = bf16[1024,1024]{1,0:T(8,128)(2,1)} fusion(bf16[768,1024]{1,0:T(8,128)(2,1)} %shard_map.406, bf16[768,1024]{1,0:T(8,128)(2,1)} %pad_maximum_fusion.4, bf16[768,1024]{1,0:T(8,128)(2,1)} %copy-done.168, bf16[768,1024]{1,0:T(8,128)(2,1)} %copy-done.160), kind=kOutput, calls=%fused_computation.97 | convolution fusion | flops 3234856960 | bytes 8388608 | tf_op jit(solution)/shard_map/dot_general | solution.py:230
  527.2 6.3 fusion.77.refs_0_.refs_2_
  610.7 7.4 %collective-permute-done.59 = f32[28,256]{1,0:T(8,128)S(1)} collective-permute-done((f32[28,256]{1,0:T(8,128)S(1)}, f32[28,256]{1,0:T(8,128)S(1)}, u32[]{:S(2)}, u32[]{:S(2)}) %collective-permute-start.59) | collective-permute-done | bytes 28704 | tf_op jit(solution)/shard_map/ppermute | solution.py:554
  630.5 15.5 %collective-permute-done.61 = f32[28,256]{1,0:T(8,128)S(1)} collective-permute-done((f32[28,256]{1,0:T(8,128)S(1)}, f32[28,256]{1,0:T(8,128)S(1)}, u32[]{:S(2)}, u32[]{:S(2)}) %collective-permute-start.61) | collective-permute-done | bytes 28704 | tf_op jit(solution)/shard_map/ppermute | solution.py:554
  646.1 6.8 slice_convert_fusion
  658.6 8.8 %collective-permute-done.87.refs_5_ = bf16[128,2048]{1,0:T(8,128)(2,1)S(1)} collective-permute-done((bf16[128,2048]{1,0:T(8,128)(2,1)S(1)}, bf16[128,2048]{1,0:T(8,128)(2,1)S(1)}, u32[]{:S(2)}, u32[]{:S(2)}) %collective-permute-start.87) | collective-permute-done | bytes 524320 | tf_op jit(solution)/shard_map/ppermute | solution.py:398
  681.0 10.7 %collective-permute-done.92.refs_8_ = bf16[64,2048]{1,0:T(8,128)(2,1)S(1)} collective-permute-done((bf16[64,2048]{1,0:T(8,128)(2,1)S(1)}, bf16[64,2048]{1,0:T(8,128)(2,1)S(1)}, u32[]{:S(2)}, u32[]{:S(2)}) %collective-permute-start.92) | collective-permute-done | bytes 262176 | tf_op jit(solution)/shard_map/ppermute | solution.py:398
  693.8 6.0 shard_map.417
  (760 shorter events, 420.7 us)
Async XLA Ops:
  7.2 402.5 %reduce-scatter.2.cloned.1.call-start = ((), (), s32[]{:S(2)}) async-start(), calls=%async_computation.1 | async-start | bytes 4718592 | tf_op jit(solution)/shard_map/reduce_scatter | solution.py:508
  8.8 73.2 %collective-permute-start.16 = (bf16[6,256]{1,0:T(8,128)(2,1)S(1)}, bf16[6,256]{1,0:T(8,128)(2,1)S(1)}, u32[]{:S(2)}, u32[]{:S(2)}) collective-permute-start(bf16[6,256]{1,0:T(8,128)(2,1)S(1)} %pad_maximum_fusion.19), channel_id=1, source_target_pairs={{0,2},{1,3},{2,0},{3,1},{4,6},{5,7},{6,4},{7,5},{8,10},{9,11},{10,... | collective-permute-start | bytes 9224 | tf_op jit(solution)/shard_map/ppermute | solution.py:237
  11.8 70.4 %collective-permute-start.15 = (bf16[6,256]{1,0:T(8,128)(2,1)S(1)}, bf16[6,256]{1,0:T(8,128)(2,1)S(1)}, u32[]{:S(2)}, u32[]{:S(2)}) collective-permute-start(bf16[6,256]{1,0:T(8,128)(2,1)S(1)} %pad_maximum_fusion.19), channel_id=1, source_target_pairs={{0,1},{1,0},{2,3},{3,2},{4,5},{5,4},{6,7},{7,6},{8,9},{9,8},{10,11... | collective-permute-start | bytes 9224 | tf_op jit(solution)/shard_map/ppermute | solution.py:237
  16.6 35.4 %collective-permute-start = (bf16[384,1024]{1,0:T(8,128)(2,1)}, bf16[384,1024]{1,0:T(8,128)(2,1)}, u32[]{:S(2)}, u32[]{:S(2)}) collective-permute-start(bf16[384,1024]{1,0:T(8,128)(2,1)} %get-tuple-element.400), channel_id=1, source_target_pairs={{0,1},{1,0},{2,3},{3,2},{4,5},{5,4},{6,7},{7,6},{8,9},{9,8},{10,11... | collective-permute-start | bytes 2359304 | tf_op jit(solution)/shard_map/ppermute | solution.py:237
  109.9 39.6 %collective-permute-start.20 = (bf16[1024,256]{1,0:T(8,128)(2,1)}, bf16[1024,256]{1,0:T(8,128)(2,1)S(1)}, u32[]{:S(2)}, u32[]{:S(2)}) collective-permute-start(bf16[1024,256]{1,0:T(8,128)(2,1)} %get-tuple-element.177), channel_id=1, source_target_pairs={{0,1},{1,0},{2,3},{3,2},{4,5},{5,4},{6,7},{7,6},{8,9},{9,8},{10,11... | collective-permute-start | bytes 1572872 | tf_op jit(solution)/shard_map/ppermute | solution.py:237
  110.7 39.1 %collective-permute-start.22 = (bf16[1024,256]{1,0:T(8,128)(2,1)}, bf16[1024,256]{1,0:T(8,128)(2,1)S(1)}, u32[]{:S(2)}, u32[]{:S(2)}) collective-permute-start(bf16[1024,256]{1,0:T(8,128)(2,1)} %get-tuple-element.178), channel_id=1, source_target_pairs={{0,1},{1,0},{2,3},{3,2},{4,5},{5,4},{6,7},{7,6},{8,9},{9,8},{10,11... | collective-permute-start | bytes 1572872 | tf_op jit(solution)/shard_map/ppermute | solution.py:237
  110.7 25.9 %collective-permute-start.10 = (bf16[1024,256]{1,0:T(8,128)(2,1)}, bf16[1024,256]{1,0:T(8,128)(2,1)S(1)}, u32[]{:S(2)}, u32[]{:S(2)}) collective-permute-start(bf16[1024,256]{1,0:T(8,128)(2,1)} %get-tuple-element.178), channel_id=1, source_target_pairs={{0,2},{1,3},{2,0},{3,1},{4,6},{5,7},{6,4},{7,5},{8,10},{9,11},{10,... | collective-permute-start | bytes 1572872 | tf_op jit(solution)/shard_map/ppermute | solution.py:237
  115.7 31.2 %collective-permute-start.11 = (bf16[256,1024]{1,0:T(8,128)(2,1)S(1)}, bf16[256,1024]{1,0:T(8,128)(2,1)S(1)}, u32[]{:S(2)}, u32[]{:S(2)}) collective-permute-start(bf16[256,1024]{1,0:T(8,128)(2,1)S(1)} %copy-done.127), channel_id=1, source_target_pairs={{0,2},{1,3},{2,0},{3,1},{4,6},{5,7},{6,4},{7,5},{8,10},{9,11},{10,... | collective-permute-start | bytes 1572872 | tf_op jit(solution)/shard_map/ppermute | solution.py:237
  316.4 226.1 %all-gather.2.cloned.1.call-start = ((), (), s32[]{:S(2)}) async-start(), calls=%async_computation.2 | async-start | bytes 4718592 | tf_op jit(solution)/shard_map/all_gather | solution.py:512
  368.0 38.6 %collective-permute-start.44 = (bf16[1024,768]{1,0:T(8,128)(2,1)}, bf16[1024,768]{1,0:T(8,128)(2,1)}, u32[]{:S(2)}, u32[]{:S(2)}) collective-permute-start(bf16[1024,768]{1,0:T(8,128)(2,1)} %add_convert_fusion.2), channel_id=1, source_target_pairs={{0,2},{1,3},{2,0},{3,1},{4,6},{5,7},{6,4},{7,5},{8,10},{9,11},{10,... | collective-permute-start | bytes 4718600 | tf_op jit(solution)/shard_map/ppermute | solution.py:237
  373.0 42.0 %collective-permute-start.62 = (bf16[1024,768]{1,0:T(8,128)(2,1)}, bf16[1024,768]{1,0:T(8,128)(2,1)}, u32[]{:S(2)}, u32[]{:S(2)}) collective-permute-start(bf16[1024,768]{1,0:T(8,128)(2,1)} %pad_maximum_fusion.5), channel_id=1, source_target_pairs={{0,1},{1,0},{2,3},{3,2},{4,5},{5,4},{6,7},{7,6},{8,9},{9,8},{10,11... | collective-permute-start | bytes 4718600 | tf_op jit(solution)/shard_map/ppermute | solution.py:237
  374.0 228.2 %collective-permute-start.56 = (bf16[6,256]{1,0:T(8,128)(2,1)S(1)}, bf16[6,256]{1,0:T(8,128)(2,1)S(1)}, u32[]{:S(2)}, u32[]{:S(2)}) collective-permute-start(bf16[6,256]{1,0:T(8,128)(2,1)S(1)} %get-tuple-element.419), channel_id=1, source_target_pairs={{0,1},{1,0},{2,3},{3,2},{4,5},{5,4},{6,7},{7,6},{8,9},{9,8},{10,11... | collective-permute-start | bytes 9224 | tf_op jit(solution)/shard_map/ppermute | solution.py:237
  447.9 30.7 %collective-permute-start.50 = (bf16[384,1024]{1,0:T(8,128)(2,1)}, bf16[384,1024]{1,0:T(8,128)(2,1)}, u32[]{:S(2)}, u32[]{:S(2)}) collective-permute-start(bf16[384,1024]{1,0:T(8,128)(2,1)} %get-tuple-element.343), channel_id=1, source_target_pairs={{0,2},{1,3},{2,0},{3,1},{4,6},{5,7},{6,4},{7,5},{8,10},{9,11},{10,... | collective-permute-start | bytes 2359304 | tf_op jit(solution)/shard_map/ppermute | solution.py:237
  449.4 29.2 %collective-permute-start.48 = (bf16[384,1024]{1,0:T(8,128)(2,1)}, bf16[384,1024]{1,0:T(8,128)(2,1)}, u32[]{:S(2)}, u32[]{:S(2)}) collective-permute-start(bf16[384,1024]{1,0:T(8,128)(2,1)} %get-tuple-element.343), channel_id=1, source_target_pairs={{0,1},{1,0},{2,3},{3,2},{4,5},{5,4},{6,7},{7,6},{8,9},{9,8},{10,11... | collective-permute-start | bytes 2359304 | tf_op jit(solution)/shard_map/ppermute | solution.py:237
  456.6 48.3 %collective-permute-start.63 = (bf16[64,2048]{1,0:T(8,128)(2,1)}, bf16[64,2048]{1,0:T(8,128)(2,1)S(1)}, u32[]{:S(2)}, u32[]{:S(2)}) collective-permute-start(bf16[64,2048]{1,0:T(8,128)(2,1)} %get-tuple-element.221), channel_id=1, source_target_pairs={{0,8},{8,16},{16,24},{24,28},{28,20},{20,12},{12,4},{4,0},{1,9},{9... | collective-permute-start | bytes 786440 | tf_op jit(solution)/shard_map/ppermute | solution.py:398
  478.1 26.8 %collective-permute-start.64 = (bf16[64,2048]{1,0:T(8,128)(2,1)}, bf16[64,2048]{1,0:T(8,128)(2,1)S(1)}, u32[]{:S(2)}, u32[]{:S(2)}) collective-permute-start(bf16[64,2048]{1,0:T(8,128)(2,1)} %get-tuple-element.222), channel_id=1, source_target_pairs={{8,0},{16,8},{24,16},{28,24},{20,28},{12,20},{4,12},{0,4},{9,1},{1... | collective-permute-start | bytes 786440 | tf_op jit(solution)/shard_map/ppermute | solution.py:398
  497.6 38.7 %collective-permute-start.49 = (bf16[384,1024]{1,0:T(8,128)(2,1)}, bf16[384,1024]{1,0:T(8,128)(2,1)}, u32[]{:S(2)}, u32[]{:S(2)}) collective-permute-start(bf16[384,1024]{1,0:T(8,128)(2,1)} %convolution_convert_fusion.9), channel_id=1, source_target_pairs={{0,1},{1,0},{2,3},{3,2},{4,5},{5,4},{6,7},{7,6},{8,9},{9,8},{10,11... | collective-permute-start | bytes 2359304 | tf_op jit(solution)/shard_map/ppermute | solution.py:237
  504.9 33.3 %collective-permute-start.53 = (bf16[384,1024]{1,0:T(8,128)(2,1)}, bf16[384,1024]{1,0:T(8,128)(2,1)}, u32[]{:S(2)}, u32[]{:S(2)}) collective-permute-start(bf16[384,1024]{1,0:T(8,128)(2,1)} %add_convert_fusion.3), channel_id=1, source_target_pairs={{0,2},{1,3},{2,0},{3,1},{4,6},{5,7},{6,4},{7,5},{8,10},{9,11},{10,... | collective-permute-start | bytes 2359304 | tf_op jit(solution)/shard_map/ppermute | solution.py:237
  509.5 33.0 %collective-permute-start.67 = (bf16[128,2048]{1,0:T(8,128)(2,1)}, bf16[128,2048]{1,0:T(8,128)(2,1)S(1)}, u32[]{:S(2)}, u32[]{:S(2)}) collective-permute-start(bf16[128,2048]{1,0:T(8,128)(2,1)} %get-tuple-element.229), channel_id=1, source_target_pairs={{0,8},{8,16},{16,24},{24,28},{28,20},{20,12},{12,4},{4,0},{1,9},{9... | collective-permute-start | bytes 1572872 | tf_op jit(solution)/shard_map/ppermute | solution.py:398
  589.7 28.4 %collective-permute-start.80 = (bf16[128,2048]{1,0:T(8,128)(2,1)}, bf16[128,2048]{1,0:T(8,128)(2,1)S(1)}, u32[]{:S(2)}, u32[]{:S(2)}) collective-permute-start(bf16[128,2048]{1,0:T(8,128)(2,1)} %shard_map.414.refs_0_), channel_id=1, source_target_pairs={{8,0},{16,8},{24,16},{28,24},{20,28},{12,20},{4,12},{0,4},{9,1},{1... | collective-permute-start | bytes 1572872 | tf_op jit(solution)/shard_map/ppermute | solution.py:398
  618.1 34.7 %collective-permute-start.83 = (bf16[128,2048]{1,0:T(8,128)(2,1)S(1)}, bf16[128,2048]{1,0:T(8,128)(2,1)S(1)}, u32[]{:S(2)}, u32[]{:S(2)}) collective-permute-start(bf16[128,2048]{1,0:T(8,128)(2,1)S(1)} %collective-permute-done.79.refs_1_), channel_id=1, source_target_pairs={{0,8},{8,16},{16,24},{24,28},{28,20},{20,12},{12,4},{4,0},{1,9},{9... | collective-permute-start | bytes 1572872 | tf_op jit(solution)/shard_map/ppermute | solution.py:398
  620.2 32.7 %collective-permute-start.84 = (bf16[128,2048]{1,0:T(8,128)(2,1)S(1)}, bf16[128,2048]{1,0:T(8,128)(2,1)S(1)}, u32[]{:S(2)}, u32[]{:S(2)}) collective-permute-start(bf16[128,2048]{1,0:T(8,128)(2,1)S(1)} %collective-permute-done.80.refs_2_), channel_id=1, source_target_pairs={{8,0},{16,8},{24,16},{28,24},{20,28},{12,20},{4,12},{0,4},{9,1},{1... | collective-permute-start | bytes 1572872 | tf_op jit(solution)/shard_map/ppermute | solution.py:398
  623.9 32.6 %collective-permute-start.82 = (bf16[128,2048]{1,0:T(8,128)(2,1)}, bf16[128,2048]{1,0:T(8,128)(2,1)S(1)}, u32[]{:S(2)}, u32[]{:S(2)}) collective-permute-start(bf16[128,2048]{1,0:T(8,128)(2,1)} %shard_map.416.refs_0_), channel_id=1, source_target_pairs={{8,0},{16,8},{24,16},{28,24},{20,28},{12,20},{4,12},{0,4},{9,1},{1... | collective-permute-start | bytes 1572872 | tf_op jit(solution)/shard_map/ppermute | solution.py:398
  624.8 31.7 %collective-permute-start.81 = (bf16[128,2048]{1,0:T(8,128)(2,1)}, bf16[128,2048]{1,0:T(8,128)(2,1)S(1)}, u32[]{:S(2)}, u32[]{:S(2)}) collective-permute-start(bf16[128,2048]{1,0:T(8,128)(2,1)} %shard_map.416.refs_0_), channel_id=1, source_target_pairs={{0,8},{8,16},{16,24},{24,28},{28,20},{20,12},{12,4},{4,0},{1,9},{9... | collective-permute-start | bytes 1572872 | tf_op jit(solution)/shard_map/ppermute | solution.py:398
  (246 other events, 2281.2 us)
Sparse Core Ops, SparseCore 0:
  316.5 93.2 reduce-scatter.1
  426.4 93.8 all-gather.1

commit v6 on v5

--- a/solution.py
+++ b/solution.py
@@ -16,7 +16,7 @@
 TK = 384
 HD = 128
 STEP = 64
-LINK_BYTES = 60_000_000
+LINK_BYTES = 180_000_000
 SM = pl.BlockSpec(memory_space=pltpu.SMEM)
 VM = pl.BlockSpec(memory_space=pltpu.VMEM)
 
@@ -242,15 +242,34 @@
     return [1 << bit for bit in range(size.bit_length() - 1)]
 
 
-def gather(own):
+def same_kernel(block_ref, out_ref):
+    pass
+
+
+def arrived(block):
+    spec = pl.BlockSpec(memory_space=pl.ANY)
+    return pl.pallas_call(
+        same_kernel,
+        in_specs=[spec],
+        out_specs=spec,
+        out_shape=jax.ShapeDtypeStruct(block.shape, block.dtype),
+        input_output_aliases={0: 0},
+        cost_estimate=pl.CostEstimate(flops=0, bytes_accessed=LINK_BYTES, transcendentals=0),
+    )(block)
+
+
+def gather(own, first=False, late=()):
     slots = {0: own}
     for distance in reversed(distances()):
         for slot in list(slots):
             slots[slot ^ distance] = swap(slots[slot], distance)
+    last = len(slots) - 1
+    if first:
+        slots[last] = after(arrived(slots[last]), late)
     return [slots[slot] for slot in range(len(slots))]
 
 
-def scatter(parts, late=()):
+def scatter(parts, late=(), add=True):
     parts = dict(enumerate(parts))
     sent = got = None
     for distance in distances():
@@ -260,7 +279,8 @@
                 if distance == distances()[-1]:
                     sent = after(sent, late)
                 got = swap(sent, distance)
-                parts[slot ^ distance] = parts[slot ^ distance].astype(F32) + got.astype(F32)
+                if add or distance != distances()[-1]:
+                    parts[slot ^ distance] = parts[slot ^ distance].astype(F32) + got.astype(F32)
     return parts[0], (sent, got)
 
 
@@ -268,23 +288,9 @@
     return lax.optimization_barrier((values, others))[0]
 
 
-def join_kernel(*refs):
-    rows = refs[0].shape[0]
-    for place, ref in enumerate(refs[:-1]):
-        refs[-1][place * rows : (place + 1) * rows] = ref[...]
-
-
-def halves(slots, weight=1):
+def halves(slots):
     half = len(slots) // 2
-    rows, width = slots[0].shape
-    far = pl.pallas_call(
-        join_kernel,
-        out_shape=sds((half * rows, width), slots[0].dtype),
-        in_specs=[VM] * half,
-        out_specs=VM,
-        cost_estimate=pl.CostEstimate(flops=0, bytes_accessed=weight * LINK_BYTES, transcendentals=0),
-    )(*slots[half:])
-    return jnp.concatenate(slots[:half], 0), far
+    return jnp.concatenate(slots[:half], 0), jnp.concatenate(slots[half:], 0)
 
 
 def pieces(near, far, weight, contract):
@@ -474,7 +480,7 @@
                 scratch_shapes=[pltpu.VMEM((length, step), F32)],
             ),
             out_shape=[sds(shape, F32) for shape in shapes],
-            compiler_params=pltpu.CompilerParams(vmem_limit_bytes=40 << 20),
+            compiler_params=pltpu.CompilerParams(vmem_limit_bytes=60 << 20),
             cost_estimate=pl.CostEstimate(flops=moved, bytes_accessed=moved, transcendentals=0),
         )(self.place.reshape(1).astype(jnp.int32), *items)
 
@@ -576,20 +582,20 @@
     near, far = halves(gather(normed.astype(B16)))
     pre, act = [], []
     for half in (near, far):
-        pre.append(dot(half, weight_up))
+        pre.append(dot(after(half, act), weight_up))
         act.append((pre[-1] * jax.nn.sigmoid(pre[-1])).astype(B16))
     total, (sent, _) = scatter(pieces(act[0], act[1], weight_down, (1, 0)))
     pre = [item.astype(B16) for item in pre]
     return (values + 0.5 * total, (unit, inverse, (near, far), pre, act), sent)
 
 
-def ffn_backward(grad, kept, gain, weight_up, weight_down, use=None):
+def ffn_backward(grad, kept, gain, weight_up, weight_down, use=None, fill=None):
     unit, inverse, wide, pre, act = kept
     own = (0.5 * grad).astype(B16)
-    cot = halves(gather(own))
+    cot = halves(gather(own) if fill is None else gather(own, True, fill(own)))
     d_pre = []
     for half in (0, 1):
-        d_act = dot(cot[half], weight_down, (1, 1))
+        d_act = dot(after(cot[half], d_pre), weight_down, (1, 1))
         d_pre.append((d_act * swish_slope(pre[half].astype(F32))).astype(B16))
     d_norm, (sent, _) = scatter(pieces(d_pre[0], d_pre[1], weight_up, (1, 1)))
     cot, d_pre = after((cot, d_pre), sent)
@@ -626,7 +632,7 @@
     normed, unit, inverse = normalize(values, gain)
     near, far = halves(gather(normed.astype(B16)))
     mixed = [dot(near, weights)]
-    far = after(far, rel, spans)
+    far = after(far, rel, spans, mixed)
     fetched, arrived = prefetch(far)
     mixed.append(dot(far, weights))
     flat = lambda bias: bias.astype(F32).reshape(1, width)
@@ -650,11 +656,13 @@
     return (values + total, kept, fetched)
 
 
-def attend_backward(grad, cot, kept, gain, weights, attend_out, table, filler):
+def attend_backward(grad, cot, kept, gain, weights, attend_out, table, filler, use):
     unit, inverse, wide, operands, heads_wide, sums, sent = kept
     slots, width = sent.shape
     _, _, reorder = places(slots)
+    cot = halves(cot)
     d_near = dot(cot[0], attend_out, (1, 1)).astype(B16)
+    cot = (cot[0], after(cot[1], d_near))
     d_heads = jnp.concatenate([d_near, dot(cot[1], attend_out, (1, 1)).astype(B16)], 0)
     if reorder:
         d_heads = to_true(d_heads)
@@ -665,13 +673,14 @@
     d_all = after(d_all, filler[1])
     half = slots // 2
     d_norm, (last, _) = scatter(pieces(d_all[:half], d_all[half:], weights, (1, 1)))
-    d_in, grad_gain = normalize_back(d_norm, unit, inverse, gain)
     cot, d_all, d_rel = after((cot, d_all, d_rel), last)
     grad_out = dot(jnp.concatenate(cot, 0), sent, (0, 0))
     grad_all = dot(jnp.concatenate(wide, 0), d_all, (0, 0))
     grad_pos = dot(table, d_rel, (0, 0))
     grads = [item.astype(B16) for item in (grad_all, grad_pos, grad_out)]
-    return (grad + d_in, grad_gain, grads, d_bias[:2])
+    d_norm = after(d_norm, use(grads, last))
+    d_in, grad_gain = normalize_back(d_norm, unit, inverse, gain)
+    return (grad + d_in, grad_gain, d_bias[:2])
 
 
 def conv_weights(point_in, depth_kernel, gain_inner, point_out, first):
@@ -731,37 +740,42 @@
     cot = grad.astype(B16)
     d_act = dot(halo(cot, reach), out, (1, 1))
     d_depth_norm = d_act * swish_slope(depth_norm)
-    grad_gain_inner = jnp.sum((d_depth_norm * inner_unit)[mine], axis=0)
     d_depth, _ = normalize_back(d_depth_norm, inner_unit, inner_inverse, gain_inner)
     d_glu = 0.0
-    kernel_rows = []
     for tap in range(taps):
         weighted = d_depth * masks[tap]
         back = 2 * reach - tap
         d_glu = d_glu + kernel[tap] * weighted[back : back + rows]
-        kernel_rows.append(jnp.sum(weighted[mine] * glu[reach + tap : reach + tap + rows], axis=0))
     d_a = (d_glu * gate).astype(B16)
     d_b = (d_glu * mixed_a * gate * (1.0 - gate)).astype(B16)
     d_norm = dot(d_a, in_a, (1, 1)) + dot(d_b, in_b, (1, 1))
     d_in, grad_gain = normalize_back(d_norm, unit, inverse, gain)
     grad = grad + d_in
-    slots = gather(grad.astype(B16))
-    next_cot = halves(slots, 3)
+    slots = gather(grad.astype(B16), True)
     low, cot, d_a, d_b, inner = after((low, cot, d_a, d_b, inner), slots[1])
     size = lax.axis_size("tp")
     width = in_a.shape[1] // size
-    parts, small_parts = [], []
+    parts = []
     grads = [
         dot(left, right, (0, 0)).astype(B16)
         for left, right in ((low, d_a), (low, d_b), (cot, inner[mine]))
     ]
-    small = jnp.stack(kernel_rows + [grad_gain_inner], 0)
+
+    def small_grads(gate):
+        d_own, norm_own = after((d_depth[mine], d_depth_norm[mine]), gate)
+        sums = []
+        for tap in range(taps):
+            near = d_own * masks[tap][mine]
+            sums.append(jnp.sum(near * glu[reach + tap : reach + tap + rows], axis=0))
+        sums.append(jnp.sum(norm_own * inner_unit[mine], axis=0))
+        small = jnp.stack(sums, 0)
+        return scatter([small[:, k * width : (k + 1) * width] for k in range(size)])[0]
+
     for slot in range(size):
         cols = slice(slot * width, (slot + 1) * width)
         parts.append(jnp.concatenate([item[:, cols] for item in grads], 1))
-        small_parts.append(small[:, cols])
-    total, ends = scatter(parts, next_cot[1])
-    return (grad, next_cot, grad_gain, (total.astype(B16), scatter(small_parts)[0]), ends)
+    total, ends = scatter(parts, slots[-1], False)
+    return (grad, slots, grad_gain, (total, small_grads), ends)
 
 
 def body(
@@ -822,24 +836,24 @@
         grad, kept_second, gain_second, up_second, down_second, start_second
     )
     grad, cot, sum_conv, conv_grads, ends = conv_backward(grad, kept_conv, gain_conv, full, masks)
-    ends = (ends[0], (ends[1], held["second"]))
-    grad, sum_attend, attend_grads, d_bias = attend_backward(
-        grad, cot, kept_attend, gain_attend, weights, attend_out, table, ends
+    ends = (ends[0], (ends, held["second"]))
+
+    def start_middle(grads, last):
+        own, got = after((conv_grads[0], ends[1][0][1]), last)
+        total = (own.astype(F32) + got.astype(F32)).astype(B16)
+        forms = [(width, plain)] * 4 + [(width, turned), (2 * width, plain), (width, turned)]
+        held["middle"] = row_sum(grads + [total], forms)
+        return held["middle"].step()
+
+    grad, sum_attend, d_bias = attend_backward(
+        grad, cot, kept_attend, gain_attend, weights, attend_out, table, ends, start_middle
     )
+    middle = held["middle"]
     second_sum = end_sum(held["second"])
     grad, sum_first, first_grads, marks = ffn_backward(
-        grad, kept_first, gain_first, up_first, down_first
+        grad, kept_first, gain_first, up_first, down_first, None, middle.step
     )
-    pairs = (sum_first, sum_attend, sum_conv, sum_second, sum_final)
-    gains = sum_cube(gain_sums(pairs, marks[1]), "tp")
-    small = jnp.concatenate([conv_grads[1], d_bias], 0)
-    small_shape = small.shape
-    pack = jnp.concatenate([gains.reshape(-1), small.reshape(-1)]).reshape(-1, width)
-    pack = sum_cube(pack, "rows")
-    forms = [(width, plain)] * 4 + [(width, turned), (2 * width, plain), (width, turned)]
-    middle = row_sum(attend_grads + [conv_grads[0]], forms)
     first = RowSums(first_grads, [(item.shape[1], plain) for item in first_grads])
-    middle.step()
     token = middle.step(marks[1])
     token = first.step(token)
     second_sum = after(second_sum, token)
@@ -852,7 +866,15 @@
             token = (token, grad)
         if first.done == 5:
             second_up, second_down = split_sum(after(second_sum, token), up_second.shape[0])
-            token = (token, second_up, second_down, pack)
+            token = (token, second_up, second_down)
+    while first.left:
+        token = first.step(token)
+    pairs = (sum_first, sum_attend, sum_conv, sum_second, sum_final)
+    gains = sum_cube(gain_sums(pairs, marks[1]), "tp")
+    small = jnp.concatenate([conv_grads[1](marks[1]), d_bias], 0)
+    small_shape = small.shape
+    pack = jnp.concatenate([gains.reshape(-1), small.reshape(-1)]).reshape(-1, width)
+    pack = sum_cube(after(pack, token), "rows")
     attend_sum = middle.finish(token)
     first_sum = first.finish(attend_sum)
     pack = pack.reshape(-1)

time: 740 us -> 693 us (0.936)
  matrix products: 127 us -> 109 us
  local copies, waits for them, and re-layouts: 65.1 us -> 52.2 us
  Pallas kernels: 98.6 us -> 87.2 us
  waiting for transfers between devices: 232 us -> 242 us
  starting transfers between devices: 107 us -> 97.2 us
    ppermute x32, waiting for transfers between devices: 47.9 us -> 73.4 us  [send(): lax.ppermute(item, 'rows', way)]
    ppermute x5, waiting for transfers between devices: 26.2 us -> 7.83 us  [sum_cube(): lax.ppermute(values, axis, [(i, i ^ distance) for i in range(size)])]
    dot_general x53, matrix products: 127 us -> 109 us  [dot(): lax.dot_general(left, right, (((contract[0],), (contract[1],)), ((), ()))...]
    unnamed x364 -> x336, local copies, waits for them, and re-layouts: 45.3 us -> 28.5 us
    pallas_call x6 -> x2, Pallas kernels: 15.9 us -> 0.01 us  [arrived(): pl.pallas_call(same_kernel, in_specs=[spec], out_specs=spec, out_shape=ja...]
    ppermute x32, starting transfers between devices: 61.6 us -> 46.7 us  [send(): lax.ppermute(item, 'rows', way)]
  transfers between devices with their start and end apart: 97 -> 97, of which waited for: 37 -> 47; matrix products, arithmetic and copies ran while one was open for 30% -> 28% of each run, Pallas kernels for 12% -> 12%
where the time goes in v6:
time: 693 us; the launch traced here: 684 us
  waiting for transfers between devices  242 us (35%)
  matrix products  109 us (16%)
  starting transfers between devices  97.2 us (14%)
  Pallas kernels  87.2 us (13%)
  other arithmetic  80.2 us (12%)
  local copies, waits for them, and re-layouts  52.2 us (8%)
  between operations  16.7 us (2%)
    ppermute x54, waiting for transfers between devices, swap(): return lax.ppermute(values, 'tp', [(i, i ^ distance) for i in range(size)])  148 us
    dot_general x53, matrix products, dot(): lax.dot_general(left, right, (((contract[0],), (contract[1],)), ((), ()))...  109 us
    ppermute x32, waiting for transfers between devices, send(): lax.ppermute(item, 'rows', way)  73.4 us
    ppermute x32, starting transfers between devices, send(): lax.ppermute(item, 'rows', way)  46.7 us
    ppermute x54, starting transfers between devices, swap(): return lax.ppermute(values, 'tp', [(i, i ^ distance) for i in range(size)])  39.3 us
    pallas_call x10, Pallas kernels, call(): pl.pallas_call(kernel, grid_spec=pltpu.PrefetchScalarGridSpec(num_scalar_...  30.7 us
    pallas_call x1, Pallas kernels, attend_back(): pl.pallas_call(functools.partial(attend_back_kernel, heads), out_shape=(s...  28.6 us
    unnamed x336, local copies, waits for them, and re-layouts  28.5 us
  transfers between devices with their start and end apart: 97, of which 47 were waited for; matrix products, arithmetic and copies ran while one was open for 28% of the time, Pallas kernels for 12%

profile of v6, /device:TPU:0, one launch (start us, length us, event | category | flops | bytes accessed | tf_op | source)
XLA Modules:
  0.0 684.4 jit_solution(13303225071615752468)
XLA Ops:
  51.1 16.9 %collective-permute-done.5 = bf16[384,1024]{1,0:T(8,128)(2,1)S(1)} collective-permute-done((bf16[384,1024]{1,0:T(8,128)(2,1)S(1)}, bf16[384,1024]{1,0:T(8,128)(2,1)S(1)}, u32[]{:S(2)}, u32[]{:S(2)}) %collective-permute-start.5) | collective-permute-done | bytes 786464 | tf_op jit(solution)/shard_map/ppermute | solution.py:237
  75.8 13.6 %collective-permute-done.7 = bf16[384,1024]{1,0:T(8,128)(2,1)S(1)} collective-permute-done((bf16[384,1024]{1,0:T(8,128)(2,1)S(1)}, bf16[384,1024]{1,0:T(8,128)(2,1)S(1)}, u32[]{:S(2)}, u32[]{:S(2)}) %collective-permute-start.7) | collective-permute-done | bytes 786464 | tf_op jit(solution)/shard_map/ppermute | solution.py:237
  101.0 12.7 %shard_map.399 = (bf16[1536,256]{1,0:T(8,128)(2,1)S(1)}, f32[1536,256]{1,0:T(8,128)S(1)}, f32[1536,2]{1,0:T(8,128)S(1)}) custom-call(s32[2,12]{1,0:T(2,128)S(1)} %pad_add_fusion.spans, s32[12]{0:T(128)S(1)} %fusion.201.q_at, s32[4]{0:T(128)S(1)} %fusion.202.k_at, bf16[1536,256]{1,0:T(8,128)(2,1)S(1)} %get-tuple-element.480.qc_ref, ...), custom_call_target="tpu_custom_call" | custom-call | flops 4000000000 | bytes 9000000 | tf_op jit(solution)/shard_map/pallas_call | solution.py:154
  113.8 6.3 collective-permute-done.10
  120.1 10.4 %collective-permute-done.11 = bf16[256,1024]{1,0:T(8,128)(2,1)S(1)} collective-permute-done((bf16[256,1024]{1,0:T(8,128)(2,1)S(1)}, bf16[256,1024]{1,0:T(8,128)(2,1)S(1)}, u32[]{:S(2)}, u32[]{:S(2)}) %collective-permute-start.11) | collective-permute-done | bytes 524320 | tf_op jit(solution)/shard_map/ppermute | solution.py:237
  137.4 17.0 %collective-permute-done.14 = bf16[384,1024]{1,0:T(8,128)(2,1)S(1)} collective-permute-done((bf16[384,1024]{1,0:T(8,128)(2,1)S(1)}, bf16[384,1024]{1,0:T(8,128)(2,1)S(1)}, u32[]{:S(2)}, u32[]{:S(2)}) %collective-permute-start.14) | collective-permute-done | bytes 786464 | tf_op jit(solution)/shard_map/ppermute | solution.py:237
  174.4 17.2 %collective-permute-done.28 = bf16[384,1024]{1,0:T(8,128)(2,1)S(1)} collective-permute-done((bf16[384,1024]{1,0:T(8,128)(2,1)S(1)}, bf16[384,1024]{1,0:T(8,128)(2,1)S(1)}, u32[]{:S(2)}, u32[]{:S(2)}) %collective-permute-start.28) | collective-permute-done | bytes 786464 | tf_op jit(solution)/shard_map/ppermute | solution.py:237
  204.5 16.9 %collective-permute-done.31 = bf16[384,1024]{1,0:T(8,128)(2,1)S(1)} collective-permute-done((bf16[384,1024]{1,0:T(8,128)(2,1)S(1)}, bf16[384,1024]{1,0:T(8,128)(2,1)S(1)}, u32[]{:S(2)}, u32[]{:S(2)}) %collective-permute-start.31) | collective-permute-done | bytes 786464 | tf_op jit(solution)/shard_map/ppermute | solution.py:237
  226.8 17.2 %collective-permute-done.34 = bf16[384,1024]{1,0:T(8,128)(2,1)S(1)} collective-permute-done((bf16[384,1024]{1,0:T(8,128)(2,1)S(1)}, bf16[384,1024]{1,0:T(8,128)(2,1)S(1)}, u32[]{:S(2)}, u32[]{:S(2)}) %collective-permute-start.34) | collective-permute-done | bytes 786464 | tf_op jit(solution)/shard_map/ppermute | solution.py:237
  263.4 10.6 %collective-permute-done.37 = bf16[384,1024]{1,0:T(8,128)(2,1)S(1)} collective-permute-done((bf16[384,1024]{1,0:T(8,128)(2,1)S(1)}, bf16[384,1024]{1,0:T(8,128)(2,1)S(1)}, u32[]{:S(2)}, u32[]{:S(2)}) %collective-permute-start.37) | collective-permute-done | bytes 786464 | tf_op jit(solution)/shard_map/ppermute | solution.py:237
  314.8 8.1 %collective-permute-done.41 = bf16[384,1024]{1,0:T(8,128)(2,1)S(1)} collective-permute-done((bf16[384,1024]{1,0:T(8,128)(2,1)S(1)}, bf16[384,1024]{1,0:T(8,128)(2,1)S(1)}, u32[]{:S(2)}, u32[]{:S(2)}) %collective-permute-start.41) | collective-permute-done | bytes 786464 | tf_op jit(solution)/shard_map/ppermute | solution.py:237
  339.5 28.6 %shard_map.401 = (bf16[1536,768]{1,0:T(8,128)(2,1)}, bf16[3072,256]{1,0:T(8,128)(2,1)}, f32[8,256]{1,0:T(8,128)S(1)}) custom-call(s32[2,12]{1,0:T(2,128)S(1)} %pad_add_fusion.spans, s32[12]{0:T(128)S(1)} %fusion.201.q_at, s32[4]{0:T(128)S(1)} %fusion.202.k_at, bf16[1536,256]{1,0:T(8,128)(2,1)S(1)} %copy-done.7, bf16[1536,256]{1,0:T(8,128)(2,1)S(1)} %copy-done.9, ...), custom_call_target="tpu_custom_call" | custom-call | flops 1000000 | bytes 1000000 | tf_op jit(solution)/shard_map/pallas_call | solution.py:165
  368.1 8.2 %reduce-scatter.2.cloned.1.call-done = bf16[256,1024]{1,0:T(8,128)(2,1)} async-done(((bf16[2048,1024]{1,0:T(8,128)(2,1)}), bf16[256,1024]{1,0:T(8,128)(2,1)}) %reduce-scatter.2.cloned.1.call-update) | async-done | bytes 524304 | tf_op jit(solution)/shard_map/reduce_scatter | solution.py:514
  418.6 7.9 %collective-permute-start.53 = (bf16[64,2048]{1,0:T(8,128)(2,1)}, bf16[64,2048]{1,0:T(8,128)(2,1)S(1)}, u32[]{:S(2)}, u32[]{:S(2)}) collective-permute-start(bf16[64,2048]{1,0:T(8,128)(2,1)} %get-tuple-element.224), channel_id=1, source_target_pairs={{0,8},{8,16},{16,24},{24,28},{28,20},{20,12},{12,4},{4,0},{1,9},{9... | collective-permute-start | bytes 786440 | tf_op jit(solution)/shard_map/ppermute | solution.py:404
  427.7 7.6 %collective-permute-done.53.refs_8_ = bf16[64,2048]{1,0:T(8,128)(2,1)S(1)} collective-permute-done((bf16[64,2048]{1,0:T(8,128)(2,1)}, bf16[64,2048]{1,0:T(8,128)(2,1)S(1)}, u32[]{:S(2)}, u32[]{:S(2)}) %collective-permute-start.53) | collective-permute-done | bytes 262176 | tf_op jit(solution)/shard_map/ppermute | solution.py:404
  435.3 9.1 %collective-permute-done.54.refs_9_ = bf16[64,2048]{1,0:T(8,128)(2,1)} collective-permute-done((bf16[64,2048]{1,0:T(8,128)(2,1)}, bf16[64,2048]{1,0:T(8,128)(2,1)}, u32[]{:S(2)}, u32[]{:S(2)}) %collective-permute-start.54) | collective-permute-done | bytes 262176 | tf_op jit(solution)/shard_map/ppermute | solution.py:404
  467.6 9.7 %collective-permute-start.62 = (bf16[128,2048]{1,0:T(8,128)(2,1)S(1)}, bf16[128,2048]{1,0:T(8,128)(2,1)S(1)}, u32[]{:S(2)}, u32[]{:S(2)}) collective-permute-start(bf16[128,2048]{1,0:T(8,128)(2,1)S(1)} %copy-done.143), channel_id=1, source_target_pairs={{0,8},{8,16},{16,24},{24,28},{28,20},{20,12},{12,4},{4,0},{1,9},{9... | collective-permute-start | bytes 1572872 | tf_op jit(solution)/shard_map/ppermute | solution.py:404
  497.7 8.0 %fusion.81.refs_0_.refs_2_ = bf16[1024,1024]{1,0:T(8,128)(2,1)} fusion(bf16[768,1024]{1,0:T(8,128)(2,1)} %copy-done.150, bf16[768,1024]{1,0:T(8,128)(2,1)} %fusion.20, bf16[384,1024]{1,0:T(8,128)(2,1)} %copy-done.83, bf16[384,1024]{1,0:T(8,128)(2,1)} %collective-permute-done.2, bf16[384,1024]{1,0:T(8,128)(2,1)} %copy-done.82, ...), kind=kOutput, calls=%fused_computation.103 | convolution fusion | flops 3241148416 | bytes 8388608 | tf_op jit(solution)/shard_map/dot_general | solution.py:230
  563.0 7.5 %collective-permute-done.72.refs_4_ = bf16[128,2048]{1,0:T(8,128)(2,1)S(1)} collective-permute-done((bf16[128,2048]{1,0:T(8,128)(2,1)}, bf16[128,2048]{1,0:T(8,128)(2,1)S(1)}, u32[]{:S(2)}, u32[]{:S(2)}) %collective-permute-start.72) | collective-permute-done | bytes 524320 | tf_op jit(solution)/shard_map/ppermute | solution.py:404
  585.4 7.6 %collective-permute-done.76.refs_2_ = bf16[128,2048]{1,0:T(8,128)(2,1)} collective-permute-done((bf16[128,2048]{1,0:T(8,128)(2,1)}, bf16[128,2048]{1,0:T(8,128)(2,1)}, u32[]{:S(2)}, u32[]{:S(2)}) %collective-permute-start.76) | collective-permute-done | bytes 524320 | tf_op jit(solution)/shard_map/ppermute | solution.py:404
  601.4 6.8 slice_convert_fusion
  618.5 7.3 %collective-permute-done.84.refs_3_ = bf16[128,2048]{1,0:T(8,128)(2,1)S(1)} collective-permute-done((bf16[128,2048]{1,0:T(8,128)(2,1)S(1)}, bf16[128,2048]{1,0:T(8,128)(2,1)S(1)}, u32[]{:S(2)}, u32[]{:S(2)}) %collective-permute-start.84) | collective-permute-done | bytes 524320 | tf_op jit(solution)/shard_map/ppermute | solution.py:404
  653.7 9.2 %shard_map.413 = (f32[1024,256]{1,0:T(8,128)}, f32[1024,256]{1,0:T(8,128)}, f32[1024,256]{1,0:T(8,128)}, f32[1024,256]{1,0:T(8,128)}, f32[256,1024]{1,0:T(8,128)...) custom-call(s32[1]{0:T(128)} %bitcast.42.at, bf16[128,2048]{1,0:T(8,128)(2,1)} %shard_map.409.refs_0_, ...), custom_call_target="tpu_custom_call" | custom-call | flops 12582912 | bytes 12582912 | tf_op jit(solution)/shard_map/pallas_call | solution.py:473
  671.3 6.1 shard_map.414
  (740 shorter events, 397.2 us)
Async XLA Ops:
  7.2 369.1 %reduce-scatter.2.cloned.1.call-start = ((), (), s32[]{:S(2)}) async-start(), calls=%async_computation.1 | async-start | bytes 4718592 | tf_op jit(solution)/shard_map/reduce_scatter | solution.py:514
  12.1 21.6 %collective-permute-start = (bf16[384,1024]{1,0:T(8,128)(2,1)}, bf16[384,1024]{1,0:T(8,128)(2,1)S(1)}, u32[]{:S(2)}, u32[]{:S(2)}) collective-permute-start(bf16[384,1024]{1,0:T(8,128)(2,1)} %get-tuple-element.419), channel_id=1, source_target_pairs={{0,1},{1,0},{2,3},{3,2},{4,5},{5,4},{6,7},{7,6},{8,9},{9,8},{10,11... | collective-permute-start | bytes 2359304 | tf_op jit(solution)/shard_map/ppermute | solution.py:237
  12.6 21.1 %collective-permute-start.2 = (bf16[384,1024]{1,0:T(8,128)(2,1)}, bf16[384,1024]{1,0:T(8,128)(2,1)}, u32[]{:S(2)}, u32[]{:S(2)}) collective-permute-start(bf16[384,1024]{1,0:T(8,128)(2,1)} %get-tuple-element.419), channel_id=1, source_target_pairs={{0,2},{1,3},{2,0},{3,1},{4,6},{5,7},{6,4},{7,5},{8,10},{9,11},{10,... | collective-permute-start | bytes 2359304 | tf_op jit(solution)/shard_map/ppermute | solution.py:237
  15.2 56.9 %collective-permute-start.16 = (bf16[6,256]{1,0:T(8,128)(2,1)S(1)}, bf16[6,256]{1,0:T(8,128)(2,1)S(1)}, u32[]{:S(2)}, u32[]{:S(2)}) collective-permute-start(bf16[6,256]{1,0:T(8,128)(2,1)S(1)} %pad_maximum_fusion.25), channel_id=1, source_target_pairs={{0,2},{1,3},{2,0},{3,1},{4,6},{5,7},{6,4},{7,5},{8,10},{9,11},{10,... | collective-permute-start | bytes 9224 | tf_op jit(solution)/shard_map/ppermute | solution.py:237
  15.3 57.0 %collective-permute-start.15 = (bf16[6,256]{1,0:T(8,128)(2,1)S(1)}, bf16[6,256]{1,0:T(8,128)(2,1)S(1)}, u32[]{:S(2)}, u32[]{:S(2)}) collective-permute-start(bf16[6,256]{1,0:T(8,128)(2,1)S(1)} %pad_maximum_fusion.25), channel_id=1, source_target_pairs={{0,1},{1,0},{2,3},{3,2},{4,5},{5,4},{6,7},{7,6},{8,9},{9,8},{10,11... | collective-permute-start | bytes 9224 | tf_op jit(solution)/shard_map/ppermute | solution.py:237
  93.5 39.1 %collective-permute-start.20 = (bf16[1024,256]{1,0:T(8,128)(2,1)S(1)}, bf16[1024,256]{1,0:T(8,128)(2,1)S(1)}, u32[]{:S(2)}, u32[]{:S(2)}) collective-permute-start(bf16[1024,256]{1,0:T(8,128)(2,1)S(1)} %get-tuple-element.190), channel_id=1, source_target_pairs={{0,1},{1,0},{2,3},{3,2},{4,5},{5,4},{6,7},{7,6},{8,9},{9,8},{10,11... | collective-permute-start | bytes 1572872 | tf_op jit(solution)/shard_map/ppermute | solution.py:237
  97.3 22.8 %collective-permute-start.10 = (bf16[1024,256]{1,0:T(8,128)(2,1)S(1)}, bf16[1024,256]{1,0:T(8,128)(2,1)S(1)}, u32[]{:S(2)}, u32[]{:S(2)}) collective-permute-start(bf16[1024,256]{1,0:T(8,128)(2,1)S(1)} %get-tuple-element.191), channel_id=1, source_target_pairs={{0,2},{1,3},{2,0},{3,1},{4,6},{5,7},{6,4},{7,5},{8,10},{9,11},{10,... | collective-permute-start | bytes 1572872 | tf_op jit(solution)/shard_map/ppermute | solution.py:237
  98.3 32.2 %collective-permute-start.11 = (bf16[256,1024]{1,0:T(8,128)(2,1)S(1)}, bf16[256,1024]{1,0:T(8,128)(2,1)S(1)}, u32[]{:S(2)}, u32[]{:S(2)}) collective-permute-start(bf16[256,1024]{1,0:T(8,128)(2,1)S(1)} %copy-done.101), channel_id=1, source_target_pairs={{0,2},{1,3},{2,0},{3,1},{4,6},{5,7},{6,4},{7,5},{8,10},{9,11},{10,... | collective-permute-start | bytes 1572872 | tf_op jit(solution)/shard_map/ppermute | solution.py:237
  136.4 23.2 %collective-permute-start.25 = (bf16[256,1024]{1,0:T(8,128)(2,1)S(1)}, bf16[256,1024]{1,0:T(8,128)(2,1)S(1)}, u32[]{:S(2)}, u32[]{:S(2)}) collective-permute-start(bf16[256,1024]{1,0:T(8,128)(2,1)S(1)} %collective-permute-done.11), channel_id=1, source_target_pairs={{0,1},{1,0},{2,3},{3,2},{4,5},{5,4},{6,7},{7,6},{8,9},{9,8},{10,11... | collective-permute-start | bytes 1572872 | tf_op jit(solution)/shard_map/ppermute | solution.py:237
  284.1 234.4 %all-gather.2.cloned.1.call-start = ((), (), s32[]{:S(2)}) async-start(), calls=%async_computation.2 | async-start | bytes 4718592 | tf_op jit(solution)/shard_map/all_gather | solution.py:518
  330.3 37.8 %collective-permute-start.44 = (bf16[1024,768]{1,0:T(8,128)(2,1)}, bf16[1024,768]{1,0:T(8,128)(2,1)}, u32[]{:S(2)}, u32[]{:S(2)}) collective-permute-start(bf16[1024,768]{1,0:T(8,128)(2,1)} %add_convert_fusion.2), channel_id=1, source_target_pairs={{0,2},{1,3},{2,0},{3,1},{4,6},{5,7},{6,4},{7,5},{8,10},{9,11},{10,... | collective-permute-start | bytes 4718600 | tf_op jit(solution)/shard_map/ppermute | solution.py:237
  333.3 45.9 %collective-permute-start.48 = (bf16[1024,768]{1,0:T(8,128)(2,1)}, bf16[1024,768]{1,0:T(8,128)(2,1)}, u32[]{:S(2)}, u32[]{:S(2)}) collective-permute-start(bf16[1024,768]{1,0:T(8,128)(2,1)} %pad_maximum_fusion.10), channel_id=1, source_target_pairs={{0,1},{1,0},{2,3},{3,2},{4,5},{5,4},{6,7},{7,6},{8,9},{9,8},{10,11... | collective-permute-start | bytes 4718600 | tf_op jit(solution)/shard_map/ppermute | solution.py:237
  383.9 23.9 %collective-permute-start.45 = (bf16[384,1024]{1,0:T(8,128)(2,1)}, bf16[384,1024]{1,0:T(8,128)(2,1)}, u32[]{:S(2)}, u32[]{:S(2)}) collective-permute-start(bf16[384,1024]{1,0:T(8,128)(2,1)} %convolution_convert_fusion.5), channel_id=1, source_target_pairs={{0,1},{1,0},{2,3},{3,2},{4,5},{5,4},{6,7},{7,6},{8,9},{9,8},{10,11... | collective-permute-start | bytes 2359304 | tf_op jit(solution)/shard_map/ppermute | solution.py:237
  417.1 30.9 %collective-permute-start.49 = (bf16[384,1024]{1,0:T(8,128)(2,1)}, bf16[384,1024]{1,0:T(8,128)(2,1)S(1)}, u32[]{:S(2)}, u32[]{:S(2)}) collective-permute-start(bf16[384,1024]{1,0:T(8,128)(2,1)} %get-tuple-element.367), channel_id=1, source_target_pairs={{0,1},{1,0},{2,3},{3,2},{4,5},{5,4},{6,7},{7,6},{8,9},{9,8},{10,11... | collective-permute-start | bytes 2359304 | tf_op jit(solution)/shard_map/ppermute | solution.py:237
  417.1 32.4 %collective-permute-start.51 = (bf16[384,1024]{1,0:T(8,128)(2,1)}, bf16[384,1024]{1,0:T(8,128)(2,1)S(1)}, u32[]{:S(2)}, u32[]{:S(2)}) collective-permute-start(bf16[384,1024]{1,0:T(8,128)(2,1)} %get-tuple-element.367), channel_id=1, source_target_pairs={{0,2},{1,3},{2,0},{3,1},{4,6},{5,7},{6,4},{7,5},{8,10},{9,11},{10,... | collective-permute-start | bytes 2359304 | tf_op jit(solution)/shard_map/ppermute | solution.py:237
  467.6 21.6 %collective-permute-start.62 = (bf16[128,2048]{1,0:T(8,128)(2,1)S(1)}, bf16[128,2048]{1,0:T(8,128)(2,1)S(1)}, u32[]{:S(2)}, u32[]{:S(2)}) collective-permute-start(bf16[128,2048]{1,0:T(8,128)(2,1)S(1)} %copy-done.143), channel_id=1, source_target_pairs={{0,8},{8,16},{16,24},{24,28},{28,20},{20,12},{12,4},{4,0},{1,9},{9... | collective-permute-start | bytes 1572872 | tf_op jit(solution)/shard_map/ppermute | solution.py:404
  482.5 46.5 %collective-permute-start.50 = (bf16[384,1024]{1,0:T(8,128)(2,1)}, bf16[384,1024]{1,0:T(8,128)(2,1)}, u32[]{:S(2)}, u32[]{:S(2)}) collective-permute-start(bf16[384,1024]{1,0:T(8,128)(2,1)} %convolution_convert_fusion.9), channel_id=1, source_target_pairs={{0,1},{1,0},{2,3},{3,2},{4,5},{5,4},{6,7},{7,6},{8,9},{9,8},{10,11... | collective-permute-start | bytes 2359304 | tf_op jit(solution)/shard_map/ppermute | solution.py:237
  485.8 43.3 %collective-permute-start.56 = (bf16[384,1024]{1,0:T(8,128)(2,1)}, bf16[384,1024]{1,0:T(8,128)(2,1)}, u32[]{:S(2)}, u32[]{:S(2)}) collective-permute-start(bf16[384,1024]{1,0:T(8,128)(2,1)} %add_convert_fusion.3), channel_id=1, source_target_pairs={{0,2},{1,3},{2,0},{3,1},{4,6},{5,7},{6,4},{7,5},{8,10},{9,11},{10,... | collective-permute-start | bytes 2359304 | tf_op jit(solution)/shard_map/ppermute | solution.py:237
  497.0 21.5 %collective-permute-start.67 = (bf16[128,2048]{1,0:T(8,128)(2,1)}, bf16[128,2048]{1,0:T(8,128)(2,1)}, u32[]{:S(2)}, u32[]{:S(2)}) collective-permute-start(bf16[128,2048]{1,0:T(8,128)(2,1)} %get-tuple-element.261), channel_id=1, source_target_pairs={{8,0},{16,8},{24,16},{28,24},{20,28},{12,20},{4,12},{0,4},{9,1},{1... | collective-permute-start | bytes 1572872 | tf_op jit(solution)/shard_map/ppermute | solution.py:404
  527.1 21.1 %collective-permute-start.68 = (bf16[128,2048]{1,0:T(8,128)(2,1)}, bf16[128,2048]{1,0:T(8,128)(2,1)}, u32[]{:S(2)}, u32[]{:S(2)}) collective-permute-start(bf16[128,2048]{1,0:T(8,128)(2,1)} %get-tuple-element.279), channel_id=1, source_target_pairs={{0,8},{8,16},{16,24},{24,28},{28,20},{20,12},{12,4},{4,0},{1,9},{9... | collective-permute-start | bytes 1572872 | tf_op jit(solution)/shard_map/ppermute | solution.py:404
  578.7 50.6 %collective-permute-start.59 = (bf16[6,256]{1,0:T(8,128)(2,1)S(1)}, bf16[6,256]{1,0:T(8,128)(2,1)S(1)}, u32[]{:S(2)}, u32[]{:S(2)}) collective-permute-start(bf16[6,256]{1,0:T(8,128)(2,1)S(1)} %get-tuple-element.438), channel_id=1, source_target_pairs={{0,1},{1,0},{2,3},{3,2},{4,5},{5,4},{6,7},{7,6},{8,9},{9,8},{10,11... | collective-permute-start | bytes 9224 | tf_op jit(solution)/shard_map/ppermute | solution.py:237
  583.4 24.8 %collective-permute-start.82 = (bf16[128,2048]{1,0:T(8,128)(2,1)}, bf16[128,2048]{1,0:T(8,128)(2,1)}, u32[]{:S(2)}, u32[]{:S(2)}) collective-permute-start(bf16[128,2048]{1,0:T(8,128)(2,1)} %collective-permute-done.78.refs_3_), channel_id=1, source_target_pairs={{0,8},{8,16},{16,24},{24,28},{28,20},{20,12},{12,4},{4,0},{1,9},{9... | collective-permute-start | bytes 1572872 | tf_op jit(solution)/shard_map/ppermute | solution.py:404
  585.4 24.3 %collective-permute-start.83 = (bf16[128,2048]{1,0:T(8,128)(2,1)}, bf16[128,2048]{1,0:T(8,128)(2,1)}, u32[]{:S(2)}, u32[]{:S(2)}) collective-permute-start(bf16[128,2048]{1,0:T(8,128)(2,1)} %collective-permute-done.79.refs_4_), channel_id=1, source_target_pairs={{8,0},{16,8},{24,16},{28,24},{20,28},{12,20},{4,12},{0,4},{9,1},{1... | collective-permute-start | bytes 1572872 | tf_op jit(solution)/shard_map/ppermute | solution.py:404
  608.2 21.2 %collective-permute-start.61 = (bf16[6,256]{1,0:T(8,128)(2,1)S(1)}, bf16[6,256]{1,0:T(8,128)(2,1)S(1)}, u32[]{:S(2)}, u32[]{:S(2)}) collective-permute-start(bf16[6,256]{1,0:T(8,128)(2,1)S(1)} %fusion.184), channel_id=1, source_target_pairs={{0,2},{1,3},{2,0},{3,1},{4,6},{5,7},{6,4},{7,5},{8,10},{9,11},{10,... | collective-permute-start | bytes 9224 | tf_op jit(solution)/shard_map/ppermute | solution.py:237
  (231 other events, 2130.4 us)
Sparse Core Ops, SparseCore 0:
  284.2 92.0 reduce-scatter.1
  384.5 86.8 all-gather.1

commit v7 on v6

--- a/solution.py
+++ b/solution.py
@@ -445,6 +445,9 @@
             to_right, to_left = [to_right[0][:half]], [to_left[0][half:]]
         return self.send(to_right, to_left)
 
+    def came(self):
+        return self.from_left + self.from_right
+
     def see(self, items, k):
         self.seen.append((items[0], (k, 0)))
 
@@ -486,6 +489,8 @@
 
 
 class WholeSum:
+    came = staticmethod(lambda: ())
+
     def __init__(self, arrays, parts):
         self.arrays, self.parts, self.steps, self.done = list(arrays), parts, 1, 0
 
@@ -531,6 +536,9 @@
         else:
             self.items = [row_sum([item], [part]) for item, part in zip(arrays, parts)]
 
+    def came(self):
+        return [item.came() for item in self.items]
+
     @property
     def done(self):
         return self.items[0].done
@@ -551,13 +559,14 @@
         return [out for item in self.items for out in item.finish(gate)]
 
 
-def sum_cube(values, axis):
+def sum_cube(values, axis, late=()):
     size = lax.axis_size(axis)
     if size & (size - 1):
         return lax.psum(values, axis)
     distance = 1
     while distance < size:
         values = values + lax.ppermute(values, axis, [(i, i ^ distance) for i in range(size)])
+        values = after(values, late)
         distance *= 2
     return values
 
@@ -579,7 +588,7 @@
 
 def ffn_forward(values, gain, weight_up, weight_down):
     normed, unit, inverse = normalize(values, gain)
-    near, far = halves(gather(normed.astype(B16)))
+    near, far = halves(gather(normed.astype(B16), True))
     pre, act = [], []
     for half in (near, far):
         pre.append(dot(after(half, act), weight_up))
@@ -589,10 +598,10 @@
     return (values + 0.5 * total, (unit, inverse, (near, far), pre, act), sent)
 
 
-def ffn_backward(grad, kept, gain, weight_up, weight_down, use=None, fill=None):
+def ffn_backward(grad, kept, gain, weight_up, weight_down, use=None):
     unit, inverse, wide, pre, act = kept
     own = (0.5 * grad).astype(B16)
-    cot = halves(gather(own) if fill is None else gather(own, True, fill(own)))
+    cot = halves(gather(own, True))
     d_pre = []
     for half in (0, 1):
         d_act = dot(after(cot[half], d_pre), weight_down, (1, 1))
@@ -630,10 +639,11 @@
     q_at, k_at, reorder = places(slots)
     where = (spans, q_at, k_at)
     normed, unit, inverse = normalize(values, gain)
-    near, far = halves(gather(normed.astype(B16)))
+    slots_in = gather(normed.astype(B16), True, (rel, spans))
+    near, far = halves(slots_in)
     mixed = [dot(near, weights)]
-    far = after(far, rel, spans, mixed)
-    fetched, arrived = prefetch(far)
+    far = after(far, mixed)
+    fetched, came = prefetch(slots_in[len(slots_in) // 2])
     mixed.append(dot(far, weights))
     flat = lambda bias: bias.astype(F32).reshape(1, width)
     join = lambda items: jnp.concatenate(items, 0)
@@ -649,7 +659,7 @@
         + (code.reshape(slots, 1), code.reshape(slots // TK, 1, TK))
     )
     heads_out, heads_wide, sums = attend(*operands)
-    sent = after(to_true(heads_out) if reorder else heads_out, arrived)
+    sent = after(to_true(heads_out) if reorder else heads_out, came)
     half = slots // 2
     total, _ = scatter(pieces(sent[:half], sent[half:], attend_out, (1, 0)))
     kept = (unit, inverse, (near, far), operands, heads_wide, sums, sent)
@@ -851,11 +861,11 @@
     middle = held["middle"]
     second_sum = end_sum(held["second"])
     grad, sum_first, first_grads, marks = ffn_backward(
-        grad, kept_first, gain_first, up_first, down_first, None, middle.step
+        grad, kept_first, gain_first, up_first, down_first
     )
     first = RowSums(first_grads, [(item.shape[1], plain) for item in first_grads])
     token = middle.step(marks[1])
-    token = first.step(token)
+    token = middle.step(first.step(token))
     second_sum = after(second_sum, token)
     token = second_sum
     while middle.done < middle.steps:
@@ -868,13 +878,14 @@
             second_up, second_down = split_sum(after(second_sum, token), up_second.shape[0])
             token = (token, second_up, second_down)
     while first.left:
-        token = first.step(token)
+        gate = (token, middle.came()) if first.left == 1 else token
+        token = first.step(gate)
     pairs = (sum_first, sum_attend, sum_conv, sum_second, sum_final)
     gains = sum_cube(gain_sums(pairs, marks[1]), "tp")
     small = jnp.concatenate([conv_grads[1](marks[1]), d_bias], 0)
     small_shape = small.shape
     pack = jnp.concatenate([gains.reshape(-1), small.reshape(-1)]).reshape(-1, width)
-    pack = sum_cube(after(pack, token), "rows")
+    pack = sum_cube(after(pack, token), "rows", first.came())
     attend_sum = middle.finish(token)
     first_sum = first.finish(attend_sum)
     pack = pack.reshape(-1)

time: 693 us -> 727 us (1.049)
  local copies, waits for them, and re-layouts: 52.2 us -> 65.1 us
  matrix products: 109 us -> 119 us
    unnamed x336 -> x404, local copies, waits for them, and re-layouts: 28.5 us -> 44.3 us
    dot_general x53, matrix products: 109 us -> 119 us  [dot(): lax.dot_general(left, right, (((contract[0],), (contract[1],)), ((), ()))...]
  transfers between devices with their start and end apart: 97 -> 97, of which waited for: 47 -> 42; matrix products, arithmetic and copies ran while one was open for 28% -> 28% of each run, Pallas kernels for 12% -> 12%
where the time goes in v7:
time: 727 us; the launch traced here: 718 us
  waiting for transfers between devices  246 us (34%)
  matrix products  119 us (16%)
  starting transfers between devices  99.1 us (14%)
  Pallas kernels  87.1 us (12%)
  other arithmetic  85.4 us (12%)
  local copies, waits for them, and re-layouts  65.1 us (9%)
  between operations  17 us (2%)
    ppermute x54, waiting for transfers between devices, swap(): return lax.ppermute(values, 'tp', [(i, i ^ distance) for i in range(size)])  150 us
    dot_general x53, matrix products, dot(): lax.dot_general(left, right, (((contract[0],), (contract[1],)), ((), ()))...  119 us
    ppermute x32, waiting for transfers between devices, send(): lax.ppermute(item, 'rows', way)  75.9 us
    ppermute x32, starting transfers between devices, send(): lax.ppermute(item, 'rows', way)  45.7 us
    unnamed x404, local copies, waits for them, and re-layouts  44.3 us
    ppermute x54, starting transfers between devices, swap(): return lax.ppermute(values, 'tp', [(i, i ^ distance) for i in range(size)])  39.7 us
    pallas_call x10, Pallas kernels, call(): pl.pallas_call(kernel, grid_spec=pltpu.PrefetchScalarGridSpec(num_scalar_...  30.1 us
    pallas_call x1, Pallas kernels, attend_back(): pl.pallas_call(functools.partial(attend_back_kernel, heads), out_shape=(s...  28.8 us
  transfers between devices with their start and end apart: 97, of which 42 were waited for; matrix products, arithmetic and copies ran while one was open for 28% of the time, Pallas kernels for 12%

profile of v7, /device:TPU:0, one launch (start us, length us, event | category | flops | bytes accessed | tf_op | source)
XLA Modules:
  0.0 718.4 jit_solution(15729369559110948315)
XLA Ops:
  54.6 16.6 %collective-permute-done.5 = bf16[384,1024]{1,0:T(8,128)(2,1)S(1)} collective-permute-done((bf16[384,1024]{1,0:T(8,128)(2,1)S(1)}, bf16[384,1024]{1,0:T(8,128)(2,1)S(1)}, u32[]{:S(2)}, u32[]{:S(2)}) %collective-permute-start.5) | collective-permute-done | bytes 786464 | tf_op jit(solution)/shard_map/ppermute | solution.py:237
  78.9 13.3 %collective-permute-done.7 = bf16[384,1024]{1,0:T(8,128)(2,1)S(1)} collective-permute-done((bf16[384,1024]{1,0:T(8,128)(2,1)S(1)}, bf16[384,1024]{1,0:T(8,128)(2,1)S(1)}, u32[]{:S(2)}, u32[]{:S(2)}) %collective-permute-start.7) | collective-permute-done | bytes 786464 | tf_op jit(solution)/shard_map/ppermute | solution.py:237
  112.6 12.8 %shard_map.401 = (bf16[1536,256]{1,0:T(8,128)(2,1)S(1)}, f32[1536,256]{1,0:T(8,128)S(1)}, f32[1536,2]{1,0:T(8,128)S(1)}) custom-call(s32[2,12]{1,0:T(2,128)S(1)} %pad_add_fusion.spans, s32[12]{0:T(128)S(1)} %fusion.201.q_at, s32[4]{0:T(128)S(1)} %fusion.202.k_at, bf16[1536,256]{1,0:T(8,128)(2,1)S(1)} %get-tuple-element.486.qc_ref, ...), custom_call_target="tpu_custom_call" | custom-call | flops 4000000000 | bytes 9000000 | tf_op jit(solution)/shard_map/pallas_call | solution.py:154
  125.5 7.1 collective-permute-done.11
  145.5 15.1 %collective-permute-done.14 = bf16[384,1024]{1,0:T(8,128)(2,1)S(1)} collective-permute-done((bf16[384,1024]{1,0:T(8,128)(2,1)S(1)}, bf16[384,1024]{1,0:T(8,128)(2,1)S(1)}, u32[]{:S(2)}, u32[]{:S(2)}) %collective-permute-start.14) | collective-permute-done | bytes 786464 | tf_op jit(solution)/shard_map/ppermute | solution.py:237
  181.6 17.2 %collective-permute-done.28 = bf16[384,1024]{1,0:T(8,128)(2,1)S(1)} collective-permute-done((bf16[384,1024]{1,0:T(8,128)(2,1)S(1)}, bf16[384,1024]{1,0:T(8,128)(2,1)S(1)}, u32[]{:S(2)}, u32[]{:S(2)}) %collective-permute-start.28) | collective-permute-done | bytes 786464 | tf_op jit(solution)/shard_map/ppermute | solution.py:237
  216.8 16.9 %collective-permute-done.31 = bf16[384,1024]{1,0:T(8,128)(2,1)S(1)} collective-permute-done((bf16[384,1024]{1,0:T(8,128)(2,1)S(1)}, bf16[384,1024]{1,0:T(8,128)(2,1)S(1)}, u32[]{:S(2)}, u32[]{:S(2)}) %collective-permute-start.31) | collective-permute-done | bytes 786464 | tf_op jit(solution)/shard_map/ppermute | solution.py:237
  239.7 17.3 %collective-permute-done.34 = bf16[384,1024]{1,0:T(8,128)(2,1)S(1)} collective-permute-done((bf16[384,1024]{1,0:T(8,128)(2,1)S(1)}, bf16[384,1024]{1,0:T(8,128)(2,1)S(1)}, u32[]{:S(2)}, u32[]{:S(2)}) %collective-permute-start.34) | collective-permute-done | bytes 786464 | tf_op jit(solution)/shard_map/ppermute | solution.py:237
  282.3 9.7 %collective-permute-done.37 = bf16[384,1024]{1,0:T(8,128)(2,1)S(1)} collective-permute-done((bf16[384,1024]{1,0:T(8,128)(2,1)S(1)}, bf16[384,1024]{1,0:T(8,128)(2,1)S(1)}, u32[]{:S(2)}, u32[]{:S(2)}) %collective-permute-start.37) | collective-permute-done | bytes 786464 | tf_op jit(solution)/shard_map/ppermute | solution.py:237
  334.1 8.1 %collective-permute-done.41 = bf16[384,1024]{1,0:T(8,128)(2,1)S(1)} collective-permute-done((bf16[384,1024]{1,0:T(8,128)(2,1)S(1)}, bf16[384,1024]{1,0:T(8,128)(2,1)S(1)}, u32[]{:S(2)}, u32[]{:S(2)}) %collective-permute-start.41) | collective-permute-done | bytes 786464 | tf_op jit(solution)/shard_map/ppermute | solution.py:237
  358.8 28.8 %shard_map.405 = (bf16[1536,768]{1,0:T(8,128)(2,1)}, bf16[3072,256]{1,0:T(8,128)(2,1)}, f32[8,256]{1,0:T(8,128)S(1)}) custom-call(s32[2,12]{1,0:T(2,128)S(1)} %pad_add_fusion.spans, s32[12]{0:T(128)S(1)} %fusion.201.q_at, s32[4]{0:T(128)S(1)} %fusion.202.k_at, bf16[1536,256]{1,0:T(8,128)(2,1)S(1)} %copy-done.7, bf16[1536,256]{1,0:T(8,128)(2,1)S(1)} %copy-done.9, ...), custom_call_target="tpu_custom_call" | custom-call | flops 1000000 | bytes 1000000 | tf_op jit(solution)/shard_map/pallas_call | solution.py:165
  387.6 9.3 %reduce-scatter.2.cloned.1.call-done = bf16[256,1024]{1,0:T(8,128)(2,1)} async-done(((bf16[2048,1024]{1,0:T(8,128)(2,1)}), bf16[256,1024]{1,0:T(8,128)(2,1)}) %reduce-scatter.2.cloned.1.call-update) | async-done | bytes 524304 | tf_op jit(solution)/shard_map/reduce_scatter | solution.py:519
  439.9 17.5 %collective-permute-done.51 = bf16[384,1024]{1,0:T(8,128)(2,1)S(1)} collective-permute-done((bf16[384,1024]{1,0:T(8,128)(2,1)S(1)}, bf16[384,1024]{1,0:T(8,128)(2,1)S(1)}, u32[]{:S(2)}, u32[]{:S(2)}) %collective-permute-start.51) | collective-permute-done | bytes 786464 | tf_op jit(solution)/shard_map/ppermute | solution.py:237
  472.8 14.2 %collective-permute-start.60 = (bf16[64,2048]{1,0:T(8,128)(2,1)}, bf16[64,2048]{1,0:T(8,128)(2,1)S(1)}, u32[]{:S(2)}, u32[]{:S(2)}) collective-permute-start(bf16[64,2048]{1,0:T(8,128)(2,1)} %get-tuple-element.228), channel_id=1, source_target_pairs={{0,8},{8,16},{16,24},{24,28},{28,20},{20,12},{12,4},{4,0},{1,9},{9... | collective-permute-start | bytes 786440 | tf_op jit(solution)/shard_map/ppermute | solution.py:404
  501.3 7.8 %fusion.81.refs_0_.refs_2_ = bf16[1024,1024]{1,0:T(8,128)(2,1)} fusion(bf16[768,1024]{1,0:T(8,128)(2,1)} %copy-done.184, bf16[768,1024]{1,0:T(8,128)(2,1)} %fusion.20, bf16[384,1024]{1,0:T(8,128)(2,1)S(1)} %copy-done.65, bf16[384,1024]{1,0:T(8,128)(2,1)} %collective-permute-done.2, bf16[384,1024]{1,0:T(8,128)(2,1)} %collective-permute-done, ...), kind=kOutput, calls=%fused_computation.103 | convolution fusion | flops 3241148416 | bytes 8388608 | tf_op jit(solution)/shard_map/dot_general | solution.py:230
  538.8 9.9 %collective-permute-done.67.refs_9_ = bf16[128,2048]{1,0:T(8,128)(2,1)} collective-permute-done((bf16[128,2048]{1,0:T(8,128)(2,1)}, bf16[128,2048]{1,0:T(8,128)(2,1)}, u32[]{:S(2)}, u32[]{:S(2)}) %collective-permute-start.67) | collective-permute-done | bytes 524320 | tf_op jit(solution)/shard_map/ppermute | solution.py:404
  572.7 5.6 collective-permute-done.68.refs_4_
  592.2 8.6 %collective-permute-done.72.refs_4_ = bf16[128,2048]{1,0:T(8,128)(2,1)S(1)} collective-permute-done((bf16[128,2048]{1,0:T(8,128)(2,1)}, bf16[128,2048]{1,0:T(8,128)(2,1)S(1)}, u32[]{:S(2)}, u32[]{:S(2)}) %collective-permute-start.72) | collective-permute-done | bytes 524320 | tf_op jit(solution)/shard_map/ppermute | solution.py:404
  614.6 8.7 %collective-permute-done.76.refs_2_ = bf16[128,2048]{1,0:T(8,128)(2,1)} collective-permute-done((bf16[128,2048]{1,0:T(8,128)(2,1)}, bf16[128,2048]{1,0:T(8,128)(2,1)}, u32[]{:S(2)}, u32[]{:S(2)}) %collective-permute-start.76) | collective-permute-done | bytes 524320 | tf_op jit(solution)/shard_map/ppermute | solution.py:404
  628.8 6.8 slice_convert_fusion
  636.9 5.9 collective-permute-done.80.refs_1_
  647.5 10.5 %collective-permute-done.84.refs_3_ = bf16[128,2048]{1,0:T(8,128)(2,1)} collective-permute-done((bf16[128,2048]{1,0:T(8,128)(2,1)S(1)}, bf16[128,2048]{1,0:T(8,128)(2,1)}, u32[]{:S(2)}, u32[]{:S(2)}) %collective-permute-start.84) | collective-permute-done | bytes 524320 | tf_op jit(solution)/shard_map/ppermute | solution.py:404
  688.0 9.2 %shard_map.417 = (f32[1024,256]{1,0:T(8,128)}, f32[1024,256]{1,0:T(8,128)}, f32[1024,256]{1,0:T(8,128)}, f32[1024,256]{1,0:T(8,128)}, f32[256,1024]{1,0:T(8,128)...) custom-call(s32[1]{0:T(128)} %bitcast.42.at, bf16[128,2048]{1,0:T(8,128)(2,1)} %shard_map.413.refs_0_, ...), custom_call_target="tpu_custom_call" | custom-call | flops 12582912 | bytes 12582912 | tf_op jit(solution)/shard_map/pallas_call | solution.py:476
  700.7 6.2 shard_map.418
  (812 shorter events, 418.6 us)
Async XLA Ops:
  7.2 389.6 %reduce-scatter.2.cloned.1.call-start = ((), (), s32[]{:S(2)}) async-start(), calls=%async_computation.1 | async-start | bytes 4718592 | tf_op jit(solution)/shard_map/reduce_scatter | solution.py:519
  12.1 21.6 %collective-permute-start = (bf16[384,1024]{1,0:T(8,128)(2,1)}, bf16[384,1024]{1,0:T(8,128)(2,1)}, u32[]{:S(2)}, u32[]{:S(2)}) collective-permute-start(bf16[384,1024]{1,0:T(8,128)(2,1)} %get-tuple-element.425), channel_id=1, source_target_pairs={{0,1},{1,0},{2,3},{3,2},{4,5},{5,4},{6,7},{7,6},{8,9},{9,8},{10,11... | collective-permute-start | bytes 2359304 | tf_op jit(solution)/shard_map/ppermute | solution.py:237
  15.2 60.0 %collective-permute-start.16 = (bf16[6,256]{1,0:T(8,128)(2,1)S(1)}, bf16[6,256]{1,0:T(8,128)(2,1)S(1)}, u32[]{:S(2)}, u32[]{:S(2)}) collective-permute-start(bf16[6,256]{1,0:T(8,128)(2,1)S(1)} %pad_maximum_fusion.27), channel_id=1, source_target_pairs={{0,2},{1,3},{2,0},{3,1},{4,6},{5,7},{6,4},{7,5},{8,10},{9,11},{10,... | collective-permute-start | bytes 9224 | tf_op jit(solution)/shard_map/ppermute | solution.py:237
  15.3 60.1 %collective-permute-start.15 = (bf16[6,256]{1,0:T(8,128)(2,1)S(1)}, bf16[6,256]{1,0:T(8,128)(2,1)S(1)}, u32[]{:S(2)}, u32[]{:S(2)}) collective-permute-start(bf16[6,256]{1,0:T(8,128)(2,1)S(1)} %pad_maximum_fusion.27), channel_id=1, source_target_pairs={{0,1},{1,0},{2,3},{3,2},{4,5},{5,4},{6,7},{7,6},{8,9},{9,8},{10,11... | collective-permute-start | bytes 9224 | tf_op jit(solution)/shard_map/ppermute | solution.py:237
  76.6 23.2 %collective-permute-start.6 = (bf16[384,1024]{1,0:T(8,128)(2,1)S(1)}, bf16[384,1024]{1,0:T(8,128)(2,1)S(1)}, u32[]{:S(2)}, u32[]{:S(2)}) collective-permute-start(bf16[384,1024]{1,0:T(8,128)(2,1)S(1)} %get-tuple-element.394), channel_id=1, source_target_pairs={{0,1},{1,0},{2,3},{3,2},{4,5},{5,4},{6,7},{7,6},{8,9},{9,8},{10,11... | collective-permute-start | bytes 2359304 | tf_op jit(solution)/shard_map/ppermute | solution.py:237
  95.4 40.7 %collective-permute-start.20 = (bf16[1024,256]{1,0:T(8,128)(2,1)}, bf16[1024,256]{1,0:T(8,128)(2,1)}, u32[]{:S(2)}, u32[]{:S(2)}) collective-permute-start(bf16[1024,256]{1,0:T(8,128)(2,1)} %get-tuple-element.194), channel_id=1, source_target_pairs={{0,1},{1,0},{2,3},{3,2},{4,5},{5,4},{6,7},{7,6},{8,9},{9,8},{10,11... | collective-permute-start | bytes 1572872 | tf_op jit(solution)/shard_map/ppermute | solution.py:237
  95.9 29.6 %collective-permute-start.9 = (bf16[1024,256]{1,0:T(8,128)(2,1)}, bf16[1024,256]{1,0:T(8,128)(2,1)}, u32[]{:S(2)}, u32[]{:S(2)}) collective-permute-start(bf16[1024,256]{1,0:T(8,128)(2,1)} %get-tuple-element.194), channel_id=1, source_target_pairs={{0,2},{1,3},{2,0},{3,1},{4,6},{5,7},{6,4},{7,5},{8,10},{9,11},{10,... | collective-permute-start | bytes 1572872 | tf_op jit(solution)/shard_map/ppermute | solution.py:237
  97.6 27.9 %collective-permute-start.10 = (bf16[1024,256]{1,0:T(8,128)(2,1)}, bf16[1024,256]{1,0:T(8,128)(2,1)}, u32[]{:S(2)}, u32[]{:S(2)}) collective-permute-start(bf16[1024,256]{1,0:T(8,128)(2,1)} %get-tuple-element.195), channel_id=1, source_target_pairs={{0,2},{1,3},{2,0},{3,1},{4,6},{5,7},{6,4},{7,5},{8,10},{9,11},{10,... | collective-permute-start | bytes 1572872 | tf_op jit(solution)/shard_map/ppermute | solution.py:237
  99.8 38.8 %collective-permute-start.22 = (bf16[1024,256]{1,0:T(8,128)(2,1)}, bf16[1024,256]{1,0:T(8,128)(2,1)}, u32[]{:S(2)}, u32[]{:S(2)}) collective-permute-start(bf16[1024,256]{1,0:T(8,128)(2,1)} %get-tuple-element.195), channel_id=1, source_target_pairs={{0,1},{1,0},{2,3},{3,2},{4,5},{5,4},{6,7},{7,6},{8,9},{9,8},{10,11... | collective-permute-start | bytes 1572872 | tf_op jit(solution)/shard_map/ppermute | solution.py:237
  103.4 29.2 %collective-permute-start.11 = (bf16[256,1024]{1,0:T(8,128)(2,1)}, bf16[256,1024]{1,0:T(8,128)(2,1)}, u32[]{:S(2)}, u32[]{:S(2)}) collective-permute-start(bf16[256,1024]{1,0:T(8,128)(2,1)} %param.43), channel_id=1, source_target_pairs={{0,2},{1,3},{2,0},{3,1},{4,6},{5,7},{6,4},{7,5},{8,10},{9,11},{10,... | collective-permute-start | bytes 1572872 | tf_op jit(solution)/shard_map/ppermute | solution.py:237
  143.7 22.1 %collective-permute-start.25 = (bf16[256,1024]{1,0:T(8,128)(2,1)}, bf16[256,1024]{1,0:T(8,128)(2,1)S(1)}, u32[]{:S(2)}, u32[]{:S(2)}) collective-permute-start(bf16[256,1024]{1,0:T(8,128)(2,1)} %collective-permute-done.11), channel_id=1, source_target_pairs={{0,1},{1,0},{2,3},{3,2},{4,5},{5,4},{6,7},{7,6},{8,9},{9,8},{10,11... | collective-permute-start | bytes 1572872 | tf_op jit(solution)/shard_map/ppermute | solution.py:237
  303.1 235.8 %all-gather.2.cloned.1.call-start = ((), (), s32[]{:S(2)}) async-start(), calls=%async_computation.2 | async-start | bytes 4718592 | tf_op jit(solution)/shard_map/all_gather | solution.py:523
  349.6 38.0 %collective-permute-start.44 = (bf16[1024,768]{1,0:T(8,128)(2,1)}, bf16[1024,768]{1,0:T(8,128)(2,1)}, u32[]{:S(2)}, u32[]{:S(2)}) collective-permute-start(bf16[1024,768]{1,0:T(8,128)(2,1)} %add_convert_fusion.2), channel_id=1, source_target_pairs={{0,2},{1,3},{2,0},{3,1},{4,6},{5,7},{6,4},{7,5},{8,10},{9,11},{10,... | collective-permute-start | bytes 4718600 | tf_op jit(solution)/shard_map/ppermute | solution.py:237
  352.6 47.2 %collective-permute-start.48 = (bf16[1024,768]{1,0:T(8,128)(2,1)}, bf16[1024,768]{1,0:T(8,128)(2,1)}, u32[]{:S(2)}, u32[]{:S(2)}) collective-permute-start(bf16[1024,768]{1,0:T(8,128)(2,1)} %pad_maximum_fusion.11), channel_id=1, source_target_pairs={{0,1},{1,0},{2,3},{3,2},{4,5},{5,4},{6,7},{7,6},{8,9},{9,8},{10,11... | collective-permute-start | bytes 4718600 | tf_op jit(solution)/shard_map/ppermute | solution.py:237
  404.4 24.0 %collective-permute-start.45 = (bf16[384,1024]{1,0:T(8,128)(2,1)}, bf16[384,1024]{1,0:T(8,128)(2,1)}, u32[]{:S(2)}, u32[]{:S(2)}) collective-permute-start(bf16[384,1024]{1,0:T(8,128)(2,1)} %convolution_convert_fusion.5), channel_id=1, source_target_pairs={{0,1},{1,0},{2,3},{3,2},{4,5},{5,4},{6,7},{7,6},{8,9},{9,8},{10,11... | collective-permute-start | bytes 2359304 | tf_op jit(solution)/shard_map/ppermute | solution.py:237
  525.9 31.8 %collective-permute-start.50 = (bf16[384,1024]{1,0:T(8,128)(2,1)}, bf16[384,1024]{1,0:T(8,128)(2,1)}, u32[]{:S(2)}, u32[]{:S(2)}) collective-permute-start(bf16[384,1024]{1,0:T(8,128)(2,1)} %convolution_convert_fusion.9), channel_id=1, source_target_pairs={{0,1},{1,0},{2,3},{3,2},{4,5},{5,4},{6,7},{7,6},{8,9},{9,8},{10,11... | collective-permute-start | bytes 2359304 | tf_op jit(solution)/shard_map/ppermute | solution.py:237
  525.9 33.3 %collective-permute-start.54 = (bf16[384,1024]{1,0:T(8,128)(2,1)}, bf16[384,1024]{1,0:T(8,128)(2,1)}, u32[]{:S(2)}, u32[]{:S(2)}) collective-permute-start(bf16[384,1024]{1,0:T(8,128)(2,1)} %add_convert_fusion.3), channel_id=1, source_target_pairs={{0,2},{1,3},{2,0},{3,1},{4,6},{5,7},{6,4},{7,5},{8,10},{9,11},{10,... | collective-permute-start | bytes 2359304 | tf_op jit(solution)/shard_map/ppermute | solution.py:237
  527.7 24.7 %collective-permute-start.62 = (bf16[64,2048]{1,0:T(8,128)(2,1)}, bf16[64,2048]{1,0:T(8,128)(2,1)S(1)}, u32[]{:S(2)}, u32[]{:S(2)}) collective-permute-start(bf16[64,2048]{1,0:T(8,128)(2,1)} %get-tuple-element.259), channel_id=1, source_target_pairs={{0,8},{8,16},{16,24},{24,28},{28,20},{20,12},{12,4},{4,0},{1,9},{9... | collective-permute-start | bytes 786440 | tf_op jit(solution)/shard_map/ppermute | solution.py:404
  529.0 25.1 %collective-permute-start.63 = (bf16[64,2048]{1,0:T(8,128)(2,1)}, bf16[64,2048]{1,0:T(8,128)(2,1)}, u32[]{:S(2)}, u32[]{:S(2)}) collective-permute-start(bf16[64,2048]{1,0:T(8,128)(2,1)} %get-tuple-element.260), channel_id=1, source_target_pairs={{8,0},{16,8},{24,16},{28,24},{20,28},{12,20},{4,12},{0,4},{9,1},{1... | collective-permute-start | bytes 786440 | tf_op jit(solution)/shard_map/ppermute | solution.py:404
  590.1 21.9 %collective-permute-start.78 = (bf16[128,2048]{1,0:T(8,128)(2,1)}, bf16[128,2048]{1,0:T(8,128)(2,1)}, u32[]{:S(2)}, u32[]{:S(2)}) collective-permute-start(bf16[128,2048]{1,0:T(8,128)(2,1)} %collective-permute-done.74.refs_1_), channel_id=1, source_target_pairs={{0,8},{8,16},{16,24},{24,28},{28,20},{20,12},{12,4},{4,0},{1,9},{9... | collective-permute-start | bytes 1572872 | tf_op jit(solution)/shard_map/ppermute | solution.py:404
  590.5 22.1 %collective-permute-start.79 = (bf16[128,2048]{1,0:T(8,128)(2,1)}, bf16[128,2048]{1,0:T(8,128)(2,1)}, u32[]{:S(2)}, u32[]{:S(2)}) collective-permute-start(bf16[128,2048]{1,0:T(8,128)(2,1)} %collective-permute-done.75.refs_2_), channel_id=1, source_target_pairs={{8,0},{16,8},{24,16},{28,24},{20,28},{12,20},{4,12},{0,4},{9,1},{1... | collective-permute-start | bytes 1572872 | tf_op jit(solution)/shard_map/ppermute | solution.py:404
  612.6 23.0 %collective-permute-start.82 = (bf16[128,2048]{1,0:T(8,128)(2,1)}, bf16[128,2048]{1,0:T(8,128)(2,1)S(1)}, u32[]{:S(2)}, u32[]{:S(2)}) collective-permute-start(bf16[128,2048]{1,0:T(8,128)(2,1)} %collective-permute-done.78.refs_3_), channel_id=1, source_target_pairs={{0,8},{8,16},{16,24},{24,28},{28,20},{20,12},{12,4},{4,0},{1,9},{9... | collective-permute-start | bytes 1572872 | tf_op jit(solution)/shard_map/ppermute | solution.py:404
  613.0 23.1 %collective-permute-start.83 = (bf16[128,2048]{1,0:T(8,128)(2,1)}, bf16[128,2048]{1,0:T(8,128)(2,1)S(1)}, u32[]{:S(2)}, u32[]{:S(2)}) collective-permute-start(bf16[128,2048]{1,0:T(8,128)(2,1)} %collective-permute-done.79.refs_4_), channel_id=1, source_target_pairs={{8,0},{16,8},{24,16},{28,24},{20,28},{12,20},{4,12},{0,4},{9,1},{1... | collective-permute-start | bytes 1572872 | tf_op jit(solution)/shard_map/ppermute | solution.py:404
  635.6 37.6 %collective-permute-start.57 = (bf16[6,256]{1,0:T(8,128)(2,1)S(1)}, bf16[6,256]{1,0:T(8,128)(2,1)S(1)}, u32[]{:S(2)}, u32[]{:S(2)}) collective-permute-start(bf16[6,256]{1,0:T(8,128)(2,1)S(1)} %get-tuple-element.444), channel_id=1, source_target_pairs={{0,1},{1,0},{2,3},{3,2},{4,5},{5,4},{6,7},{7,6},{8,9},{9,8},{10,11... | collective-permute-start | bytes 9224 | tf_op jit(solution)/shard_map/ppermute | solution.py:237
  (266 other events, 2357.0 us)
Sparse Core Ops, SparseCore 0:
  303.2 93.6 reduce-scatter.1
  405.1 84.0 all-gather.1

commit v8 on v6

--- a/solution.py
+++ b/solution.py
@@ -12,7 +12,7 @@
 NEG = -1e30
 F32 = jnp.float32
 B16 = jnp.bfloat16
-TQ = 128
+TQ = 384
 TK = 384
 HD = 128
 STEP = 64
@@ -98,8 +98,10 @@
         cols = [slice(h * HD, (h + 1) * HD) for h in range(heads)]
         qc = [qc_ref[pl.ds(at, TQ), c] for c in cols]
         qp = [qp_ref[pl.ds(at, TQ), c] for c in cols]
-        qp_flipped = [dotx(flip_low, item, 1, 0).astype(B16) for item in qp]
+        qp_turned = [dotx(item, flip_low, 0, 0).astype(B16) for item in qp]
         d_out = [d_out_ref[pl.ds(at, TQ), c] for c in cols]
+        qc_turned = [item.T for item in qc]
+        d_out_turned = [item.T for item in d_out]
         lse = [lse_ref[pl.ds(at, TQ), h:h + 1] for h in range(heads)]
         delta = [jnp.sum(d_out[h].astype(F32) * wide_ref[pl.ds(at, TQ), cols[h]], axis=1, keepdims=True)
                  for h in range(heads)]
@@ -121,9 +123,9 @@
                 d_raw = probs * (d_probs - delta[h]) * scale
                 d_low = d_raw.astype(B16)
                 d_grid = unskew_flipped(dotx(flip_low, d_low, 1, 0)).astype(B16)
-                dv_acc[pl.ds(ko, TK), lanes] += dotx(probs.astype(B16), d_out[h], 0, 0)
-                dk_acc[pl.ds(ko, TK), lanes] += dotx(d_low, qc[h], 0, 0)
-                drel_acc[pl.ds(to, TK + TQ), lanes] += dotx(d_grid, qp_flipped[h], 0, 0)
+                dv_acc[lanes, pl.ds(ko, TK)] += dotx(d_out_turned[h], probs.astype(B16), 1, 0)
+                dk_acc[lanes, pl.ds(ko, TK)] += dotx(qc_turned[h], d_low, 1, 0)
+                drel_acc[lanes, pl.ds(to, TK + TQ)] += dotx(qp_turned[h], d_grid, 1, 0)
                 d_content = d_content + dotx(d_low, key, 1, 0)
                 d_position = d_position + dotx(d_grid, window, 1, 0)
                 new.append((d_content, d_position))
@@ -141,10 +143,10 @@
         return 0
 
     lax.fori_loop(0, blocks, q_step, 0)
-    width = dk_acc.shape[1]
-    all_ref[:, width : 2 * width] = dk_acc[...].astype(B16)
-    all_ref[:, 2 * width :] = dv_acc[...].astype(B16)
-    drel_ref[...] = drel_acc[...].astype(B16)
+    width = dk_acc.shape[0]
+    all_ref[:, width : 2 * width] = dk_acc[...].astype(B16).T
+    all_ref[:, 2 * width :] = dv_acc[...].astype(B16).T
+    drel_ref[...] = drel_acc[...].astype(B16).T
 
 def sds(s, d): return jax.ShapeDtypeStruct(s, d)
 
@@ -166,7 +168,7 @@
         functools.partial(attend_back_kernel, heads),
         out_shape=(sds((slots, 3 * width), B16), sds((2 * slots, width), B16), sds((8, width), F32)),
         in_specs=[SM] * 3 + [VM] * 10, out_specs=(VM,) * 3,
-        scratch_shapes=[pltpu.VMEM((slots, width), F32), pltpu.VMEM((slots, width), F32), pltpu.VMEM((2 * slots, width), F32)],
+        scratch_shapes=[pltpu.VMEM((width, slots), F32), pltpu.VMEM((width, slots), F32), pltpu.VMEM((width, 2 * slots), F32)],
         compiler_params=pltpu.CompilerParams(vmem_limit_bytes=48 << 20),
         cost_estimate=pl.CostEstimate(flops=int(1e6), bytes_accessed=int(1e6), transcendentals=0),
     )(spans, q_at, k_at, qc, qp, k, v, rel, code_q, code_k, d_out, wide, lse)

time: 693 us -> 682 us (0.984)
  Pallas kernels: 87.2 us -> 76.5 us
    ppermute x54, waiting for transfers between devices: 148 us -> 157 us  [swap(): return lax.ppermute(values, 'tp', [(i, i ^ distance) for i in range(size)])]
    ppermute x32, waiting for transfers between devices: 73.4 us -> 66.4 us  [send(): lax.ppermute(item, 'rows', way)]
    unnamed x336 -> x338, local copies, waits for them, and re-layouts: 28.5 us -> 30.3 us
  transfers between devices with their start and end apart: 97 -> 97, of which waited for: 47 -> 48; matrix products, arithmetic and copies ran while one was open for 28% -> 29% of each run, Pallas kernels for 12% -> 10%
where the time goes in v8:
time: 682 us; the launch traced here: 678 us
  waiting for transfers between devices  243 us (36%)
  matrix products  109 us (16%)
  starting transfers between devices  98.4 us (14%)
  other arithmetic  80.2 us (12%)
  Pallas kernels  76.5 us (11%)
  local copies, waits for them, and re-layouts  54.2 us (8%)
  between operations  16.9 us (2%)
    ppermute x54, waiting for transfers between devices, swap(): return lax.ppermute(values, 'tp', [(i, i ^ distance) for i in range(size)])  157 us
    dot_general x53, matrix products, dot(): lax.dot_general(left, right, (((contract[0],), (contract[1],)), ((), ()))...  109 us
    ppermute x32, waiting for transfers between devices, send(): lax.ppermute(item, 'rows', way)  66.4 us
    ppermute x32, starting transfers between devices, send(): lax.ppermute(item, 'rows', way)  47 us
    ppermute x54, starting transfers between devices, swap(): return lax.ppermute(values, 'tp', [(i, i ^ distance) for i in range(size)])  39.6 us
    unnamed x338, local copies, waits for them, and re-layouts  30.3 us
    pallas_call x10, Pallas kernels, call(): pl.pallas_call(kernel, grid_spec=pltpu.PrefetchScalarGridSpec(num_scalar_...  30.2 us
    pallas_call x1, Pallas kernels, attend_back(): pl.pallas_call(functools.partial(attend_back_kernel, heads), out_shape=(s...  22.2 us
  transfers between devices with their start and end apart: 97, of which 48 were waited for; matrix products, arithmetic and copies ran while one was open for 29% of the time, Pallas kernels for 10%

profile of v8, /device:TPU:0, one launch (start us, length us, event | category | flops | bytes accessed | tf_op | source)
XLA Modules:
  0.0 678.4 jit_solution(834662891642031957)
XLA Ops:
  51.1 16.9 %collective-permute-done.5 = bf16[384,1024]{1,0:T(8,128)(2,1)S(1)} collective-permute-done((bf16[384,1024]{1,0:T(8,128)(2,1)S(1)}, bf16[384,1024]{1,0:T(8,128)(2,1)S(1)}, u32[]{:S(2)}, u32[]{:S(2)}) %collective-permute-start.5) | collective-permute-done | bytes 786464 | tf_op jit(solution)/shard_map/ppermute | solution.py:239
  75.7 13.7 %collective-permute-done.7 = bf16[384,1024]{1,0:T(8,128)(2,1)S(1)} collective-permute-done((bf16[384,1024]{1,0:T(8,128)(2,1)S(1)}, bf16[384,1024]{1,0:T(8,128)(2,1)S(1)}, u32[]{:S(2)}, u32[]{:S(2)}) %collective-permute-start.7) | collective-permute-done | bytes 786464 | tf_op jit(solution)/shard_map/ppermute | solution.py:239
  100.6 8.9 %shard_map.399 = (bf16[1536,256]{1,0:T(8,128)(2,1)S(1)}, f32[1536,256]{1,0:T(8,128)S(1)}, f32[1536,2]{1,0:T(8,128)S(1)}) custom-call(s32[2,4]{1,0:T(2,128)S(1)} %pad_add_fusion.spans, s32[4]{0:T(128)S(1)} %fusion.201.q_at.k_at, s32[4]{0:T(128)S(1)} %fusion.201.q_at.k_at, bf16[1536,256]{1,0:T(8,128)(2,1)S(1)} %get-tuple-element.480.qc_ref, ...), custom_call_target="tpu_custom_call" | custom-call | flops 4000000000 | bytes 9000000 | tf_op jit(solution)/shard_map/pallas_call | solution.py:156
  109.5 10.1 %collective-permute-done.10 = bf16[1024,256]{1,0:T(8,128)(2,1)S(1)} collective-permute-done((bf16[1024,256]{1,0:T(8,128)(2,1)S(1)}, bf16[1024,256]{1,0:T(8,128)(2,1)S(1)}, u32[]{:S(2)}, u32[]{:S(2)}) %collective-permute-start.10) | collective-permute-done | bytes 524320 | tf_op jit(solution)/shard_map/ppermute | solution.py:239
  119.7 10.4 %collective-permute-done.11 = bf16[256,1024]{1,0:T(8,128)(2,1)S(1)} collective-permute-done((bf16[256,1024]{1,0:T(8,128)(2,1)S(1)}, bf16[256,1024]{1,0:T(8,128)(2,1)S(1)}, u32[]{:S(2)}, u32[]{:S(2)}) %collective-permute-start.11) | collective-permute-done | bytes 524320 | tf_op jit(solution)/shard_map/ppermute | solution.py:239
  137.0 17.0 %collective-permute-done.14 = bf16[384,1024]{1,0:T(8,128)(2,1)S(1)} collective-permute-done((bf16[384,1024]{1,0:T(8,128)(2,1)S(1)}, bf16[384,1024]{1,0:T(8,128)(2,1)S(1)}, u32[]{:S(2)}, u32[]{:S(2)}) %collective-permute-start.14) | collective-permute-done | bytes 786464 | tf_op jit(solution)/shard_map/ppermute | solution.py:239
  174.0 17.2 %collective-permute-done.28 = bf16[384,1024]{1,0:T(8,128)(2,1)S(1)} collective-permute-done((bf16[384,1024]{1,0:T(8,128)(2,1)S(1)}, bf16[384,1024]{1,0:T(8,128)(2,1)S(1)}, u32[]{:S(2)}, u32[]{:S(2)}) %collective-permute-start.28) | collective-permute-done | bytes 786464 | tf_op jit(solution)/shard_map/ppermute | solution.py:239
  204.2 16.7 %collective-permute-done.31 = bf16[384,1024]{1,0:T(8,128)(2,1)S(1)} collective-permute-done((bf16[384,1024]{1,0:T(8,128)(2,1)S(1)}, bf16[384,1024]{1,0:T(8,128)(2,1)S(1)}, u32[]{:S(2)}, u32[]{:S(2)}) %collective-permute-start.31) | collective-permute-done | bytes 786464 | tf_op jit(solution)/shard_map/ppermute | solution.py:239
  226.4 17.2 %collective-permute-done.34 = bf16[384,1024]{1,0:T(8,128)(2,1)S(1)} collective-permute-done((bf16[384,1024]{1,0:T(8,128)(2,1)S(1)}, bf16[384,1024]{1,0:T(8,128)(2,1)S(1)}, u32[]{:S(2)}, u32[]{:S(2)}) %collective-permute-start.34) | collective-permute-done | bytes 786464 | tf_op jit(solution)/shard_map/ppermute | solution.py:239
  262.8 10.8 %collective-permute-done.37 = bf16[384,1024]{1,0:T(8,128)(2,1)S(1)} collective-permute-done((bf16[384,1024]{1,0:T(8,128)(2,1)S(1)}, bf16[384,1024]{1,0:T(8,128)(2,1)S(1)}, u32[]{:S(2)}, u32[]{:S(2)}) %collective-permute-start.37) | collective-permute-done | bytes 786464 | tf_op jit(solution)/shard_map/ppermute | solution.py:239
  314.4 8.1 %collective-permute-done.41 = bf16[384,1024]{1,0:T(8,128)(2,1)S(1)} collective-permute-done((bf16[384,1024]{1,0:T(8,128)(2,1)S(1)}, bf16[384,1024]{1,0:T(8,128)(2,1)S(1)}, u32[]{:S(2)}, u32[]{:S(2)}) %collective-permute-start.41) | collective-permute-done | bytes 786464 | tf_op jit(solution)/shard_map/ppermute | solution.py:239
  339.1 22.2 %shard_map.401 = (bf16[1536,768]{1,0:T(8,128)(2,1)}, bf16[3072,256]{1,0:T(8,128)(2,1)}, f32[8,256]{1,0:T(8,128)S(1)}) custom-call(s32[2,4]{1,0:T(2,128)S(1)} %pad_add_fusion.spans, s32[4]{0:T(128)S(1)} %fusion.201.q_at.k_at, s32[4]{0:T(128)S(1)} %fusion.201.q_at.k_at, bf16[1536,256]{1,0:T(8,128)(2,1)S(1)} %copy-done.7, bf16[1536,256]{1,0:T(8,128)(2,1)S(1)} %copy-done.9, ...), custom_call_target="tpu_custom_call" | custom-call | flops 1000000 | bytes 1000000 | tf_op jit(solution)/shard_map/pallas_call | solution.py:167
  366.7 9.2 %reduce-scatter.2.cloned.1.call-done = bf16[256,1024]{1,0:T(8,128)(2,1)} async-done(((bf16[2048,1024]{1,0:T(8,128)(2,1)}), bf16[256,1024]{1,0:T(8,128)(2,1)}) %reduce-scatter.2.cloned.1.call-update) | async-done | bytes 524304 | tf_op jit(solution)/shard_map/reduce_scatter | solution.py:516
  427.0 11.6 %collective-permute-done.53.refs_8_ = bf16[64,2048]{1,0:T(8,128)(2,1)S(1)} collective-permute-done((bf16[64,2048]{1,0:T(8,128)(2,1)}, bf16[64,2048]{1,0:T(8,128)(2,1)S(1)}, u32[]{:S(2)}, u32[]{:S(2)}) %collective-permute-start.53) | collective-permute-done | bytes 262176 | tf_op jit(solution)/shard_map/ppermute | solution.py:406
  464.5 8.5 %collective-permute-start.63 = (bf16[128,2048]{1,0:T(8,128)(2,1)S(1)}, bf16[128,2048]{1,0:T(8,128)(2,1)S(1)}, u32[]{:S(2)}, u32[]{:S(2)}) collective-permute-start(bf16[128,2048]{1,0:T(8,128)(2,1)S(1)} %copy-done.143), channel_id=1, source_target_pairs={{8,0},{16,8},{24,16},{28,24},{20,28},{12,20},{4,12},{0,4},{9,1},{1... | collective-permute-start | bytes 1572872 | tf_op jit(solution)/shard_map/ppermute | solution.py:406
  492.2 7.6 %fusion.81.refs_0_.refs_2_ = bf16[1024,1024]{1,0:T(8,128)(2,1)} fusion(bf16[768,1024]{1,0:T(8,128)(2,1)} %copy-done.151, bf16[768,1024]{1,0:T(8,128)(2,1)} %fusion.20, bf16[384,1024]{1,0:T(8,128)(2,1)} %copy-done.83, bf16[384,1024]{1,0:T(8,128)(2,1)} %collective-permute-done.2, bf16[384,1024]{1,0:T(8,128)(2,1)} %copy-done.82, ...), kind=kOutput, calls=%fused_computation.103 | convolution fusion | flops 3241148416 | bytes 8388608 | tf_op jit(solution)/shard_map/dot_general | solution.py:232
  536.7 5.6 collective-permute-done.68.refs_4_
  555.7 9.0 %collective-permute-done.72.refs_4_ = bf16[128,2048]{1,0:T(8,128)(2,1)S(1)} collective-permute-done((bf16[128,2048]{1,0:T(8,128)(2,1)}, bf16[128,2048]{1,0:T(8,128)(2,1)S(1)}, u32[]{:S(2)}, u32[]{:S(2)}) %collective-permute-start.72) | collective-permute-done | bytes 524320 | tf_op jit(solution)/shard_map/ppermute | solution.py:406
  578.2 9.1 %collective-permute-done.76.refs_2_ = bf16[128,2048]{1,0:T(8,128)(2,1)} collective-permute-done((bf16[128,2048]{1,0:T(8,128)(2,1)}, bf16[128,2048]{1,0:T(8,128)(2,1)}, u32[]{:S(2)}, u32[]{:S(2)}) %collective-permute-start.76) | collective-permute-done | bytes 524320 | tf_op jit(solution)/shard_map/ppermute | solution.py:406
  593.9 6.8 %slice_convert_fusion = (f32[1024,1024]{1,0:T(8,128)}, f32[1024,1024]{1,0:T(8,128)}) fusion(bf16[2048,1024]{1,0:T(8,128)(2,1)} %all-gather.2.cloned.1.call-done), kind=kLoop, calls=%fused_computation.93 | loop fusion | flops 2097152 | bytes 12582912 | tf_op jit(solution)/shard_map/convert_element_type | solution.py:526
  612.1 7.9 %collective-permute-done.84.refs_3_ = bf16[128,2048]{1,0:T(8,128)(2,1)S(1)} collective-permute-done((bf16[128,2048]{1,0:T(8,128)(2,1)S(1)}, bf16[128,2048]{1,0:T(8,128)(2,1)S(1)}, u32[]{:S(2)}, u32[]{:S(2)}) %collective-permute-start.84) | collective-permute-done | bytes 524320 | tf_op jit(solution)/shard_map/ppermute | solution.py:406
  627.9 6.4 collective-permute-done.86.refs_5_
  647.3 9.2 %shard_map.413 = (f32[1024,256]{1,0:T(8,128)}, f32[1024,256]{1,0:T(8,128)}, f32[1024,256]{1,0:T(8,128)}, f32[1024,256]{1,0:T(8,128)}, f32[256,1024]{1,0:T(8,128)...) custom-call(s32[1]{0:T(128)} %bitcast.42.at, bf16[128,2048]{1,0:T(8,128)(2,1)} %shard_map.409.refs_0_, ...), custom_call_target="tpu_custom_call" | custom-call | flops 12582912 | bytes 12582912 | tf_op jit(solution)/shard_map/pallas_call | solution.py:475
  665.0 6.1 shard_map.414
  (743 shorter events, 395.3 us)
Async XLA Ops:
  7.2 368.7 %reduce-scatter.2.cloned.1.call-start = ((), (), s32[]{:S(2)}) async-start(), calls=%async_computation.1 | async-start | bytes 4718592 | tf_op jit(solution)/shard_map/reduce_scatter | solution.py:516
  12.1 21.6 %collective-permute-start = (bf16[384,1024]{1,0:T(8,128)(2,1)}, bf16[384,1024]{1,0:T(8,128)(2,1)S(1)}, u32[]{:S(2)}, u32[]{:S(2)}) collective-permute-start(bf16[384,1024]{1,0:T(8,128)(2,1)} %get-tuple-element.419), channel_id=1, source_target_pairs={{0,1},{1,0},{2,3},{3,2},{4,5},{5,4},{6,7},{7,6},{8,9},{9,8},{10,11... | collective-permute-start | bytes 2359304 | tf_op jit(solution)/shard_map/ppermute | solution.py:239
  15.2 56.8 %collective-permute-start.16 = (bf16[6,256]{1,0:T(8,128)(2,1)S(1)}, bf16[6,256]{1,0:T(8,128)(2,1)S(1)}, u32[]{:S(2)}, u32[]{:S(2)}) collective-permute-start(bf16[6,256]{1,0:T(8,128)(2,1)S(1)} %pad_maximum_fusion.25), channel_id=1, source_target_pairs={{0,2},{1,3},{2,0},{3,1},{4,6},{5,7},{6,4},{7,5},{8,10},{9,11},{10,... | collective-permute-start | bytes 9224 | tf_op jit(solution)/shard_map/ppermute | solution.py:239
  15.3 56.9 %collective-permute-start.15 = (bf16[6,256]{1,0:T(8,128)(2,1)S(1)}, bf16[6,256]{1,0:T(8,128)(2,1)S(1)}, u32[]{:S(2)}, u32[]{:S(2)}) collective-permute-start(bf16[6,256]{1,0:T(8,128)(2,1)S(1)} %pad_maximum_fusion.25), channel_id=1, source_target_pairs={{0,1},{1,0},{2,3},{3,2},{4,5},{5,4},{6,7},{7,6},{8,9},{9,8},{10,11... | collective-permute-start | bytes 9224 | tf_op jit(solution)/shard_map/ppermute | solution.py:239
  93.1 39.1 %collective-permute-start.20 = (bf16[1024,256]{1,0:T(8,128)(2,1)S(1)}, bf16[1024,256]{1,0:T(8,128)(2,1)S(1)}, u32[]{:S(2)}, u32[]{:S(2)}) collective-permute-start(bf16[1024,256]{1,0:T(8,128)(2,1)S(1)} %get-tuple-element.190), channel_id=1, source_target_pairs={{0,1},{1,0},{2,3},{3,2},{4,5},{5,4},{6,7},{7,6},{8,9},{9,8},{10,11... | collective-permute-start | bytes 1572872 | tf_op jit(solution)/shard_map/ppermute | solution.py:239
  96.9 22.8 %collective-permute-start.10 = (bf16[1024,256]{1,0:T(8,128)(2,1)S(1)}, bf16[1024,256]{1,0:T(8,128)(2,1)S(1)}, u32[]{:S(2)}, u32[]{:S(2)}) collective-permute-start(bf16[1024,256]{1,0:T(8,128)(2,1)S(1)} %get-tuple-element.191), channel_id=1, source_target_pairs={{0,2},{1,3},{2,0},{3,1},{4,6},{5,7},{6,4},{7,5},{8,10},{9,11},{10,... | collective-permute-start | bytes 1572872 | tf_op jit(solution)/shard_map/ppermute | solution.py:239
  97.8 32.2 %collective-permute-start.11 = (bf16[256,1024]{1,0:T(8,128)(2,1)S(1)}, bf16[256,1024]{1,0:T(8,128)(2,1)S(1)}, u32[]{:S(2)}, u32[]{:S(2)}) collective-permute-start(bf16[256,1024]{1,0:T(8,128)(2,1)S(1)} %copy-done.101), channel_id=1, source_target_pairs={{0,2},{1,3},{2,0},{3,1},{4,6},{5,7},{6,4},{7,5},{8,10},{9,11},{10,... | collective-permute-start | bytes 1572872 | tf_op jit(solution)/shard_map/ppermute | solution.py:239
  136.0 23.2 %collective-permute-start.25 = (bf16[256,1024]{1,0:T(8,128)(2,1)S(1)}, bf16[256,1024]{1,0:T(8,128)(2,1)S(1)}, u32[]{:S(2)}, u32[]{:S(2)}) collective-permute-start(bf16[256,1024]{1,0:T(8,128)(2,1)S(1)} %collective-permute-done.11), channel_id=1, source_target_pairs={{0,1},{1,0},{2,3},{3,2},{4,5},{5,4},{6,7},{7,6},{8,9},{9,8},{10,11... | collective-permute-start | bytes 1572872 | tf_op jit(solution)/shard_map/ppermute | solution.py:239
  283.7 228.9 %all-gather.2.cloned.1.call-start = ((), (), s32[]{:S(2)}) async-start(), calls=%async_computation.2 | async-start | bytes 4718592 | tf_op jit(solution)/shard_map/all_gather | solution.py:520
  329.9 36.8 %collective-permute-start.44 = (bf16[1024,768]{1,0:T(8,128)(2,1)}, bf16[1024,768]{1,0:T(8,128)(2,1)}, u32[]{:S(2)}, u32[]{:S(2)}) collective-permute-start(bf16[1024,768]{1,0:T(8,128)(2,1)} %add_convert_fusion.2), channel_id=1, source_target_pairs={{0,2},{1,3},{2,0},{3,1},{4,6},{5,7},{6,4},{7,5},{8,10},{9,11},{10,... | collective-permute-start | bytes 4718600 | tf_op jit(solution)/shard_map/ppermute | solution.py:239
  332.9 45.9 %collective-permute-start.48 = (bf16[1024,768]{1,0:T(8,128)(2,1)}, bf16[1024,768]{1,0:T(8,128)(2,1)}, u32[]{:S(2)}, u32[]{:S(2)}) collective-permute-start(bf16[1024,768]{1,0:T(8,128)(2,1)} %pad_maximum_fusion.10), channel_id=1, source_target_pairs={{0,1},{1,0},{2,3},{3,2},{4,5},{5,4},{6,7},{7,6},{8,9},{9,8},{10,11... | collective-permute-start | bytes 4718600 | tf_op jit(solution)/shard_map/ppermute | solution.py:239
  383.5 24.1 %collective-permute-start.45 = (bf16[384,1024]{1,0:T(8,128)(2,1)}, bf16[384,1024]{1,0:T(8,128)(2,1)}, u32[]{:S(2)}, u32[]{:S(2)}) collective-permute-start(bf16[384,1024]{1,0:T(8,128)(2,1)} %convolution_convert_fusion.5), channel_id=1, source_target_pairs={{0,1},{1,0},{2,3},{3,2},{4,5},{5,4},{6,7},{7,6},{8,9},{9,8},{10,11... | collective-permute-start | bytes 2359304 | tf_op jit(solution)/shard_map/ppermute | solution.py:239
  416.7 26.5 %collective-permute-start.49 = (bf16[384,1024]{1,0:T(8,128)(2,1)}, bf16[384,1024]{1,0:T(8,128)(2,1)S(1)}, u32[]{:S(2)}, u32[]{:S(2)}) collective-permute-start(bf16[384,1024]{1,0:T(8,128)(2,1)} %get-tuple-element.367), channel_id=1, source_target_pairs={{0,1},{1,0},{2,3},{3,2},{4,5},{5,4},{6,7},{7,6},{8,9},{9,8},{10,11... | collective-permute-start | bytes 2359304 | tf_op jit(solution)/shard_map/ppermute | solution.py:239
  416.7 27.9 %collective-permute-start.51 = (bf16[384,1024]{1,0:T(8,128)(2,1)}, bf16[384,1024]{1,0:T(8,128)(2,1)S(1)}, u32[]{:S(2)}, u32[]{:S(2)}) collective-permute-start(bf16[384,1024]{1,0:T(8,128)(2,1)} %get-tuple-element.367), channel_id=1, source_target_pairs={{0,2},{1,3},{2,0},{3,1},{4,6},{5,7},{6,4},{7,5},{8,10},{9,11},{10,... | collective-permute-start | bytes 2359304 | tf_op jit(solution)/shard_map/ppermute | solution.py:239
  462.7 22.5 %collective-permute-start.62 = (bf16[128,2048]{1,0:T(8,128)(2,1)S(1)}, bf16[128,2048]{1,0:T(8,128)(2,1)S(1)}, u32[]{:S(2)}, u32[]{:S(2)}) collective-permute-start(bf16[128,2048]{1,0:T(8,128)(2,1)S(1)} %copy-done.144), channel_id=1, source_target_pairs={{0,8},{8,16},{16,24},{24,28},{28,20},{20,12},{12,4},{4,0},{1,9},{9... | collective-permute-start | bytes 1572872 | tf_op jit(solution)/shard_map/ppermute | solution.py:406
  478.3 42.9 %collective-permute-start.50 = (bf16[384,1024]{1,0:T(8,128)(2,1)}, bf16[384,1024]{1,0:T(8,128)(2,1)}, u32[]{:S(2)}, u32[]{:S(2)}) collective-permute-start(bf16[384,1024]{1,0:T(8,128)(2,1)} %convolution_convert_fusion.9), channel_id=1, source_target_pairs={{0,1},{1,0},{2,3},{3,2},{4,5},{5,4},{6,7},{7,6},{8,9},{9,8},{10,11... | collective-permute-start | bytes 2359304 | tf_op jit(solution)/shard_map/ppermute | solution.py:239
  481.5 41.6 %collective-permute-start.56 = (bf16[384,1024]{1,0:T(8,128)(2,1)}, bf16[384,1024]{1,0:T(8,128)(2,1)}, u32[]{:S(2)}, u32[]{:S(2)}) collective-permute-start(bf16[384,1024]{1,0:T(8,128)(2,1)} %add_convert_fusion.3), channel_id=1, source_target_pairs={{0,2},{1,3},{2,0},{3,1},{4,6},{5,7},{6,4},{7,5},{8,10},{9,11},{10,... | collective-permute-start | bytes 2359304 | tf_op jit(solution)/shard_map/ppermute | solution.py:239
  490.2 22.4 %collective-permute-start.67 = (bf16[128,2048]{1,0:T(8,128)(2,1)}, bf16[128,2048]{1,0:T(8,128)(2,1)}, u32[]{:S(2)}, u32[]{:S(2)}) collective-permute-start(bf16[128,2048]{1,0:T(8,128)(2,1)} %get-tuple-element.261), channel_id=1, source_target_pairs={{8,0},{16,8},{24,16},{28,24},{20,28},{12,20},{4,12},{0,4},{9,1},{1... | collective-permute-start | bytes 1572872 | tf_op jit(solution)/shard_map/ppermute | solution.py:406
  553.7 22.3 %collective-permute-start.78 = (bf16[128,2048]{1,0:T(8,128)(2,1)}, bf16[128,2048]{1,0:T(8,128)(2,1)}, u32[]{:S(2)}, u32[]{:S(2)}) collective-permute-start(bf16[128,2048]{1,0:T(8,128)(2,1)} %collective-permute-done.74.refs_1_), channel_id=1, source_target_pairs={{0,8},{8,16},{16,24},{24,28},{28,20},{20,12},{12,4},{4,0},{1,9},{9... | collective-permute-start | bytes 1572872 | tf_op jit(solution)/shard_map/ppermute | solution.py:406
  553.7 22.4 %collective-permute-start.79 = (bf16[128,2048]{1,0:T(8,128)(2,1)}, bf16[128,2048]{1,0:T(8,128)(2,1)}, u32[]{:S(2)}, u32[]{:S(2)}) collective-permute-start(bf16[128,2048]{1,0:T(8,128)(2,1)} %collective-permute-done.75.refs_2_), channel_id=1, source_target_pairs={{8,0},{16,8},{24,16},{28,24},{20,28},{12,20},{4,12},{0,4},{9,1},{1... | collective-permute-start | bytes 1572872 | tf_op jit(solution)/shard_map/ppermute | solution.py:406
  572.0 50.8 %collective-permute-start.59 = (bf16[6,256]{1,0:T(8,128)(2,1)S(1)}, bf16[6,256]{1,0:T(8,128)(2,1)S(1)}, u32[]{:S(2)}, u32[]{:S(2)}) collective-permute-start(bf16[6,256]{1,0:T(8,128)(2,1)S(1)} %get-tuple-element.438), channel_id=1, source_target_pairs={{0,1},{1,0},{2,3},{3,2},{4,5},{5,4},{6,7},{7,6},{8,9},{9,8},{10,11... | collective-permute-start | bytes 9224 | tf_op jit(solution)/shard_map/ppermute | solution.py:239
  576.1 24.6 %collective-permute-start.82 = (bf16[128,2048]{1,0:T(8,128)(2,1)}, bf16[128,2048]{1,0:T(8,128)(2,1)}, u32[]{:S(2)}, u32[]{:S(2)}) collective-permute-start(bf16[128,2048]{1,0:T(8,128)(2,1)} %collective-permute-done.78.refs_3_), channel_id=1, source_target_pairs={{0,8},{8,16},{16,24},{24,28},{28,20},{20,12},{12,4},{4,0},{1,9},{9... | collective-permute-start | bytes 1572872 | tf_op jit(solution)/shard_map/ppermute | solution.py:406
  576.2 26.2 %collective-permute-start.83 = (bf16[128,2048]{1,0:T(8,128)(2,1)}, bf16[128,2048]{1,0:T(8,128)(2,1)}, u32[]{:S(2)}, u32[]{:S(2)}) collective-permute-start(bf16[128,2048]{1,0:T(8,128)(2,1)} %collective-permute-done.79.refs_4_), channel_id=1, source_target_pairs={{8,0},{16,8},{24,16},{28,24},{20,28},{12,20},{4,12},{0,4},{9,1},{1... | collective-permute-start | bytes 1572872 | tf_op jit(solution)/shard_map/ppermute | solution.py:406
  600.7 22.0 %collective-permute-start.61 = (bf16[6,256]{1,0:T(8,128)(2,1)S(1)}, bf16[6,256]{1,0:T(8,128)(2,1)S(1)}, u32[]{:S(2)}, u32[]{:S(2)}) collective-permute-start(bf16[6,256]{1,0:T(8,128)(2,1)S(1)} %fusion.184), channel_id=1, source_target_pairs={{0,2},{1,3},{2,0},{3,1},{4,6},{5,7},{6,4},{7,5},{8,10},{9,11},{10,... | collective-permute-start | bytes 9224 | tf_op jit(solution)/shard_map/ppermute | solution.py:239
  (232 other events, 2152.4 us)
Sparse Core Ops, SparseCore 0:
  283.8 92.0 reduce-scatter.1
  384.1 79.9 all-gather.1

commit v9 on v8

--- a/solution.py
+++ b/solution.py
@@ -447,6 +447,9 @@
             to_right, to_left = [to_right[0][:half]], [to_left[0][half:]]
         return self.send(to_right, to_left)
 
+    def came(self):
+        return self.from_left + self.from_right
+
     def see(self, items, k):
         self.seen.append((items[0], (k, 0)))
 
@@ -488,6 +491,8 @@
 
 
 class WholeSum:
+    came = staticmethod(lambda: ())
+
     def __init__(self, arrays, parts):
         self.arrays, self.parts, self.steps, self.done = list(arrays), parts, 1, 0
 
@@ -513,7 +518,8 @@
 def start_sum(arrays):
     if arrays[0].shape[1] == arrays[1].shape[1]:
         arrays = [jnp.concatenate(arrays, 0)]
-    return [lax.psum_scatter(item, "rows", scatter_dimension=0, tiled=True) for item in arrays]
+    sums = [lax.psum_scatter(item, "rows", scatter_dimension=0, tiled=True) for item in arrays]
+    return sums, arrays
 
 
 def end_sum(shares):
@@ -533,6 +539,9 @@
         else:
             self.items = [row_sum([item], [part]) for item, part in zip(arrays, parts)]
 
+    def came(self):
+        return [item.came() for item in self.items]
+
     @property
     def done(self):
         return self.items[0].done
@@ -553,13 +562,14 @@
         return [out for item in self.items for out in item.finish(gate)]
 
 
-def sum_cube(values, axis):
+def sum_cube(values, axis, late=()):
     size = lax.axis_size(axis)
     if size & (size - 1):
         return lax.psum(values, axis)
     distance = 1
     while distance < size:
         values = values + lax.ppermute(values, axis, [(i, i ^ distance) for i in range(size)])
+        values = after(values, late)
         distance *= 2
     return values
 
@@ -831,8 +841,8 @@
     held = {}
 
     def start_second(grads):
-        held["second"] = start_sum(grads)
-        return grads
+        held["second"], arrays = start_sum(grads)
+        return arrays
 
     grad, sum_second, _, _ = ffn_backward(
         grad, kept_second, gain_second, up_second, down_second, start_second
@@ -869,16 +879,23 @@
         if first.done == 5:
             second_up, second_down = split_sum(after(second_sum, token), up_second.shape[0])
             token = (token, second_up, second_down)
+    attend_sum = None
     while first.left:
+        if first.left == 2:
+            token = (token, middle.came())
+        if first.left == 1:
+            attend_sum = middle.finish(token)
+            token = (token, attend_sum)
         token = first.step(token)
     pairs = (sum_first, sum_attend, sum_conv, sum_second, sum_final)
     gains = sum_cube(gain_sums(pairs, marks[1]), "tp")
     small = jnp.concatenate([conv_grads[1](marks[1]), d_bias], 0)
     small_shape = small.shape
     pack = jnp.concatenate([gains.reshape(-1), small.reshape(-1)]).reshape(-1, width)
-    pack = sum_cube(after(pack, token), "rows")
-    attend_sum = middle.finish(token)
-    first_sum = first.finish(attend_sum)
+    pack = sum_cube(after(pack, token), "rows", first.came())
+    if attend_sum is None:
+        attend_sum = middle.finish(token)
+    first_sum = first.finish()
     pack = pack.reshape(-1)
     gains, small = pack[: gains.size].reshape(gains.shape), pack[gains.size :].reshape(small_shape)
     bias_shape = content_bias.shape

time: 682 us -> 686 us (level)
  waiting for transfers between devices: 243 us -> 264 us
  starting transfers between devices: 98.4 us -> 79.1 us
    ppermute x32, waiting for transfers between devices: 66.4 us -> 81.7 us  [send(): lax.ppermute(item, 'rows', way)]
    ppermute x32, starting transfers between devices: 47 us -> 34.4 us  [send(): lax.ppermute(item, 'rows', way)]
  transfers between devices with their start and end apart: 97 -> 97, of which waited for: 48 -> 45; matrix products, arithmetic and copies ran while one was open for 29% -> 27% of each run, Pallas kernels for 10% -> 11%
where the time goes in v9:
time: 686 us; the launch traced here: 678 us
  waiting for transfers between devices  264 us (38%)
  matrix products  111 us (16%)
  other arithmetic  81.1 us (12%)
  starting transfers between devices  79.1 us (12%)
  Pallas kernels  76.5 us (11%)
  local copies, waits for them, and re-layouts  49.3 us (7%)
  between operations  17 us (2%)
    ppermute x54, waiting for transfers between devices, swap(): return lax.ppermute(values, 'tp', [(i, i ^ distance) for i in range(size)])  158 us
    dot_general x53, matrix products, dot(): lax.dot_general(left, right, (((contract[0],), (contract[1],)), ((), ()))...  111 us
    ppermute x32, waiting for transfers between devices, send(): lax.ppermute(item, 'rows', way)  81.7 us
    ppermute x54, starting transfers between devices, swap(): return lax.ppermute(values, 'tp', [(i, i ^ distance) for i in range(size)])  34.8 us
    ppermute x32, starting transfers between devices, send(): lax.ppermute(item, 'rows', way)  34.4 us
    pallas_call x10, Pallas kernels, call(): pl.pallas_call(kernel, grid_spec=pltpu.PrefetchScalarGridSpec(num_scalar_...  30.2 us
    unnamed x338, local copies, waits for them, and re-layouts  29.7 us
    pallas_call x1, Pallas kernels, attend_back(): pl.pallas_call(functools.partial(attend_back_kernel, heads), out_shape=(s...  22.2 us
  transfers between devices with their start and end apart: 97, of which 45 were waited for; matrix products, arithmetic and copies ran while one was open for 27% of the time, Pallas kernels for 11%

profile of v9, /device:TPU:0, one launch (start us, length us, event | category | flops | bytes accessed | tf_op | source)
XLA Modules:
  0.0 677.5 jit_solution(8170808849638945390)
XLA Ops:
  51.0 16.9 %collective-permute-done.5 = bf16[384,1024]{1,0:T(8,128)(2,1)S(1)} collective-permute-done((bf16[384,1024]{1,0:T(8,128)(2,1)S(1)}, bf16[384,1024]{1,0:T(8,128)(2,1)S(1)}, u32[]{:S(2)}, u32[]{:S(2)}) %collective-permute-start.5) | collective-permute-done | bytes 786464 | tf_op jit(solution)/shard_map/ppermute | solution.py:239
  75.6 13.7 %collective-permute-done.7 = bf16[384,1024]{1,0:T(8,128)(2,1)S(1)} collective-permute-done((bf16[384,1024]{1,0:T(8,128)(2,1)S(1)}, bf16[384,1024]{1,0:T(8,128)(2,1)S(1)}, u32[]{:S(2)}, u32[]{:S(2)}) %collective-permute-start.7) | collective-permute-done | bytes 786464 | tf_op jit(solution)/shard_map/ppermute | solution.py:239
  100.6 8.9 %shard_map.399 = (bf16[1536,256]{1,0:T(8,128)(2,1)S(1)}, f32[1536,256]{1,0:T(8,128)S(1)}, f32[1536,2]{1,0:T(8,128)S(1)}) custom-call(s32[2,4]{1,0:T(2,128)S(1)} %pad_add_fusion.spans, s32[4]{0:T(128)S(1)} %fusion.201.q_at.k_at, s32[4]{0:T(128)S(1)} %fusion.201.q_at.k_at, bf16[1536,256]{1,0:T(8,128)(2,1)S(1)} %get-tuple-element.486.qc_ref, ...), custom_call_target="tpu_custom_call" | custom-call | flops 4000000000 | bytes 9000000 | tf_op jit(solution)/shard_map/pallas_call | solution.py:156
  109.5 10.1 %collective-permute-done.10 = bf16[1024,256]{1,0:T(8,128)(2,1)S(1)} collective-permute-done((bf16[1024,256]{1,0:T(8,128)(2,1)S(1)}, bf16[1024,256]{1,0:T(8,128)(2,1)S(1)}, u32[]{:S(2)}, u32[]{:S(2)}) %collective-permute-start.10) | collective-permute-done | bytes 524320 | tf_op jit(solution)/shard_map/ppermute | solution.py:239
  119.6 10.4 %collective-permute-done.11 = bf16[256,1024]{1,0:T(8,128)(2,1)S(1)} collective-permute-done((bf16[256,1024]{1,0:T(8,128)(2,1)S(1)}, bf16[256,1024]{1,0:T(8,128)(2,1)S(1)}, u32[]{:S(2)}, u32[]{:S(2)}) %collective-permute-start.11) | collective-permute-done | bytes 524320 | tf_op jit(solution)/shard_map/ppermute | solution.py:239
  137.0 17.0 %collective-permute-done.14 = bf16[384,1024]{1,0:T(8,128)(2,1)S(1)} collective-permute-done((bf16[384,1024]{1,0:T(8,128)(2,1)S(1)}, bf16[384,1024]{1,0:T(8,128)(2,1)S(1)}, u32[]{:S(2)}, u32[]{:S(2)}) %collective-permute-start.14) | collective-permute-done | bytes 786464 | tf_op jit(solution)/shard_map/ppermute | solution.py:239
  174.9 17.2 %collective-permute-done.28 = bf16[384,1024]{1,0:T(8,128)(2,1)S(1)} collective-permute-done((bf16[384,1024]{1,0:T(8,128)(2,1)S(1)}, bf16[384,1024]{1,0:T(8,128)(2,1)S(1)}, u32[]{:S(2)}, u32[]{:S(2)}) %collective-permute-start.28) | collective-permute-done | bytes 786464 | tf_op jit(solution)/shard_map/ppermute | solution.py:239
  205.3 16.7 %collective-permute-done.31 = bf16[384,1024]{1,0:T(8,128)(2,1)S(1)} collective-permute-done((bf16[384,1024]{1,0:T(8,128)(2,1)S(1)}, bf16[384,1024]{1,0:T(8,128)(2,1)S(1)}, u32[]{:S(2)}, u32[]{:S(2)}) %collective-permute-start.31) | collective-permute-done | bytes 786464 | tf_op jit(solution)/shard_map/ppermute | solution.py:239
  227.7 17.5 %collective-permute-done.34 = bf16[384,1024]{1,0:T(8,128)(2,1)S(1)} collective-permute-done((bf16[384,1024]{1,0:T(8,128)(2,1)S(1)}, bf16[384,1024]{1,0:T(8,128)(2,1)S(1)}, u32[]{:S(2)}, u32[]{:S(2)}) %collective-permute-start.34) | collective-permute-done | bytes 786464 | tf_op jit(solution)/shard_map/ppermute | solution.py:239
  270.1 8.7 %collective-permute-done.37 = bf16[384,1024]{1,0:T(8,128)(2,1)} collective-permute-done((bf16[384,1024]{1,0:T(8,128)(2,1)}, bf16[384,1024]{1,0:T(8,128)(2,1)}, u32[]{:S(2)}, u32[]{:S(2)}) %collective-permute-start.37) | collective-permute-done | bytes 786464 | tf_op jit(solution)/shard_map/ppermute | solution.py:239
  320.2 7.7 %collective-permute-done.41 = bf16[384,1024]{1,0:T(8,128)(2,1)S(1)} collective-permute-done((bf16[384,1024]{1,0:T(8,128)(2,1)S(1)}, bf16[384,1024]{1,0:T(8,128)(2,1)S(1)}, u32[]{:S(2)}, u32[]{:S(2)}) %collective-permute-start.41) | collective-permute-done | bytes 786464 | tf_op jit(solution)/shard_map/ppermute | solution.py:239
  343.4 22.2 %shard_map.401 = (bf16[1536,768]{1,0:T(8,128)(2,1)}, bf16[3072,256]{1,0:T(8,128)(2,1)}, f32[8,256]{1,0:T(8,128)S(1)}) custom-call(s32[2,4]{1,0:T(2,128)S(1)} %pad_add_fusion.spans, s32[4]{0:T(128)S(1)} %fusion.201.q_at.k_at, s32[4]{0:T(128)S(1)} %fusion.201.q_at.k_at, bf16[1536,256]{1,0:T(8,128)(2,1)S(1)} %copy-done.7, bf16[1536,256]{1,0:T(8,128)(2,1)S(1)} %copy-done.9, ...), custom_call_target="tpu_custom_call" | custom-call | flops 1000000 | bytes 1000000 | tf_op jit(solution)/shard_map/pallas_call | solution.py:167
  365.6 6.5 collective-permute-done.44
  372.1 8.3 %reduce-scatter.2.cloned.1.call-done = bf16[256,1024]{1,0:T(8,128)(2,1)} async-done(((bf16[2048,1024]{1,0:T(8,128)(2,1)}), bf16[256,1024]{1,0:T(8,128)(2,1)}) %reduce-scatter.2.cloned.1.call-update) | async-done | bytes 524304 | tf_op jit(solution)/shard_map/reduce_scatter | solution.py:521
  427.0 11.1 %collective-permute-done.53.refs_8_ = bf16[64,2048]{1,0:T(8,128)(2,1)S(1)} collective-permute-done((bf16[64,2048]{1,0:T(8,128)(2,1)}, bf16[64,2048]{1,0:T(8,128)(2,1)S(1)}, u32[]{:S(2)}, u32[]{:S(2)}) %collective-permute-start.53) | collective-permute-done | bytes 262176 | tf_op jit(solution)/shard_map/ppermute | solution.py:406
  438.1 7.8 %collective-permute-done.54.refs_9_ = bf16[64,2048]{1,0:T(8,128)(2,1)} collective-permute-done((bf16[64,2048]{1,0:T(8,128)(2,1)}, bf16[64,2048]{1,0:T(8,128)(2,1)}, u32[]{:S(2)}, u32[]{:S(2)}) %collective-permute-start.54) | collective-permute-done | bytes 262176 | tf_op jit(solution)/shard_map/ppermute | solution.py:406
  475.4 8.0 %collective-permute-done.62.refs_8_ = bf16[128,2048]{1,0:T(8,128)(2,1)} collective-permute-done((bf16[128,2048]{1,0:T(8,128)(2,1)S(1)}, bf16[128,2048]{1,0:T(8,128)(2,1)}, u32[]{:S(2)}, u32[]{:S(2)}) %collective-permute-start.62) | collective-permute-done | bytes 524320 | tf_op jit(solution)/shard_map/ppermute | solution.py:406
  490.6 8.1 %fusion.81.refs_0_.refs_2_ = bf16[1024,1024]{1,0:T(8,128)(2,1)} fusion(bf16[768,1024]{1,0:T(8,128)(2,1)} %copy-done.152, bf16[768,1024]{1,0:T(8,128)(2,1)} %fusion.20, bf16[384,1024]{1,0:T(8,128)(2,1)} %copy-done.88, bf16[384,1024]{1,0:T(8,128)(2,1)} %collective-permute-done.2, bf16[384,1024]{1,0:T(8,128)(2,1)} %copy-done.87, ...), kind=kOutput, calls=%fused_computation.103 | convolution fusion | flops 3241148416 | bytes 8388608 | tf_op jit(solution)/shard_map/dot_general | solution.py:232
  556.1 8.3 %collective-permute-done.72.refs_4_ = bf16[128,2048]{1,0:T(8,128)(2,1)S(1)} collective-permute-done((bf16[128,2048]{1,0:T(8,128)(2,1)}, bf16[128,2048]{1,0:T(8,128)(2,1)S(1)}, u32[]{:S(2)}, u32[]{:S(2)}) %collective-permute-start.72) | collective-permute-done | bytes 524320 | tf_op jit(solution)/shard_map/ppermute | solution.py:406
  578.4 8.6 %collective-permute-done.76.refs_2_ = bf16[128,2048]{1,0:T(8,128)(2,1)} collective-permute-done((bf16[128,2048]{1,0:T(8,128)(2,1)}, bf16[128,2048]{1,0:T(8,128)(2,1)}, u32[]{:S(2)}, u32[]{:S(2)}) %collective-permute-start.76) | collective-permute-done | bytes 524320 | tf_op jit(solution)/shard_map/ppermute | solution.py:406
  592.5 6.8 %slice_convert_fusion = (f32[1024,1024]{1,0:T(8,128)}, f32[1024,1024]{1,0:T(8,128)}) fusion(bf16[2048,1024]{1,0:T(8,128)(2,1)} %all-gather.2.cloned.1.call-done), kind=kLoop, calls=%fused_computation.93 | loop fusion | flops 2097152 | bytes 12582912 | tf_op jit(solution)/shard_map/convert_element_type | solution.py:532
  599.9 6.7 collective-permute-done.80.refs_1_
  611.8 11.7 %collective-permute-done.86.refs_7_ = bf16[64,2048]{1,0:T(8,128)(2,1)S(1)} collective-permute-done((bf16[64,2048]{1,0:T(8,128)(2,1)S(1)}, bf16[64,2048]{1,0:T(8,128)(2,1)S(1)}, u32[]{:S(2)}, u32[]{:S(2)}) %collective-permute-start.86) | collective-permute-done | bytes 262176 | tf_op jit(solution)/shard_map/ppermute | solution.py:406
  630.2 9.2 %shard_map.413 = (f32[1024,256]{1,0:T(8,128)}, f32[1024,256]{1,0:T(8,128)}, f32[1024,256]{1,0:T(8,128)}, f32[1024,256]{1,0:T(8,128)}, f32[256,1024]{1,0:T(8,128)...) custom-call(s32[1]{0:T(128)} %bitcast.42.at, bf16[128,2048]{1,0:T(8,128)(2,1)} %shard_map.409.refs_0_, ...), custom_call_target="tpu_custom_call" | custom-call | flops 12582912 | bytes 12582912 | tf_op jit(solution)/shard_map/pallas_call | solution.py:478
  (743 shorter events, 392.5 us)
Async XLA Ops:
  7.2 373.1 %reduce-scatter.2.cloned.1.call-start = ((), (), s32[]{:S(2)}) async-start(), calls=%async_computation.1 | async-start | bytes 4718592 | tf_op jit(solution)/shard_map/reduce_scatter | solution.py:521
  12.1 21.6 %collective-permute-start = (bf16[384,1024]{1,0:T(8,128)(2,1)}, bf16[384,1024]{1,0:T(8,128)(2,1)S(1)}, u32[]{:S(2)}, u32[]{:S(2)}) collective-permute-start(bf16[384,1024]{1,0:T(8,128)(2,1)} %get-tuple-element.425), channel_id=1, source_target_pairs={{0,1},{1,0},{2,3},{3,2},{4,5},{5,4},{6,7},{7,6},{8,9},{9,8},{10,11... | collective-permute-start | bytes 2359304 | tf_op jit(solution)/shard_map/ppermute | solution.py:239
  15.2 56.8 %collective-permute-start.16 = (bf16[6,256]{1,0:T(8,128)(2,1)S(1)}, bf16[6,256]{1,0:T(8,128)(2,1)S(1)}, u32[]{:S(2)}, u32[]{:S(2)}) collective-permute-start(bf16[6,256]{1,0:T(8,128)(2,1)S(1)} %pad_maximum_fusion.25), channel_id=1, source_target_pairs={{0,2},{1,3},{2,0},{3,1},{4,6},{5,7},{6,4},{7,5},{8,10},{9,11},{10,... | collective-permute-start | bytes 9224 | tf_op jit(solution)/shard_map/ppermute | solution.py:239
  15.3 56.8 %collective-permute-start.15 = (bf16[6,256]{1,0:T(8,128)(2,1)S(1)}, bf16[6,256]{1,0:T(8,128)(2,1)S(1)}, u32[]{:S(2)}, u32[]{:S(2)}) collective-permute-start(bf16[6,256]{1,0:T(8,128)(2,1)S(1)} %pad_maximum_fusion.25), channel_id=1, source_target_pairs={{0,1},{1,0},{2,3},{3,2},{4,5},{5,4},{6,7},{7,6},{8,9},{9,8},{10,11... | collective-permute-start | bytes 9224 | tf_op jit(solution)/shard_map/ppermute | solution.py:239
  93.1 39.1 %collective-permute-start.20 = (bf16[1024,256]{1,0:T(8,128)(2,1)S(1)}, bf16[1024,256]{1,0:T(8,128)(2,1)S(1)}, u32[]{:S(2)}, u32[]{:S(2)}) collective-permute-start(bf16[1024,256]{1,0:T(8,128)(2,1)S(1)} %get-tuple-element.193), channel_id=1, source_target_pairs={{0,1},{1,0},{2,3},{3,2},{4,5},{5,4},{6,7},{7,6},{8,9},{9,8},{10,11... | collective-permute-start | bytes 1572872 | tf_op jit(solution)/shard_map/ppermute | solution.py:239
  96.8 22.8 %collective-permute-start.10 = (bf16[1024,256]{1,0:T(8,128)(2,1)S(1)}, bf16[1024,256]{1,0:T(8,128)(2,1)S(1)}, u32[]{:S(2)}, u32[]{:S(2)}) collective-permute-start(bf16[1024,256]{1,0:T(8,128)(2,1)S(1)} %get-tuple-element.194), channel_id=1, source_target_pairs={{0,2},{1,3},{2,0},{3,1},{4,6},{5,7},{6,4},{7,5},{8,10},{9,11},{10,... | collective-permute-start | bytes 1572872 | tf_op jit(solution)/shard_map/ppermute | solution.py:239
  97.8 32.2 %collective-permute-start.11 = (bf16[256,1024]{1,0:T(8,128)(2,1)S(1)}, bf16[256,1024]{1,0:T(8,128)(2,1)S(1)}, u32[]{:S(2)}, u32[]{:S(2)}) collective-permute-start(bf16[256,1024]{1,0:T(8,128)(2,1)S(1)} %copy-done.102), channel_id=1, source_target_pairs={{0,2},{1,3},{2,0},{3,1},{4,6},{5,7},{6,4},{7,5},{8,10},{9,11},{10,... | collective-permute-start | bytes 1572872 | tf_op jit(solution)/shard_map/ppermute | solution.py:239
  136.0 23.2 %collective-permute-start.25 = (bf16[256,1024]{1,0:T(8,128)(2,1)S(1)}, bf16[256,1024]{1,0:T(8,128)(2,1)S(1)}, u32[]{:S(2)}, u32[]{:S(2)}) collective-permute-start(bf16[256,1024]{1,0:T(8,128)(2,1)S(1)} %collective-permute-done.11), channel_id=1, source_target_pairs={{0,1},{1,0},{2,3},{3,2},{4,5},{5,4},{6,7},{7,6},{8,9},{9,8},{10,11... | collective-permute-start | bytes 1572872 | tf_op jit(solution)/shard_map/ppermute | solution.py:239
  288.0 224.3 %all-gather.2.cloned.1.call-start = ((), (), s32[]{:S(2)}) async-start(), calls=%async_computation.2 | async-start | bytes 4718592 | tf_op jit(solution)/shard_map/all_gather | solution.py:526
  335.4 36.7 %collective-permute-start.44 = (bf16[1024,768]{1,0:T(8,128)(2,1)}, bf16[1024,768]{1,0:T(8,128)(2,1)}, u32[]{:S(2)}, u32[]{:S(2)}) collective-permute-start(bf16[1024,768]{1,0:T(8,128)(2,1)} %add_convert_fusion.2), channel_id=1, source_target_pairs={{0,2},{1,3},{2,0},{3,1},{4,6},{5,7},{6,4},{7,5},{8,10},{9,11},{10,... | collective-permute-start | bytes 4718600 | tf_op jit(solution)/shard_map/ppermute | solution.py:239
  337.2 46.0 %collective-permute-start.48 = (bf16[1024,768]{1,0:T(8,128)(2,1)}, bf16[1024,768]{1,0:T(8,128)(2,1)}, u32[]{:S(2)}, u32[]{:S(2)}) collective-permute-start(bf16[1024,768]{1,0:T(8,128)(2,1)} %pad_maximum_fusion.10), channel_id=1, source_target_pairs={{0,1},{1,0},{2,3},{3,2},{4,5},{5,4},{6,7},{7,6},{8,9},{9,8},{10,11... | collective-permute-start | bytes 4718600 | tf_op jit(solution)/shard_map/ppermute | solution.py:239
  387.9 24.4 %collective-permute-start.45 = (bf16[384,1024]{1,0:T(8,128)(2,1)}, bf16[384,1024]{1,0:T(8,128)(2,1)}, u32[]{:S(2)}, u32[]{:S(2)}) collective-permute-start(bf16[384,1024]{1,0:T(8,128)(2,1)} %convolution_convert_fusion.5), channel_id=1, source_target_pairs={{0,1},{1,0},{2,3},{3,2},{4,5},{5,4},{6,7},{7,6},{8,9},{9,8},{10,11... | collective-permute-start | bytes 2359304 | tf_op jit(solution)/shard_map/ppermute | solution.py:239
  421.2 28.0 %collective-permute-start.49 = (bf16[384,1024]{1,0:T(8,128)(2,1)}, bf16[384,1024]{1,0:T(8,128)(2,1)S(1)}, u32[]{:S(2)}, u32[]{:S(2)}) collective-permute-start(bf16[384,1024]{1,0:T(8,128)(2,1)} %get-tuple-element.373), channel_id=1, source_target_pairs={{0,1},{1,0},{2,3},{3,2},{4,5},{5,4},{6,7},{7,6},{8,9},{9,8},{10,11... | collective-permute-start | bytes 2359304 | tf_op jit(solution)/shard_map/ppermute | solution.py:239
  421.2 29.4 %collective-permute-start.51 = (bf16[384,1024]{1,0:T(8,128)(2,1)}, bf16[384,1024]{1,0:T(8,128)(2,1)S(1)}, u32[]{:S(2)}, u32[]{:S(2)}) collective-permute-start(bf16[384,1024]{1,0:T(8,128)(2,1)} %get-tuple-element.373), channel_id=1, source_target_pairs={{0,2},{1,3},{2,0},{3,1},{4,6},{5,7},{6,4},{7,5},{8,10},{9,11},{10,... | collective-permute-start | bytes 2359304 | tf_op jit(solution)/shard_map/ppermute | solution.py:239
  424.3 21.6 %collective-permute-start.54 = (bf16[64,2048]{1,0:T(8,128)(2,1)}, bf16[64,2048]{1,0:T(8,128)(2,1)}, u32[]{:S(2)}, u32[]{:S(2)}) collective-permute-start(bf16[64,2048]{1,0:T(8,128)(2,1)} %get-tuple-element.228), channel_id=1, source_target_pairs={{8,0},{16,8},{24,16},{28,24},{20,28},{12,20},{4,12},{0,4},{9,1},{1... | collective-permute-start | bytes 786440 | tf_op jit(solution)/shard_map/ppermute | solution.py:406
  473.1 48.3 %collective-permute-start.50 = (bf16[384,1024]{1,0:T(8,128)(2,1)}, bf16[384,1024]{1,0:T(8,128)(2,1)}, u32[]{:S(2)}, u32[]{:S(2)}) collective-permute-start(bf16[384,1024]{1,0:T(8,128)(2,1)} %convolution_convert_fusion.9), channel_id=1, source_target_pairs={{0,1},{1,0},{2,3},{3,2},{4,5},{5,4},{6,7},{7,6},{8,9},{9,8},{10,11... | collective-permute-start | bytes 2359304 | tf_op jit(solution)/shard_map/ppermute | solution.py:239
  475.2 47.7 %collective-permute-start.56 = (bf16[384,1024]{1,0:T(8,128)(2,1)}, bf16[384,1024]{1,0:T(8,128)(2,1)}, u32[]{:S(2)}, u32[]{:S(2)}) collective-permute-start(bf16[384,1024]{1,0:T(8,128)(2,1)} %add_convert_fusion.3), channel_id=1, source_target_pairs={{0,2},{1,3},{2,0},{3,1},{4,6},{5,7},{6,4},{7,5},{8,10},{9,11},{10,... | collective-permute-start | bytes 2359304 | tf_op jit(solution)/shard_map/ppermute | solution.py:239
  489.2 23.2 %collective-permute-start.67 = (bf16[128,2048]{1,0:T(8,128)(2,1)}, bf16[128,2048]{1,0:T(8,128)(2,1)}, u32[]{:S(2)}, u32[]{:S(2)}) collective-permute-start(bf16[128,2048]{1,0:T(8,128)(2,1)} %get-tuple-element.264), channel_id=1, source_target_pairs={{8,0},{16,8},{24,16},{28,24},{20,28},{12,20},{4,12},{0,4},{9,1},{1... | collective-permute-start | bytes 1572872 | tf_op jit(solution)/shard_map/ppermute | solution.py:406
  520.9 21.2 %collective-permute-start.68 = (bf16[128,2048]{1,0:T(8,128)(2,1)}, bf16[128,2048]{1,0:T(8,128)(2,1)}, u32[]{:S(2)}, u32[]{:S(2)}) collective-permute-start(bf16[128,2048]{1,0:T(8,128)(2,1)} %get-tuple-element.282), channel_id=1, source_target_pairs={{0,8},{8,16},{16,24},{24,28},{28,20},{20,12},{12,4},{4,0},{1,9},{9... | collective-permute-start | bytes 1572872 | tf_op jit(solution)/shard_map/ppermute | solution.py:406
  521.4 21.2 %collective-permute-start.69 = (bf16[128,2048]{1,0:T(8,128)(2,1)}, bf16[128,2048]{1,0:T(8,128)(2,1)}, u32[]{:S(2)}, u32[]{:S(2)}) collective-permute-start(bf16[128,2048]{1,0:T(8,128)(2,1)} %get-tuple-element.283), channel_id=1, source_target_pairs={{8,0},{16,8},{24,16},{28,24},{20,28},{12,20},{4,12},{0,4},{9,1},{1... | collective-permute-start | bytes 1572872 | tf_op jit(solution)/shard_map/ppermute | solution.py:406
  553.9 21.9 %collective-permute-start.78 = (bf16[128,2048]{1,0:T(8,128)(2,1)}, bf16[128,2048]{1,0:T(8,128)(2,1)}, u32[]{:S(2)}, u32[]{:S(2)}) collective-permute-start(bf16[128,2048]{1,0:T(8,128)(2,1)} %collective-permute-done.74.refs_1_), channel_id=1, source_target_pairs={{0,8},{8,16},{16,24},{24,28},{28,20},{20,12},{12,4},{4,0},{1,9},{9... | collective-permute-start | bytes 1572872 | tf_op jit(solution)/shard_map/ppermute | solution.py:406
  576.4 23.0 %collective-permute-start.82 = (bf16[128,2048]{1,0:T(8,128)(2,1)}, bf16[128,2048]{1,0:T(8,128)(2,1)S(1)}, u32[]{:S(2)}, u32[]{:S(2)}) collective-permute-start(bf16[128,2048]{1,0:T(8,128)(2,1)} %collective-permute-done.78.refs_3_), channel_id=1, source_target_pairs={{0,8},{8,16},{16,24},{24,28},{28,20},{20,12},{12,4},{4,0},{1,9},{9... | collective-permute-start | bytes 1572872 | tf_op jit(solution)/shard_map/ppermute | solution.py:406
  577.8 22.0 %collective-permute-start.83 = (bf16[128,2048]{1,0:T(8,128)(2,1)}, bf16[128,2048]{1,0:T(8,128)(2,1)S(1)}, u32[]{:S(2)}, u32[]{:S(2)}) collective-permute-start(bf16[128,2048]{1,0:T(8,128)(2,1)} %collective-permute-done.79.refs_4_), channel_id=1, source_target_pairs={{8,0},{16,8},{24,16},{28,24},{20,28},{12,20},{4,12},{0,4},{9,1},{1... | collective-permute-start | bytes 1572872 | tf_op jit(solution)/shard_map/ppermute | solution.py:406
  599.3 43.0 %collective-permute-start.59 = (bf16[6,256]{1,0:T(8,128)(2,1)S(1)}, bf16[6,256]{1,0:T(8,128)(2,1)S(1)}, u32[]{:S(2)}, u32[]{:S(2)}) collective-permute-start(bf16[6,256]{1,0:T(8,128)(2,1)S(1)} %get-tuple-element.444), channel_id=1, source_target_pairs={{0,1},{1,0},{2,3},{3,2},{4,5},{5,4},{6,7},{7,6},{8,9},{9,8},{10,11... | collective-permute-start | bytes 9224 | tf_op jit(solution)/shard_map/ppermute | solution.py:239
  (232 other events, 2012.1 us)
Sparse Core Ops, SparseCore 0:
  288.1 92.1 reduce-scatter.1
  388.6 78.5 all-gather.1

commit v10 on v8

--- a/solution.py
+++ b/solution.py
@@ -447,6 +447,9 @@
             to_right, to_left = [to_right[0][:half]], [to_left[0][half:]]
         return self.send(to_right, to_left)
 
+    def came(self):
+        return self.from_left + self.from_right
+
     def see(self, items, k):
         self.seen.append((items[0], (k, 0)))
 
@@ -488,6 +491,8 @@
 
 
 class WholeSum:
+    came = staticmethod(lambda: ())
+
     def __init__(self, arrays, parts):
         self.arrays, self.parts, self.steps, self.done = list(arrays), parts, 1, 0
 
@@ -533,6 +538,9 @@
         else:
             self.items = [row_sum([item], [part]) for item, part in zip(arrays, parts)]
 
+    def came(self):
+        return [item.came() for item in self.items]
+
     @property
     def done(self):
         return self.items[0].done
@@ -553,13 +561,14 @@
         return [out for item in self.items for out in item.finish(gate)]
 
 
-def sum_cube(values, axis):
+def sum_cube(values, axis, late=()):
     size = lax.axis_size(axis)
     if size & (size - 1):
         return lax.psum(values, axis)
     distance = 1
     while distance < size:
         values = values + lax.ppermute(values, axis, [(i, i ^ distance) for i in range(size)])
+        values = after(values, late)
         distance *= 2
     return values
 
@@ -876,7 +885,7 @@
     small = jnp.concatenate([conv_grads[1](marks[1]), d_bias], 0)
     small_shape = small.shape
     pack = jnp.concatenate([gains.reshape(-1), small.reshape(-1)]).reshape(-1, width)
-    pack = sum_cube(after(pack, token), "rows")
+    pack = sum_cube(after(pack, token), "rows", first.came())
     attend_sum = middle.finish(token)
     first_sum = first.finish(attend_sum)
     pack = pack.reshape(-1)

time: 682 us -> 685 us (level)
  waiting for transfers between devices: 243 us -> 258 us
  starting transfers between devices: 98.4 us -> 88.9 us
    ppermute x32, waiting for transfers between devices: 66.4 us -> 80.8 us  [send(): lax.ppermute(item, 'rows', way)]
    ppermute x32, starting transfers between devices: 47 us -> 38.8 us  [send(): lax.ppermute(item, 'rows', way)]
  transfers between devices with their start and end apart: 97 -> 97, of which waited for: 48 -> 47; matrix products, arithmetic and copies ran while one was open for 29% -> 27% of each run, Pallas kernels for 10% -> 11%
where the time goes in v10:
time: 685 us; the launch traced here: 679 us
  waiting for transfers between devices  258 us (38%)
  matrix products  108 us (16%)
  starting transfers between devices  88.9 us (13%)
  other arithmetic  78.8 us (12%)
  Pallas kernels  76.7 us (11%)
  local copies, waits for them, and re-layouts  51.6 us (8%)
  between operations  17 us (2%)
    ppermute x54, waiting for transfers between devices, swap(): return lax.ppermute(values, 'tp', [(i, i ^ distance) for i in range(size)])  157 us
    dot_general x53, matrix products, dot(): lax.dot_general(left, right, (((contract[0],), (contract[1],)), ((), ()))...  108 us
    ppermute x32, waiting for transfers between devices, send(): lax.ppermute(item, 'rows', way)  80.8 us
    ppermute x54, starting transfers between devices, swap(): return lax.ppermute(values, 'tp', [(i, i ^ distance) for i in range(size)])  39.6 us
    ppermute x32, starting transfers between devices, send(): lax.ppermute(item, 'rows', way)  38.8 us
    unnamed x338, local copies, waits for them, and re-layouts  30.8 us
    pallas_call x10, Pallas kernels, call(): pl.pallas_call(kernel, grid_spec=pltpu.PrefetchScalarGridSpec(num_scalar_...  30.2 us
    pallas_call x1, Pallas kernels, attend_back(): pl.pallas_call(functools.partial(attend_back_kernel, heads), out_shape=(s...  22.2 us
  transfers between devices with their start and end apart: 97, of which 47 were waited for; matrix products, arithmetic and copies ran while one was open for 27% of the time, Pallas kernels for 11%

profile of v10, /device:TPU:0, one launch (start us, length us, event | category | flops | bytes accessed | tf_op | source)
XLA Modules:
  0.0 678.7 jit_solution(6181875170038915982)
XLA Ops:
  51.1 16.9 %collective-permute-done.5 = bf16[384,1024]{1,0:T(8,128)(2,1)S(1)} collective-permute-done((bf16[384,1024]{1,0:T(8,128)(2,1)S(1)}, bf16[384,1024]{1,0:T(8,128)(2,1)S(1)}, u32[]{:S(2)}, u32[]{:S(2)}) %collective-permute-start.5) | collective-permute-done | bytes 786464 | tf_op jit(solution)/shard_map/ppermute | solution.py:239
  75.6 13.7 %collective-permute-done.7 = bf16[384,1024]{1,0:T(8,128)(2,1)S(1)} collective-permute-done((bf16[384,1024]{1,0:T(8,128)(2,1)S(1)}, bf16[384,1024]{1,0:T(8,128)(2,1)S(1)}, u32[]{:S(2)}, u32[]{:S(2)}) %collective-permute-start.7) | collective-permute-done | bytes 786464 | tf_op jit(solution)/shard_map/ppermute | solution.py:239
  100.6 8.9 %shard_map.399 = (bf16[1536,256]{1,0:T(8,128)(2,1)S(1)}, f32[1536,256]{1,0:T(8,128)S(1)}, f32[1536,2]{1,0:T(8,128)S(1)}) custom-call(s32[2,4]{1,0:T(2,128)S(1)} %pad_add_fusion.spans, s32[4]{0:T(128)S(1)} %fusion.201.q_at.k_at, s32[4]{0:T(128)S(1)} %fusion.201.q_at.k_at, bf16[1536,256]{1,0:T(8,128)(2,1)S(1)} %get-tuple-element.486.qc_ref, ...), custom_call_target="tpu_custom_call" | custom-call | flops 4000000000 | bytes 9000000 | tf_op jit(solution)/shard_map/pallas_call | solution.py:156
  109.5 10.1 %collective-permute-done.10 = bf16[1024,256]{1,0:T(8,128)(2,1)S(1)} collective-permute-done((bf16[1024,256]{1,0:T(8,128)(2,1)S(1)}, bf16[1024,256]{1,0:T(8,128)(2,1)S(1)}, u32[]{:S(2)}, u32[]{:S(2)}) %collective-permute-start.10) | collective-permute-done | bytes 524320 | tf_op jit(solution)/shard_map/ppermute | solution.py:239
  119.7 10.4 %collective-permute-done.11 = bf16[256,1024]{1,0:T(8,128)(2,1)S(1)} collective-permute-done((bf16[256,1024]{1,0:T(8,128)(2,1)S(1)}, bf16[256,1024]{1,0:T(8,128)(2,1)S(1)}, u32[]{:S(2)}, u32[]{:S(2)}) %collective-permute-start.11) | collective-permute-done | bytes 524320 | tf_op jit(solution)/shard_map/ppermute | solution.py:239
  137.0 17.0 %collective-permute-done.14 = bf16[384,1024]{1,0:T(8,128)(2,1)S(1)} collective-permute-done((bf16[384,1024]{1,0:T(8,128)(2,1)S(1)}, bf16[384,1024]{1,0:T(8,128)(2,1)S(1)}, u32[]{:S(2)}, u32[]{:S(2)}) %collective-permute-start.14) | collective-permute-done | bytes 786464 | tf_op jit(solution)/shard_map/ppermute | solution.py:239
  174.0 17.2 %collective-permute-done.28 = bf16[384,1024]{1,0:T(8,128)(2,1)S(1)} collective-permute-done((bf16[384,1024]{1,0:T(8,128)(2,1)S(1)}, bf16[384,1024]{1,0:T(8,128)(2,1)S(1)}, u32[]{:S(2)}, u32[]{:S(2)}) %collective-permute-start.28) | collective-permute-done | bytes 786464 | tf_op jit(solution)/shard_map/ppermute | solution.py:239
  204.2 16.7 %collective-permute-done.31 = bf16[384,1024]{1,0:T(8,128)(2,1)S(1)} collective-permute-done((bf16[384,1024]{1,0:T(8,128)(2,1)S(1)}, bf16[384,1024]{1,0:T(8,128)(2,1)S(1)}, u32[]{:S(2)}, u32[]{:S(2)}) %collective-permute-start.31) | collective-permute-done | bytes 786464 | tf_op jit(solution)/shard_map/ppermute | solution.py:239
  226.3 17.2 %collective-permute-done.34 = bf16[384,1024]{1,0:T(8,128)(2,1)S(1)} collective-permute-done((bf16[384,1024]{1,0:T(8,128)(2,1)S(1)}, bf16[384,1024]{1,0:T(8,128)(2,1)S(1)}, u32[]{:S(2)}, u32[]{:S(2)}) %collective-permute-start.34) | collective-permute-done | bytes 786464 | tf_op jit(solution)/shard_map/ppermute | solution.py:239
  263.3 10.8 %collective-permute-done.37 = bf16[384,1024]{1,0:T(8,128)(2,1)S(1)} collective-permute-done((bf16[384,1024]{1,0:T(8,128)(2,1)S(1)}, bf16[384,1024]{1,0:T(8,128)(2,1)S(1)}, u32[]{:S(2)}, u32[]{:S(2)}) %collective-permute-start.37) | collective-permute-done | bytes 786464 | tf_op jit(solution)/shard_map/ppermute | solution.py:239
  315.0 8.1 %collective-permute-done.41 = bf16[384,1024]{1,0:T(8,128)(2,1)S(1)} collective-permute-done((bf16[384,1024]{1,0:T(8,128)(2,1)S(1)}, bf16[384,1024]{1,0:T(8,128)(2,1)S(1)}, u32[]{:S(2)}, u32[]{:S(2)}) %collective-permute-start.41) | collective-permute-done | bytes 786464 | tf_op jit(solution)/shard_map/ppermute | solution.py:239
  339.6 22.2 %shard_map.401 = (bf16[1536,768]{1,0:T(8,128)(2,1)}, bf16[3072,256]{1,0:T(8,128)(2,1)}, f32[8,256]{1,0:T(8,128)S(1)}) custom-call(s32[2,4]{1,0:T(2,128)S(1)} %pad_add_fusion.spans, s32[4]{0:T(128)S(1)} %fusion.201.q_at.k_at, s32[4]{0:T(128)S(1)} %fusion.201.q_at.k_at, bf16[1536,256]{1,0:T(8,128)(2,1)S(1)} %copy-done.7, bf16[1536,256]{1,0:T(8,128)(2,1)S(1)} %copy-done.9, ...), custom_call_target="tpu_custom_call" | custom-call | flops 1000000 | bytes 1000000 | tf_op jit(solution)/shard_map/pallas_call | solution.py:167
  367.3 9.3 %reduce-scatter.2.cloned.1.call-done = bf16[256,1024]{1,0:T(8,128)(2,1)} async-done(((bf16[2048,1024]{1,0:T(8,128)(2,1)}), bf16[256,1024]{1,0:T(8,128)(2,1)}) %reduce-scatter.2.cloned.1.call-update) | async-done | bytes 524304 | tf_op jit(solution)/shard_map/reduce_scatter | solution.py:521
  418.9 7.5 %collective-permute-start.53 = (bf16[64,2048]{1,0:T(8,128)(2,1)}, bf16[64,2048]{1,0:T(8,128)(2,1)S(1)}, u32[]{:S(2)}, u32[]{:S(2)}) collective-permute-start(bf16[64,2048]{1,0:T(8,128)(2,1)} %get-tuple-element.227), channel_id=1, source_target_pairs={{0,8},{8,16},{16,24},{24,28},{28,20},{20,12},{12,4},{4,0},{1,9},{9... | collective-permute-start | bytes 786440 | tf_op jit(solution)/shard_map/ppermute | solution.py:406
  427.6 11.1 %collective-permute-done.53.refs_8_ = bf16[64,2048]{1,0:T(8,128)(2,1)S(1)} collective-permute-done((bf16[64,2048]{1,0:T(8,128)(2,1)}, bf16[64,2048]{1,0:T(8,128)(2,1)S(1)}, u32[]{:S(2)}, u32[]{:S(2)}) %collective-permute-start.53) | collective-permute-done | bytes 262176 | tf_op jit(solution)/shard_map/ppermute | solution.py:406
  438.7 7.4 %collective-permute-done.54.refs_9_ = bf16[64,2048]{1,0:T(8,128)(2,1)} collective-permute-done((bf16[64,2048]{1,0:T(8,128)(2,1)}, bf16[64,2048]{1,0:T(8,128)(2,1)}, u32[]{:S(2)}, u32[]{:S(2)}) %collective-permute-start.54) | collective-permute-done | bytes 262176 | tf_op jit(solution)/shard_map/ppermute | solution.py:406
  491.1 7.8 %fusion.81.refs_0_.refs_2_ = bf16[1024,1024]{1,0:T(8,128)(2,1)} fusion(bf16[768,1024]{1,0:T(8,128)(2,1)} %copy-done.152, bf16[768,1024]{1,0:T(8,128)(2,1)} %fusion.20, bf16[384,1024]{1,0:T(8,128)(2,1)} %copy-done.85, bf16[384,1024]{1,0:T(8,128)(2,1)} %collective-permute-done.2, bf16[384,1024]{1,0:T(8,128)(2,1)} %copy-done.84, ...), kind=kOutput, calls=%fused_computation.103 | convolution fusion | flops 3241148416 | bytes 8388608 | tf_op jit(solution)/shard_map/dot_general | solution.py:232
  556.1 8.6 %collective-permute-done.72.refs_4_ = bf16[128,2048]{1,0:T(8,128)(2,1)S(1)} collective-permute-done((bf16[128,2048]{1,0:T(8,128)(2,1)}, bf16[128,2048]{1,0:T(8,128)(2,1)S(1)}, u32[]{:S(2)}, u32[]{:S(2)}) %collective-permute-start.72) | collective-permute-done | bytes 524320 | tf_op jit(solution)/shard_map/ppermute | solution.py:406
  578.4 8.9 %collective-permute-done.76.refs_2_ = bf16[128,2048]{1,0:T(8,128)(2,1)} collective-permute-done((bf16[128,2048]{1,0:T(8,128)(2,1)}, bf16[128,2048]{1,0:T(8,128)(2,1)}, u32[]{:S(2)}, u32[]{:S(2)}) %collective-permute-start.76) | collective-permute-done | bytes 524320 | tf_op jit(solution)/shard_map/ppermute | solution.py:406
  592.5 6.8 %slice_convert_fusion = (f32[1024,1024]{1,0:T(8,128)}, f32[1024,1024]{1,0:T(8,128)}) fusion(bf16[2048,1024]{1,0:T(8,128)(2,1)} %all-gather.2.cloned.1.call-done), kind=kLoop, calls=%fused_computation.93 | loop fusion | flops 2097152 | bytes 12582912 | tf_op jit(solution)/shard_map/convert_element_type | solution.py:531
  600.6 6.5 collective-permute-done.80.refs_1_
  624.3 6.9 %collective-permute-done.86.refs_5_ = bf16[128,2048]{1,0:T(8,128)(2,1)S(1)} collective-permute-done((bf16[128,2048]{1,0:T(8,128)(2,1)}, bf16[128,2048]{1,0:T(8,128)(2,1)S(1)}, u32[]{:S(2)}, u32[]{:S(2)}) %collective-permute-start.86) | collective-permute-done | bytes 524320 | tf_op jit(solution)/shard_map/ppermute | solution.py:406
  648.3 9.2 %shard_map.413 = (f32[1024,256]{1,0:T(8,128)}, f32[1024,256]{1,0:T(8,128)}, f32[1024,256]{1,0:T(8,128)}, f32[1024,256]{1,0:T(8,128)}, f32[256,1024]{1,0:T(8,128)...) custom-call(s32[1]{0:T(128)} %bitcast.42.at, bf16[128,2048]{1,0:T(8,128)(2,1)} %shard_map.409.refs_0_, ...), custom_call_target="tpu_custom_call" | custom-call | flops 12582912 | bytes 12582912 | tf_op jit(solution)/shard_map/pallas_call | solution.py:478
  661.0 6.2 shard_map.414
  (743 shorter events, 396.4 us)
Async XLA Ops:
  7.2 369.4 %reduce-scatter.2.cloned.1.call-start = ((), (), s32[]{:S(2)}) async-start(), calls=%async_computation.1 | async-start | bytes 4718592 | tf_op jit(solution)/shard_map/reduce_scatter | solution.py:521
  12.1 21.6 %collective-permute-start = (bf16[384,1024]{1,0:T(8,128)(2,1)}, bf16[384,1024]{1,0:T(8,128)(2,1)S(1)}, u32[]{:S(2)}, u32[]{:S(2)}) collective-permute-start(bf16[384,1024]{1,0:T(8,128)(2,1)} %get-tuple-element.425), channel_id=1, source_target_pairs={{0,1},{1,0},{2,3},{3,2},{4,5},{5,4},{6,7},{7,6},{8,9},{9,8},{10,11... | collective-permute-start | bytes 2359304 | tf_op jit(solution)/shard_map/ppermute | solution.py:239
  15.2 56.8 %collective-permute-start.16 = (bf16[6,256]{1,0:T(8,128)(2,1)S(1)}, bf16[6,256]{1,0:T(8,128)(2,1)S(1)}, u32[]{:S(2)}, u32[]{:S(2)}) collective-permute-start(bf16[6,256]{1,0:T(8,128)(2,1)S(1)} %pad_maximum_fusion.25), channel_id=1, source_target_pairs={{0,2},{1,3},{2,0},{3,1},{4,6},{5,7},{6,4},{7,5},{8,10},{9,11},{10,... | collective-permute-start | bytes 9224 | tf_op jit(solution)/shard_map/ppermute | solution.py:239
  15.3 56.9 %collective-permute-start.15 = (bf16[6,256]{1,0:T(8,128)(2,1)S(1)}, bf16[6,256]{1,0:T(8,128)(2,1)S(1)}, u32[]{:S(2)}, u32[]{:S(2)}) collective-permute-start(bf16[6,256]{1,0:T(8,128)(2,1)S(1)} %pad_maximum_fusion.25), channel_id=1, source_target_pairs={{0,1},{1,0},{2,3},{3,2},{4,5},{5,4},{6,7},{7,6},{8,9},{9,8},{10,11... | collective-permute-start | bytes 9224 | tf_op jit(solution)/shard_map/ppermute | solution.py:239
  93.1 39.1 %collective-permute-start.20 = (bf16[1024,256]{1,0:T(8,128)(2,1)S(1)}, bf16[1024,256]{1,0:T(8,128)(2,1)S(1)}, u32[]{:S(2)}, u32[]{:S(2)}) collective-permute-start(bf16[1024,256]{1,0:T(8,128)(2,1)S(1)} %get-tuple-element.193), channel_id=1, source_target_pairs={{0,1},{1,0},{2,3},{3,2},{4,5},{5,4},{6,7},{7,6},{8,9},{9,8},{10,11... | collective-permute-start | bytes 1572872 | tf_op jit(solution)/shard_map/ppermute | solution.py:239
  96.8 22.8 %collective-permute-start.10 = (bf16[1024,256]{1,0:T(8,128)(2,1)S(1)}, bf16[1024,256]{1,0:T(8,128)(2,1)S(1)}, u32[]{:S(2)}, u32[]{:S(2)}) collective-permute-start(bf16[1024,256]{1,0:T(8,128)(2,1)S(1)} %get-tuple-element.194), channel_id=1, source_target_pairs={{0,2},{1,3},{2,0},{3,1},{4,6},{5,7},{6,4},{7,5},{8,10},{9,11},{10,... | collective-permute-start | bytes 1572872 | tf_op jit(solution)/shard_map/ppermute | solution.py:239
  97.8 32.2 %collective-permute-start.11 = (bf16[256,1024]{1,0:T(8,128)(2,1)S(1)}, bf16[256,1024]{1,0:T(8,128)(2,1)S(1)}, u32[]{:S(2)}, u32[]{:S(2)}) collective-permute-start(bf16[256,1024]{1,0:T(8,128)(2,1)S(1)} %copy-done.99), channel_id=1, source_target_pairs={{0,2},{1,3},{2,0},{3,1},{4,6},{5,7},{6,4},{7,5},{8,10},{9,11},{10,... | collective-permute-start | bytes 1572872 | tf_op jit(solution)/shard_map/ppermute | solution.py:239
  136.0 23.3 %collective-permute-start.25 = (bf16[256,1024]{1,0:T(8,128)(2,1)S(1)}, bf16[256,1024]{1,0:T(8,128)(2,1)S(1)}, u32[]{:S(2)}, u32[]{:S(2)}) collective-permute-start(bf16[256,1024]{1,0:T(8,128)(2,1)S(1)} %collective-permute-done.11), channel_id=1, source_target_pairs={{0,1},{1,0},{2,3},{3,2},{4,5},{5,4},{6,7},{7,6},{8,9},{9,8},{10,11... | collective-permute-start | bytes 1572872 | tf_op jit(solution)/shard_map/ppermute | solution.py:239
  284.2 228.4 %all-gather.2.cloned.1.call-start = ((), (), s32[]{:S(2)}) async-start(), calls=%async_computation.2 | async-start | bytes 4718592 | tf_op jit(solution)/shard_map/all_gather | solution.py:525
  330.5 36.8 %collective-permute-start.44 = (bf16[1024,768]{1,0:T(8,128)(2,1)}, bf16[1024,768]{1,0:T(8,128)(2,1)}, u32[]{:S(2)}, u32[]{:S(2)}) collective-permute-start(bf16[1024,768]{1,0:T(8,128)(2,1)} %add_convert_fusion.2), channel_id=1, source_target_pairs={{0,2},{1,3},{2,0},{3,1},{4,6},{5,7},{6,4},{7,5},{8,10},{9,11},{10,... | collective-permute-start | bytes 4718600 | tf_op jit(solution)/shard_map/ppermute | solution.py:239
  333.4 46.0 %collective-permute-start.48 = (bf16[1024,768]{1,0:T(8,128)(2,1)}, bf16[1024,768]{1,0:T(8,128)(2,1)}, u32[]{:S(2)}, u32[]{:S(2)}) collective-permute-start(bf16[1024,768]{1,0:T(8,128)(2,1)} %pad_maximum_fusion.10), channel_id=1, source_target_pairs={{0,1},{1,0},{2,3},{3,2},{4,5},{5,4},{6,7},{7,6},{8,9},{9,8},{10,11... | collective-permute-start | bytes 4718600 | tf_op jit(solution)/shard_map/ppermute | solution.py:239
  384.2 24.1 %collective-permute-start.45 = (bf16[384,1024]{1,0:T(8,128)(2,1)}, bf16[384,1024]{1,0:T(8,128)(2,1)}, u32[]{:S(2)}, u32[]{:S(2)}) collective-permute-start(bf16[384,1024]{1,0:T(8,128)(2,1)} %convolution_convert_fusion.5), channel_id=1, source_target_pairs={{0,1},{1,0},{2,3},{3,2},{4,5},{5,4},{6,7},{7,6},{8,9},{9,8},{10,11... | collective-permute-start | bytes 2359304 | tf_op jit(solution)/shard_map/ppermute | solution.py:239
  417.4 31.9 %collective-permute-start.49 = (bf16[384,1024]{1,0:T(8,128)(2,1)}, bf16[384,1024]{1,0:T(8,128)(2,1)S(1)}, u32[]{:S(2)}, u32[]{:S(2)}) collective-permute-start(bf16[384,1024]{1,0:T(8,128)(2,1)} %get-tuple-element.373), channel_id=1, source_target_pairs={{0,1},{1,0},{2,3},{3,2},{4,5},{5,4},{6,7},{7,6},{8,9},{9,8},{10,11... | collective-permute-start | bytes 2359304 | tf_op jit(solution)/shard_map/ppermute | solution.py:239
  417.4 33.4 %collective-permute-start.51 = (bf16[384,1024]{1,0:T(8,128)(2,1)}, bf16[384,1024]{1,0:T(8,128)(2,1)S(1)}, u32[]{:S(2)}, u32[]{:S(2)}) collective-permute-start(bf16[384,1024]{1,0:T(8,128)(2,1)} %get-tuple-element.373), channel_id=1, source_target_pairs={{0,2},{1,3},{2,0},{3,1},{4,6},{5,7},{6,4},{7,5},{8,10},{9,11},{10,... | collective-permute-start | bytes 2359304 | tf_op jit(solution)/shard_map/ppermute | solution.py:239
  473.6 47.8 %collective-permute-start.50 = (bf16[384,1024]{1,0:T(8,128)(2,1)}, bf16[384,1024]{1,0:T(8,128)(2,1)}, u32[]{:S(2)}, u32[]{:S(2)}) collective-permute-start(bf16[384,1024]{1,0:T(8,128)(2,1)} %convolution_convert_fusion.9), channel_id=1, source_target_pairs={{0,1},{1,0},{2,3},{3,2},{4,5},{5,4},{6,7},{7,6},{8,9},{9,8},{10,11... | collective-permute-start | bytes 2359304 | tf_op jit(solution)/shard_map/ppermute | solution.py:239
  475.7 47.5 %collective-permute-start.56 = (bf16[384,1024]{1,0:T(8,128)(2,1)}, bf16[384,1024]{1,0:T(8,128)(2,1)}, u32[]{:S(2)}, u32[]{:S(2)}) collective-permute-start(bf16[384,1024]{1,0:T(8,128)(2,1)} %add_convert_fusion.3), channel_id=1, source_target_pairs={{0,2},{1,3},{2,0},{3,1},{4,6},{5,7},{6,4},{7,5},{8,10},{9,11},{10,... | collective-permute-start | bytes 2359304 | tf_op jit(solution)/shard_map/ppermute | solution.py:239
  489.4 23.2 %collective-permute-start.67 = (bf16[128,2048]{1,0:T(8,128)(2,1)}, bf16[128,2048]{1,0:T(8,128)(2,1)}, u32[]{:S(2)}, u32[]{:S(2)}) collective-permute-start(bf16[128,2048]{1,0:T(8,128)(2,1)} %get-tuple-element.264), channel_id=1, source_target_pairs={{8,0},{16,8},{24,16},{28,24},{20,28},{12,20},{4,12},{0,4},{9,1},{1... | collective-permute-start | bytes 1572872 | tf_op jit(solution)/shard_map/ppermute | solution.py:406
  521.4 21.2 %collective-permute-start.69 = (bf16[128,2048]{1,0:T(8,128)(2,1)}, bf16[128,2048]{1,0:T(8,128)(2,1)}, u32[]{:S(2)}, u32[]{:S(2)}) collective-permute-start(bf16[128,2048]{1,0:T(8,128)(2,1)} %get-tuple-element.283), channel_id=1, source_target_pairs={{8,0},{16,8},{24,16},{28,24},{20,28},{12,20},{4,12},{0,4},{9,1},{1... | collective-permute-start | bytes 1572872 | tf_op jit(solution)/shard_map/ppermute | solution.py:406
  553.9 22.1 %collective-permute-start.78 = (bf16[128,2048]{1,0:T(8,128)(2,1)}, bf16[128,2048]{1,0:T(8,128)(2,1)}, u32[]{:S(2)}, u32[]{:S(2)}) collective-permute-start(bf16[128,2048]{1,0:T(8,128)(2,1)} %collective-permute-done.74.refs_1_), channel_id=1, source_target_pairs={{0,8},{8,16},{16,24},{24,28},{28,20},{20,12},{12,4},{4,0},{1,9},{9... | collective-permute-start | bytes 1572872 | tf_op jit(solution)/shard_map/ppermute | solution.py:406
  553.9 22.4 %collective-permute-start.79 = (bf16[128,2048]{1,0:T(8,128)(2,1)}, bf16[128,2048]{1,0:T(8,128)(2,1)}, u32[]{:S(2)}, u32[]{:S(2)}) collective-permute-start(bf16[128,2048]{1,0:T(8,128)(2,1)} %collective-permute-done.75.refs_2_), channel_id=1, source_target_pairs={{8,0},{16,8},{24,16},{28,24},{20,28},{12,20},{4,12},{0,4},{9,1},{1... | collective-permute-start | bytes 1572872 | tf_op jit(solution)/shard_map/ppermute | solution.py:406
  576.3 23.0 %collective-permute-start.82 = (bf16[128,2048]{1,0:T(8,128)(2,1)}, bf16[128,2048]{1,0:T(8,128)(2,1)S(1)}, u32[]{:S(2)}, u32[]{:S(2)}) collective-permute-start(bf16[128,2048]{1,0:T(8,128)(2,1)} %collective-permute-done.78.refs_3_), channel_id=1, source_target_pairs={{0,8},{8,16},{16,24},{24,28},{28,20},{20,12},{12,4},{4,0},{1,9},{9... | collective-permute-start | bytes 1572872 | tf_op jit(solution)/shard_map/ppermute | solution.py:406
  576.4 23.4 %collective-permute-start.83 = (bf16[128,2048]{1,0:T(8,128)(2,1)}, bf16[128,2048]{1,0:T(8,128)(2,1)S(1)}, u32[]{:S(2)}, u32[]{:S(2)}) collective-permute-start(bf16[128,2048]{1,0:T(8,128)(2,1)} %collective-permute-done.79.refs_4_), channel_id=1, source_target_pairs={{8,0},{16,8},{24,16},{28,24},{20,28},{12,20},{4,12},{0,4},{9,1},{1... | collective-permute-start | bytes 1572872 | tf_op jit(solution)/shard_map/ppermute | solution.py:406
  599.3 34.5 %collective-permute-start.59 = (bf16[6,256]{1,0:T(8,128)(2,1)S(1)}, bf16[6,256]{1,0:T(8,128)(2,1)S(1)}, u32[]{:S(2)}, u32[]{:S(2)}) collective-permute-start(bf16[6,256]{1,0:T(8,128)(2,1)S(1)} %get-tuple-element.444), channel_id=1, source_target_pairs={{0,1},{1,0},{2,3},{3,2},{4,5},{5,4},{6,7},{7,6},{8,9},{9,8},{10,11... | collective-permute-start | bytes 9224 | tf_op jit(solution)/shard_map/ppermute | solution.py:239
  609.6 24.2 %collective-permute-start.61 = (bf16[6,256]{1,0:T(8,128)(2,1)S(1)}, bf16[6,256]{1,0:T(8,128)(2,1)S(1)}, u32[]{:S(2)}, u32[]{:S(2)}) collective-permute-start(bf16[6,256]{1,0:T(8,128)(2,1)S(1)} %fusion.184), channel_id=1, source_target_pairs={{0,2},{1,3},{2,0},{3,1},{4,6},{5,7},{6,4},{7,5},{8,10},{9,11},{10,... | collective-permute-start | bytes 9224 | tf_op jit(solution)/shard_map/ppermute | solution.py:239
  (232 other events, 2216.4 us)
Sparse Core Ops, SparseCore 0:
  284.3 92.2 reduce-scatter.1
  384.8 79.6 all-gather.1

commit v11 on v10

--- a/solution.py
+++ b/solution.py
@@ -871,6 +871,8 @@
     token = second_sum
     while middle.done < middle.steps:
         token = middle.step(token)
+        if middle.done == middle.steps:
+            token = (token, middle.came())
         if first.left > 1:
             token = first.step(token)
         if first.done == 3:
@@ -878,6 +880,8 @@
         if first.done == 5:
             second_up, second_down = split_sum(after(second_sum, token), up_second.shape[0])
             token = (token, second_up, second_down)
+    attend_sum = middle.finish(token)
+    token = (token, attend_sum)
     while first.left:
         token = first.step(token)
     pairs = (sum_first, sum_attend, sum_conv, sum_second, sum_final)
@@ -886,8 +890,7 @@
     small_shape = small.shape
     pack = jnp.concatenate([gains.reshape(-1), small.reshape(-1)]).reshape(-1, width)
     pack = sum_cube(after(pack, token), "rows", first.came())
-    attend_sum = middle.finish(token)
-    first_sum = first.finish(attend_sum)
+    first_sum = first.finish()
     pack = pack.reshape(-1)
     gains, small = pack[: gains.size].reshape(gains.shape), pack[gains.size :].reshape(small_shape)
     bias_shape = content_bias.shape

time: 685 us -> 689 us (level)
    ppermute x32, waiting for transfers between devices: 80.8 us -> 73.5 us  [send(): lax.ppermute(item, 'rows', way)]
    unnamed x338 -> x336, local copies, waits for them, and re-layouts: 30.8 us -> 31.9 us
  transfers between devices with their start and end apart: 97 -> 97, of which waited for: 47 -> 48; matrix products, arithmetic and copies ran while one was open for 27% -> 28% of each run, Pallas kernels for 11% -> 11%
where the time goes in v11:
time: 689 us; the launch traced here: 684 us
  waiting for transfers between devices  253 us (37%)
  matrix products  111 us (16%)
  starting transfers between devices  92.1 us (13%)
  other arithmetic  79.1 us (11%)
  Pallas kernels  76.6 us (11%)
  local copies, waits for them, and re-layouts  55.1 us (8%)
  between operations  17 us (2%)
    ppermute x54, waiting for transfers between devices, swap(): return lax.ppermute(values, 'tp', [(i, i ^ distance) for i in range(size)])  157 us
    dot_general x53, matrix products, dot(): lax.dot_general(left, right, (((contract[0],), (contract[1],)), ((), ()))...  111 us
    ppermute x32, waiting for transfers between devices, send(): lax.ppermute(item, 'rows', way)  73.5 us
    ppermute x32, starting transfers between devices, send(): lax.ppermute(item, 'rows', way)  41 us
    ppermute x54, starting transfers between devices, swap(): return lax.ppermute(values, 'tp', [(i, i ^ distance) for i in range(size)])  39.5 us
    unnamed x336, local copies, waits for them, and re-layouts  31.9 us
    pallas_call x10, Pallas kernels, call(): pl.pallas_call(kernel, grid_spec=pltpu.PrefetchScalarGridSpec(num_scalar_...  30.2 us
    pallas_call x1, Pallas kernels, attend_back(): pl.pallas_call(functools.partial(attend_back_kernel, heads), out_shape=(s...  22.2 us
  transfers between devices with their start and end apart: 97, of which 48 were waited for; matrix products, arithmetic and copies ran while one was open for 28% of the time, Pallas kernels for 11%

profile of v11, /device:TPU:0, one launch (start us, length us, event | category | flops | bytes accessed | tf_op | source)
XLA Modules:
  0.0 683.6 jit_solution(12695921927135482866)
XLA Ops:
  51.0 16.9 %collective-permute-done.5 = bf16[384,1024]{1,0:T(8,128)(2,1)S(1)} collective-permute-done((bf16[384,1024]{1,0:T(8,128)(2,1)S(1)}, bf16[384,1024]{1,0:T(8,128)(2,1)S(1)}, u32[]{:S(2)}, u32[]{:S(2)}) %collective-permute-start.5) | collective-permute-done | bytes 786464 | tf_op jit(solution)/shard_map/ppermute | solution.py:239
  75.6 13.7 %collective-permute-done.7 = bf16[384,1024]{1,0:T(8,128)(2,1)S(1)} collective-permute-done((bf16[384,1024]{1,0:T(8,128)(2,1)S(1)}, bf16[384,1024]{1,0:T(8,128)(2,1)S(1)}, u32[]{:S(2)}, u32[]{:S(2)}) %collective-permute-start.7) | collective-permute-done | bytes 786464 | tf_op jit(solution)/shard_map/ppermute | solution.py:239
  100.6 8.9 %shard_map.399 = (bf16[1536,256]{1,0:T(8,128)(2,1)S(1)}, f32[1536,256]{1,0:T(8,128)S(1)}, f32[1536,2]{1,0:T(8,128)S(1)}) custom-call(s32[2,4]{1,0:T(2,128)S(1)} %pad_add_fusion.spans, s32[4]{0:T(128)S(1)} %fusion.201.q_at.k_at, s32[4]{0:T(128)S(1)} %fusion.201.q_at.k_at, bf16[1536,256]{1,0:T(8,128)(2,1)S(1)} %get-tuple-element.486.qc_ref, ...), custom_call_target="tpu_custom_call" | custom-call | flops 4000000000 | bytes 9000000 | tf_op jit(solution)/shard_map/pallas_call | solution.py:156
  109.5 10.1 %collective-permute-done.10 = bf16[1024,256]{1,0:T(8,128)(2,1)S(1)} collective-permute-done((bf16[1024,256]{1,0:T(8,128)(2,1)S(1)}, bf16[1024,256]{1,0:T(8,128)(2,1)S(1)}, u32[]{:S(2)}, u32[]{:S(2)}) %collective-permute-start.10) | collective-permute-done | bytes 524320 | tf_op jit(solution)/shard_map/ppermute | solution.py:239
  119.6 10.4 %collective-permute-done.11 = bf16[256,1024]{1,0:T(8,128)(2,1)S(1)} collective-permute-done((bf16[256,1024]{1,0:T(8,128)(2,1)S(1)}, bf16[256,1024]{1,0:T(8,128)(2,1)S(1)}, u32[]{:S(2)}, u32[]{:S(2)}) %collective-permute-start.11) | collective-permute-done | bytes 524320 | tf_op jit(solution)/shard_map/ppermute | solution.py:239
  137.0 17.0 %collective-permute-done.14 = bf16[384,1024]{1,0:T(8,128)(2,1)S(1)} collective-permute-done((bf16[384,1024]{1,0:T(8,128)(2,1)S(1)}, bf16[384,1024]{1,0:T(8,128)(2,1)S(1)}, u32[]{:S(2)}, u32[]{:S(2)}) %collective-permute-start.14) | collective-permute-done | bytes 786464 | tf_op jit(solution)/shard_map/ppermute | solution.py:239
  174.0 17.2 %collective-permute-done.28 = bf16[384,1024]{1,0:T(8,128)(2,1)S(1)} collective-permute-done((bf16[384,1024]{1,0:T(8,128)(2,1)S(1)}, bf16[384,1024]{1,0:T(8,128)(2,1)S(1)}, u32[]{:S(2)}, u32[]{:S(2)}) %collective-permute-start.28) | collective-permute-done | bytes 786464 | tf_op jit(solution)/shard_map/ppermute | solution.py:239
  204.2 16.7 %collective-permute-done.31 = bf16[384,1024]{1,0:T(8,128)(2,1)S(1)} collective-permute-done((bf16[384,1024]{1,0:T(8,128)(2,1)S(1)}, bf16[384,1024]{1,0:T(8,128)(2,1)S(1)}, u32[]{:S(2)}, u32[]{:S(2)}) %collective-permute-start.31) | collective-permute-done | bytes 786464 | tf_op jit(solution)/shard_map/ppermute | solution.py:239
  226.4 17.2 %collective-permute-done.34 = bf16[384,1024]{1,0:T(8,128)(2,1)S(1)} collective-permute-done((bf16[384,1024]{1,0:T(8,128)(2,1)S(1)}, bf16[384,1024]{1,0:T(8,128)(2,1)S(1)}, u32[]{:S(2)}, u32[]{:S(2)}) %collective-permute-start.34) | collective-permute-done | bytes 786464 | tf_op jit(solution)/shard_map/ppermute | solution.py:239
  263.3 10.8 %collective-permute-done.37 = bf16[384,1024]{1,0:T(8,128)(2,1)S(1)} collective-permute-done((bf16[384,1024]{1,0:T(8,128)(2,1)S(1)}, bf16[384,1024]{1,0:T(8,128)(2,1)S(1)}, u32[]{:S(2)}, u32[]{:S(2)}) %collective-permute-start.37) | collective-permute-done | bytes 786464 | tf_op jit(solution)/shard_map/ppermute | solution.py:239
  315.0 8.1 %collective-permute-done.41 = bf16[384,1024]{1,0:T(8,128)(2,1)S(1)} collective-permute-done((bf16[384,1024]{1,0:T(8,128)(2,1)S(1)}, bf16[384,1024]{1,0:T(8,128)(2,1)S(1)}, u32[]{:S(2)}, u32[]{:S(2)}) %collective-permute-start.41) | collective-permute-done | bytes 786464 | tf_op jit(solution)/shard_map/ppermute | solution.py:239
  339.7 22.2 %shard_map.401 = (bf16[1536,768]{1,0:T(8,128)(2,1)}, bf16[3072,256]{1,0:T(8,128)(2,1)}, f32[8,256]{1,0:T(8,128)S(1)}) custom-call(s32[2,4]{1,0:T(2,128)S(1)} %pad_add_fusion.spans, s32[4]{0:T(128)S(1)} %fusion.201.q_at.k_at, s32[4]{0:T(128)S(1)} %fusion.201.q_at.k_at, bf16[1536,256]{1,0:T(8,128)(2,1)S(1)} %copy-done.7, bf16[1536,256]{1,0:T(8,128)(2,1)S(1)} %copy-done.9, ...), custom_call_target="tpu_custom_call" | custom-call | flops 1000000 | bytes 1000000 | tf_op jit(solution)/shard_map/pallas_call | solution.py:167
  361.9 5.4 collective-permute-done.44
  367.3 9.3 %reduce-scatter.2.cloned.1.call-done = bf16[256,1024]{1,0:T(8,128)(2,1)} async-done(((bf16[2048,1024]{1,0:T(8,128)(2,1)}), bf16[256,1024]{1,0:T(8,128)(2,1)}) %reduce-scatter.2.cloned.1.call-update) | async-done | bytes 524304 | tf_op jit(solution)/shard_map/reduce_scatter | solution.py:521
  421.7 7.9 %collective-permute-done.53.refs_8_ = bf16[64,2048]{1,0:T(8,128)(2,1)S(1)} collective-permute-done((bf16[64,2048]{1,0:T(8,128)(2,1)}, bf16[64,2048]{1,0:T(8,128)(2,1)S(1)}, u32[]{:S(2)}, u32[]{:S(2)}) %collective-permute-start.53) | collective-permute-done | bytes 262176 | tf_op jit(solution)/shard_map/ppermute | solution.py:406
  473.7 5.8 collective-permute-done.63.refs_9_
  486.1 7.8 %fusion.81.refs_0_.refs_2_ = bf16[1024,1024]{1,0:T(8,128)(2,1)} fusion(bf16[768,1024]{1,0:T(8,128)(2,1)} %copy-done.150, bf16[768,1024]{1,0:T(8,128)(2,1)} %fusion.20, bf16[384,1024]{1,0:T(8,128)(2,1)} %copy-done.83, bf16[384,1024]{1,0:T(8,128)(2,1)} %collective-permute-done.2, bf16[384,1024]{1,0:T(8,128)(2,1)} %copy-done.82, ...), kind=kOutput, calls=%fused_computation.103 | convolution fusion | flops 3241148416 | bytes 8388608 | tf_op jit(solution)/shard_map/dot_general | solution.py:232
  501.2 9.1 %collective-permute-start.64 = (bf16[64,2048]{1,0:T(8,128)(2,1)}, bf16[64,2048]{1,0:T(8,128)(2,1)S(1)}, u32[]{:S(2)}, u32[]{:S(2)}) collective-permute-start(bf16[64,2048]{1,0:T(8,128)(2,1)} %get-tuple-element.267), channel_id=1, source_target_pairs={{0,8},{8,16},{16,24},{24,28},{28,20},{20,12},{12,4},{4,0},{1,9},{9... | collective-permute-start | bytes 786440 | tf_op jit(solution)/shard_map/ppermute | solution.py:406
  559.4 6.9 %collective-permute-done.72.refs_4_ = bf16[128,2048]{1,0:T(8,128)(2,1)S(1)} collective-permute-done((bf16[128,2048]{1,0:T(8,128)(2,1)}, bf16[128,2048]{1,0:T(8,128)(2,1)S(1)}, u32[]{:S(2)}, u32[]{:S(2)}) %collective-permute-start.72) | collective-permute-done | bytes 524320 | tf_op jit(solution)/shard_map/ppermute | solution.py:406
  581.9 7.0 %collective-permute-done.76.refs_2_ = bf16[128,2048]{1,0:T(8,128)(2,1)} collective-permute-done((bf16[128,2048]{1,0:T(8,128)(2,1)}, bf16[128,2048]{1,0:T(8,128)(2,1)}, u32[]{:S(2)}, u32[]{:S(2)}) %collective-permute-start.76) | collective-permute-done | bytes 524320 | tf_op jit(solution)/shard_map/ppermute | solution.py:406
  596.0 6.7 slice_convert_fusion
  622.6 9.3 %shard_map.413 = (f32[1024,256]{1,0:T(8,128)}, f32[1024,256]{1,0:T(8,128)}, f32[1024,256]{1,0:T(8,128)}, f32[1024,256]{1,0:T(8,128)}, f32[256,1024]{1,0:T(8,128)...) custom-call(s32[1]{0:T(128)} %bitcast.42.at, bf16[128,2048]{1,0:T(8,128)(2,1)} %shard_map.409.refs_0_, ...), custom_call_target="tpu_custom_call" | custom-call | flops 12582912 | bytes 12582912 | tf_op jit(solution)/shard_map/pallas_call | solution.py:478
  638.0 5.3 collective-permute-done.88.refs_5_
  666.0 6.1 shard_map.414
  (741 shorter events, 411.0 us)
Async XLA Ops:
  7.2 369.4 %reduce-scatter.2.cloned.1.call-start = ((), (), s32[]{:S(2)}) async-start(), calls=%async_computation.1 | async-start | bytes 4718592 | tf_op jit(solution)/shard_map/reduce_scatter | solution.py:521
  12.1 21.6 %collective-permute-start = (bf16[384,1024]{1,0:T(8,128)(2,1)}, bf16[384,1024]{1,0:T(8,128)(2,1)S(1)}, u32[]{:S(2)}, u32[]{:S(2)}) collective-permute-start(bf16[384,1024]{1,0:T(8,128)(2,1)} %get-tuple-element.425), channel_id=1, source_target_pairs={{0,1},{1,0},{2,3},{3,2},{4,5},{5,4},{6,7},{7,6},{8,9},{9,8},{10,11... | collective-permute-start | bytes 2359304 | tf_op jit(solution)/shard_map/ppermute | solution.py:239
  12.6 21.1 %collective-permute-start.2 = (bf16[384,1024]{1,0:T(8,128)(2,1)}, bf16[384,1024]{1,0:T(8,128)(2,1)}, u32[]{:S(2)}, u32[]{:S(2)}) collective-permute-start(bf16[384,1024]{1,0:T(8,128)(2,1)} %get-tuple-element.425), channel_id=1, source_target_pairs={{0,2},{1,3},{2,0},{3,1},{4,6},{5,7},{6,4},{7,5},{8,10},{9,11},{10,... | collective-permute-start | bytes 2359304 | tf_op jit(solution)/shard_map/ppermute | solution.py:239
  15.2 56.8 %collective-permute-start.16 = (bf16[6,256]{1,0:T(8,128)(2,1)S(1)}, bf16[6,256]{1,0:T(8,128)(2,1)S(1)}, u32[]{:S(2)}, u32[]{:S(2)}) collective-permute-start(bf16[6,256]{1,0:T(8,128)(2,1)S(1)} %pad_maximum_fusion.25), channel_id=1, source_target_pairs={{0,2},{1,3},{2,0},{3,1},{4,6},{5,7},{6,4},{7,5},{8,10},{9,11},{10,... | collective-permute-start | bytes 9224 | tf_op jit(solution)/shard_map/ppermute | solution.py:239
  15.3 56.9 %collective-permute-start.15 = (bf16[6,256]{1,0:T(8,128)(2,1)S(1)}, bf16[6,256]{1,0:T(8,128)(2,1)S(1)}, u32[]{:S(2)}, u32[]{:S(2)}) collective-permute-start(bf16[6,256]{1,0:T(8,128)(2,1)S(1)} %pad_maximum_fusion.25), channel_id=1, source_target_pairs={{0,1},{1,0},{2,3},{3,2},{4,5},{5,4},{6,7},{7,6},{8,9},{9,8},{10,11... | collective-permute-start | bytes 9224 | tf_op jit(solution)/shard_map/ppermute | solution.py:239
  93.1 39.1 %collective-permute-start.20 = (bf16[1024,256]{1,0:T(8,128)(2,1)S(1)}, bf16[1024,256]{1,0:T(8,128)(2,1)S(1)}, u32[]{:S(2)}, u32[]{:S(2)}) collective-permute-start(bf16[1024,256]{1,0:T(8,128)(2,1)S(1)} %get-tuple-element.193), channel_id=1, source_target_pairs={{0,1},{1,0},{2,3},{3,2},{4,5},{5,4},{6,7},{7,6},{8,9},{9,8},{10,11... | collective-permute-start | bytes 1572872 | tf_op jit(solution)/shard_map/ppermute | solution.py:239
  96.8 22.8 %collective-permute-start.10 = (bf16[1024,256]{1,0:T(8,128)(2,1)S(1)}, bf16[1024,256]{1,0:T(8,128)(2,1)S(1)}, u32[]{:S(2)}, u32[]{:S(2)}) collective-permute-start(bf16[1024,256]{1,0:T(8,128)(2,1)S(1)} %get-tuple-element.194), channel_id=1, source_target_pairs={{0,2},{1,3},{2,0},{3,1},{4,6},{5,7},{6,4},{7,5},{8,10},{9,11},{10,... | collective-permute-start | bytes 1572872 | tf_op jit(solution)/shard_map/ppermute | solution.py:239
  97.8 32.2 %collective-permute-start.11 = (bf16[256,1024]{1,0:T(8,128)(2,1)S(1)}, bf16[256,1024]{1,0:T(8,128)(2,1)S(1)}, u32[]{:S(2)}, u32[]{:S(2)}) collective-permute-start(bf16[256,1024]{1,0:T(8,128)(2,1)S(1)} %copy-done.97), channel_id=1, source_target_pairs={{0,2},{1,3},{2,0},{3,1},{4,6},{5,7},{6,4},{7,5},{8,10},{9,11},{10,... | collective-permute-start | bytes 1572872 | tf_op jit(solution)/shard_map/ppermute | solution.py:239
  136.0 23.3 %collective-permute-start.25 = (bf16[256,1024]{1,0:T(8,128)(2,1)S(1)}, bf16[256,1024]{1,0:T(8,128)(2,1)S(1)}, u32[]{:S(2)}, u32[]{:S(2)}) collective-permute-start(bf16[256,1024]{1,0:T(8,128)(2,1)S(1)} %collective-permute-done.11), channel_id=1, source_target_pairs={{0,1},{1,0},{2,3},{3,2},{4,5},{5,4},{6,7},{7,6},{8,9},{9,8},{10,11... | collective-permute-start | bytes 1572872 | tf_op jit(solution)/shard_map/ppermute | solution.py:239
  284.2 230.0 %all-gather.2.cloned.1.call-start = ((), (), s32[]{:S(2)}) async-start(), calls=%async_computation.2 | async-start | bytes 4718592 | tf_op jit(solution)/shard_map/all_gather | solution.py:525
  330.5 36.8 %collective-permute-start.44 = (bf16[1024,768]{1,0:T(8,128)(2,1)}, bf16[1024,768]{1,0:T(8,128)(2,1)}, u32[]{:S(2)}, u32[]{:S(2)}) collective-permute-start(bf16[1024,768]{1,0:T(8,128)(2,1)} %add_convert_fusion.2), channel_id=1, source_target_pairs={{0,2},{1,3},{2,0},{3,1},{4,6},{5,7},{6,4},{7,5},{8,10},{9,11},{10,... | collective-permute-start | bytes 4718600 | tf_op jit(solution)/shard_map/ppermute | solution.py:239
  333.5 46.0 %collective-permute-start.48 = (bf16[1024,768]{1,0:T(8,128)(2,1)}, bf16[1024,768]{1,0:T(8,128)(2,1)}, u32[]{:S(2)}, u32[]{:S(2)}) collective-permute-start(bf16[1024,768]{1,0:T(8,128)(2,1)} %pad_maximum_fusion.10), channel_id=1, source_target_pairs={{0,1},{1,0},{2,3},{3,2},{4,5},{5,4},{6,7},{7,6},{8,9},{9,8},{10,11... | collective-permute-start | bytes 4718600 | tf_op jit(solution)/shard_map/ppermute | solution.py:239
  384.2 24.1 %collective-permute-start.45 = (bf16[384,1024]{1,0:T(8,128)(2,1)}, bf16[384,1024]{1,0:T(8,128)(2,1)}, u32[]{:S(2)}, u32[]{:S(2)}) collective-permute-start(bf16[384,1024]{1,0:T(8,128)(2,1)} %convolution_convert_fusion.5), channel_id=1, source_target_pairs={{0,1},{1,0},{2,3},{3,2},{4,5},{5,4},{6,7},{7,6},{8,9},{9,8},{10,11... | collective-permute-start | bytes 2359304 | tf_op jit(solution)/shard_map/ppermute | solution.py:239
  417.4 21.8 %collective-permute-start.51 = (bf16[384,1024]{1,0:T(8,128)(2,1)}, bf16[384,1024]{1,0:T(8,128)(2,1)S(1)}, u32[]{:S(2)}, u32[]{:S(2)}) collective-permute-start(bf16[384,1024]{1,0:T(8,128)(2,1)} %get-tuple-element.373), channel_id=1, source_target_pairs={{0,2},{1,3},{2,0},{3,1},{4,6},{5,7},{6,4},{7,5},{8,10},{9,11},{10,... | collective-permute-start | bytes 2359304 | tf_op jit(solution)/shard_map/ppermute | solution.py:239
  463.1 63.1 %collective-permute-start.50 = (bf16[384,1024]{1,0:T(8,128)(2,1)}, bf16[384,1024]{1,0:T(8,128)(2,1)}, u32[]{:S(2)}, u32[]{:S(2)}) collective-permute-start(bf16[384,1024]{1,0:T(8,128)(2,1)} %convolution_convert_fusion.9), channel_id=1, source_target_pairs={{0,1},{1,0},{2,3},{3,2},{4,5},{5,4},{6,7},{7,6},{8,9},{9,8},{10,11... | collective-permute-start | bytes 2359304 | tf_op jit(solution)/shard_map/ppermute | solution.py:239
  466.1 60.1 %collective-permute-start.56 = (bf16[384,1024]{1,0:T(8,128)(2,1)}, bf16[384,1024]{1,0:T(8,128)(2,1)}, u32[]{:S(2)}, u32[]{:S(2)}) collective-permute-start(bf16[384,1024]{1,0:T(8,128)(2,1)} %add_convert_fusion.3), channel_id=1, source_target_pairs={{0,2},{1,3},{2,0},{3,1},{4,6},{5,7},{6,4},{7,5},{8,10},{9,11},{10,... | collective-permute-start | bytes 2359304 | tf_op jit(solution)/shard_map/ppermute | solution.py:239
  483.6 26.7 %collective-permute-start.66 = (bf16[128,2048]{1,0:T(8,128)(2,1)}, bf16[128,2048]{1,0:T(8,128)(2,1)}, u32[]{:S(2)}, u32[]{:S(2)}) collective-permute-start(bf16[128,2048]{1,0:T(8,128)(2,1)} %get-tuple-element.263), channel_id=1, source_target_pairs={{0,8},{8,16},{16,24},{24,28},{28,20},{20,12},{12,4},{4,0},{1,9},{9... | collective-permute-start | bytes 1572872 | tf_op jit(solution)/shard_map/ppermute | solution.py:406
  486.1 28.2 %collective-permute-start.67 = (bf16[128,2048]{1,0:T(8,128)(2,1)}, bf16[128,2048]{1,0:T(8,128)(2,1)}, u32[]{:S(2)}, u32[]{:S(2)}) collective-permute-start(bf16[128,2048]{1,0:T(8,128)(2,1)} %get-tuple-element.264), channel_id=1, source_target_pairs={{8,0},{16,8},{24,16},{28,24},{20,28},{12,20},{4,12},{0,4},{9,1},{1... | collective-permute-start | bytes 1572872 | tf_op jit(solution)/shard_map/ppermute | solution.py:406
  559.4 20.4 %collective-permute-start.79 = (bf16[128,2048]{1,0:T(8,128)(2,1)}, bf16[128,2048]{1,0:T(8,128)(2,1)}, u32[]{:S(2)}, u32[]{:S(2)}) collective-permute-start(bf16[128,2048]{1,0:T(8,128)(2,1)} %collective-permute-done.75.refs_2_), channel_id=1, source_target_pairs={{8,0},{16,8},{24,16},{28,24},{20,28},{12,20},{4,12},{0,4},{9,1},{1... | collective-permute-start | bytes 1572872 | tf_op jit(solution)/shard_map/ppermute | solution.py:406
  579.8 22.8 %collective-permute-start.82 = (bf16[128,2048]{1,0:T(8,128)(2,1)}, bf16[128,2048]{1,0:T(8,128)(2,1)S(1)}, u32[]{:S(2)}, u32[]{:S(2)}) collective-permute-start(bf16[128,2048]{1,0:T(8,128)(2,1)} %collective-permute-done.78.refs_3_), channel_id=1, source_target_pairs={{0,8},{8,16},{16,24},{24,28},{28,20},{20,12},{12,4},{4,0},{1,9},{9... | collective-permute-start | bytes 1572872 | tf_op jit(solution)/shard_map/ppermute | solution.py:406
  581.9 20.8 %collective-permute-start.83 = (bf16[128,2048]{1,0:T(8,128)(2,1)}, bf16[128,2048]{1,0:T(8,128)(2,1)S(1)}, u32[]{:S(2)}, u32[]{:S(2)}) collective-permute-start(bf16[128,2048]{1,0:T(8,128)(2,1)} %collective-permute-done.79.refs_4_), channel_id=1, source_target_pairs={{8,0},{16,8},{24,16},{28,24},{20,28},{12,20},{4,12},{0,4},{9,1},{1... | collective-permute-start | bytes 1572872 | tf_op jit(solution)/shard_map/ppermute | solution.py:406
  581.9 36.8 %collective-permute-start.60 = (bf16[6,256]{1,0:T(8,128)(2,1)S(1)}, bf16[6,256]{1,0:T(8,128)(2,1)S(1)}, u32[]{:S(2)}, u32[]{:S(2)}) collective-permute-start(bf16[6,256]{1,0:T(8,128)(2,1)S(1)} %get-tuple-element.445), channel_id=1, source_target_pairs={{0,1},{1,0},{2,3},{3,2},{4,5},{5,4},{6,7},{7,6},{8,9},{9,8},{10,11... | collective-permute-start | bytes 9224 | tf_op jit(solution)/shard_map/ppermute | solution.py:239
  611.3 36.1 %collective-permute-start.59 = (bf16[6,256]{1,0:T(8,128)(2,1)S(1)}, bf16[6,256]{1,0:T(8,128)(2,1)S(1)}, u32[]{:S(2)}, u32[]{:S(2)}) collective-permute-start(bf16[6,256]{1,0:T(8,128)(2,1)S(1)} %get-tuple-element.444), channel_id=1, source_target_pairs={{0,1},{1,0},{2,3},{3,2},{4,5},{5,4},{6,7},{7,6},{8,9},{9,8},{10,11... | collective-permute-start | bytes 9224 | tf_op jit(solution)/shard_map/ppermute | solution.py:239
  618.7 28.8 %collective-permute-start.61 = (bf16[6,256]{1,0:T(8,128)(2,1)S(1)}, bf16[6,256]{1,0:T(8,128)(2,1)S(1)}, u32[]{:S(2)}, u32[]{:S(2)}) collective-permute-start(bf16[6,256]{1,0:T(8,128)(2,1)S(1)} %fusion.184), channel_id=1, source_target_pairs={{0,2},{1,3},{2,0},{3,1},{4,6},{5,7},{6,4},{7,5},{8,10},{9,11},{10,... | collective-permute-start | bytes 9224 | tf_op jit(solution)/shard_map/ppermute | solution.py:239
  (231 other events, 2083.1 us)
Sparse Core Ops, SparseCore 0:
  284.4 92.2 reduce-scatter.1
  384.8 80.4 all-gather.1
